TPU v7x, 256 devices: a whole 4x4x8 slice. The times are simulated.
256 devices in a mesh: blk: 16 (over z, y_lo), img: 16 (over x, y_hi, core).
Axes of the slice: x: 4, y: 4 (y_hi: 2, y_lo: 2; y = y_hi * 2 + y_lo), z: 8, core: 2. Of those that a mesh axis runs over, the one named last changes fastest.
Arguments:
- hidden: bfloat16 [16, 2048, 1536], P('img', 'blk'), may hold values from -6 to 6
- text_hidden: bfloat16 [16, 154, 1536], P('img'), may hold values from -6 to 6
- latent: float32 [16, 64, 2048], P('img', 'blk'), may hold values from -6 to 6
- image_mod: float32 [16, 6, 1536], P('img'), may hold values from -10 to 10
- text_mod: float32 [16, 2, 1536], P('img'), may hold values from -3 to 3
- final_mod: float32 [16, 2, 1536], P('img'), may hold values from -3 to 3
- counts: int32 [16], P('img'), may hold values from 512 to 2048, as said below
- step_index: int32 [16], P('img'), may hold values from 0 to 7
- qkv_weight: bfloat16 [1536, 2304], P(None, 'img'), may hold values from -0.21875 to 0.21875
- text_weight: bfloat16 [1536, 1536], replicated, may hold values from -0.21875 to 0.21875
- out_weight: bfloat16 [768, 1536], replicated, may hold values from -0.21875 to 0.21875
- mlp_in_weight: bfloat16 [1536, 3072], P(None, 'img'), may hold values from -0.15625 to 0.15625
- mlp_out_weight: bfloat16 [3072, 1536], P(None, 'img'), may hold values from -0.109375 to 0.109375
- final_weight: bfloat16 [1536, 64], replicated, may hold values from -0.15625 to 0.15625
- conv_weight: bfloat16 [144, 512], replicated, may hold values from -0.5 to 0.5
- conv_bias: float32 [512], replicated, may hold values from -3 to 3
Outputs:
- velocity: float32 [16, 64, 2048], P('img', 'blk')
- next_latent: float32 [16, 64, 2048], P('img', 'blk')
- features: bfloat16 [16, 64, 128, 512], P('img', 'blk')
Inputs may be any that keep to these rules, and one draw needn't show every extreme that they name: `counts`: each count is a multiple of 128; in every draw one image has all 2048 patches.
All inputs are finite; a program needn't handle non-finite values.
Results may differ from a plain program's by a relative error of at most 0.015.
The roundings to bfloat16 on the way count: a program that leaves them out, or rounds other values in their place, can miss the bound.
Values may be sent and summed in bfloat16 or wider, within the bound.
No kernel may reach another device: no remote copies, remote signals or barrier semaphores. Data moves between devices by JAX's collectives and lax.ppermute only.
A program may use at most 128 MiB of HBM per device.

v0:
```python
import jax
import jax.numpy as jnp
from jax import lax
from jax.sharding import PartitionSpec as P

HEAD = 64
CH = 16
HEADS = 12
W_P = 64
STEPS = 8


norm_eps = 1e-06
sigma_shift = 3.0
vae_scale = 1.5305
vae_offset = 0.0609
masked_score = -1e30


def padded(x, sides, width):
    for axis, dim in sides:
        size, length = (lax.axis_size(axis), x.shape[dim])
        up = [(i, (i + 1) % size) for i in range(size - 1)]
        down = [(j, i) for i, j in up]
        last = lax.slice_in_dim(x, length - width, length, axis=dim)
        first = lax.slice_in_dim(x, 0, width, axis=dim)
        before = lax.ppermute(last, axis, up)
        after = lax.ppermute(first, axis, down)
        x = jnp.concatenate([before, x, after], axis=dim)
    return x


def modulate(inputs, shift_row, scale_row):
    values = inputs.astype(jnp.float32)
    center = jnp.mean(values, axis=-1, keepdims=True)
    spread = jnp.mean(jnp.square(values - center), axis=-1, keepdims=True)
    normed = (values - center) * lax.rsqrt(spread + norm_eps)
    return (normed * (1.0 + scale_row) + shift_row).astype(jnp.bfloat16)


def plan(step_value):
    remain = 1.0 - step_value / STEPS
    return sigma_shift * remain / (1.0 + (sigma_shift - 1.0) * remain)


def absorb(running, queries, key_rows, value_rows, key_valid):
    run_max, run_sum, run_out = running
    key_heads = key_rows.reshape(key_rows.shape[0], HEADS, HEAD)
    value_heads = value_rows.reshape(value_rows.shape[0], HEADS, HEAD)
    scores = (
        jnp.einsum("qhd,khd->hqk", queries, key_heads, preferred_element_type=jnp.float32) * 0.125
    )
    scores = jnp.where(key_valid[None, None, :], scores, masked_score)
    new_max = jnp.maximum(run_max, jnp.max(scores, axis=-1))
    factor = jnp.exp(run_max - new_max)
    numer = jnp.exp(scores - new_max[:, :, None])
    run_sum = run_sum * factor + jnp.sum(numer, axis=-1)
    run_out = run_out * factor[:, :, None] + jnp.einsum(
        "hqk,khd->hqd", numer.astype(jnp.bfloat16), value_heads, preferred_element_type=jnp.float32
    )
    return (new_max, run_sum, run_out)


def per_device(
    hidden,
    text_hidden,
    latent,
    image_mod,
    text_mod,
    final_mod,
    counts,
    step_index,
    qkv_weight,
    text_weight,
    out_weight,
    mlp_in_weight,
    mlp_out_weight,
    final_weight,
    conv_weight,
    conv_bias,
):
    tok_rows = hidden.shape[1]
    width_attn = HEADS * HEAD
    patch_count = counts[0]
    image_terms = image_mod[0]
    image_in = modulate(hidden[0], image_terms[0], image_terms[1])
    text_in = modulate(text_hidden[0], text_mod[0, 0], text_mod[0, 1])
    text_kv = jnp.dot(text_in, text_weight, preferred_element_type=jnp.float32).astype(jnp.bfloat16)
    qkv_all = jnp.dot(
        image_in,
        lax.all_gather(qkv_weight, "img", axis=1, tiled=True),
        preferred_element_type=jnp.float32,
    ).astype(jnp.bfloat16)
    queries = qkv_all[:, :width_attn].reshape(tok_rows, HEADS, HEAD)
    own_keys = qkv_all[:, width_attn : 2 * width_attn]
    own_values = qkv_all[:, 2 * width_attn :]
    start_state = (
        jnp.full((HEADS, tok_rows), -jnp.inf, jnp.float32),
        jnp.zeros((HEADS, tok_rows), jnp.float32),
        jnp.zeros((HEADS, tok_rows, HEAD), jnp.float32),
    )
    text_valid = jnp.ones((text_kv.shape[0],), dtype=bool)
    text_state = absorb(
        start_state, queries, text_kv[:, :width_attn], text_kv[:, width_attn:], text_valid
    )
    folded = text_state
    key_rows = lax.all_gather(own_keys, "blk", axis=0, tiled=True)
    value_rows = lax.all_gather(own_values, "blk", axis=0, tiled=True)
    blocks = key_rows.shape[0] // tok_rows
    key_blocks = key_rows.reshape(blocks, tok_rows, width_attn)
    value_blocks = value_rows.reshape(blocks, tok_rows, width_attn)

    def visit(running, block_item):
        key_block, value_block, block_pos = block_item
        block_first = block_pos * tok_rows
        key_valid = block_first + jnp.arange(tok_rows, dtype=jnp.int32) < patch_count
        running = absorb(running, queries, key_block, value_block, key_valid)
        return (running, None)

    folded, _ = lax.scan(
        visit, folded, (key_blocks, value_blocks, jnp.arange(blocks, dtype=jnp.int32))
    )
    run_max, run_sum, run_out = folded
    attended = (
        (run_out / run_sum[:, :, None])
        .transpose(1, 0, 2)
        .reshape(tok_rows, width_attn)
        .astype(jnp.bfloat16)
    )
    projected = jnp.dot(attended, out_weight, preferred_element_type=jnp.float32)
    updated = hidden[0].astype(jnp.float32) + image_terms[2] * projected
    mlp_in = modulate(updated, image_terms[3], image_terms[4])
    mlp_hidden = jax.nn.gelu(
        jnp.dot(
            mlp_in,
            lax.all_gather(mlp_in_weight, "img", axis=1, tiled=True),
            preferred_element_type=jnp.float32,
        ),
        approximate=True,
    ).astype(jnp.bfloat16)
    mlp_out = jnp.dot(
        mlp_hidden,
        lax.all_gather(mlp_out_weight, "img", axis=1, tiled=True),
        preferred_element_type=jnp.float32,
    )
    refined = updated + image_terms[5] * mlp_out
    final_in = modulate(refined, final_mod[0, 0], final_mod[0, 1])
    predicted = jnp.dot(final_in, final_weight, preferred_element_type=jnp.float32)
    patch_rows = tok_rows // W_P
    lat_rows = 2 * patch_rows
    vel_lat = (
        predicted.reshape(patch_rows, W_P, 2, 2, CH)
        .transpose(0, 2, 1, 3, 4)
        .reshape(lat_rows, 2 * W_P * CH)
    )
    global_rows = lax.axis_index("blk") * lat_rows + jnp.arange(lat_rows, dtype=jnp.int32)
    live_rows = (global_rows < 2 * (patch_count // W_P))[:, None]
    velocity = jnp.where(live_rows, vel_lat, 0.0)
    step_value = step_index[0].astype(jnp.float32)
    sigma_gap = plan(step_value + 1.0) - plan(step_value)
    next_lat = jnp.where(live_rows, latent[0] + sigma_gap * vel_lat, 0.0)
    scaled = jnp.where(live_rows, next_lat / vae_scale + vae_offset, 0.0).astype(jnp.bfloat16)
    framed = padded(scaled, (("blk", 0),), 1)
    padded_grid = jnp.pad(framed.reshape(lat_rows + 2, 2 * W_P, CH), ((0, 0), (1, 1), (0, 0)))
    columns = jnp.concatenate(
        [
            padded_grid[row_off : row_off + lat_rows, col_off : col_off + 2 * W_P, :]
            for row_off in range(3)
            for col_off in range(3)
        ],
        axis=-1,
    ).reshape(lat_rows * 2 * W_P, 9 * CH)
    feature = jnp.dot(columns, conv_weight, preferred_element_type=jnp.float32) + conv_bias
    feature = jnp.where(live_rows[:, :, None], feature.reshape(lat_rows, 2 * W_P, -1), 0.0).astype(
        jnp.bfloat16
    )
    return (velocity[None], next_lat[None], feature[None])


def solution(mesh):
    placed = (
        P("img", "blk", None),
        P("img", None, None),
        P("img", "blk", None),
        P("img", None, None),
        P("img", None, None),
        P("img", None, None),
        P("img"),
        P("img"),
        P(None, "img"),
        P(),
        P(),
        P(None, "img"),
        P(None, "img"),
        P(),
        P(),
        P(),
    )
    return jax.shard_map(
        per_device,
        mesh=mesh,
        in_specs=placed,
        out_specs=(P("img", "blk", None), P("img", "blk", None), P("img", "blk", None, None)),
        check_vma=False,
    )
```

profile of v0, /device:TPU:104, one launch (start us, length us, event | category | flops | bytes accessed | tf_op | source)
XLA Modules:
  0.0 461.3 jit_solution(7038986041568204380)
XLA Ops:
  9.3 1.4 slice_reduce_fusion.2
  13.1 71.2 %all-gather.6.cloned.1.call-done = bf16[1536,2304]{0,1:T(8,128)(2,1)} async-done(((bf16[1536,144]{0,1:T(8,128)(2,1)}), bf16[1536,2304]{0,1:T(8,128)(2,1)}) %all-gather.6.cloned.1.call-update) | async-done | bytes 7077904 | tf_op jit(solution)/shard_map/all_gather | solution.py:91
  84.3 5.6 %convolution_convert_fusion = bf16[128,2304]{1,0:T(8,128)(2,1)S(1)} fusion(bf16[1536,2304]{0,1:T(8,128)(2,1)} %all-gather.6.cloned.1.call-done, bf16[1,128,1536]{2,1,0:T(8,128)(2,1)} %param.18, f32[1536]{0:T(1024)S(1)} %get-tuple-element.72, f32[1536]{0:T(1024)S(1)} %get-tuple-element.76, f32[128]{0:T(128)S(1)} %add_rsqrt_fusion.3, ...), kind=kOutput, calls=%fused_computation.13 | convolution fusion | flops 907444224 | bytes 8074240 | tf_op jit(solution)/shard_map/dot_general | solution.py:89
  93.8 3.3 convolution_convert_fusion.1
  100.4 1.8 copy.32
  105.3 64.7 %all-gather.8.cloned.1.call-done = bf16[2048,768]{1,0:T(8,128)(2,1)} async-done(((bf16[128,768]{1,0:T(8,128)(2,1)}), bf16[2048,768]{1,0:T(8,128)(2,1)}) %all-gather.8.cloned.1.call-update) | async-done | bytes 3145744 | tf_op jit(solution)/shard_map/all_gather | solution.py:107
  170.0 81.6 %all-gather.10.cloned.1.call-done = bf16[2048,768]{1,0:T(8,128)(2,1)} async-done(((bf16[128,768]{1,0:T(8,128)(2,1)}), bf16[2048,768]{1,0:T(8,128)(2,1)}) %all-gather.10.cloned.1.call-update) | async-done | bytes 3145744 | tf_op jit(solution)/shard_map/all_gather | solution.py:108
  252.1 138.2 %while.14 = (s32[]{:T(128)}, f32[12,128]{1,0:T(8,128)S(1)}, f32[12,128]{1,0:T(8,128)}, f32[12,128,64]{1,2,0:T(8,128)}, s32[16]{0:T(128)}, /*index=5*/s32[]{:T(12...) while((s32[]{:T(128)}, f32[12,128]{1,0:T(8,128)S(1)}, ...), condition=%wide.region_9.10_spmd, body=%wide.region_6.9_spmd.sunk | while | flops 51907840 | bytes 5407121 | solution.py:120
  258.7 2.0 convolution_add_fusion.4
  267.3 2.0 convolution_add_fusion.4
  276.0 2.0 convolution_add_fusion.4
  284.6 2.0 convolution_add_fusion.4
  293.2 2.0 convolution_add_fusion.4
  301.9 2.0 convolution_add_fusion.4
  310.5 2.0 convolution_add_fusion.4
  319.2 2.0 convolution_add_fusion.4
  327.8 2.0 convolution_add_fusion.4
  336.5 2.0 convolution_add_fusion.4
  345.1 2.0 convolution_add_fusion.4
  353.7 2.0 convolution_add_fusion.4
  362.3 2.0 convolution_add_fusion.4
  371.0 2.0 convolution_add_fusion.4
  379.7 2.0 convolution_add_fusion.4
  388.3 2.0 convolution_add_fusion.4
  391.4 1.6 fusion.76
  393.3 25.1 %all-gather.14.cloned.1.call-done = bf16[3072,1536]{0,1:T(8,128)(2,1)} async-done(((bf16[3072,96]{0,1:T(8,128)(2,1)}), bf16[3072,1536]{0,1:T(8,128)(2,1)}) %all-gather.14.cloned.1.call-update) | async-done | bytes 9437200 | tf_op jit(solution)/shard_map/all_gather | solution.py:143
  418.4 13.7 %fusion.77 = (f32[128]{0:T(128)S(1)}, f32[128,1536]{1,0:T(8,128)}) fusion(f32[128,1536]{1,0:T(8,128)S(1)} %get-tuple-element.127, bf16[3072,1536]{0,1:T(8,128)(2,1)} %all-gather.14.cloned.1.call-done, bf16[1536,3072]{0,1:T(8,128)(2,1)} %all-gather.12.cloned.1.call-done, f32[1536]{0:T(1024)S(1)} %copy-done.9, f32[1536]{0:T(1024)S(1)} %copy-done.7, ...), kind=kOutput, calls=%fused_computation.130 | convolution fusion | flops 2421030912 | bytes 20467200 | tf_op jit(solution)/shard_map/dot_general | solution.py:141
  433.6 1.5 fusion.58
  435.9 5.6 %collective-permute-start = (bf16[1,2048]{1,0:T(2,128)(2,1)S(1)}, bf16[1,2048]{1,0:T(2,128)(2,1)S(1)}, u32[]{:S(2)}, u32[]{:S(2)}) collective-permute-start(bf16[1,2048]{1,0:T(2,128)(2,1)S(1)} %get-tuple-element.120), channel_id=1, source_target_pairs={{0,16},{16,32},{32,48},{48,64},{64,80},{80,96},{96,112},{112,128},... | collective-permute-start | bytes 12296 | tf_op jit(solution)/shard_map/ppermute | solution.py:27
  441.5 1.9 collective-permute-start.1
  445.2 3.9 collective-permute-done.1
  450.5 2.0 concatenate.40
  (253 shorter events, 118.0 us)
Async XLA Ops:
  7.2 384.2 %copy-start = (bf16[768,1536]{1,0:T(8,128)(2,1)S(1)}, bf16[768,1536]{1,0:T(8,128)(2,1)}, u32[]{:S(2)}) copy-start(bf16[768,1536]{1,0:T(8,128)(2,1)} %param.28) | copy-start | bytes 7077892
  7.2 77.1 %all-gather.6.cloned.1.call-start = ((), (), s32[]{:S(2)}) async-start(), calls=%async_computation | async-start | bytes 7520256 | tf_op jit(solution)/shard_map/all_gather | solution.py:91
  7.9 162.1 %all-gather.8.cloned.1.call-start = ((), (), s32[]{:S(2)}) async-start(), calls=%async_computation.1 | async-start | bytes 3342336 | tf_op jit(solution)/shard_map/all_gather | solution.py:107
  84.3 9.0 %copy-start.5 = (f32[1,2,1536]{2,1,0:T(2,128)S(1)}, f32[1,2,1536]{2,1,0:T(2,128)}, u32[]{:S(2)}) copy-start(f32[1,2,1536]{2,1,0:T(2,128)} %param.22) | copy-start | bytes 36868
  89.9 3.5 copy-start.1
  90.7 160.9 %all-gather.10.cloned.1.call-start = ((), (), s32[]{:S(2)}) async-start(), calls=%async_computation.2 | async-start | bytes 3342336 | tf_op jit(solution)/shard_map/all_gather | solution.py:108
  91.5 301.8 %all-gather.12.cloned.1.call-start = ((), (), s32[]{:S(2)}) async-start(), calls=%async_computation.3 | async-start | bytes 10027008 | tf_op jit(solution)/shard_map/all_gather | solution.py:136
  92.1 326.3 %all-gather.14.cloned.1.call-start = ((), (), s32[]{:S(2)}) async-start(), calls=%async_computation.4 | async-start | bytes 10027008 | tf_op jit(solution)/shard_map/all_gather | solution.py:143
  93.8 3.8 copy-start.6
  93.8 5.6 %copy-start.3 = (f32[1,4,2048]{2,1,0:T(4,128)S(1)}, f32[1,4,2048]{2,1,0:T(4,128)}, u32[]{:S(2)}) copy-start(f32[1,4,2048]{2,1,0:T(4,128)} %param.20) | copy-start | bytes 98308
  98.9 153.2 %copy-start.12 = (pred[4]{0:T(512)(128)(4,1)}, pred[4]{0:T(512)(128)(4,1)S(1)}, u32[]{:S(2)}) copy-start(pred[4]{0:T(512)(128)(4,1)S(1)} %add_compare_fusion.1) | copy-start | bytes 16
  390.3 28.1 %copy-start.7 = (f32[1536]{0:T(1024)S(1)}, f32[1536]{0:T(1024)}, u32[]{:S(2)}) copy-start(f32[1536]{0:T(1024)} %get-tuple-element.75) | copy-start | bytes 18436
  390.3 28.1 %copy-start.8 = (f32[1536]{0:T(1024)S(1)}, f32[1536]{0:T(1024)}, u32[]{:S(2)}) copy-start(f32[1536]{0:T(1024)} %get-tuple-element.71) | copy-start | bytes 18436
  390.3 28.1 %copy-start.9 = (f32[1536]{0:T(1024)S(1)}, f32[1536]{0:T(1024)}, u32[]{:S(2)}) copy-start(f32[1536]{0:T(1024)} %get-tuple-element.74) | copy-start | bytes 18436
  418.4 15.2 %copy-start.10 = (f32[1536]{0:T(1024)S(1)}, f32[1536]{0:T(1024)}, u32[]{:S(2)}) copy-start(f32[1536]{0:T(1024)} %get-tuple-element.77) | copy-start | bytes 18436
  418.4 15.2 %copy-start.11 = (f32[1536]{0:T(1024)S(1)}, f32[1536]{0:T(1024)}, u32[]{:S(2)}) copy-start(f32[1536]{0:T(1024)} %get-tuple-element.78) | copy-start | bytes 18436
  418.4 15.2 %copy-start.15 = (bf16[1536,64]{0,1:T(8,128)(2,1)S(1)}, bf16[1536,64]{0,1:T(8,128)(2,1)}, u32[]{:S(2)}) copy-start(bf16[1536,64]{0,1:T(8,128)(2,1)} %param.31) | copy-start | bytes 589828
  418.4 17.4 %copy-start.4 = (f32[1,4,2048]{2,1,0:T(4,128)S(1)}, f32[1,4,2048]{2,1,0:T(4,128)}, u32[]{:S(2)}) copy-start(f32[1,4,2048]{2,1,0:T(4,128)} %param.20) | copy-start | bytes 98308
  418.4 17.4 %copy-start.13 = (pred[4]{0:T(512)(128)(4,1)S(1)}, pred[4]{0:T(512)(128)(4,1)}, u32[]{:S(2)}) copy-start(pred[4]{0:T(512)(128)(4,1)} %copy-done.12) | copy-start | bytes 16
  432.1 12.3 %copy-start.2 = (f32[512,16]{1,0:T(8,128)S(1)}, f32[512,16]{1,0:T(8,128)}, u32[]{:S(2)}) copy-start(f32[512,16]{1,0:T(8,128)} %squeeze.13) | copy-start | bytes 98308
  432.1 12.3 %copy-start.14 = (pred[512]{0:T(512)(128)(4,1)S(1)}, pred[512]{0:T(512)(128)(4,1)}, u32[]{:S(2)}) copy-start(pred[512]{0:T(512)(128)(4,1)} %broadcast_bitcast_fusion) | copy-start | bytes 1540
  433.6 18.9 %copy-start.16 = (f32[512]{0:T(512)S(1)}, f32[512]{0:T(512)}, u32[]{:S(2)}) copy-start(f32[512]{0:T(512)} %param.33) | copy-start | bytes 6148
  435.9 9.3 %collective-permute-start = (bf16[1,2048]{1,0:T(2,128)(2,1)S(1)}, bf16[1,2048]{1,0:T(2,128)(2,1)S(1)}, u32[]{:S(2)}, u32[]{:S(2)}) collective-permute-start(bf16[1,2048]{1,0:T(2,128)(2,1)S(1)} %get-tuple-element.120), channel_id=1, source_target_pairs={{0,16},{16,32},{32,48},{48,64},{64,80},{80,96},{96,112},{112,128},... | collective-permute-start | bytes 12296 | tf_op jit(solution)/shard_map/ppermute | solution.py:27
  441.5 7.7 %collective-permute-start.1 = (bf16[1,2048]{1,0:T(2,128)(2,1)S(1)}, bf16[1,2048]{1,0:T(2,128)(2,1)S(1)}, u32[]{:S(2)}, u32[]{:S(2)}) collective-permute-start(bf16[1,2048]{1,0:T(2,128)(2,1)S(1)} %get-tuple-element.121), channel_id=1, source_target_pairs={{16,0},{32,16},{48,32},{64,48},{80,64},{96,80},{112,96},{128,112},... | collective-permute-start | bytes 12296 | tf_op jit(solution)/shard_map/ppermute | solution.py:28
Sparse Core Ops, SparseCore 0:
  10.7 73.5 all-gather.5
  90.9 79.1 all-gather.7
  171.8 79.7 all-gather.9
  254.2 81.4 all-gather.11
  338.2 80.0 all-gather.13
where the time goes:
time: 464 us; the launch traced here: 461 us
  waiting for transfers between devices  249 us (54%)
  matrix products  81.7 us (18%)
  local copies, waits for them, and re-layouts  52.2 us (11%)
  other arithmetic  44.4 us (10%)
  between operations  15.6 us (3%)
  loops' own time  10.9 us (2%)
  starting transfers between devices  7.67 us (2%)
    all_gather x1, waiting for transfers between devices, per_device(): value_rows = lax.all_gather(own_values, 'blk', axis=0, tiled=True)  81.6 us
    all_gather x1, waiting for transfers between devices, per_device(): lax.all_gather(qkv_weight, 'img', axis=1, tiled=True)  71.2 us
    all_gather x1, waiting for transfers between devices, per_device(): key_rows = lax.all_gather(own_keys, 'blk', axis=0, tiled=True)  64.7 us
    dynamic_slice x64, local copies, waits for them, and re-layouts, per_device(): lax.scan(visit, folded, (key_blocks, value_blocks, jnp.arange(blocks, dty...  41.5 us
    dot_general x17, matrix products, absorb(): jnp.einsum('hqk,khd->hqd', numer.astype(jnp.bfloat16), value_heads, prefe...  33.1 us
    all_gather x1, waiting for transfers between devices, per_device(): lax.all_gather(mlp_out_weight, 'img', axis=1, tiled=True)  25.1 us
    dot_general x17, matrix products, absorb(): jnp.einsum('qhd,khd->hqk', queries, key_heads, preferred_element_type=jnp...  21.6 us
    add x16, other arithmetic, absorb(): run_sum = run_sum * factor + jnp.sum(numer, axis=-1)  20.8 us
  transfers between devices with their start and end apart: 7, of which 5 were waited for; matrix products, arithmetic and copies ran while one was open for 32% of the time, Pallas kernels for 0%

commit v1 on v0

v1 whole, which is shorter than its diff:
```python
import jax
import jax.numpy as jnp
from jax import lax
from jax.experimental import pallas as pl
from jax.experimental.pallas import tpu as pltpu
from jax.sharding import PartitionSpec as P

HEAD = 64
CH = 16
HEADS = 12
W_P = 64
STEPS = 8

norm_eps = 1e-06
sigma_shift = 3.0
vae_scale = 1.5305
vae_offset = 0.0609
masked_score = -1e30

F32 = jnp.float32
BF16 = jnp.bfloat16


def modulate(inputs, shift_row, scale_row):
    values = inputs.astype(F32)
    center = jnp.mean(values, axis=-1, keepdims=True)
    spread = jnp.mean(jnp.square(values - center), axis=-1, keepdims=True)
    normed = (values - center) * lax.rsqrt(spread + norm_eps)
    return (normed * (1.0 + scale_row) + shift_row).astype(BF16)


def plan(step_value):
    remain = 1.0 - step_value / STEPS
    return sigma_shift * remain / (1.0 + (sigma_shift - 1.0) * remain)


def swap(x, axis, bits):
    return lax.ppermute(x, axis, [(i, i ^ bits) for i in range(lax.axis_size(axis))])


def vmem_specs(count):
    return [pl.BlockSpec(memory_space=pltpu.VMEM)] * count


OFFSETS = ((0, 0), (-1, 0), (1, 0), (0, 1), (2, 0), (-1, 1), (1, 1), (2, 1))


def ring(x, axis, step):
    size = lax.axis_size(axis)
    return lax.ppermute(x, axis, [(i, (i + step) % size) for i in range(size)])


def ring_first(x):
    return ring(x, "img", 4), ring(x, "img", -4), swap(x, "img", 2)


def ring_second(left, right, across):
    half = left.shape[0] // 2
    return (
        ring(left[:half], "img", 4),
        ring(right[half:], "img", -4),
        ring(across, "img", 4),
        ring(across, "img", -4),
    )


def ring_third(low, high):
    far = jnp.concatenate([low, high], axis=0)
    return far, swap(far, "img", 2)


def place_of(chip, k):
    dx, dy = OFFSETS[k]
    column = jnp.bitwise_and(chip // 2 + dx + 4, 3)
    return 2 * column + jnp.bitwise_xor(jnp.bitwise_and(chip, 1), dy)


def qkv_body(chip_ref, own_x, peer_x, *refs):
    weights, (own_out, peer_out) = refs[:-2], refs[-2:]
    rows = own_x.shape[0]
    both = jnp.concatenate([own_x[...], peer_x[...]], axis=0)
    for k, weight in enumerate(weights):
        part = lax.dot_general(
            weight[...], both, (((1,), (1,)), ((), ())), preferred_element_type=F32
        ).astype(BF16)
        place = place_of(chip_ref[0], k)
        own_out[place] = part[:, :rows]
        peer_out[place] = part[:, rows:]


def project_qkv(chip, own_x, peer_x, weights):
    cols, rows = weights[0].shape[0], own_x.shape[0]
    shape = jax.ShapeDtypeStruct((len(weights), cols, rows), BF16)
    flops = 4 * len(weights) * cols * rows * own_x.shape[1]
    return pl.pallas_call(
        qkv_body,
        out_shape=(shape, shape),
        in_specs=[pl.BlockSpec(memory_space=pltpu.SMEM)] + vmem_specs(2 + len(weights)),
        out_specs=tuple(vmem_specs(2)),
        compiler_params=pltpu.CompilerParams(vmem_limit_bytes=32 << 20),
        cost_estimate=pl.CostEstimate(flops=flops, bytes_accessed=5 << 20, transcendentals=0),
        name="project_qkv",
    )(chip, own_x, peer_x, *weights)


def attend_body(count_ref, parts, text, out, keys, values, queries):
    blocks, _, rows = parts.shape
    text_blocks = text.shape[1] // rows
    text_len = 154
    tile = 2 * rows
    lane = lax.broadcasted_iota(jnp.int32, (8, rows), 1)
    row = lax.broadcasted_iota(jnp.int32, (8, rows), 0)
    top = row == 0
    zeros = jnp.zeros((HEAD - 8, rows), F32)

    def place_keys(index, key_part, limit):
        bias = jnp.where(jnp.logical_and(top, lane >= limit), masked_score, 0.0)
        full = jnp.concatenate([key_part.astype(F32), bias, zeros], axis=0)
        keys[pl.ds(index * rows, rows), :] = full.T.astype(BF16)

    ones = jnp.concatenate([jnp.where(top, 1.0, 0.0).astype(F32), zeros], axis=0)
    for b in range(blocks):
        part = parts[b]
        place_keys(b, part[HEAD : 2 * HEAD], count_ref[0] - b * rows)
        values[:, b * rows : (b + 1) * rows] = part[2 * HEAD :]
        scaled = part[:HEAD].astype(F32) * 0.125
        queries[:, b * rows : (b + 1) * rows] = jnp.concatenate([scaled, ones], axis=0).astype(BF16)
    for t in range(text_blocks):
        cols = slice(t * rows, (t + 1) * rows)
        place_keys(blocks + t, text[:HEAD, cols], text_len - t * rows)
        values[:, (blocks + t) * rows : (blocks + t + 1) * rows] = text[HEAD:, cols]

    def step(t, carry):
        first = pl.multiple_of(t * tile, tile)
        scores = jnp.dot(keys[...], queries[:, pl.ds(first, tile)], preferred_element_type=F32)
        top_score = jnp.max(scores, axis=0, keepdims=True)
        numer = jnp.exp(scores - top_score)
        total = jnp.sum(numer, axis=0, keepdims=True)
        mixed = jnp.dot(values[...], numer.astype(BF16), preferred_element_type=F32) / total
        mixed = mixed.astype(BF16)
        out[2 * t] = mixed[:, :rows]
        out[2 * t + 1] = mixed[:, rows:]
        return carry

    lax.fori_loop(0, blocks // 2, step, 0)


def attend(count, parts, text):
    blocks, _, rows = parts.shape
    keys = blocks * rows + text.shape[1]
    queries = blocks * rows
    return pl.pallas_call(
        attend_body,
        out_shape=jax.ShapeDtypeStruct((blocks, HEAD, rows), BF16),
        in_specs=[pl.BlockSpec(memory_space=pltpu.SMEM)] + vmem_specs(2),
        out_specs=vmem_specs(1)[0],
        scratch_shapes=[
            pltpu.VMEM((keys, 2 * HEAD), BF16),
            pltpu.VMEM((HEAD, keys), BF16),
            pltpu.VMEM((2 * HEAD, queries), BF16),
        ],
        compiler_params=pltpu.CompilerParams(vmem_limit_bytes=40 << 20),
        cost_estimate=pl.CostEstimate(
            flops=4 * keys * queries * HEAD, bytes_accessed=2 << 20, transcendentals=keys * queries
        ),
        name="attend",
    )(count, parts, text)


def layer_norm(values, shift_row, scale_row):
    center = jnp.mean(values, axis=-1, keepdims=True)
    spread = jnp.mean(jnp.square(values - center), axis=-1, keepdims=True)
    normed = (values - center) * lax.rsqrt(spread + norm_eps)
    return (normed * (1.0 + scale_row) + shift_row).astype(BF16)


def gelu(v):
    return 0.5 * v * (1.0 + jnp.tanh(0.7978845608028654 * (v + 0.044715 * v * v * v)))


def middle_body(mixed, hidden, mods, out_w, updated, mlp_in):
    attended = mixed[...].astype(F32).T.astype(BF16)
    projected = jnp.dot(attended, out_w[...], preferred_element_type=F32)
    now = hidden[...].astype(F32) + mods[2:3] * projected
    updated[...] = now
    mlp_in[...] = layer_norm(now, mods[3:4], mods[4:5])


def middle(mixed, hidden, mods, out_w):
    rows, width = hidden.shape
    return pl.pallas_call(
        middle_body,
        out_shape=(
            jax.ShapeDtypeStruct((rows, width), F32),
            jax.ShapeDtypeStruct((rows, width), BF16),
        ),
        in_specs=vmem_specs(4),
        out_specs=tuple(vmem_specs(2)),
        compiler_params=pltpu.CompilerParams(vmem_limit_bytes=24 << 20),
        cost_estimate=pl.CostEstimate(
            flops=2 * mixed.shape[0] * rows * width, bytes_accessed=5 << 20, transcendentals=rows
        ),
        name="middle",
    )(mixed, hidden, mods, out_w)


def first_body(chip_ref, own_x, peer_x, *refs):
    weights, out = refs[:-1], refs[-1]
    both = jnp.concatenate([own_x[...], peer_x[...]], axis=0)
    cols = out.shape[1]
    for k, weight in enumerate(weights):
        part = lax.dot_general(
            weight[:cols], both, (((1,), (1,)), ((), ())), preferred_element_type=F32
        )
        out[place_of(chip_ref[0], k)] = gelu(part).astype(BF16)


def mlp_first(chip, own_x, peer_x, weights):
    rows, width = own_x.shape
    cols = weights[0].shape[0] // 2
    count = len(weights)
    return pl.pallas_call(
        first_body,
        out_shape=jax.ShapeDtypeStruct((count, cols, 2 * rows), BF16),
        in_specs=[pl.BlockSpec(memory_space=pltpu.SMEM)] + vmem_specs(2 + count),
        out_specs=vmem_specs(1)[0],
        compiler_params=pltpu.CompilerParams(vmem_limit_bytes=32 << 20),
        cost_estimate=pl.CostEstimate(
            flops=4 * count * cols * rows * width,
            bytes_accessed=6 << 20,
            transcendentals=2 * count * cols * rows,
        ),
        name="mlp_first",
    )(chip, own_x, peer_x, *weights)


def second_body(chip_ref, core_ref, own_act, peer_act, *refs):
    weights, (own_out, peer_out), act = refs[:-3], refs[-3:-1], refs[-1]
    count, cols, tokens = own_act.shape
    core = core_ref[0]
    for c in range(count):
        start = pl.multiple_of((2 * c + core) * cols, cols)
        act[pl.ds(start, cols), :] = own_act[c]
        start = pl.multiple_of((2 * c + 1 - core) * cols, cols)
        act[pl.ds(start, cols), : tokens // 2] = peer_act[c, :, tokens // 2 :]
        act[pl.ds(start, cols), tokens // 2 :] = peer_act[c, :, : tokens // 2]
    width = weights[0].shape[1]
    half = cols // 2
    for k, weight in enumerate(weights):
        part = jnp.dot(weight[cols : cols + half], act[:width], preferred_element_type=F32)
        part += jnp.dot(weight[cols + half :], act[width:], preferred_element_type=F32)
        place = place_of(chip_ref[0], k)
        own_out[place] = part[:, : tokens // 2]
        peer_out[place] = part[:, tokens // 2 :]


def mlp_second(chip, core, own_act, peer_act, weights):
    count, cols, tokens = own_act.shape
    width = weights[0].shape[1]
    shape = jax.ShapeDtypeStruct((count, cols // 2, tokens // 2), F32)
    return pl.pallas_call(
        second_body,
        out_shape=(shape, shape),
        in_specs=[pl.BlockSpec(memory_space=pltpu.SMEM)] * 2 + vmem_specs(2 + count),
        out_specs=tuple(vmem_specs(2)),
        scratch_shapes=[pltpu.VMEM((2 * count * cols, tokens), BF16)],
        compiler_params=pltpu.CompilerParams(vmem_limit_bytes=32 << 20),
        cost_estimate=pl.CostEstimate(
            flops=2 * count * cols * tokens * width, bytes_accessed=6 << 20, transcendentals=0
        ),
        name="mlp_second",
    )(chip, core, own_act, peer_act, *weights)


def last_body(core_ref, own_part, peer_part, updated, mods, finals, final_w, predicted, mlp_t):
    count, half, _ = own_part.shape
    for source, parity in ((own_part, core_ref[0]), (peer_part, 1 - core_ref[0])):
        for c in range(count):
            start = pl.multiple_of((2 * c + parity) * half, half)
            mlp_t[pl.ds(start, half), :] = source[c]
    refined = updated[...] + mods[5:6] * mlp_t[...].T
    final_in = layer_norm(refined, finals[0:1], finals[1:2])
    predicted[...] = jnp.dot(final_in, final_w[...], preferred_element_type=F32)


def last(core, own_part, peer_part, updated, mods, finals, final_w):
    rows, width = updated.shape
    return pl.pallas_call(
        last_body,
        out_shape=jax.ShapeDtypeStruct((rows, final_w.shape[1]), F32),
        in_specs=[pl.BlockSpec(memory_space=pltpu.SMEM)] + vmem_specs(6),
        out_specs=vmem_specs(1)[0],
        scratch_shapes=[pltpu.VMEM((width, rows), F32)],
        compiler_params=pltpu.CompilerParams(vmem_limit_bytes=24 << 20),
        cost_estimate=pl.CostEstimate(
            flops=2 * rows * width * final_w.shape[1], bytes_accessed=3 << 20, transcendentals=rows
        ),
        name="last",
    )(core, own_part, peer_part, updated, mods, finals, final_w)


def padded(x, axis, width):
    size, length = lax.axis_size(axis), x.shape[0]
    up = [(i, i + 1) for i in range(size - 1)]
    down = [(j, i) for i, j in up]
    before = lax.ppermute(x[length - width :], axis, up)
    after = lax.ppermute(x[:width], axis, down)
    return jnp.concatenate([before, x, after], axis=0)


def per_device(
    hidden,
    text_hidden,
    latent,
    image_mod,
    text_mod,
    final_mod,
    counts,
    step_index,
    qkv_weight,
    text_weight,
    out_weight,
    mlp_in_weight,
    mlp_out_weight,
    final_weight,
    conv_weight,
    conv_bias,
):
    tok_rows, width = hidden.shape[1:]
    width_attn = HEADS * HEAD
    blocks = lax.axis_size("blk")
    blk, img = lax.axis_index("blk"), lax.axis_index("img")
    chip, core = img // 2, img % 2
    mods = image_mod[0]
    chip, core = chip[None], core[None]

    qkv_t = qkv_weight.T
    mlp_mine = jnp.concatenate(
        [mlp_in_weight.T, mlp_out_weight[:width].T, mlp_out_weight[width:].T], axis=0
    )
    qkv_near = ring_first(qkv_t)
    qkv_next = ring_second(*qkv_near)
    qkv_far = ring_third(*qkv_next[:2])
    qkv_pieces = [qkv_t, *qkv_near, qkv_far[0], *qkv_next[2:], qkv_far[1]]

    mlp_mine, qkv_next = lax.optimization_barrier((mlp_mine, qkv_next))
    mlp_near = ring_first(mlp_mine)

    image_in = modulate(hidden[0], mods[0], mods[1])
    peer_in = swap(image_in, "img", 1)
    mine, theirs = project_qkv(chip, image_in, peer_in, qkv_pieces)
    other = swap(theirs, "img", 1)
    first = jnp.where(core[0] == 0, mine, other)
    second = jnp.where(core[0] == 0, other, mine)
    qkv = jnp.stack([first, second], axis=1).reshape(3, HEADS, HEAD, tok_rows)
    heads = qkv.transpose(1, 0, 2, 3).reshape(HEADS, 3 * HEAD, tok_rows)
    heads = jnp.pad(heads, ((0, blocks - HEADS), (0, 0), (0, 0)))
    parts = lax.all_to_all(heads, "blk", 0, 0, tiled=True)

    head = jnp.minimum(blk, HEADS - 1)
    text_in = modulate(text_hidden[0], text_mod[0, 0], text_mod[0, 1])
    text_cols = jnp.concatenate(
        [
            lax.dynamic_slice(text_weight, (0, start + head * HEAD), (width, HEAD))
            for start in (0, width_attn)
        ],
        axis=1,
    )
    text_kv = lax.dot_general(
        text_cols, text_in, (((0,), (1,)), ((), ())), preferred_element_type=F32
    ).astype(BF16)
    text_kv = jnp.pad(text_kv, ((0, 0), (0, -text_kv.shape[1] % tok_rows)))

    parts, mlp_near = lax.optimization_barrier((parts, mlp_near))
    mlp_next = ring_second(*mlp_near)
    mixed = attend(counts, parts, text_kv)
    mixed = lax.all_to_all(mixed, "blk", 0, 0, tiled=True)[:HEADS].reshape(width_attn, tok_rows)

    mixed, mlp_low, mlp_high = lax.optimization_barrier((mixed, mlp_next[0], mlp_next[1]))
    mlp_far = ring_third(mlp_low, mlp_high)
    mlp_pieces = [mlp_mine, *mlp_near, mlp_far[0], *mlp_next[2:], mlp_far[1]]

    updated, mlp_in = middle(mixed, hidden[0], mods, out_weight)
    act = mlp_first(chip, mlp_in, swap(mlp_in, "img", 1), mlp_pieces)
    peer_act = swap(act, "img", 1)
    own_part, sent_part = mlp_second(chip, core, act, peer_act, mlp_pieces)
    peer_part = swap(sent_part, "img", 1)
    predicted = last(core, own_part, peer_part, updated, mods, final_mod[0], final_weight)

    patch_count = counts[0]
    patch_rows = tok_rows // W_P
    lat_rows = 2 * patch_rows
    vel_lat = (
        predicted.reshape(patch_rows, W_P, 2, 2, CH)
        .transpose(0, 2, 1, 3, 4)
        .reshape(lat_rows, 2 * W_P * CH)
    )
    global_rows = blk * lat_rows + jnp.arange(lat_rows, dtype=jnp.int32)
    live_rows = (global_rows < 2 * (patch_count // W_P))[:, None]
    velocity = jnp.where(live_rows, vel_lat, 0.0)
    step_value = step_index[0].astype(F32)
    sigma_gap = plan(step_value + 1.0) - plan(step_value)
    next_lat = jnp.where(live_rows, latent[0] + sigma_gap * vel_lat, 0.0)
    scaled = jnp.where(live_rows, next_lat / vae_scale + vae_offset, 0.0).astype(BF16)
    framed = padded(scaled, "blk", 1)
    padded_grid = jnp.pad(framed.reshape(lat_rows + 2, 2 * W_P, CH), ((0, 0), (1, 1), (0, 0)))
    columns = jnp.concatenate(
        [
            padded_grid[row_off : row_off + lat_rows, col_off : col_off + 2 * W_P, :]
            for row_off in range(3)
            for col_off in range(3)
        ],
        axis=-1,
    ).reshape(lat_rows * 2 * W_P, 9 * CH)
    feature = jnp.dot(columns, conv_weight, preferred_element_type=F32) + conv_bias
    feature = jnp.where(live_rows[:, :, None], feature.reshape(lat_rows, 2 * W_P, -1), 0.0).astype(
        BF16
    )
    return (velocity[None], next_lat[None], feature[None])


def solution(mesh):
    placed = (
        P("img", "blk", None),
        P("img", None, None),
        P("img", "blk", None),
        P("img", None, None),
        P("img", None, None),
        P("img", None, None),
        P("img"),
        P("img"),
        P(None, "img"),
        P(),
        P(),
        P(None, "img"),
        P(None, "img"),
        P(),
        P(),
        P(),
    )
    return jax.shard_map(
        per_device,
        mesh=mesh,
        in_specs=placed,
        out_specs=(P("img", "blk", None), P("img", "blk", None), P("img", "blk", None, None)),
        check_vma=False,
    )
```

time: 464 us -> 183 us (0.39)
  waiting for transfers between devices: 249 us -> 78.7 us
  matrix products: 81.7 us -> 0.77 us
  starting transfers between devices: 7.67 us -> 52.2 us
  local copies, waits for them, and re-layouts: 52.2 us -> 13.3 us
  other arithmetic: 44.4 us -> 6.13 us
  Pallas kernels: 0 us -> 26.5 us
  between operations: 15.6 us -> 2.64 us
  loops' own time: 10.9 us -> 0 us
    all_gather x5 -> x0, waiting for transfers between devices: 243 us -> none  [the longest x1 81.6 us: per_device(): value_rows = lax.all_gather(own_values, 'blk', axis=0, tiled=True)]
    dot_general x40 -> x2, matrix products: 81.7 us -> 0.77 us  [the longest x1 0.49 us: per_device(): lax.dot_general(text_cols, text_in, (((0,), (1,)), ((), ())), preferred_e...]
    ppermute x2 -> x23, waiting for transfers between devices: 3.89 us -> 74.7 us  [the longest x12 41.4 us: ring(): return lax.ppermute(x, axis, [(i, (i + step) % size) for i in range(size)])]
    dynamic_slice x64 -> x1, local copies, waits for them, and re-layouts: 41.5 us -> 1.41 us  [per_device(): lax.dynamic_slice(text_weight, (0, start + head * HEAD), (width, HEAD))]
    ppermute x2 -> x23, starting transfers between devices: 7.47 us -> 35.5 us  [the longest x12 19.7 us: ring(): return lax.ppermute(x, axis, [(i, (i + step) % size) for i in range(size)])]
    pallas_call x0 -> x6, Pallas kernels: none -> 26.5 us  [the longest x1 12.1 us: attend(): pl.pallas_call(attend_body, out_shape=jax.ShapeDtypeStruct((blocks, HEAD,...]
    add x19 -> x2, other arithmetic: 22.8 us -> 0.8 us  [modulate(): return (normed * (1.0 + scale_row) + shift_row).astype(BF16)]
    all_to_all x0 -> x2, starting transfers between devices: none -> 16.8 us  [the longest x1 8.72 us: per_device(): parts = lax.all_to_all(heads, 'blk', 0, 0, tiled=True)]
  transfers between devices with their start and end apart: 7 -> 25, of which waited for: 5 -> 14; matrix products, arithmetic and copies ran while one was open for 32% -> 8% of each run, Pallas kernels for 0% -> 7%
where the time goes in v1:
time: 183 us; the launch traced here: 180 us
  waiting for transfers between devices  78.7 us (43%)
  starting transfers between devices  52.2 us (29%)
  Pallas kernels  26.5 us (14%)
  local copies, waits for them, and re-layouts  13.3 us (7%)
  other arithmetic  6.13 us (3%)
  between operations  2.64 us (1%)
    ppermute x12, waiting for transfers between devices, ring(): return lax.ppermute(x, axis, [(i, (i + step) % size) for i in range(size)])  41.4 us
    ppermute x9, waiting for transfers between devices, swap(): lax.ppermute(x, axis, [(i, i ^ bits) for i in range(lax.axis_size(axis))])  29.4 us
    ppermute x12, starting transfers between devices, ring(): return lax.ppermute(x, axis, [(i, (i + step) % size) for i in range(size)])  19.7 us
    pallas_call x1, Pallas kernels, attend(): pl.pallas_call(attend_body, out_shape=jax.ShapeDtypeStruct((blocks, HEAD,...  12.1 us
    ppermute x9, starting transfers between devices, swap(): lax.ppermute(x, axis, [(i, i ^ bits) for i in range(lax.axis_size(axis))])  9.91 us
    all_to_all x1, starting transfers between devices, per_device(): parts = lax.all_to_all(heads, 'blk', 0, 0, tiled=True)  8.72 us
    all_to_all x1, starting transfers between devices, per_device(): lax.all_to_all(mixed, 'blk', 0, 0, tiled=True)[:HEADS]  8.04 us
    pallas_call x1, Pallas kernels, mlp_second(): pl.pallas_call(second_body, out_shape=(shape, shape), in_specs=[pl.BlockS...  4.65 us
  transfers between devices with their start and end apart: 25, of which 14 were waited for; matrix products, arithmetic and copies ran while one was open for 8% of the time, Pallas kernels for 7%

profile of v1, /device:TPU:104, one launch (start us, length us, event | category | flops | bytes accessed | tf_op | source)
XLA Modules:
  0.0 180.3 jit_solution(13062248675009320692)
XLA Ops:
  2.2 1.7 collective-permute-start.2
  4.0 2.3 %collective-permute-start.3 = (bf16[144,1536]{1,0:T(8,128)(2,1)}, bf16[144,1536]{1,0:T(8,128)(2,1)S(1)}, u32[]{:S(2)}, u32[]{:S(2)}) collective-permute-start(bf16[144,1536]{1,0:T(8,128)(2,1)} %bitcast.87), channel_id=1, source_target_pairs={{0,2},{1,3},{2,0},{3,1},{4,6},{5,7},{6,4},{7,5},{8,10},{9,11},{10,... | collective-permute-start | bytes 1327112 | tf_op jit(solution)/shard_map/ppermute | solution.py:38
  10.1 3.9 %collective-permute-done.1.refs_1_ = bf16[144,1536]{1,0:T(8,128)(2,1)S(1)} collective-permute-done((bf16[144,1536]{1,0:T(8,128)(2,1)}, bf16[144,1536]{1,0:T(8,128)(2,1)S(1)}, u32[]{:S(2)}, u32[]{:S(2)}) %collective-permute-start.1) | collective-permute-done | bytes 442400 | tf_op jit(solution)/shard_map/ppermute | solution.py:50
  14.5 3.0 %collective-permute-start.5 = (bf16[72,1536]{1,0:T(8,128)(2,1)S(1)}, bf16[72,1536]{1,0:T(8,128)(2,1)S(1)}, u32[]{:S(2)}, u32[]{:S(2)}) collective-permute-start(bf16[72,1536]{1,0:T(8,128)(2,1)S(1)} %slice.96), channel_id=1, source_target_pairs={{0,12},{1,13},{2,14},{3,15},{4,0},{5,1},{6,2},{7,3},{8,4},{9,5},{1... | collective-permute-start | bytes 663560 | tf_op jit(solution)/shard_map/ppermute | solution.py:50
  17.5 3.2 %collective-permute-start.7 = (bf16[144,1536]{1,0:T(8,128)(2,1)S(1)}, bf16[144,1536]{1,0:T(8,128)(2,1)}, u32[]{:S(2)}, u32[]{:S(2)}) collective-permute-start(bf16[144,1536]{1,0:T(8,128)(2,1)S(1)} %collective-permute-done.3.refs_3_), channel_id=1, source_target_pairs={{0,12},{1,13},{2,14},{3,15},{4,0},{5,1},{6,2},{7,3},{8,4},{9,5},{1... | collective-permute-start | bytes 1327112 | tf_op jit(solution)/shard_map/ppermute | solution.py:50
  20.7 2.9 %collective-permute-done.4 = bf16[72,1536]{1,0:T(8,128)(2,1)S(1)} collective-permute-done((bf16[72,1536]{1,0:T(8,128)(2,1)S(1)}, bf16[72,1536]{1,0:T(8,128)(2,1)S(1)}, u32[]{:S(2)}, u32[]{:S(2)}) %collective-permute-start.4) | collective-permute-done | bytes 221216 | tf_op jit(solution)/shard_map/ppermute | solution.py:50
  23.7 2.4 %collective-permute-start.8 = (bf16[144,1536]{1,0:T(8,128)(2,1)S(1)}, bf16[144,1536]{1,0:T(8,128)(2,1)}, u32[]{:S(2)}, u32[]{:S(2)}) collective-permute-start(bf16[144,1536]{1,0:T(8,128)(2,1)S(1)} %constant_dynamic-update-slice_fusion.refs_4_), channel_id=1, source_target_pairs={{0,2},{1,3},{2,0},{3,1},{4,6},{5,7},{6,4},{7,5},{8,10},{9,11},{10,... | collective-permute-start | bytes 1327112 | tf_op jit(solution)/shard_map/ppermute | solution.py:38
  26.5 1.8 %collective-permute-done.peer_x = bf16[128,1536]{1,0:T(8,128)(2,1)} collective-permute-done((bf16[128,1536]{1,0:T(8,128)(2,1)S(1)}, bf16[128,1536]{1,0:T(8,128)(2,1)}, u32[]{:S(2)}, u32[]{:S(2)}) %collective-permute-start) | collective-permute-done | bytes 393248 | tf_op jit(solution)/shard_map/ppermute | solution.py:38
  28.3 2.9 %collective-permute-done.6.refs_5_ = bf16[144,1536]{1,0:T(8,128)(2,1)} collective-permute-done((bf16[144,1536]{1,0:T(8,128)(2,1)S(1)}, bf16[144,1536]{1,0:T(8,128)(2,1)}, u32[]{:S(2)}, u32[]{:S(2)}) %collective-permute-start.6) | collective-permute-done | bytes 442400 | tf_op jit(solution)/shard_map/ppermute | solution.py:50
  31.3 2.4 %collective-permute-done.8.refs_7_ = bf16[144,1536]{1,0:T(8,128)(2,1)} collective-permute-done((bf16[144,1536]{1,0:T(8,128)(2,1)S(1)}, bf16[144,1536]{1,0:T(8,128)(2,1)}, u32[]{:S(2)}, u32[]{:S(2)}) %collective-permute-start.8) | collective-permute-done | bytes 442400 | tf_op jit(solution)/shard_map/ppermute | solution.py:38
  33.7 3.6 %project_qkv.1 = (bf16[8,144,128]{2,1,0:T(8,128)(2,1)S(1)}, bf16[8,144,128]{2,1,0:T(8,128)(2,1)S(1)}) custom-call(s32[1]{0:T(128)} %bitcast.2.chip_ref, bf16[128,1536]{1,0:T(8,128)(2,1)S(1)} %fusion.12.own_x, bf16[128,1536]{1,0:T(8,128)(2,1)} %collective-permute-done.peer_x, bf16[144,1536]{1,0:T(8,128)(2,1)S(1)} %bitcast.88, ...), custom_call_target="tpu_custom_call" | custom-call | flops 905969664 | bytes 5242880 | tf_op jit(solution)/shard_map/project_qkv/pallas_call | solution.py:95
  40.2 8.7 %all-to-all-start = ((bf16[16,192,128]{2,1,0:T(8,128)(2,1)}), bf16[16,192,128]{2,1,0:T(8,128)(2,1)}, u32[]{:S(2)}, u32[]{:S(2)}) async-start(bf16[16,192,128]{2,1,0:T(8,128)(2,1)} %pad.12), calls=%async_computation | async-start | bytes 1572864 | tf_op jit(solution)/shard_map/all_to_all | solution.py:358
  50.0 2.5 %collective-permute-start.11 = (bf16[384,1536]{1,0:T(8,128)(2,1)S(1)}, bf16[384,1536]{1,0:T(8,128)(2,1)}, u32[]{:S(2)}, u32[]{:S(2)}) collective-permute-start(bf16[384,1536]{1,0:T(8,128)(2,1)S(1)} %pad_maximum_fusion.refs_0_), channel_id=1, source_target_pairs={{0,12},{1,13},{2,14},{3,15},{4,0},{5,1},{6,2},{7,3},{8,4},{9,5},{1... | collective-permute-start | bytes 3538952 | tf_op jit(solution)/shard_map/ppermute | solution.py:50
  52.5 2.3 %collective-permute-start.12 = (bf16[384,1536]{1,0:T(8,128)(2,1)S(1)}, bf16[384,1536]{1,0:T(8,128)(2,1)}, u32[]{:S(2)}, u32[]{:S(2)}) collective-permute-start(bf16[384,1536]{1,0:T(8,128)(2,1)S(1)} %pad_maximum_fusion.refs_0_), channel_id=1, source_target_pairs={{0,2},{1,3},{2,0},{3,1},{4,6},{5,7},{6,4},{7,5},{8,10},{9,11},{10,... | collective-permute-start | bytes 3538952 | tf_op jit(solution)/shard_map/ppermute | solution.py:38
  57.8 20.3 %collective-permute-done.10.refs_1_ = bf16[384,1536]{1,0:T(8,128)(2,1)S(1)} collective-permute-done((bf16[384,1536]{1,0:T(8,128)(2,1)S(1)}, bf16[384,1536]{1,0:T(8,128)(2,1)S(1)}, u32[]{:S(2)}, u32[]{:S(2)}) %collective-permute-start.10) | collective-permute-done | bytes 1179680 | tf_op jit(solution)/shard_map/ppermute | solution.py:50
  78.1 10.5 %collective-permute-done.12.refs_3_ = bf16[384,1536]{1,0:T(8,128)(2,1)} collective-permute-done((bf16[384,1536]{1,0:T(8,128)(2,1)S(1)}, bf16[384,1536]{1,0:T(8,128)(2,1)}, u32[]{:S(2)}, u32[]{:S(2)}) %collective-permute-start.12) | collective-permute-done | bytes 1179680 | tf_op jit(solution)/shard_map/ppermute | solution.py:38
  89.5 1.9 %slice.84 = bf16[192,1536]{1,0:T(8,128)(2,1)} slice(bf16[384,1536]{1,0:T(8,128)(2,1)} %collective-permute-done.11.refs_2_), slice={[192:384], [0:1536]} | slice | bytes 1179648 | tf_op jit(solution)/shard_map/slice | solution.py:61
  91.4 3.2 %collective-permute-start.14 = (bf16[192,1536]{1,0:T(8,128)(2,1)}, bf16[192,1536]{1,0:T(8,128)(2,1)}, u32[]{:S(2)}, u32[]{:S(2)}) collective-permute-start(bf16[192,1536]{1,0:T(8,128)(2,1)} %slice.84), channel_id=1, source_target_pairs={{0,12},{1,13},{2,14},{3,15},{4,0},{5,1},{6,2},{7,3},{8,4},{9,5},{1... | collective-permute-start | bytes 1769480 | tf_op jit(solution)/shard_map/ppermute | solution.py:50
  94.6 12.1 %attend.1 = bf16[16,64,128]{2,1,0:T(8,128)(2,1)} custom-call(s32[1]{0:T(128)} %copy.53.count_ref, bf16[16,192,128]{2,1,0:T(8,128)(2,1)} %all-to-all-done.parts, bf16[128,256]{1,0:T(8,128)(2,1)S(1)} %pad.13.text), custom_call_target="tpu_custom_call" | custom-call | flops 1207959552 | bytes 2097152 | tf_op jit(solution)/shard_map/attend/pallas_call | solution.py:152
  106.7 8.0 %all-to-all-start.1 = ((bf16[16,64,128]{2,1,0:T(8,128)(2,1)}), bf16[16,64,128]{2,1,0:T(8,128)(2,1)S(1)}, u32[]{:S(2)}, u32[]{:S(2)}) async-start(bf16[16,64,128]{2,1,0:T(8,128)(2,1)} %attend.1), calls=%async_computation.1 | async-start | bytes 524288 | tf_op jit(solution)/shard_map/all_to_all | solution.py:377
  114.8 3.2 %collective-permute-start.17 = (bf16[384,1536]{1,0:T(8,128)(2,1)}, bf16[384,1536]{1,0:T(8,128)(2,1)}, u32[]{:S(2)}, u32[]{:S(2)}) collective-permute-start(bf16[384,1536]{1,0:T(8,128)(2,1)} %collective-permute-done.12.refs_3_), channel_id=1, source_target_pairs={{0,12},{1,13},{2,14},{3,15},{4,0},{5,1},{6,2},{7,3},{8,4},{9,5},{1... | collective-permute-start | bytes 3538952 | tf_op jit(solution)/shard_map/ppermute | solution.py:50
  118.0 4.0 %all-to-all-done.1 = bf16[16,64,128]{2,1,0:T(8,128)(2,1)S(1)} async-done(((bf16[16,64,128]{2,1,0:T(8,128)(2,1)}), bf16[16,64,128]{2,1,0:T(8,128)(2,1)S(1)}, u32[]{:S(2)}, u32[]{:S(2)}) %all-to-all-start.1) | async-done | bytes 262176 | tf_op jit(solution)/shard_map/all_to_all | solution.py:377
  124.4 2.2 %collective-permute-start.18 = (bf16[384,1536]{1,0:T(8,128)(2,1)S(1)}, bf16[384,1536]{1,0:T(8,128)(2,1)S(1)}, u32[]{:S(2)}, u32[]{:S(2)}) collective-permute-start(bf16[384,1536]{1,0:T(8,128)(2,1)S(1)} %constant_dynamic-update-slice_fusion.2.refs_4_), channel_id=1, source_target_pairs={{0,2},{1,3},{2,0},{3,1},{4,6},{5,7},{6,4},{7,5},{8,10},{9,11},{10,... | collective-permute-start | bytes 3538952 | tf_op jit(solution)/shard_map/ppermute | solution.py:38
  128.4 1.7 collective-permute-done.15.peer_x
  130.1 11.4 %collective-permute-done.16.refs_5_ = bf16[384,1536]{1,0:T(8,128)(2,1)} collective-permute-done((bf16[384,1536]{1,0:T(8,128)(2,1)}, bf16[384,1536]{1,0:T(8,128)(2,1)}, u32[]{:S(2)}, u32[]{:S(2)}) %collective-permute-start.16) | collective-permute-done | bytes 1179680 | tf_op jit(solution)/shard_map/ppermute | solution.py:50
  141.6 9.1 %collective-permute-done.18.refs_7_ = bf16[384,1536]{1,0:T(8,128)(2,1)S(1)} collective-permute-done((bf16[384,1536]{1,0:T(8,128)(2,1)S(1)}, bf16[384,1536]{1,0:T(8,128)(2,1)S(1)}, u32[]{:S(2)}, u32[]{:S(2)}) %collective-permute-start.18) | collective-permute-done | bytes 1179680 | tf_op jit(solution)/shard_map/ppermute | solution.py:38
  150.7 4.6 %mlp_first.1.own_act = bf16[8,192,256]{2,1,0:T(8,128)(2,1)S(1)} custom-call(s32[1]{0:T(128)} %bitcast.2.chip_ref, bf16[128,1536]{1,0:T(8,128)(2,1)S(1)} %get-tuple-element.24.own_x, bf16[128,1536]{1,0:T(8,128)(2,1)S(1)} %collective-permute-done.15.peer_x, bf16[384,1536]{1,0:T(8,128)(2,1)S(1)} %pad_maximum_fusion.refs_0_, ...), custom_call_target="tpu_custom_call" | custom-call | flops 1207959552 | bytes 6291456 | tf_op jit(solution)/shard_map/mlp_first/pallas_call | solution.py:222
  155.4 2.3 %collective-permute-done.19.peer_act = bf16[8,192,256]{2,1,0:T(8,128)(2,1)S(1)} collective-permute-done((bf16[8,192,256]{2,1,0:T(8,128)(2,1)S(1)}, bf16[8,192,256]{2,1,0:T(8,128)(2,1)S(1)}, u32[]{:S(2)}, u32[]{:S(2)}) %collective-permute-start.19) | collective-permute-done | bytes 786464 | tf_op jit(solution)/shard_map/ppermute | solution.py:38
  157.7 4.7 %mlp_second.1 = (f32[8,96,128]{2,1,0:T(8,128)S(1)}, f32[8,96,128]{2,1,0:T(8,128)S(1)}) custom-call(s32[1]{0:T(128)} %bitcast.2.chip_ref, s32[1]{0:T(128)} %bitcast.1.core_ref, bf16[8,192,256]{2,1,0:T(8,128)(2,1)S(1)} %mlp_first.1.own_act, bf16[8,192,256]{2,1,0:T(8,128)(2,1)S(1)} %collective-permute-done.19.peer_act, ...), custom_call_target="tpu_custom_call" | custom-call | flops 1207959552 | bytes 6291456 | tf_op jit(solution)/shard_map/mlp_second/pallas_call | solution.py:261
  166.6 3.4 %collective-permute-start.21 = (bf16[1,2048]{1,0:T(2,128)(2,1)S(1)}, bf16[1,2048]{1,0:T(2,128)(2,1)S(1)}, u32[]{:S(2)}, u32[]{:S(2)}) collective-permute-start(bf16[1,2048]{1,0:T(2,128)(2,1)S(1)} %get-tuple-element.49), channel_id=1, source_target_pairs={{0,16},{16,32},{32,48},{48,64},{64,80},{80,96},{96,112},{112,128},... | collective-permute-start | bytes 12296 | tf_op jit(solution)/shard_map/ppermute | solution.py:306
  170.0 2.5 %collective-permute-start.22 = (bf16[1,2048]{1,0:T(2,128)(2,1)S(1)}, bf16[1,2048]{1,0:T(2,128)(2,1)S(1)}, u32[]{:S(2)}, u32[]{:S(2)}) collective-permute-start(bf16[1,2048]{1,0:T(2,128)(2,1)S(1)} %get-tuple-element.50), channel_id=1, source_target_pairs={{16,0},{32,16},{48,32},{64,48},{80,64},{96,80},{112,96},{128,112},... | collective-permute-start | bytes 12296 | tf_op jit(solution)/shard_map/ppermute | solution.py:307
  173.8 3.8 %collective-permute-done.22 = bf16[1,2048]{1,0:T(2,128)(2,1)S(1)} collective-permute-done((bf16[1,2048]{1,0:T(2,128)(2,1)S(1)}, bf16[1,2048]{1,0:T(2,128)(2,1)S(1)}, u32[]{:S(2)}, u32[]{:S(2)}) %collective-permute-start.22) | collective-permute-done | bytes 4128 | tf_op jit(solution)/shard_map/ppermute | solution.py:307
  (110 shorter events, 24.8 us)
Async XLA Ops:
  0.6 178.3 %copy-start = (bf16[144,512]{1,0:T(8,128)(2,1)S(1)}, bf16[144,512]{1,0:T(8,128)(2,1)}, u32[]{:S(2)}) copy-start(bf16[144,512]{1,0:T(8,128)(2,1)} %param.30) | copy-start | bytes 442372
  0.6 13.4 %collective-permute-start.1 = (bf16[144,1536]{1,0:T(8,128)(2,1)}, bf16[144,1536]{1,0:T(8,128)(2,1)S(1)}, u32[]{:S(2)}, u32[]{:S(2)}) collective-permute-start(bf16[144,1536]{1,0:T(8,128)(2,1)} %bitcast.85), channel_id=1, source_target_pairs={{0,4},{1,5},{2,6},{3,7},{4,8},{5,9},{6,10},{7,11},{8,12},{9,13},{1... | collective-permute-start | bytes 1327112 | tf_op jit(solution)/shard_map/ppermute | solution.py:50
  2.2 12.2 %collective-permute-start.2 = (bf16[144,1536]{1,0:T(8,128)(2,1)}, bf16[144,1536]{1,0:T(8,128)(2,1)S(1)}, u32[]{:S(2)}, u32[]{:S(2)}) collective-permute-start(bf16[144,1536]{1,0:T(8,128)(2,1)} %bitcast.86), channel_id=1, source_target_pairs={{0,12},{1,13},{2,14},{3,15},{4,0},{5,1},{6,2},{7,3},{8,4},{9,5},{1... | collective-permute-start | bytes 1327112 | tf_op jit(solution)/shard_map/ppermute | solution.py:50
  4.0 13.5 %collective-permute-start.3 = (bf16[144,1536]{1,0:T(8,128)(2,1)}, bf16[144,1536]{1,0:T(8,128)(2,1)S(1)}, u32[]{:S(2)}, u32[]{:S(2)}) collective-permute-start(bf16[144,1536]{1,0:T(8,128)(2,1)} %bitcast.87), channel_id=1, source_target_pairs={{0,2},{1,3},{2,0},{3,1},{4,6},{5,7},{6,4},{7,5},{8,10},{9,11},{10,... | collective-permute-start | bytes 1327112 | tf_op jit(solution)/shard_map/ppermute | solution.py:38
  7.4 18.7 %copy-start.1 = (bf16[1,128,1536]{2,1,0:T(8,128)(2,1)S(1)}, bf16[1,128,1536]{2,1,0:T(8,128)(2,1)}, u32[]{:S(2)}) copy-start(bf16[1,128,1536]{2,1,0:T(8,128)(2,1)} %param.16) | copy-start | bytes 1179652
  14.1 19.6 %copy-start.5 = (bf16[1536,144]{0,1:T(8,128)(2,1)S(1)}, bf16[1536,144]{0,1:T(8,128)(2,1)}, u32[]{:S(2)}) copy-start(bf16[1536,144]{0,1:T(8,128)(2,1)} %param.24) | copy-start | bytes 1327108
  14.1 9.6 %collective-permute-start.4 = (bf16[72,1536]{1,0:T(8,128)(2,1)S(1)}, bf16[72,1536]{1,0:T(8,128)(2,1)S(1)}, u32[]{:S(2)}, u32[]{:S(2)}) collective-permute-start(bf16[72,1536]{1,0:T(8,128)(2,1)S(1)} %slice.95), channel_id=1, source_target_pairs={{0,4},{1,5},{2,6},{3,7},{4,8},{5,9},{6,10},{7,11},{8,12},{9,13},{1... | collective-permute-start | bytes 663560 | tf_op jit(solution)/shard_map/ppermute | solution.py:50
  14.5 9.2 %collective-permute-start.5 = (bf16[72,1536]{1,0:T(8,128)(2,1)S(1)}, bf16[72,1536]{1,0:T(8,128)(2,1)S(1)}, u32[]{:S(2)}, u32[]{:S(2)}) collective-permute-start(bf16[72,1536]{1,0:T(8,128)(2,1)S(1)} %slice.96), channel_id=1, source_target_pairs={{0,12},{1,13},{2,14},{3,15},{4,0},{5,1},{6,2},{7,3},{8,4},{9,5},{1... | collective-permute-start | bytes 663560 | tf_op jit(solution)/shard_map/ppermute | solution.py:50
  17.5 13.7 %collective-permute-start.6 = (bf16[144,1536]{1,0:T(8,128)(2,1)S(1)}, bf16[144,1536]{1,0:T(8,128)(2,1)}, u32[]{:S(2)}, u32[]{:S(2)}) collective-permute-start(bf16[144,1536]{1,0:T(8,128)(2,1)S(1)} %collective-permute-done.3.refs_3_), channel_id=1, source_target_pairs={{0,4},{1,5},{2,6},{3,7},{4,8},{5,9},{6,10},{7,11},{8,12},{9,13},{1... | collective-permute-start | bytes 1327112 | tf_op jit(solution)/shard_map/ppermute | solution.py:50
  17.5 13.7 %collective-permute-start.7 = (bf16[144,1536]{1,0:T(8,128)(2,1)S(1)}, bf16[144,1536]{1,0:T(8,128)(2,1)}, u32[]{:S(2)}, u32[]{:S(2)}) collective-permute-start(bf16[144,1536]{1,0:T(8,128)(2,1)S(1)} %collective-permute-done.3.refs_3_), channel_id=1, source_target_pairs={{0,12},{1,13},{2,14},{3,15},{4,0},{5,1},{6,2},{7,3},{8,4},{9,5},{1... | collective-permute-start | bytes 1327112 | tf_op jit(solution)/shard_map/ppermute | solution.py:50
  23.7 10.0 %collective-permute-start.8 = (bf16[144,1536]{1,0:T(8,128)(2,1)S(1)}, bf16[144,1536]{1,0:T(8,128)(2,1)}, u32[]{:S(2)}, u32[]{:S(2)}) collective-permute-start(bf16[144,1536]{1,0:T(8,128)(2,1)S(1)} %constant_dynamic-update-slice_fusion.refs_4_), channel_id=1, source_target_pairs={{0,2},{1,3},{2,0},{3,1},{4,6},{5,7},{6,4},{7,5},{8,10},{9,11},{10,... | collective-permute-start | bytes 1327112 | tf_op jit(solution)/shard_map/ppermute | solution.py:38
  26.4 1.9 %collective-permute-start = (bf16[128,1536]{1,0:T(8,128)(2,1)S(1)}, bf16[128,1536]{1,0:T(8,128)(2,1)}, u32[]{:S(2)}, u32[]{:S(2)}) collective-permute-start(bf16[128,1536]{1,0:T(8,128)(2,1)S(1)} %fusion.12.own_x), channel_id=1, source_target_pairs={{0,1},{1,0},{2,3},{3,2},{4,5},{5,4},{6,7},{7,6},{8,9},{9,8},{10,11... | collective-permute-start | bytes 1179656 | tf_op jit(solution)/shard_map/ppermute | solution.py:38
  37.3 1.7 collective-permute-start.9
  39.2 9.7 %copy-start.7 = (bf16[1,154,1536]{2,1,0:T(8,128)(2,1)S(1)}, bf16[1,154,1536]{2,1,0:T(8,128)(2,1)}, u32[]{:S(2)}) copy-start(bf16[1,154,1536]{2,1,0:T(8,128)(2,1)} %param.17) | copy-start | bytes 1419268
  40.2 8.9 %copy-start.9 = (bf16[1536,192]{0,1:T(8,128)(2,1)S(1)}, bf16[1536,192]{0,1:T(8,128)(2,1)}, u32[]{:S(2)}) copy-start(bf16[1536,192]{0,1:T(8,128)(2,1)} %param.27) | copy-start | bytes 1769476
  40.2 48.4 %all-to-all-start = ((bf16[16,192,128]{2,1,0:T(8,128)(2,1)}), bf16[16,192,128]{2,1,0:T(8,128)(2,1)}, u32[]{:S(2)}, u32[]{:S(2)}) async-start(bf16[16,192,128]{2,1,0:T(8,128)(2,1)} %pad.12), calls=%async_computation | async-start | bytes 1572864 | tf_op jit(solution)/shard_map/all_to_all | solution.py:358
  49.2 28.9 %collective-permute-start.10 = (bf16[384,1536]{1,0:T(8,128)(2,1)S(1)}, bf16[384,1536]{1,0:T(8,128)(2,1)S(1)}, u32[]{:S(2)}, u32[]{:S(2)}) collective-permute-start(bf16[384,1536]{1,0:T(8,128)(2,1)S(1)} %pad_maximum_fusion.refs_0_), channel_id=1, source_target_pairs={{0,4},{1,5},{2,6},{3,7},{4,8},{5,9},{6,10},{7,11},{8,12},{9,13},{1... | collective-permute-start | bytes 3538952 | tf_op jit(solution)/shard_map/ppermute | solution.py:50
  50.0 28.1 %collective-permute-start.11 = (bf16[384,1536]{1,0:T(8,128)(2,1)S(1)}, bf16[384,1536]{1,0:T(8,128)(2,1)}, u32[]{:S(2)}, u32[]{:S(2)}) collective-permute-start(bf16[384,1536]{1,0:T(8,128)(2,1)S(1)} %pad_maximum_fusion.refs_0_), channel_id=1, source_target_pairs={{0,12},{1,13},{2,14},{3,15},{4,0},{5,1},{6,2},{7,3},{8,4},{9,5},{1... | collective-permute-start | bytes 3538952 | tf_op jit(solution)/shard_map/ppermute | solution.py:50
  52.5 36.1 %collective-permute-start.12 = (bf16[384,1536]{1,0:T(8,128)(2,1)S(1)}, bf16[384,1536]{1,0:T(8,128)(2,1)}, u32[]{:S(2)}, u32[]{:S(2)}) collective-permute-start(bf16[384,1536]{1,0:T(8,128)(2,1)S(1)} %pad_maximum_fusion.refs_0_), channel_id=1, source_target_pairs={{0,2},{1,3},{2,0},{3,1},{4,6},{5,7},{6,4},{7,5},{8,10},{9,11},{10,... | collective-permute-start | bytes 3538952 | tf_op jit(solution)/shard_map/ppermute | solution.py:38
  89.5 32.5 %collective-permute-start.13 = (bf16[192,1536]{1,0:T(8,128)(2,1)}, bf16[192,1536]{1,0:T(8,128)(2,1)}, u32[]{:S(2)}, u32[]{:S(2)}) collective-permute-start(bf16[192,1536]{1,0:T(8,128)(2,1)} %slice.83), channel_id=1, source_target_pairs={{0,4},{1,5},{2,6},{3,7},{4,8},{5,9},{6,10},{7,11},{8,12},{9,13},{1... | collective-permute-start | bytes 1769480 | tf_op jit(solution)/shard_map/ppermute | solution.py:50
  91.4 30.6 %collective-permute-start.14 = (bf16[192,1536]{1,0:T(8,128)(2,1)}, bf16[192,1536]{1,0:T(8,128)(2,1)}, u32[]{:S(2)}, u32[]{:S(2)}) collective-permute-start(bf16[192,1536]{1,0:T(8,128)(2,1)} %slice.84), channel_id=1, source_target_pairs={{0,12},{1,13},{2,14},{3,15},{4,0},{5,1},{6,2},{7,3},{8,4},{9,5},{1... | collective-permute-start | bytes 1769480 | tf_op jit(solution)/shard_map/ppermute | solution.py:50
  106.7 15.3 %all-to-all-start.1 = ((bf16[16,64,128]{2,1,0:T(8,128)(2,1)}), bf16[16,64,128]{2,1,0:T(8,128)(2,1)S(1)}, u32[]{:S(2)}, u32[]{:S(2)}) async-start(bf16[16,64,128]{2,1,0:T(8,128)(2,1)} %attend.1), calls=%async_computation.1 | async-start | bytes 524288 | tf_op jit(solution)/shard_map/all_to_all | solution.py:377
  114.8 26.8 %collective-permute-start.16 = (bf16[384,1536]{1,0:T(8,128)(2,1)}, bf16[384,1536]{1,0:T(8,128)(2,1)}, u32[]{:S(2)}, u32[]{:S(2)}) collective-permute-start(bf16[384,1536]{1,0:T(8,128)(2,1)} %collective-permute-done.12.refs_3_), channel_id=1, source_target_pairs={{0,4},{1,5},{2,6},{3,7},{4,8},{5,9},{6,10},{7,11},{8,12},{9,13},{1... | collective-permute-start | bytes 3538952 | tf_op jit(solution)/shard_map/ppermute | solution.py:50
  114.8 26.8 %collective-permute-start.17 = (bf16[384,1536]{1,0:T(8,128)(2,1)}, bf16[384,1536]{1,0:T(8,128)(2,1)}, u32[]{:S(2)}, u32[]{:S(2)}) collective-permute-start(bf16[384,1536]{1,0:T(8,128)(2,1)} %collective-permute-done.12.refs_3_), channel_id=1, source_target_pairs={{0,12},{1,13},{2,14},{3,15},{4,0},{5,1},{6,2},{7,3},{8,4},{9,5},{1... | collective-permute-start | bytes 3538952 | tf_op jit(solution)/shard_map/ppermute | solution.py:50
  124.4 26.3 %collective-permute-start.18 = (bf16[384,1536]{1,0:T(8,128)(2,1)S(1)}, bf16[384,1536]{1,0:T(8,128)(2,1)S(1)}, u32[]{:S(2)}, u32[]{:S(2)}) collective-permute-start(bf16[384,1536]{1,0:T(8,128)(2,1)S(1)} %constant_dynamic-update-slice_fusion.2.refs_4_), channel_id=1, source_target_pairs={{0,2},{1,3},{2,0},{3,1},{4,6},{5,7},{6,4},{7,5},{8,10},{9,11},{10,... | collective-permute-start | bytes 3538952 | tf_op jit(solution)/shard_map/ppermute | solution.py:38
  128.4 1.7 collective-permute-start.15
  155.3 2.4 %collective-permute-start.19 = (bf16[8,192,256]{2,1,0:T(8,128)(2,1)S(1)}, bf16[8,192,256]{2,1,0:T(8,128)(2,1)S(1)}, u32[]{:S(2)}, u32[]{:S(2)}) collective-permute-start(bf16[8,192,256]{2,1,0:T(8,128)(2,1)S(1)} %mlp_first.1.own_act), channel_id=1, source_target_pairs={{0,1},{1,0},{2,3},{3,2},{4,5},{5,4},{6,7},{7,6},{8,9},{9,8},{10,11... | collective-permute-start | bytes 2359304 | tf_op jit(solution)/shard_map/ppermute | solution.py:38
  157.7 7.0 %copy-start.10 = (f32[1,4,2048]{2,1,0:T(4,128)S(1)}, f32[1,4,2048]{2,1,0:T(4,128)}, u32[]{:S(2)}) copy-start(f32[1,4,2048]{2,1,0:T(4,128)} %param.18) | copy-start | bytes 98308
  157.7 7.3 %copy-start.6 = (f32[1,2,1536]{2,1,0:T(2,128)S(1)}, f32[1,2,1536]{2,1,0:T(2,128)}, u32[]{:S(2)}) copy-start(f32[1,2,1536]{2,1,0:T(2,128)} %param.21) | copy-start | bytes 36868
  162.3 2.6 %collective-permute-start.20 = (f32[8,96,128]{2,1,0:T(8,128)S(1)}, f32[8,96,128]{2,1,0:T(8,128)S(1)}, u32[]{:S(2)}, u32[]{:S(2)}) collective-permute-start(f32[8,96,128]{2,1,0:T(8,128)S(1)} %get-tuple-element.29), channel_id=1, source_target_pairs={{0,1},{1,0},{2,3},{3,2},{4,5},{5,4},{6,7},{7,6},{8,9},{9,8},{10,11... | collective-permute-start | bytes 1179656 | tf_op jit(solution)/shard_map/ppermute | solution.py:38
  166.6 7.2 %collective-permute-start.21 = (bf16[1,2048]{1,0:T(2,128)(2,1)S(1)}, bf16[1,2048]{1,0:T(2,128)(2,1)S(1)}, u32[]{:S(2)}, u32[]{:S(2)}) collective-permute-start(bf16[1,2048]{1,0:T(2,128)(2,1)S(1)} %get-tuple-element.49), channel_id=1, source_target_pairs={{0,16},{16,32},{32,48},{48,64},{64,80},{80,96},{96,112},{112,128},... | collective-permute-start | bytes 12296 | tf_op jit(solution)/shard_map/ppermute | solution.py:306
  170.0 7.7 %collective-permute-start.22 = (bf16[1,2048]{1,0:T(2,128)(2,1)S(1)}, bf16[1,2048]{1,0:T(2,128)(2,1)S(1)}, u32[]{:S(2)}, u32[]{:S(2)}) collective-permute-start(bf16[1,2048]{1,0:T(2,128)(2,1)S(1)} %get-tuple-element.50), channel_id=1, source_target_pairs={{16,0},{32,16},{48,32},{64,48},{80,64},{96,80},{112,96},{128,112},... | collective-permute-start | bytes 12296 | tf_op jit(solution)/shard_map/ppermute | solution.py:307
  (7 other events, 23.0 us)

commit v2 on v1

--- a/solution.py
+++ b/solution.py
@@ -98,7 +98,7 @@
         in_specs=[pl.BlockSpec(memory_space=pltpu.SMEM)] + vmem_specs(2 + len(weights)),
         out_specs=tuple(vmem_specs(2)),
         compiler_params=pltpu.CompilerParams(vmem_limit_bytes=32 << 20),
-        cost_estimate=pl.CostEstimate(flops=flops, bytes_accessed=5 << 20, transcendentals=0),
+        cost_estimate=pl.CostEstimate(flops=1000, bytes_accessed=1000, transcendentals=0),
         name="project_qkv",
     )(chip, own_x, peer_x, *weights)
 
@@ -160,9 +160,7 @@
             pltpu.VMEM((2 * HEAD, queries), BF16),
         ],
         compiler_params=pltpu.CompilerParams(vmem_limit_bytes=40 << 20),
-        cost_estimate=pl.CostEstimate(
-            flops=4 * keys * queries * HEAD, bytes_accessed=2 << 20, transcendentals=keys * queries
-        ),
+        cost_estimate=pl.CostEstimate(flops=1000, bytes_accessed=1000, transcendentals=0),
         name="attend",
     )(count, parts, text)
 
@@ -197,9 +195,7 @@
         in_specs=vmem_specs(4),
         out_specs=tuple(vmem_specs(2)),
         compiler_params=pltpu.CompilerParams(vmem_limit_bytes=24 << 20),
-        cost_estimate=pl.CostEstimate(
-            flops=2 * mixed.shape[0] * rows * width, bytes_accessed=5 << 20, transcendentals=rows
-        ),
+        cost_estimate=pl.CostEstimate(flops=1000, bytes_accessed=1000, transcendentals=0),
         name="middle",
     )(mixed, hidden, mods, out_w)
 
@@ -215,9 +211,8 @@
         out[place_of(chip_ref[0], k)] = gelu(part).astype(BF16)
 
 
-def mlp_first(chip, own_x, peer_x, weights):
-    rows, width = own_x.shape
-    cols = weights[0].shape[0] // 2
+def mlp_first(chip, own_x, peer_x, weights, cols):
+    rows = own_x.shape[0]
     count = len(weights)
     return pl.pallas_call(
         first_body,
@@ -225,51 +220,48 @@
         in_specs=[pl.BlockSpec(memory_space=pltpu.SMEM)] + vmem_specs(2 + count),
         out_specs=vmem_specs(1)[0],
         compiler_params=pltpu.CompilerParams(vmem_limit_bytes=32 << 20),
-        cost_estimate=pl.CostEstimate(
-            flops=4 * count * cols * rows * width,
-            bytes_accessed=6 << 20,
-            transcendentals=2 * count * cols * rows,
-        ),
+        cost_estimate=pl.CostEstimate(flops=1000, bytes_accessed=1000, transcendentals=0),
         name="mlp_first",
     )(chip, own_x, peer_x, *weights)
 
 
-def second_body(chip_ref, core_ref, own_act, peer_act, *refs):
+def second_body(chip_ref, core_ref, own_a, peer_a, own_b, peer_b, *refs):
     weights, (own_out, peer_out), act = refs[:-3], refs[-3:-1], refs[-1]
-    count, cols, tokens = own_act.shape
+    count, early, tokens = own_a.shape
+    late = own_b.shape[1]
+    cols, mid = early + late, tokens // 2
     core = core_ref[0]
     for c in range(count):
-        start = pl.multiple_of((2 * c + core) * cols, cols)
-        act[pl.ds(start, cols), :] = own_act[c]
-        start = pl.multiple_of((2 * c + 1 - core) * cols, cols)
-        act[pl.ds(start, cols), : tokens // 2] = peer_act[c, :, tokens // 2 :]
-        act[pl.ds(start, cols), tokens // 2 :] = peer_act[c, :, : tokens // 2]
+        for own, peer, shift, size in ((own_a, peer_a, 0, early), (own_b, peer_b, early, late)):
+            mine = pl.ds(pl.multiple_of((2 * c + core) * cols + shift, 16), size)
+            act[mine, :] = own[c]
+            other = pl.ds(pl.multiple_of((2 * c + 1 - core) * cols + shift, 16), size)
+            act[other, :mid] = peer[c, :, mid:]
+            act[other, mid:] = peer[c, :, :mid]
     width = weights[0].shape[1]
     half = cols // 2
     for k, weight in enumerate(weights):
-        part = jnp.dot(weight[cols : cols + half], act[:width], preferred_element_type=F32)
-        part += jnp.dot(weight[cols + half :], act[width:], preferred_element_type=F32)
+        part = jnp.dot(weight[late : late + half], act[:width], preferred_element_type=F32)
+        part += jnp.dot(weight[late + half :], act[width:], preferred_element_type=F32)
         place = place_of(chip_ref[0], k)
-        own_out[place] = part[:, : tokens // 2]
-        peer_out[place] = part[:, tokens // 2 :]
-
-
-def mlp_second(chip, core, own_act, peer_act, weights):
-    count, cols, tokens = own_act.shape
-    width = weights[0].shape[1]
+        own_out[place] = part[:, :mid]
+        peer_out[place] = part[:, mid:]
+
+
+def mlp_second(chip, core, own_a, peer_a, own_b, peer_b, weights):
+    count, early, tokens = own_a.shape
+    cols = early + own_b.shape[1]
     shape = jax.ShapeDtypeStruct((count, cols // 2, tokens // 2), F32)
     return pl.pallas_call(
         second_body,
         out_shape=(shape, shape),
-        in_specs=[pl.BlockSpec(memory_space=pltpu.SMEM)] * 2 + vmem_specs(2 + count),
+        in_specs=[pl.BlockSpec(memory_space=pltpu.SMEM)] * 2 + vmem_specs(4 + count),
         out_specs=tuple(vmem_specs(2)),
         scratch_shapes=[pltpu.VMEM((2 * count * cols, tokens), BF16)],
         compiler_params=pltpu.CompilerParams(vmem_limit_bytes=32 << 20),
-        cost_estimate=pl.CostEstimate(
-            flops=2 * count * cols * tokens * width, bytes_accessed=6 << 20, transcendentals=0
-        ),
+        cost_estimate=pl.CostEstimate(flops=1000, bytes_accessed=1000, transcendentals=0),
         name="mlp_second",
-    )(chip, core, own_act, peer_act, *weights)
+    )(chip, core, own_a, peer_a, own_b, peer_b, *weights)
 
 
 def last_body(core_ref, own_part, peer_part, updated, mods, finals, final_w, predicted, mlp_t):
@@ -292,9 +284,7 @@
         out_specs=vmem_specs(1)[0],
         scratch_shapes=[pltpu.VMEM((width, rows), F32)],
         compiler_params=pltpu.CompilerParams(vmem_limit_bytes=24 << 20),
-        cost_estimate=pl.CostEstimate(
-            flops=2 * rows * width * final_w.shape[1], bytes_accessed=3 << 20, transcendentals=rows
-        ),
+        cost_estimate=pl.CostEstimate(flops=1000, bytes_accessed=1000, transcendentals=0),
         name="last",
     )(core, own_part, peer_part, updated, mods, finals, final_w)
 
@@ -335,28 +325,24 @@
     chip, core = chip[None], core[None]
 
     qkv_t = qkv_weight.T
-    mlp_mine = jnp.concatenate(
-        [mlp_in_weight.T, mlp_out_weight[:width].T, mlp_out_weight[width:].T], axis=0
+    early = 7 * tok_rows // 8
+    mlp_cols = mlp_in_weight.shape[1]
+    mlp_in_t = mlp_in_weight.T
+    part_a = mlp_in_t[:early]
+    part_b = jnp.concatenate(
+        [mlp_in_t[early:], mlp_out_weight[:width].T, mlp_out_weight[width:].T], axis=0
     )
     qkv_near = ring_first(qkv_t)
+    part_a, part_b, qkv_near = lax.optimization_barrier((part_a, part_b, qkv_near))
     qkv_next = ring_second(*qkv_near)
     qkv_far = ring_third(*qkv_next[:2])
     qkv_pieces = [qkv_t, *qkv_near, qkv_far[0], *qkv_next[2:], qkv_far[1]]
 
-    mlp_mine, qkv_next = lax.optimization_barrier((mlp_mine, qkv_next))
-    mlp_near = ring_first(mlp_mine)
+    part_a, qkv_low, qkv_high = lax.optimization_barrier((part_a, qkv_next[2], qkv_next[3]))
+    near_a = ring_first(part_a)
 
     image_in = modulate(hidden[0], mods[0], mods[1])
     peer_in = swap(image_in, "img", 1)
-    mine, theirs = project_qkv(chip, image_in, peer_in, qkv_pieces)
-    other = swap(theirs, "img", 1)
-    first = jnp.where(core[0] == 0, mine, other)
-    second = jnp.where(core[0] == 0, other, mine)
-    qkv = jnp.stack([first, second], axis=1).reshape(3, HEADS, HEAD, tok_rows)
-    heads = qkv.transpose(1, 0, 2, 3).reshape(HEADS, 3 * HEAD, tok_rows)
-    heads = jnp.pad(heads, ((0, blocks - HEADS), (0, 0), (0, 0)))
-    parts = lax.all_to_all(heads, "blk", 0, 0, tiled=True)
-
     head = jnp.minimum(blk, HEADS - 1)
     text_in = modulate(text_hidden[0], text_mod[0, 0], text_mod[0, 1])
     text_cols = jnp.concatenate(
@@ -370,20 +356,37 @@
         text_cols, text_in, (((0,), (1,)), ((), ())), preferred_element_type=F32
     ).astype(BF16)
     text_kv = jnp.pad(text_kv, ((0, 0), (0, -text_kv.shape[1] % tok_rows)))
-
-    parts, mlp_near = lax.optimization_barrier((parts, mlp_near))
-    mlp_next = ring_second(*mlp_near)
+    text_kv, peer_in = lax.optimization_barrier((text_kv, peer_in))
+
+    mine, theirs = project_qkv(chip, image_in, peer_in, qkv_pieces)
+    theirs, near_a, part_b = lax.optimization_barrier((theirs, near_a, part_b))
+    other = swap(theirs, "img", 1)
+    first = jnp.where(core[0] == 0, mine, other)
+    second = jnp.where(core[0] == 0, other, mine)
+    qkv = jnp.stack([first, second], axis=1).reshape(3, HEADS, HEAD, tok_rows)
+    heads = qkv.transpose(1, 0, 2, 3).reshape(HEADS, 3 * HEAD, tok_rows)
+    heads = jnp.pad(heads, ((0, blocks - HEADS), (0, 0), (0, 0)))
+    next_a = ring_second(*near_a)
+    near_b = ring_first(part_b)
+    parts = lax.all_to_all(heads, "blk", 0, 0, tiled=True)
+
+    parts, next_a, near_b = lax.optimization_barrier((parts, next_a, near_b))
+    far_a = ring_third(*next_a[:2])
+    next_b = ring_second(*near_b)
     mixed = attend(counts, parts, text_kv)
+    mixed, far_a, low_b, high_b = lax.optimization_barrier((mixed, far_a, next_b[0], next_b[1]))
+    far_b = ring_third(low_b, high_b)
     mixed = lax.all_to_all(mixed, "blk", 0, 0, tiled=True)[:HEADS].reshape(width_attn, tok_rows)
-
-    mixed, mlp_low, mlp_high = lax.optimization_barrier((mixed, mlp_next[0], mlp_next[1]))
-    mlp_far = ring_third(mlp_low, mlp_high)
-    mlp_pieces = [mlp_mine, *mlp_near, mlp_far[0], *mlp_next[2:], mlp_far[1]]
+    pieces_a = [part_a, *near_a, far_a[0], *next_a[2:], far_a[1]]
+    pieces_b = [part_b, *near_b, far_b[0], *next_b[2:], far_b[1]]
 
     updated, mlp_in = middle(mixed, hidden[0], mods, out_weight)
-    act = mlp_first(chip, mlp_in, swap(mlp_in, "img", 1), mlp_pieces)
-    peer_act = swap(act, "img", 1)
-    own_part, sent_part = mlp_second(chip, core, act, peer_act, mlp_pieces)
+    peer_mlp = swap(mlp_in, "img", 1)
+    act_a = mlp_first(chip, mlp_in, peer_mlp, pieces_a, early)
+    peer_a = swap(act_a, "img", 1)
+    act_b = mlp_first(chip, mlp_in, peer_mlp, pieces_b, mlp_cols - early)
+    peer_b = swap(act_b, "img", 1)
+    own_part, sent_part = mlp_second(chip, core, act_a, peer_a, act_b, peer_b, pieces_b)
     peer_part = swap(sent_part, "img", 1)
     predicted = last(core, own_part, peer_part, updated, mods, final_mod[0], final_weight)
 

time: 183 us -> 193 us (1.055)
  waiting for transfers between devices: 78.7 us -> 56.3 us
  starting transfers between devices: 52.2 us -> 65.9 us
  local copies, waits for them, and re-layouts: 13.3 us -> 24.5 us
  Pallas kernels: 26.5 us -> 29.9 us
  other arithmetic: 6.13 us -> 9.05 us
    ppermute x9 -> x12, waiting for transfers between devices: 29.4 us -> 19.2 us  [swap(): lax.ppermute(x, axis, [(i, i ^ bits) for i in range(lax.axis_size(axis))])]
    unnamed x32 -> x61, local copies, waits for them, and re-layouts: 3.41 us -> 12.4 us
    ppermute x12 -> x18, starting transfers between devices: 19.7 us -> 28.6 us  [ring(): return lax.ppermute(x, axis, [(i, (i + step) % size) for i in range(size)])]
    ppermute x12 -> x18, waiting for transfers between devices: 41.4 us -> 33.3 us  [ring(): return lax.ppermute(x, axis, [(i, (i + step) % size) for i in range(size)])]
    ppermute x1, waiting for transfers between devices: 3.81 us -> 0.01 us  [padded(): after = lax.ppermute(x[:width], axis, down)]
    pallas_call x1 -> x2, Pallas kernels: 4.59 us -> 7.45 us  [mlp_first(): pl.pallas_call(first_body, out_shape=jax.ShapeDtypeStruct((count, cols, 2...]
    ppermute x9 -> x12, starting transfers between devices: 9.91 us -> 12.6 us  [swap(): lax.ppermute(x, axis, [(i, i ^ bits) for i in range(lax.axis_size(axis))])]
    ppermute x1, starting transfers between devices: 3.39 us -> 5.43 us  [padded(): before = lax.ppermute(x[length - width:], axis, up)]
  transfers between devices with their start and end apart: 25 -> 34, of which waited for: 14 -> 12; matrix products, arithmetic and copies ran while one was open for 8% -> 10% of each run, Pallas kernels for 7% -> 13%
where the time goes in v2:
time: 193 us; the launch traced here: 190 us
  starting transfers between devices  65.9 us (34%)
  waiting for transfers between devices  56.3 us (29%)
  Pallas kernels  29.9 us (15%)
  local copies, waits for them, and re-layouts  24.5 us (13%)
  other arithmetic  9.05 us (5%)
  between operations  2.73 us (1%)
  matrix products  2.03 us (1%)
    ppermute x18, waiting for transfers between devices, ring(): return lax.ppermute(x, axis, [(i, (i + step) % size) for i in range(size)])  33.3 us
    ppermute x18, starting transfers between devices, ring(): return lax.ppermute(x, axis, [(i, (i + step) % size) for i in range(size)])  28.6 us
    ppermute x12, waiting for transfers between devices, swap(): lax.ppermute(x, axis, [(i, i ^ bits) for i in range(lax.axis_size(axis))])  19.2 us
    ppermute x12, starting transfers between devices, swap(): lax.ppermute(x, axis, [(i, i ^ bits) for i in range(lax.axis_size(axis))])  12.6 us
    unnamed x61, local copies, waits for them, and re-layouts  12.4 us
    pallas_call x1, Pallas kernels, attend(): pl.pallas_call(attend_body, out_shape=jax.ShapeDtypeStruct((blocks, HEAD,...  11.4 us
    all_to_all x1, starting transfers between devices, per_device(): parts = lax.all_to_all(heads, 'blk', 0, 0, tiled=True)  8.59 us
    all_to_all x1, starting transfers between devices, per_device(): lax.all_to_all(mixed, 'blk', 0, 0, tiled=True)[:HEADS]  8.13 us
  transfers between devices with their start and end apart: 34, of which 12 were waited for; matrix products, arithmetic and copies ran while one was open for 10% of the time, Pallas kernels for 13%

profile of v2, /device:TPU:104, one launch (start us, length us, event | category | flops | bytes accessed | tf_op | source)
XLA Modules:
  0.0 190.4 jit_solution(551573792453177843)
XLA Ops:
  4.0 2.3 %collective-permute-start.3 = (bf16[144,1536]{1,0:T(8,128)(2,1)}, bf16[144,1536]{1,0:T(8,128)(2,1)S(1)}, u32[]{:S(2)}, u32[]{:S(2)}) collective-permute-start(bf16[144,1536]{1,0:T(8,128)(2,1)} %bitcast.87), channel_id=1, source_target_pairs={{0,2},{1,3},{2,0},{3,1},{4,6},{5,7},{6,4},{7,5},{8,10},{9,11},{10,... | collective-permute-start | bytes 1327112 | tf_op jit(solution)/shard_map/ppermute | solution.py:38
  14.6 2.5 %collective-permute-done.3.refs_3_ = bf16[144,1536]{1,0:T(8,128)(2,1)S(1)} collective-permute-done((bf16[144,1536]{1,0:T(8,128)(2,1)}, bf16[144,1536]{1,0:T(8,128)(2,1)S(1)}, u32[]{:S(2)}, u32[]{:S(2)}) %collective-permute-start.3) | collective-permute-done | bytes 442400 | tf_op jit(solution)/shard_map/ppermute | solution.py:38
  17.4 2.3 %constant_dynamic-slice_fusion.1 = (bf16[1536,64]{1,0:T(8,128)(2,1)}, bf16[1536,64]{1,0:T(8,128)(2,1)}) fusion(bf16[1536,1536]{1,0:T(8,128)(2,1)} %param.25, s32[]{:T(128)S(6)} %select_n.75, s32[]{:T(128)S(6)} %select_n.76), kind=kLoop, calls=%fused_computation.70 | loop fusion | bytes 786440 | tf_op jit(solution)/shard_map/dynamic_slice | solution.py:350
  23.0 1.8 collective-permute-start.5
  24.8 1.9 %collective-permute-done.4 = bf16[72,1536]{1,0:T(8,128)(2,1)S(1)} collective-permute-done((bf16[72,1536]{1,0:T(8,128)(2,1)S(1)}, bf16[72,1536]{1,0:T(8,128)(2,1)S(1)}, u32[]{:S(2)}, u32[]{:S(2)}) %collective-permute-start.4) | collective-permute-done | bytes 221216 | tf_op jit(solution)/shard_map/ppermute | solution.py:50
  26.7 9.1 %collective-permute-done.5 = bf16[72,1536]{1,0:T(8,128)(2,1)S(1)} collective-permute-done((bf16[72,1536]{1,0:T(8,128)(2,1)S(1)}, bf16[72,1536]{1,0:T(8,128)(2,1)S(1)}, u32[]{:S(2)}, u32[]{:S(2)}) %collective-permute-start.5) | collective-permute-done | bytes 221216 | tf_op jit(solution)/shard_map/ppermute | solution.py:50
  35.8 2.4 %collective-permute-start.8 = (bf16[144,1536]{1,0:T(8,128)(2,1)S(1)}, bf16[144,1536]{1,0:T(8,128)(2,1)}, u32[]{:S(2)}, u32[]{:S(2)}) collective-permute-start(bf16[144,1536]{1,0:T(8,128)(2,1)S(1)} %constant_dynamic-update-slice_fusion.refs_4_), channel_id=1, source_target_pairs={{0,2},{1,3},{2,0},{3,1},{4,6},{5,7},{6,4},{7,5},{8,10},{9,11},{10,... | collective-permute-start | bytes 1327112 | tf_op jit(solution)/shard_map/ppermute | solution.py:38
  39.5 2.0 %collective-permute-start.10 = (bf16[112,1536]{1,0:T(8,128)(2,1)S(1)}, bf16[112,1536]{1,0:T(8,128)(2,1)}, u32[]{:S(2)}, u32[]{:S(2)}) collective-permute-start(bf16[112,1536]{1,0:T(8,128)(2,1)S(1)} %slice.111.refs_0_), channel_id=1, source_target_pairs={{0,12},{1,13},{2,14},{3,15},{4,0},{5,1},{6,2},{7,3},{8,4},{9,5},{1... | collective-permute-start | bytes 1032200 | tf_op jit(solution)/shard_map/ppermute | solution.py:50
  44.7 5.5 %collective-permute-done.8.refs_7_ = bf16[144,1536]{1,0:T(8,128)(2,1)} collective-permute-done((bf16[144,1536]{1,0:T(8,128)(2,1)S(1)}, bf16[144,1536]{1,0:T(8,128)(2,1)}, u32[]{:S(2)}, u32[]{:S(2)}) %collective-permute-start.8) | collective-permute-done | bytes 442400 | tf_op jit(solution)/shard_map/ppermute | solution.py:38
  52.3 4.3 %project_qkv.1 = (bf16[8,144,128]{2,1,0:T(8,128)(2,1)S(1)}, bf16[8,144,128]{2,1,0:T(8,128)(2,1)}) custom-call(s32[1]{0:T(128)} %bitcast.2.chip_ref, bf16[128,1536]{1,0:T(8,128)(2,1)S(1)} %fusion.12.own_x, bf16[128,1536]{1,0:T(8,128)(2,1)} %collective-permute-done.peer_x, bf16[144,1536]{1,0:T(8,128)(2,1)S(1)} %bitcast.88, ...), custom_call_target="tpu_custom_call" | custom-call | flops 1000 | bytes 1000 | tf_op jit(solution)/shard_map/project_qkv/pallas_call | solution.py:95
  57.6 1.8 collective-permute-done.12
  61.5 8.6 %all-to-all-start = ((bf16[16,192,128]{2,1,0:T(8,128)(2,1)}), bf16[16,192,128]{2,1,0:T(8,128)(2,1)}, u32[]{:S(2)}, u32[]{:S(2)}) async-start(bf16[16,192,128]{2,1,0:T(8,128)(2,1)} %pad.13), calls=%async_computation | async-start | bytes 1572864 | tf_op jit(solution)/shard_map/all_to_all | solution.py:371
  71.3 2.0 %collective-permute-start.18 = (bf16[272,1536]{1,0:T(8,128)(2,1)S(1)}, bf16[272,1536]{1,0:T(8,128)(2,1)S(1)}, u32[]{:S(2)}, u32[]{:S(2)}) collective-permute-start(bf16[272,1536]{1,0:T(8,128)(2,1)S(1)} %pad_maximum_fusion.refs_0_), channel_id=1, source_target_pairs={{0,12},{1,13},{2,14},{3,15},{4,0},{5,1},{6,2},{7,3},{8,4},{9,5},{1... | collective-permute-start | bytes 2506760 | tf_op jit(solution)/shard_map/ppermute | solution.py:50
  73.3 2.3 %collective-permute-start.19 = (bf16[272,1536]{1,0:T(8,128)(2,1)S(1)}, bf16[272,1536]{1,0:T(8,128)(2,1)}, u32[]{:S(2)}, u32[]{:S(2)}) collective-permute-start(bf16[272,1536]{1,0:T(8,128)(2,1)S(1)} %pad_maximum_fusion.refs_0_), channel_id=1, source_target_pairs={{0,2},{1,3},{2,0},{3,1},{4,6},{5,7},{6,4},{7,5},{8,10},{9,11},{10,... | collective-permute-start | bytes 2506760 | tf_op jit(solution)/shard_map/ppermute | solution.py:38
  76.7 3.3 %collective-permute-start.14 = (bf16[56,1536]{1,0:T(8,128)(2,1)S(1)}, bf16[56,1536]{1,0:T(8,128)(2,1)S(1)}, u32[]{:S(2)}, u32[]{:S(2)}) collective-permute-start(bf16[56,1536]{1,0:T(8,128)(2,1)S(1)} %slice.97), channel_id=1, source_target_pairs={{0,12},{1,13},{2,14},{3,15},{4,0},{5,1},{6,2},{7,3},{8,4},{9,5},{1... | collective-permute-start | bytes 516104 | tf_op jit(solution)/shard_map/ppermute | solution.py:50
  80.0 15.2 %collective-permute-done.13 = bf16[56,1536]{1,0:T(8,128)(2,1)S(1)} collective-permute-done((bf16[56,1536]{1,0:T(8,128)(2,1)S(1)}, bf16[56,1536]{1,0:T(8,128)(2,1)S(1)}, u32[]{:S(2)}, u32[]{:S(2)}) %collective-permute-start.13) | collective-permute-done | bytes 172064 | tf_op jit(solution)/shard_map/ppermute | solution.py:50
  95.2 3.2 %collective-permute-start.16 = (bf16[112,1536]{1,0:T(8,128)(2,1)}, bf16[112,1536]{1,0:T(8,128)(2,1)S(1)}, u32[]{:S(2)}, u32[]{:S(2)}) collective-permute-start(bf16[112,1536]{1,0:T(8,128)(2,1)} %collective-permute-done.11.refs_3_), channel_id=1, source_target_pairs={{0,12},{1,13},{2,14},{3,15},{4,0},{5,1},{6,2},{7,3},{8,4},{9,5},{1... | collective-permute-start | bytes 1032200 | tf_op jit(solution)/shard_map/ppermute | solution.py:50
  98.5 7.0 %collective-permute-done.15.refs_5_ = bf16[112,1536]{1,0:T(8,128)(2,1)S(1)} collective-permute-done((bf16[112,1536]{1,0:T(8,128)(2,1)}, bf16[112,1536]{1,0:T(8,128)(2,1)S(1)}, u32[]{:S(2)}, u32[]{:S(2)}) %collective-permute-start.15) | collective-permute-done | bytes 344096 | tf_op jit(solution)/shard_map/ppermute | solution.py:50
  107.1 3.3 %collective-permute-start.22 = (bf16[136,1536]{1,0:T(8,128)(2,1)S(1)}, bf16[136,1536]{1,0:T(8,128)(2,1)}, u32[]{:S(2)}, u32[]{:S(2)}) collective-permute-start(bf16[136,1536]{1,0:T(8,128)(2,1)S(1)} %slice.99), channel_id=1, source_target_pairs={{0,12},{1,13},{2,14},{3,15},{4,0},{5,1},{6,2},{7,3},{8,4},{9,5},{1... | collective-permute-start | bytes 1253384 | tf_op jit(solution)/shard_map/ppermute | solution.py:50
  110.5 2.5 %collective-permute-start.20 = (bf16[112,1536]{1,0:T(8,128)(2,1)S(1)}, bf16[112,1536]{1,0:T(8,128)(2,1)S(1)}, u32[]{:S(2)}, u32[]{:S(2)}) collective-permute-start(bf16[112,1536]{1,0:T(8,128)(2,1)S(1)} %constant_dynamic-update-slice_fusion.2.refs_4_), channel_id=1, source_target_pairs={{0,2},{1,3},{2,0},{3,1},{4,6},{5,7},{6,4},{7,5},{8,10},{9,11},{10,... | collective-permute-start | bytes 1032200 | tf_op jit(solution)/shard_map/ppermute | solution.py:38
  113.7 3.2 %collective-permute-start.26 = (bf16[272,1536]{1,0:T(8,128)(2,1)}, bf16[272,1536]{1,0:T(8,128)(2,1)}, u32[]{:S(2)}, u32[]{:S(2)}) collective-permute-start(bf16[272,1536]{1,0:T(8,128)(2,1)} %collective-permute-done.19.refs_3_), channel_id=1, source_target_pairs={{0,12},{1,13},{2,14},{3,15},{4,0},{5,1},{6,2},{7,3},{8,4},{9,5},{1... | collective-permute-start | bytes 2506760 | tf_op jit(solution)/shard_map/ppermute | solution.py:50
  116.9 11.4 %attend.1 = bf16[16,64,128]{2,1,0:T(8,128)(2,1)S(1)} custom-call(s32[1]{0:T(128)} %copy.54.count_ref, bf16[16,192,128]{2,1,0:T(8,128)(2,1)} %all-to-all-done.parts, bf16[128,256]{1,0:T(8,128)(2,1)S(1)} %pad.12.text), custom_call_target="tpu_custom_call" | custom-call | flops 1000 | bytes 1000 | tf_op jit(solution)/shard_map/attend/pallas_call | solution.py:152
  129.8 8.1 %all-to-all-start.1 = ((bf16[16,64,128]{2,1,0:T(8,128)(2,1)}), bf16[16,64,128]{2,1,0:T(8,128)(2,1)}, u32[]{:S(2)}, u32[]{:S(2)}) async-start(bf16[16,64,128]{2,1,0:T(8,128)(2,1)} %copy-done.3), calls=%async_computation.1 | async-start | bytes 524288 | tf_op jit(solution)/shard_map/all_to_all | solution.py:379
  137.9 1.8 constant_dynamic-update-slice_fusion.5
  139.7 1.8 constant_dynamic-update-slice_fusion.4.refs_4_
  142.6 2.7 %all-to-all-done.1 = bf16[16,64,128]{2,1,0:T(8,128)(2,1)} async-done(((bf16[16,64,128]{2,1,0:T(8,128)(2,1)}), bf16[16,64,128]{2,1,0:T(8,128)(2,1)}, u32[]{:S(2)}, u32[]{:S(2)}) %all-to-all-start.1) | async-done | bytes 262176 | tf_op jit(solution)/shard_map/all_to_all | solution.py:379
  151.5 3.2 %mlp_first.2.own_a = bf16[8,112,256]{2,1,0:T(8,128)(2,1)S(1)} custom-call(s32[1]{0:T(128)} %bitcast.2.chip_ref, bf16[128,1536]{1,0:T(8,128)(2,1)S(1)} %get-tuple-element.56.own_x, bf16[128,1536]{1,0:T(8,128)(2,1)S(1)} %collective-permute-done.23.peer_x, bf16[112,1536]{1,0:T(8,128)(2,1)S(1)} %slice.111.refs_0_, bf16[112,1536]{1,0:T(8,128)(2,1)S(1)} %copy-done.7, ...), custom_call_target="tpu_custom_call" | custom-call | flops 1000 | bytes 1000 | tf_op jit(solution)/shard_map/mlp_first/pallas_call | solution.py:217
  155.0 6.1 %collective-permute-done.27.refs_7_ = bf16[272,1536]{1,0:T(8,128)(2,1)} collective-permute-done((bf16[272,1536]{1,0:T(8,128)(2,1)}, bf16[272,1536]{1,0:T(8,128)(2,1)}, u32[]{:S(2)}, u32[]{:S(2)}) %collective-permute-start.27) | collective-permute-done | bytes 835616 | tf_op jit(solution)/shard_map/ppermute | solution.py:38
  161.1 4.2 %mlp_first.3.own_b = bf16[8,80,256]{2,1,0:T(8,128)(2,1)S(1)} custom-call(s32[1]{0:T(128)} %bitcast.2.chip_ref, bf16[128,1536]{1,0:T(8,128)(2,1)S(1)} %get-tuple-element.56.own_x, bf16[128,1536]{1,0:T(8,128)(2,1)S(1)} %collective-permute-done.23.peer_x, bf16[272,1536]{1,0:T(8,128)(2,1)S(1)} %pad_maximum_fusion.refs_0_, ...), custom_call_target="tpu_custom_call" | custom-call | flops 1000 | bytes 1000 | tf_op jit(solution)/shard_map/mlp_first/pallas_call | solution.py:217
  167.0 5.2 %mlp_second.1 = (f32[8,96,128]{2,1,0:T(8,128)S(1)}, f32[8,96,128]{2,1,0:T(8,128)}) custom-call(s32[1]{0:T(128)} %bitcast.2.chip_ref, s32[1]{0:T(128)} %bitcast.1.core_ref, bf16[8,112,256]{2,1,0:T(8,128)(2,1)S(1)} %mlp_first.2.own_a, bf16[8,112,256]{2,1,0:T(8,128)(2,1)S(1)} %collective-permute-done.24.peer_a, bf16[8,80,256]{2,1,0:T(8,128)(2,1)S(1)} %mlp_first.3.own_b, ...), custom_call_target="tpu_custom_call" | custom-call | flops 1000 | bytes 1000 | tf_op jit(solution)/shard_map/mlp_second/pallas_call | solution.py:255
  178.5 2.5 %collective-permute-start.31 = (bf16[1,2048]{1,0:T(2,128)(2,1)S(1)}, bf16[1,2048]{1,0:T(2,128)(2,1)S(1)}, u32[]{:S(2)}, u32[]{:S(2)}) collective-permute-start(bf16[1,2048]{1,0:T(2,128)(2,1)S(1)} %get-tuple-element.86), channel_id=1, source_target_pairs={{16,0},{32,16},{48,32},{64,48},{80,64},{96,80},{112,96},{128,112},... | collective-permute-start | bytes 12296 | tf_op jit(solution)/shard_map/ppermute | solution.py:297
  181.1 5.4 %collective-permute-start.30 = (bf16[1,2048]{1,0:T(2,128)(2,1)S(1)}, bf16[1,2048]{1,0:T(2,128)(2,1)S(1)}, u32[]{:S(2)}, u32[]{:S(2)}) collective-permute-start(bf16[1,2048]{1,0:T(2,128)(2,1)S(1)} %get-tuple-element.85), channel_id=1, source_target_pairs={{0,16},{16,32},{32,48},{48,64},{64,80},{80,96},{96,112},{112,128},... | collective-permute-start | bytes 12296 | tf_op jit(solution)/shard_map/ppermute | solution.py:296
  (163 shorter events, 48.6 us)
Async XLA Ops:
  0.7 13.9 %collective-permute-start.1 = (bf16[144,1536]{1,0:T(8,128)(2,1)}, bf16[144,1536]{1,0:T(8,128)(2,1)S(1)}, u32[]{:S(2)}, u32[]{:S(2)}) collective-permute-start(bf16[144,1536]{1,0:T(8,128)(2,1)} %bitcast.85), channel_id=1, source_target_pairs={{0,4},{1,5},{2,6},{3,7},{4,8},{5,9},{6,10},{7,11},{8,12},{9,13},{1... | collective-permute-start | bytes 1327112 | tf_op jit(solution)/shard_map/ppermute | solution.py:50
  2.2 12.3 %collective-permute-start.2 = (bf16[144,1536]{1,0:T(8,128)(2,1)}, bf16[144,1536]{1,0:T(8,128)(2,1)S(1)}, u32[]{:S(2)}, u32[]{:S(2)}) collective-permute-start(bf16[144,1536]{1,0:T(8,128)(2,1)} %bitcast.86), channel_id=1, source_target_pairs={{0,12},{1,13},{2,14},{3,15},{4,0},{5,1},{6,2},{7,3},{8,4},{9,5},{1... | collective-permute-start | bytes 1327112 | tf_op jit(solution)/shard_map/ppermute | solution.py:50
  4.0 13.1 %collective-permute-start.3 = (bf16[144,1536]{1,0:T(8,128)(2,1)}, bf16[144,1536]{1,0:T(8,128)(2,1)S(1)}, u32[]{:S(2)}, u32[]{:S(2)}) collective-permute-start(bf16[144,1536]{1,0:T(8,128)(2,1)} %bitcast.87), channel_id=1, source_target_pairs={{0,2},{1,3},{2,0},{3,1},{4,6},{5,7},{6,4},{7,5},{8,10},{9,11},{10,... | collective-permute-start | bytes 1327112 | tf_op jit(solution)/shard_map/ppermute | solution.py:38
  11.4 33.3 %collective-permute-start = (bf16[128,1536]{1,0:T(8,128)(2,1)S(1)}, bf16[128,1536]{1,0:T(8,128)(2,1)}, u32[]{:S(2)}, u32[]{:S(2)}) collective-permute-start(bf16[128,1536]{1,0:T(8,128)(2,1)S(1)} %fusion.12.own_x), channel_id=1, source_target_pairs={{0,1},{1,0},{2,3},{3,2},{4,5},{5,4},{6,7},{7,6},{8,9},{9,8},{10,11... | collective-permute-start | bytes 1179656 | tf_op jit(solution)/shard_map/ppermute | solution.py:38
  17.1 9.7 %collective-permute-start.4 = (bf16[72,1536]{1,0:T(8,128)(2,1)S(1)}, bf16[72,1536]{1,0:T(8,128)(2,1)S(1)}, u32[]{:S(2)}, u32[]{:S(2)}) collective-permute-start(bf16[72,1536]{1,0:T(8,128)(2,1)S(1)} %slice.94), channel_id=1, source_target_pairs={{0,4},{1,5},{2,6},{3,7},{4,8},{5,9},{6,10},{7,11},{8,12},{9,13},{1... | collective-permute-start | bytes 663560 | tf_op jit(solution)/shard_map/ppermute | solution.py:50
  19.7 18.5 %collective-permute-start.6 = (bf16[144,1536]{1,0:T(8,128)(2,1)S(1)}, bf16[144,1536]{1,0:T(8,128)(2,1)}, u32[]{:S(2)}, u32[]{:S(2)}) collective-permute-start(bf16[144,1536]{1,0:T(8,128)(2,1)S(1)} %collective-permute-done.3.refs_3_), channel_id=1, source_target_pairs={{0,4},{1,5},{2,6},{3,7},{4,8},{5,9},{6,10},{7,11},{8,12},{9,13},{1... | collective-permute-start | bytes 1327112 | tf_op jit(solution)/shard_map/ppermute | solution.py:50
  21.2 17.0 %collective-permute-start.7 = (bf16[144,1536]{1,0:T(8,128)(2,1)S(1)}, bf16[144,1536]{1,0:T(8,128)(2,1)}, u32[]{:S(2)}, u32[]{:S(2)}) collective-permute-start(bf16[144,1536]{1,0:T(8,128)(2,1)S(1)} %collective-permute-done.3.refs_3_), channel_id=1, source_target_pairs={{0,12},{1,13},{2,14},{3,15},{4,0},{5,1},{6,2},{7,3},{8,4},{9,5},{1... | collective-permute-start | bytes 1327112 | tf_op jit(solution)/shard_map/ppermute | solution.py:50
  23.0 12.8 %collective-permute-start.5 = (bf16[72,1536]{1,0:T(8,128)(2,1)S(1)}, bf16[72,1536]{1,0:T(8,128)(2,1)S(1)}, u32[]{:S(2)}, u32[]{:S(2)}) collective-permute-start(bf16[72,1536]{1,0:T(8,128)(2,1)S(1)} %slice.95), channel_id=1, source_target_pairs={{0,12},{1,13},{2,14},{3,15},{4,0},{5,1},{6,2},{7,3},{8,4},{9,5},{1... | collective-permute-start | bytes 663560 | tf_op jit(solution)/shard_map/ppermute | solution.py:50
  35.8 14.4 %collective-permute-start.8 = (bf16[144,1536]{1,0:T(8,128)(2,1)S(1)}, bf16[144,1536]{1,0:T(8,128)(2,1)}, u32[]{:S(2)}, u32[]{:S(2)}) collective-permute-start(bf16[144,1536]{1,0:T(8,128)(2,1)S(1)} %constant_dynamic-update-slice_fusion.refs_4_), channel_id=1, source_target_pairs={{0,2},{1,3},{2,0},{3,1},{4,6},{5,7},{6,4},{7,5},{8,10},{9,11},{10,... | collective-permute-start | bytes 1327112 | tf_op jit(solution)/shard_map/ppermute | solution.py:38
  38.2 19.1 %collective-permute-start.9 = (bf16[112,1536]{1,0:T(8,128)(2,1)S(1)}, bf16[112,1536]{1,0:T(8,128)(2,1)S(1)}, u32[]{:S(2)}, u32[]{:S(2)}) collective-permute-start(bf16[112,1536]{1,0:T(8,128)(2,1)S(1)} %slice.111.refs_0_), channel_id=1, source_target_pairs={{0,4},{1,5},{2,6},{3,7},{4,8},{5,9},{6,10},{7,11},{8,12},{9,13},{1... | collective-permute-start | bytes 1032200 | tf_op jit(solution)/shard_map/ppermute | solution.py:50
  39.5 17.8 %collective-permute-start.10 = (bf16[112,1536]{1,0:T(8,128)(2,1)S(1)}, bf16[112,1536]{1,0:T(8,128)(2,1)}, u32[]{:S(2)}, u32[]{:S(2)}) collective-permute-start(bf16[112,1536]{1,0:T(8,128)(2,1)S(1)} %slice.111.refs_0_), channel_id=1, source_target_pairs={{0,12},{1,13},{2,14},{3,15},{4,0},{5,1},{6,2},{7,3},{8,4},{9,5},{1... | collective-permute-start | bytes 1032200 | tf_op jit(solution)/shard_map/ppermute | solution.py:50
  41.5 15.8 %collective-permute-start.11 = (bf16[112,1536]{1,0:T(8,128)(2,1)S(1)}, bf16[112,1536]{1,0:T(8,128)(2,1)}, u32[]{:S(2)}, u32[]{:S(2)}) collective-permute-start(bf16[112,1536]{1,0:T(8,128)(2,1)S(1)} %slice.111.refs_0_), channel_id=1, source_target_pairs={{0,2},{1,3},{2,0},{3,1},{4,6},{5,7},{6,4},{7,5},{8,10},{9,11},{10,... | collective-permute-start | bytes 1032200 | tf_op jit(solution)/shard_map/ppermute | solution.py:38
  57.3 2.1 %collective-permute-start.12 = (bf16[8,144,128]{2,1,0:T(8,128)(2,1)}, bf16[8,144,128]{2,1,0:T(8,128)(2,1)S(1)}, u32[]{:S(2)}, u32[]{:S(2)}) collective-permute-start(bf16[8,144,128]{2,1,0:T(8,128)(2,1)} %get-tuple-element.44), channel_id=1, source_target_pairs={{0,1},{1,0},{2,3},{3,2},{4,5},{5,4},{6,7},{7,6},{8,9},{9,8},{10,11... | collective-permute-start | bytes 884744 | tf_op jit(solution)/shard_map/ppermute | solution.py:38
  61.5 45.4 %all-to-all-start = ((bf16[16,192,128]{2,1,0:T(8,128)(2,1)}), bf16[16,192,128]{2,1,0:T(8,128)(2,1)}, u32[]{:S(2)}, u32[]{:S(2)}) async-start(bf16[16,192,128]{2,1,0:T(8,128)(2,1)} %pad.13), calls=%async_computation | async-start | bytes 1572864 | tf_op jit(solution)/shard_map/all_to_all | solution.py:371
  70.1 36.8 %collective-permute-start.17 = (bf16[272,1536]{1,0:T(8,128)(2,1)S(1)}, bf16[272,1536]{1,0:T(8,128)(2,1)S(1)}, u32[]{:S(2)}, u32[]{:S(2)}) collective-permute-start(bf16[272,1536]{1,0:T(8,128)(2,1)S(1)} %pad_maximum_fusion.refs_0_), channel_id=1, source_target_pairs={{0,4},{1,5},{2,6},{3,7},{4,8},{5,9},{6,10},{7,11},{8,12},{9,13},{1... | collective-permute-start | bytes 2506760 | tf_op jit(solution)/shard_map/ppermute | solution.py:50
  71.3 35.6 %collective-permute-start.18 = (bf16[272,1536]{1,0:T(8,128)(2,1)S(1)}, bf16[272,1536]{1,0:T(8,128)(2,1)S(1)}, u32[]{:S(2)}, u32[]{:S(2)}) collective-permute-start(bf16[272,1536]{1,0:T(8,128)(2,1)S(1)} %pad_maximum_fusion.refs_0_), channel_id=1, source_target_pairs={{0,12},{1,13},{2,14},{3,15},{4,0},{5,1},{6,2},{7,3},{8,4},{9,5},{1... | collective-permute-start | bytes 2506760 | tf_op jit(solution)/shard_map/ppermute | solution.py:50
  73.3 33.6 %collective-permute-start.19 = (bf16[272,1536]{1,0:T(8,128)(2,1)S(1)}, bf16[272,1536]{1,0:T(8,128)(2,1)}, u32[]{:S(2)}, u32[]{:S(2)}) collective-permute-start(bf16[272,1536]{1,0:T(8,128)(2,1)S(1)} %pad_maximum_fusion.refs_0_), channel_id=1, source_target_pairs={{0,2},{1,3},{2,0},{3,1},{4,6},{5,7},{6,4},{7,5},{8,10},{9,11},{10,... | collective-permute-start | bytes 2506760 | tf_op jit(solution)/shard_map/ppermute | solution.py:38
  75.7 19.6 %collective-permute-start.13 = (bf16[56,1536]{1,0:T(8,128)(2,1)S(1)}, bf16[56,1536]{1,0:T(8,128)(2,1)S(1)}, u32[]{:S(2)}, u32[]{:S(2)}) collective-permute-start(bf16[56,1536]{1,0:T(8,128)(2,1)S(1)} %slice.96), channel_id=1, source_target_pairs={{0,4},{1,5},{2,6},{3,7},{4,8},{5,9},{6,10},{7,11},{8,12},{9,13},{1... | collective-permute-start | bytes 516104 | tf_op jit(solution)/shard_map/ppermute | solution.py:50
  76.7 18.6 %collective-permute-start.14 = (bf16[56,1536]{1,0:T(8,128)(2,1)S(1)}, bf16[56,1536]{1,0:T(8,128)(2,1)S(1)}, u32[]{:S(2)}, u32[]{:S(2)}) collective-permute-start(bf16[56,1536]{1,0:T(8,128)(2,1)S(1)} %slice.97), channel_id=1, source_target_pairs={{0,12},{1,13},{2,14},{3,15},{4,0},{5,1},{6,2},{7,3},{8,4},{9,5},{1... | collective-permute-start | bytes 516104 | tf_op jit(solution)/shard_map/ppermute | solution.py:50
  95.2 10.2 %collective-permute-start.15 = (bf16[112,1536]{1,0:T(8,128)(2,1)}, bf16[112,1536]{1,0:T(8,128)(2,1)S(1)}, u32[]{:S(2)}, u32[]{:S(2)}) collective-permute-start(bf16[112,1536]{1,0:T(8,128)(2,1)} %collective-permute-done.11.refs_3_), channel_id=1, source_target_pairs={{0,4},{1,5},{2,6},{3,7},{4,8},{5,9},{6,10},{7,11},{8,12},{9,13},{1... | collective-permute-start | bytes 1032200 | tf_op jit(solution)/shard_map/ppermute | solution.py:50
  95.2 10.9 %collective-permute-start.16 = (bf16[112,1536]{1,0:T(8,128)(2,1)}, bf16[112,1536]{1,0:T(8,128)(2,1)S(1)}, u32[]{:S(2)}, u32[]{:S(2)}) collective-permute-start(bf16[112,1536]{1,0:T(8,128)(2,1)} %collective-permute-done.11.refs_3_), channel_id=1, source_target_pairs={{0,12},{1,13},{2,14},{3,15},{4,0},{5,1},{6,2},{7,3},{8,4},{9,5},{1... | collective-permute-start | bytes 1032200 | tf_op jit(solution)/shard_map/ppermute | solution.py:50
  107.0 22.8 %collective-permute-start.21 = (bf16[136,1536]{1,0:T(8,128)(2,1)S(1)}, bf16[136,1536]{1,0:T(8,128)(2,1)}, u32[]{:S(2)}, u32[]{:S(2)}) collective-permute-start(bf16[136,1536]{1,0:T(8,128)(2,1)S(1)} %slice.98), channel_id=1, source_target_pairs={{0,4},{1,5},{2,6},{3,7},{4,8},{5,9},{6,10},{7,11},{8,12},{9,13},{1... | collective-permute-start | bytes 1253384 | tf_op jit(solution)/shard_map/ppermute | solution.py:50
  107.1 22.7 %collective-permute-start.22 = (bf16[136,1536]{1,0:T(8,128)(2,1)S(1)}, bf16[136,1536]{1,0:T(8,128)(2,1)}, u32[]{:S(2)}, u32[]{:S(2)}) collective-permute-start(bf16[136,1536]{1,0:T(8,128)(2,1)S(1)} %slice.99), channel_id=1, source_target_pairs={{0,12},{1,13},{2,14},{3,15},{4,0},{5,1},{6,2},{7,3},{8,4},{9,5},{1... | collective-permute-start | bytes 1253384 | tf_op jit(solution)/shard_map/ppermute | solution.py:50
  110.5 18.6 %collective-permute-start.20 = (bf16[112,1536]{1,0:T(8,128)(2,1)S(1)}, bf16[112,1536]{1,0:T(8,128)(2,1)S(1)}, u32[]{:S(2)}, u32[]{:S(2)}) collective-permute-start(bf16[112,1536]{1,0:T(8,128)(2,1)S(1)} %constant_dynamic-update-slice_fusion.2.refs_4_), channel_id=1, source_target_pairs={{0,2},{1,3},{2,0},{3,1},{4,6},{5,7},{6,4},{7,5},{8,10},{9,11},{10,... | collective-permute-start | bytes 1032200 | tf_op jit(solution)/shard_map/ppermute | solution.py:38
  113.6 41.3 %collective-permute-start.25 = (bf16[272,1536]{1,0:T(8,128)(2,1)}, bf16[272,1536]{1,0:T(8,128)(2,1)}, u32[]{:S(2)}, u32[]{:S(2)}) collective-permute-start(bf16[272,1536]{1,0:T(8,128)(2,1)} %collective-permute-done.19.refs_3_), channel_id=1, source_target_pairs={{0,4},{1,5},{2,6},{3,7},{4,8},{5,9},{6,10},{7,11},{8,12},{9,13},{1... | collective-permute-start | bytes 2506760 | tf_op jit(solution)/shard_map/ppermute | solution.py:50
  113.7 41.2 %collective-permute-start.26 = (bf16[272,1536]{1,0:T(8,128)(2,1)}, bf16[272,1536]{1,0:T(8,128)(2,1)}, u32[]{:S(2)}, u32[]{:S(2)}) collective-permute-start(bf16[272,1536]{1,0:T(8,128)(2,1)} %collective-permute-done.19.refs_3_), channel_id=1, source_target_pairs={{0,12},{1,13},{2,14},{3,15},{4,0},{5,1},{6,2},{7,3},{8,4},{9,5},{1... | collective-permute-start | bytes 2506760 | tf_op jit(solution)/shard_map/ppermute | solution.py:50
  129.8 15.6 %all-to-all-start.1 = ((bf16[16,64,128]{2,1,0:T(8,128)(2,1)}), bf16[16,64,128]{2,1,0:T(8,128)(2,1)}, u32[]{:S(2)}, u32[]{:S(2)}) async-start(bf16[16,64,128]{2,1,0:T(8,128)(2,1)} %copy-done.3), calls=%async_computation.1 | async-start | bytes 524288 | tf_op jit(solution)/shard_map/all_to_all | solution.py:379
  141.5 19.6 %collective-permute-start.27 = (bf16[272,1536]{1,0:T(8,128)(2,1)}, bf16[272,1536]{1,0:T(8,128)(2,1)}, u32[]{:S(2)}, u32[]{:S(2)}) collective-permute-start(bf16[272,1536]{1,0:T(8,128)(2,1)} %constant_dynamic-update-slice_fusion.4.refs_4_), channel_id=1, source_target_pairs={{0,2},{1,3},{2,0},{3,1},{4,6},{5,7},{6,4},{7,5},{8,10},{9,11},{10,... | collective-permute-start | bytes 2506760 | tf_op jit(solution)/shard_map/ppermute | solution.py:38
  154.7 12.3 %collective-permute-start.24 = (bf16[8,112,256]{2,1,0:T(8,128)(2,1)S(1)}, bf16[8,112,256]{2,1,0:T(8,128)(2,1)S(1)}, u32[]{:S(2)}, u32[]{:S(2)}) collective-permute-start(bf16[8,112,256]{2,1,0:T(8,128)(2,1)S(1)} %mlp_first.2.own_a), channel_id=1, source_target_pairs={{0,1},{1,0},{2,3},{3,2},{4,5},{5,4},{6,7},{7,6},{8,9},{9,8},{10,11... | collective-permute-start | bytes 1376264 | tf_op jit(solution)/shard_map/ppermute | solution.py:38
  172.2 2.3 %collective-permute-start.29 = (f32[8,96,128]{2,1,0:T(8,128)}, f32[8,96,128]{2,1,0:T(8,128)S(1)}, u32[]{:S(2)}, u32[]{:S(2)}) collective-permute-start(f32[8,96,128]{2,1,0:T(8,128)} %get-tuple-element.65), channel_id=1, source_target_pairs={{0,1},{1,0},{2,3},{3,2},{4,5},{5,4},{6,7},{7,6},{8,9},{9,8},{10,11... | collective-permute-start | bytes 1179656 | tf_op jit(solution)/shard_map/ppermute | solution.py:38
  178.5 8.1 %collective-permute-start.31 = (bf16[1,2048]{1,0:T(2,128)(2,1)S(1)}, bf16[1,2048]{1,0:T(2,128)(2,1)S(1)}, u32[]{:S(2)}, u32[]{:S(2)}) collective-permute-start(bf16[1,2048]{1,0:T(2,128)(2,1)S(1)} %get-tuple-element.86), channel_id=1, source_target_pairs={{16,0},{32,16},{48,32},{64,48},{80,64},{96,80},{112,96},{128,112},... | collective-permute-start | bytes 12296 | tf_op jit(solution)/shard_map/ppermute | solution.py:297
  181.1 6.8 %collective-permute-start.30 = (bf16[1,2048]{1,0:T(2,128)(2,1)S(1)}, bf16[1,2048]{1,0:T(2,128)(2,1)S(1)}, u32[]{:S(2)}, u32[]{:S(2)}) collective-permute-start(bf16[1,2048]{1,0:T(2,128)(2,1)S(1)} %get-tuple-element.85), channel_id=1, source_target_pairs={{0,16},{16,32},{32,48},{48,64},{64,80},{80,96},{96,112},{112,128},... | collective-permute-start | bytes 12296 | tf_op jit(solution)/shard_map/ppermute | solution.py:296
  (30 other events, 420.4 us)

commit v3 on v2

--- a/solution.py
+++ b/solution.py
@@ -79,13 +79,15 @@
     weights, (own_out, peer_out) = refs[:-2], refs[-2:]
     rows = own_x.shape[0]
     both = jnp.concatenate([own_x[...], peer_x[...]], axis=0)
-    for k, weight in enumerate(weights):
-        part = lax.dot_general(
-            weight[...], both, (((1,), (1,)), ((), ())), preferred_element_type=F32
-        ).astype(BF16)
+    cols = own_out.shape[1]
+    stacked = jnp.concatenate([weight[...] for weight in weights], axis=0)
+    parts = lax.dot_general(
+        stacked, both, (((1,), (1,)), ((), ())), preferred_element_type=F32
+    ).astype(BF16)
+    for k in range(len(weights)):
         place = place_of(chip_ref[0], k)
-        own_out[place] = part[:, :rows]
-        peer_out[place] = part[:, rows:]
+        own_out[place] = parts[k * cols : (k + 1) * cols, :rows]
+        peer_out[place] = parts[k * cols : (k + 1) * cols, rows:]
 
 
 def project_qkv(chip, own_x, peer_x, weights):
@@ -201,92 +203,81 @@
 
 
 def first_body(chip_ref, own_x, peer_x, *refs):
-    weights, out = refs[:-1], refs[-1]
+    weights, (own_out, peer_out) = refs[:-2], refs[-2:]
+    rows = own_x.shape[0]
     both = jnp.concatenate([own_x[...], peer_x[...]], axis=0)
-    cols = out.shape[1]
-    for k, weight in enumerate(weights):
-        part = lax.dot_general(
-            weight[:cols], both, (((1,), (1,)), ((), ())), preferred_element_type=F32
-        )
-        out[place_of(chip_ref[0], k)] = gelu(part).astype(BF16)
-
-
-def mlp_first(chip, own_x, peer_x, weights, cols):
+    cols = own_out.shape[1]
+    stacked = jnp.concatenate([weight[...] for weight in weights], axis=0)
+    parts = lax.dot_general(stacked, both, (((1,), (1,)), ((), ())), preferred_element_type=F32)
+    for k in range(len(weights)):
+        place = place_of(chip_ref[0], k)
+        act = gelu(parts[k * cols : (k + 1) * cols]).astype(BF16)
+        own_out[place] = act[:, :rows]
+        peer_out[place] = act[:, rows:]
+
+
+def mlp_first(chip, own_x, peer_x, weights):
     rows = own_x.shape[0]
     count = len(weights)
+    shape = jax.ShapeDtypeStruct((count, weights[0].shape[0], rows), BF16)
     return pl.pallas_call(
         first_body,
-        out_shape=jax.ShapeDtypeStruct((count, cols, 2 * rows), BF16),
+        out_shape=(shape, shape),
         in_specs=[pl.BlockSpec(memory_space=pltpu.SMEM)] + vmem_specs(2 + count),
-        out_specs=vmem_specs(1)[0],
-        compiler_params=pltpu.CompilerParams(vmem_limit_bytes=32 << 20),
+        out_specs=tuple(vmem_specs(2)),
+        compiler_params=pltpu.CompilerParams(vmem_limit_bytes=40 << 20),
         cost_estimate=pl.CostEstimate(flops=1000, bytes_accessed=1000, transcendentals=0),
         name="mlp_first",
     )(chip, own_x, peer_x, *weights)
 
 
-def second_body(chip_ref, core_ref, own_a, peer_a, own_b, peer_b, *refs):
-    weights, (own_out, peer_out), act = refs[:-3], refs[-3:-1], refs[-1]
-    count, early, tokens = own_a.shape
-    late = own_b.shape[1]
-    cols, mid = early + late, tokens // 2
-    core = core_ref[0]
-    for c in range(count):
-        for own, peer, shift, size in ((own_a, peer_a, 0, early), (own_b, peer_b, early, late)):
-            mine = pl.ds(pl.multiple_of((2 * c + core) * cols + shift, 16), size)
-            act[mine, :] = own[c]
-            other = pl.ds(pl.multiple_of((2 * c + 1 - core) * cols + shift, 16), size)
-            act[other, :mid] = peer[c, :, mid:]
-            act[other, mid:] = peer[c, :, :mid]
-    width = weights[0].shape[1]
-    half = cols // 2
-    for k, weight in enumerate(weights):
-        part = jnp.dot(weight[late : late + half], act[:width], preferred_element_type=F32)
-        part += jnp.dot(weight[late + half :], act[width:], preferred_element_type=F32)
-        place = place_of(chip_ref[0], k)
-        own_out[place] = part[:, :mid]
-        peer_out[place] = part[:, mid:]
-
-
-def mlp_second(chip, core, own_a, peer_a, own_b, peer_b, weights):
-    count, early, tokens = own_a.shape
-    cols = early + own_b.shape[1]
-    shape = jax.ShapeDtypeStruct((count, cols // 2, tokens // 2), F32)
+def second_body(core_ref, own_act, peer_act, updated, mods, finals, final_t, weight, predicted, act, mlp_t):
+    i = pl.program_id(0)
+    count, cols, _ = own_act.shape
+    half = weight.shape[0]
+
+    @pl.when(i == 0)
+    def _():
+        for source, parity in ((own_act, core_ref[0]), (peer_act, 1 - core_ref[0])):
+            for c in range(count):
+                start = pl.multiple_of((2 * c + parity) * cols, cols)
+                act[pl.ds(start, cols), :] = source[c]
+
+    mlp_t[pl.ds(pl.multiple_of(i * half, half), half), :] = jnp.dot(
+        weight[...], act[...], preferred_element_type=F32
+    )
+
+    @pl.when(i == pl.num_programs(0) - 1)
+    def _():
+        refined = updated[...] + mods[5:6] * mlp_t[...].T
+        final_in = layer_norm(refined, finals[0:1], finals[1:2])
+        predicted[...] = lax.dot_general(
+            final_in, final_t[...], (((1,), (1,)), ((), ())), preferred_element_type=F32
+        )
+
+
+def mlp_second(core, own_act, peer_act, updated, mods, finals, final_t, weight):
+    rows, width = updated.shape
+    steps = 6
+    half = width // steps
+    wide = weight.shape[1]
+
+    def whole(x):
+        return pl.BlockSpec(x.shape, lambda i: (0,) * x.ndim)
+
     return pl.pallas_call(
         second_body,
-        out_shape=(shape, shape),
-        in_specs=[pl.BlockSpec(memory_space=pltpu.SMEM)] * 2 + vmem_specs(4 + count),
-        out_specs=tuple(vmem_specs(2)),
-        scratch_shapes=[pltpu.VMEM((2 * count * cols, tokens), BF16)],
+        out_shape=jax.ShapeDtypeStruct((rows, final_t.shape[0]), F32),
+        grid=(steps,),
+        in_specs=[pl.BlockSpec(memory_space=pltpu.SMEM)]
+        + [whole(x) for x in (own_act, peer_act, updated, mods, finals, final_t)]
+        + [pl.BlockSpec((half, wide), lambda i: (i, 0))],
+        out_specs=pl.BlockSpec((rows, final_t.shape[0]), lambda i: (0, 0)),
+        scratch_shapes=[pltpu.VMEM((wide, rows), BF16), pltpu.VMEM((width, rows), F32)],
         compiler_params=pltpu.CompilerParams(vmem_limit_bytes=32 << 20),
         cost_estimate=pl.CostEstimate(flops=1000, bytes_accessed=1000, transcendentals=0),
         name="mlp_second",
-    )(chip, core, own_a, peer_a, own_b, peer_b, *weights)
-
-
-def last_body(core_ref, own_part, peer_part, updated, mods, finals, final_w, predicted, mlp_t):
-    count, half, _ = own_part.shape
-    for source, parity in ((own_part, core_ref[0]), (peer_part, 1 - core_ref[0])):
-        for c in range(count):
-            start = pl.multiple_of((2 * c + parity) * half, half)
-            mlp_t[pl.ds(start, half), :] = source[c]
-    refined = updated[...] + mods[5:6] * mlp_t[...].T
-    final_in = layer_norm(refined, finals[0:1], finals[1:2])
-    predicted[...] = jnp.dot(final_in, final_w[...], preferred_element_type=F32)
-
-
-def last(core, own_part, peer_part, updated, mods, finals, final_w):
-    rows, width = updated.shape
-    return pl.pallas_call(
-        last_body,
-        out_shape=jax.ShapeDtypeStruct((rows, final_w.shape[1]), F32),
-        in_specs=[pl.BlockSpec(memory_space=pltpu.SMEM)] + vmem_specs(6),
-        out_specs=vmem_specs(1)[0],
-        scratch_shapes=[pltpu.VMEM((width, rows), F32)],
-        compiler_params=pltpu.CompilerParams(vmem_limit_bytes=24 << 20),
-        cost_estimate=pl.CostEstimate(flops=1000, bytes_accessed=1000, transcendentals=0),
-        name="last",
-    )(core, own_part, peer_part, updated, mods, finals, final_w)
+    )(core, own_act, peer_act, updated, mods, finals, final_t, weight)
 
 
 def padded(x, axis, width):
@@ -324,22 +315,14 @@
     mods = image_mod[0]
     chip, core = chip[None], core[None]
 
-    qkv_t = qkv_weight.T
-    early = 7 * tok_rows // 8
-    mlp_cols = mlp_in_weight.shape[1]
-    mlp_in_t = mlp_in_weight.T
-    part_a = mlp_in_t[:early]
-    part_b = jnp.concatenate(
-        [mlp_in_t[early:], mlp_out_weight[:width].T, mlp_out_weight[width:].T], axis=0
-    )
+    mlp_out_t = lax.all_gather(mlp_out_weight.T, "img", axis=0, tiled=True)
+    qkv_t, mlp_in_t = qkv_weight.T, mlp_in_weight.T
     qkv_near = ring_first(qkv_t)
-    part_a, part_b, qkv_near = lax.optimization_barrier((part_a, part_b, qkv_near))
     qkv_next = ring_second(*qkv_near)
     qkv_far = ring_third(*qkv_next[:2])
     qkv_pieces = [qkv_t, *qkv_near, qkv_far[0], *qkv_next[2:], qkv_far[1]]
-
-    part_a, qkv_low, qkv_high = lax.optimization_barrier((part_a, qkv_next[2], qkv_next[3]))
-    near_a = ring_first(part_a)
+    mlp_in_t, qkv_left, qkv_right = lax.optimization_barrier((mlp_in_t, *qkv_next[2:]))
+    mlp_near = ring_first(mlp_in_t)
 
     image_in = modulate(hidden[0], mods[0], mods[1])
     peer_in = swap(image_in, "img", 1)
@@ -359,36 +342,28 @@
     text_kv, peer_in = lax.optimization_barrier((text_kv, peer_in))
 
     mine, theirs = project_qkv(chip, image_in, peer_in, qkv_pieces)
-    theirs, near_a, part_b = lax.optimization_barrier((theirs, near_a, part_b))
     other = swap(theirs, "img", 1)
     first = jnp.where(core[0] == 0, mine, other)
     second = jnp.where(core[0] == 0, other, mine)
     qkv = jnp.stack([first, second], axis=1).reshape(3, HEADS, HEAD, tok_rows)
     heads = qkv.transpose(1, 0, 2, 3).reshape(HEADS, 3 * HEAD, tok_rows)
     heads = jnp.pad(heads, ((0, blocks - HEADS), (0, 0), (0, 0)))
-    next_a = ring_second(*near_a)
-    near_b = ring_first(part_b)
     parts = lax.all_to_all(heads, "blk", 0, 0, tiled=True)
 
-    parts, next_a, near_b = lax.optimization_barrier((parts, next_a, near_b))
-    far_a = ring_third(*next_a[:2])
-    next_b = ring_second(*near_b)
+    parts, mlp_near = lax.optimization_barrier((parts, mlp_near))
+    mlp_next = ring_second(*mlp_near)
     mixed = attend(counts, parts, text_kv)
-    mixed, far_a, low_b, high_b = lax.optimization_barrier((mixed, far_a, next_b[0], next_b[1]))
-    far_b = ring_third(low_b, high_b)
+    mixed, low, high = lax.optimization_barrier((mixed, mlp_next[0], mlp_next[1]))
+    mlp_far = ring_third(low, high)
     mixed = lax.all_to_all(mixed, "blk", 0, 0, tiled=True)[:HEADS].reshape(width_attn, tok_rows)
-    pieces_a = [part_a, *near_a, far_a[0], *next_a[2:], far_a[1]]
-    pieces_b = [part_b, *near_b, far_b[0], *next_b[2:], far_b[1]]
+    mlp_pieces = [mlp_in_t, *mlp_near, mlp_far[0], *mlp_next[2:], mlp_far[1]]
 
     updated, mlp_in = middle(mixed, hidden[0], mods, out_weight)
-    peer_mlp = swap(mlp_in, "img", 1)
-    act_a = mlp_first(chip, mlp_in, peer_mlp, pieces_a, early)
-    peer_a = swap(act_a, "img", 1)
-    act_b = mlp_first(chip, mlp_in, peer_mlp, pieces_b, mlp_cols - early)
-    peer_b = swap(act_b, "img", 1)
-    own_part, sent_part = mlp_second(chip, core, act_a, peer_a, act_b, peer_b, pieces_b)
-    peer_part = swap(sent_part, "img", 1)
-    predicted = last(core, own_part, peer_part, updated, mods, final_mod[0], final_weight)
+    act, sent_act = mlp_first(chip, mlp_in, swap(mlp_in, "img", 1), mlp_pieces)
+    peer_act = swap(sent_act, "img", 1)
+    predicted = mlp_second(
+        core, act, peer_act, updated, mods, final_mod[0], final_weight.T, mlp_out_t
+    )
 
     patch_count = counts[0]
     patch_rows = tok_rows // W_P

time: 193 us -> 187 us (0.969)
  starting transfers between devices: 65.9 us -> 52 us
  between operations: 2.73 us -> 15.9 us
  waiting for transfers between devices: 56.3 us -> 68.8 us
  local copies, waits for them, and re-layouts: 24.5 us -> 14.9 us
  Pallas kernels: 29.9 us -> 23 us
    ppermute x12 -> x8, waiting for transfers between devices: 19.2 us -> 31 us  [swap(): lax.ppermute(x, axis, [(i, i ^ bits) for i in range(lax.axis_size(axis))])]
    ppermute x18 -> x12, starting transfers between devices: 28.6 us -> 19.9 us  [ring(): return lax.ppermute(x, axis, [(i, (i + step) % size) for i in range(size)])]
    pallas_call x4 -> x2, Pallas kernels: 13.4 us -> 8.21 us  [the longest x1 4.22 us: mlp_second(): pl.pallas_call(second_body, out_shape=jax.ShapeDtypeStruct((rows, final_t...]
    ppermute x18 -> x12, waiting for transfers between devices: 33.3 us -> 28.1 us  [ring(): return lax.ppermute(x, axis, [(i, (i + step) % size) for i in range(size)])]
    unnamed x61 -> x27, local copies, waits for them, and re-layouts: 12.4 us -> 7.26 us
    ppermute x1, waiting for transfers between devices: 0.01 us -> 4.35 us  [padded(): after = lax.ppermute(x[:width], axis, down)]
    ppermute x12 -> x8, starting transfers between devices: 12.6 us -> 8.87 us  [swap(): lax.ppermute(x, axis, [(i, i ^ bits) for i in range(lax.axis_size(axis))])]
    all_to_all x1, waiting for transfers between devices: 2.73 us -> 4.69 us  [per_device(): lax.all_to_all(mixed, 'blk', 0, 0, tiled=True)[:HEADS]]
  transfers between devices with their start and end apart: 34 -> 25, of which waited for: 12 -> 11; matrix products, arithmetic and copies ran while one was open for 10% -> 9% of each run, Pallas kernels for 13% -> 10%
where the time goes in v3:
time: 187 us; the launch traced here: 186 us
  waiting for transfers between devices  68.8 us (37%)
  starting transfers between devices  52 us (28%)
  Pallas kernels  23 us (12%)
  between operations  15.9 us (9%)
  local copies, waits for them, and re-layouts  14.9 us (8%)
  other arithmetic  9.07 us (5%)
  matrix products  2.04 us (1%)
    ppermute x8, waiting for transfers between devices, swap(): lax.ppermute(x, axis, [(i, i ^ bits) for i in range(lax.axis_size(axis))])  31 us
    ppermute x12, waiting for transfers between devices, ring(): return lax.ppermute(x, axis, [(i, (i + step) % size) for i in range(size)])  28.1 us
    ppermute x12, starting transfers between devices, ring(): return lax.ppermute(x, axis, [(i, (i + step) % size) for i in range(size)])  19.9 us
    pallas_call x1, Pallas kernels, attend(): pl.pallas_call(attend_body, out_shape=jax.ShapeDtypeStruct((blocks, HEAD,...  10.9 us
    ppermute x8, starting transfers between devices, swap(): lax.ppermute(x, axis, [(i, i ^ bits) for i in range(lax.axis_size(axis))])  8.87 us
    all_to_all x1, starting transfers between devices, per_device(): parts = lax.all_to_all(heads, 'blk', 0, 0, tiled=True)  8.58 us
    all_to_all x1, starting transfers between devices, per_device(): lax.all_to_all(mixed, 'blk', 0, 0, tiled=True)[:HEADS]  7.91 us
    unnamed x27, local copies, waits for them, and re-layouts  7.26 us
  transfers between devices with their start and end apart: 25, of which 11 were waited for; matrix products, arithmetic and copies ran while one was open for 9% of the time, Pallas kernels for 10%

profile of v3, /device:TPU:104, one launch (start us, length us, event | category | flops | bytes accessed | tf_op | source)
XLA Modules:
  0.0 185.8 jit_solution(6074980033574053949)
XLA Ops:
  7.9 1.6 collective-permute-start.1
  9.5 1.7 collective-permute-start.2
  11.2 2.3 %collective-permute-start.3 = (bf16[144,1536]{1,0:T(8,128)(2,1)}, bf16[144,1536]{1,0:T(8,128)(2,1)S(1)}, u32[]{:S(2)}, u32[]{:S(2)}) collective-permute-start(bf16[144,1536]{1,0:T(8,128)(2,1)} %bitcast.91), channel_id=1, source_target_pairs={{0,2},{1,3},{2,0},{3,1},{4,6},{5,7},{6,4},{7,5},{8,10},{9,11},{10,... | collective-permute-start | bytes 1327112 | tf_op jit(solution)/shard_map/ppermute | solution.py:38
  21.7 2.3 %constant_dynamic-slice_fusion.1 = (bf16[1536,64]{1,0:T(8,128)(2,1)}, bf16[1536,64]{1,0:T(8,128)(2,1)}) fusion(bf16[1536,1536]{1,0:T(8,128)(2,1)} %param.25, s32[]{:T(128)S(6)} %select_n.75, s32[]{:T(128)S(6)} %select_n.76), kind=kLoop, calls=%fused_computation.65 | loop fusion | bytes 786440 | tf_op jit(solution)/shard_map/dynamic_slice | solution.py:333
  24.0 3.0 %collective-permute-start.5 = (bf16[72,1536]{1,0:T(8,128)(2,1)S(1)}, bf16[72,1536]{1,0:T(8,128)(2,1)S(1)}, u32[]{:S(2)}, u32[]{:S(2)}) collective-permute-start(bf16[72,1536]{1,0:T(8,128)(2,1)S(1)} %slice.88), channel_id=1, source_target_pairs={{0,12},{1,13},{2,14},{3,15},{4,0},{5,1},{6,2},{7,3},{8,4},{9,5},{1... | collective-permute-start | bytes 663560 | tf_op jit(solution)/shard_map/ppermute | solution.py:50
  27.1 3.2 %collective-permute-start.7 = (bf16[144,1536]{1,0:T(8,128)(2,1)S(1)}, bf16[144,1536]{1,0:T(8,128)(2,1)}, u32[]{:S(2)}, u32[]{:S(2)}) collective-permute-start(bf16[144,1536]{1,0:T(8,128)(2,1)S(1)} %collective-permute-done.3.refs_3_), channel_id=1, source_target_pairs={{0,12},{1,13},{2,14},{3,15},{4,0},{5,1},{6,2},{7,3},{8,4},{9,5},{1... | collective-permute-start | bytes 1327112 | tf_op jit(solution)/shard_map/ppermute | solution.py:50
  30.3 2.2 %collective-permute-done.4 = bf16[72,1536]{1,0:T(8,128)(2,1)S(1)} collective-permute-done((bf16[72,1536]{1,0:T(8,128)(2,1)S(1)}, bf16[72,1536]{1,0:T(8,128)(2,1)S(1)}, u32[]{:S(2)}, u32[]{:S(2)}) %collective-permute-start.4) | collective-permute-done | bytes 221216 | tf_op jit(solution)/shard_map/ppermute | solution.py:50
  32.6 4.2 %collective-permute-done.5 = bf16[72,1536]{1,0:T(8,128)(2,1)S(1)} collective-permute-done((bf16[72,1536]{1,0:T(8,128)(2,1)S(1)}, bf16[72,1536]{1,0:T(8,128)(2,1)S(1)}, u32[]{:S(2)}, u32[]{:S(2)}) %collective-permute-start.5) | collective-permute-done | bytes 221216 | tf_op jit(solution)/shard_map/ppermute | solution.py:50
  36.7 3.2 %collective-permute-start.8 = (bf16[144,1536]{1,0:T(8,128)(2,1)S(1)}, bf16[144,1536]{1,0:T(8,128)(2,1)}, u32[]{:S(2)}, u32[]{:S(2)}) collective-permute-start(bf16[144,1536]{1,0:T(8,128)(2,1)S(1)} %constant_dynamic-update-slice_fusion.refs_4_), channel_id=1, source_target_pairs={{0,2},{1,3},{2,0},{3,1},{4,6},{5,7},{6,4},{7,5},{8,10},{9,11},{10,... | collective-permute-start | bytes 1327112 | tf_op jit(solution)/shard_map/ppermute | solution.py:38
  40.0 1.8 convolution_convert_fusion
  41.9 7.5 %collective-permute-done.6.refs_5_ = bf16[144,1536]{1,0:T(8,128)(2,1)S(1)} collective-permute-done((bf16[144,1536]{1,0:T(8,128)(2,1)S(1)}, bf16[144,1536]{1,0:T(8,128)(2,1)S(1)}, u32[]{:S(2)}, u32[]{:S(2)}) %collective-permute-start.6) | collective-permute-done | bytes 442400 | tf_op jit(solution)/shard_map/ppermute | solution.py:50
  50.7 3.1 %project_qkv.1 = (bf16[8,144,128]{2,1,0:T(8,128)(2,1)S(1)}, bf16[8,144,128]{2,1,0:T(8,128)(2,1)}) custom-call(s32[1]{0:T(128)} %bitcast.2.chip_ref, bf16[128,1536]{1,0:T(8,128)(2,1)S(1)} %fusion.12.own_x, bf16[128,1536]{1,0:T(8,128)(2,1)} %collective-permute-done.peer_x, bf16[144,1536]{1,0:T(8,128)(2,1)S(1)} %bitcast.92, ...), custom_call_target="tpu_custom_call" | custom-call | flops 1000 | bytes 1000 | tf_op jit(solution)/shard_map/project_qkv/pallas_call | solution.py:97
  53.8 1.8 collective-permute-done.9
  56.8 8.6 %all-to-all-start = ((bf16[16,192,128]{2,1,0:T(8,128)(2,1)}), bf16[16,192,128]{2,1,0:T(8,128)(2,1)S(1)}, u32[]{:S(2)}, u32[]{:S(2)}) async-start(bf16[16,192,128]{2,1,0:T(8,128)(2,1)} %pad.13), calls=%async_computation | async-start | bytes 1572864 | tf_op jit(solution)/shard_map/all_to_all | solution.py:351
  65.4 1.5 collective-permute-start.10
  66.9 1.8 collective-permute-start.11
  70.2 12.9 %collective-permute-done.10.refs_1_ = bf16[192,1536]{1,0:T(8,128)(2,1)S(1)} collective-permute-done((bf16[192,1536]{1,0:T(8,128)(2,1)S(1)}, bf16[192,1536]{1,0:T(8,128)(2,1)S(1)}, u32[]{:S(2)}, u32[]{:S(2)}) %collective-permute-start.10) | collective-permute-done | bytes 589856 | tf_op jit(solution)/shard_map/ppermute | solution.py:50
  83.1 22.8 %collective-permute-done.12.refs_3_ = bf16[192,1536]{1,0:T(8,128)(2,1)} collective-permute-done((bf16[192,1536]{1,0:T(8,128)(2,1)S(1)}, bf16[192,1536]{1,0:T(8,128)(2,1)}, u32[]{:S(2)}, u32[]{:S(2)}) %collective-permute-start.12) | collective-permute-done | bytes 589856 | tf_op jit(solution)/shard_map/ppermute | solution.py:38
  106.2 3.1 %collective-permute-start.14 = (bf16[96,1536]{1,0:T(8,128)(2,1)S(1)}, bf16[96,1536]{1,0:T(8,128)(2,1)S(1)}, u32[]{:S(2)}, u32[]{:S(2)}) collective-permute-start(bf16[96,1536]{1,0:T(8,128)(2,1)S(1)} %slice.75), channel_id=1, source_target_pairs={{0,12},{1,13},{2,14},{3,15},{4,0},{5,1},{6,2},{7,3},{8,4},{9,5},{1... | collective-permute-start | bytes 884744 | tf_op jit(solution)/shard_map/ppermute | solution.py:50
  110.0 3.2 %collective-permute-start.17 = (bf16[192,1536]{1,0:T(8,128)(2,1)}, bf16[192,1536]{1,0:T(8,128)(2,1)}, u32[]{:S(2)}, u32[]{:S(2)}) collective-permute-start(bf16[192,1536]{1,0:T(8,128)(2,1)} %collective-permute-done.12.refs_3_), channel_id=1, source_target_pairs={{0,12},{1,13},{2,14},{3,15},{4,0},{5,1},{6,2},{7,3},{8,4},{9,5},{1... | collective-permute-start | bytes 1769480 | tf_op jit(solution)/shard_map/ppermute | solution.py:50
  113.2 10.9 %attend.1 = bf16[16,64,128]{2,1,0:T(8,128)(2,1)} custom-call(s32[1]{0:T(128)} %copy.50.count_ref, bf16[16,192,128]{2,1,0:T(8,128)(2,1)S(1)} %all-to-all-done.parts, bf16[128,256]{1,0:T(8,128)(2,1)S(1)} %pad.12.text), custom_call_target="tpu_custom_call" | custom-call | flops 1000 | bytes 1000 | tf_op jit(solution)/shard_map/attend/pallas_call | solution.py:154
  124.1 7.9 %all-to-all-start.1 = ((bf16[16,64,128]{2,1,0:T(8,128)(2,1)}), bf16[16,64,128]{2,1,0:T(8,128)(2,1)S(1)}, u32[]{:S(2)}, u32[]{:S(2)}) async-start(bf16[16,64,128]{2,1,0:T(8,128)(2,1)} %attend.1), calls=%async_computation.1 | async-start | bytes 524288 | tf_op jit(solution)/shard_map/all_to_all | solution.py:358
  132.1 1.7 collective-permute-start.18
  134.6 4.7 %all-to-all-done.1 = bf16[16,64,128]{2,1,0:T(8,128)(2,1)S(1)} async-done(((bf16[16,64,128]{2,1,0:T(8,128)(2,1)}), bf16[16,64,128]{2,1,0:T(8,128)(2,1)S(1)}, u32[]{:S(2)}, u32[]{:S(2)}) %all-to-all-start.1) | async-done | bytes 262176 | tf_op jit(solution)/shard_map/all_to_all | solution.py:358
  139.3 1.7 copy-done.3
  141.9 6.2 %collective-permute-done.18.refs_7_ = bf16[192,1536]{1,0:T(8,128)(2,1)} collective-permute-done((bf16[192,1536]{1,0:T(8,128)(2,1)S(1)}, bf16[192,1536]{1,0:T(8,128)(2,1)}, u32[]{:S(2)}, u32[]{:S(2)}) %collective-permute-start.18) | collective-permute-done | bytes 589856 | tf_op jit(solution)/shard_map/ppermute | solution.py:38
  149.2 4.0 %mlp_first.1 = (bf16[8,192,128]{2,1,0:T(8,128)(2,1)S(1)}, bf16[8,192,128]{2,1,0:T(8,128)(2,1)}) custom-call(s32[1]{0:T(128)} %bitcast.2.chip_ref, bf16[128,1536]{1,0:T(8,128)(2,1)S(1)} %get-tuple-element.28.own_x, bf16[128,1536]{1,0:T(8,128)(2,1)S(1)} %collective-permute-done.15.peer_x, bf16[192,1536]{1,0:T(8,128)(2,1)S(1)} %bitcast.86, ...), custom_call_target="tpu_custom_call" | custom-call | flops 1000 | bytes 1000 | tf_op jit(solution)/shard_map/mlp_first/pallas_call | solution.py:223
  155.2 3.7 %copy-done.1 = bf16[1536,3072]{1,0:T(8,128)(2,1)S(1)} copy-done((bf16[1536,3072]{1,0:T(8,128)(2,1)S(1)}, bf16[1536,3072]{1,0:T(8,128)(2,1)}, u32[]{:S(2)}) %copy-start.1) | copy-done | bytes 9437208
  158.8 4.2 %mlp_second.1 = f32[128,64]{1,0:T(8,128)S(1)} custom-call(s32[1]{0:T(128)} %bitcast.1.core_ref, bf16[8,192,128]{2,1,0:T(8,128)(2,1)S(1)} %get-tuple-element.32.own_act, bf16[8,192,128]{2,1,0:T(8,128)(2,1)S(1)} %collective-permute-done.19.peer_act, f32[128,1536]{1,0:T(8,128)S(1)} %get-tuple-element.34.updated, f32[6,1536]{1,0:T(8,128)S(1)} %bitcast.88, ...), custom_call_target="tpu_custom_call" | custom-call | flops 1000 | bytes 1000 | tf_op jit(solution)/shard_map/mlp_second/pallas_call | solution.py:268
  163.9 4.8 %collective-permute-start.20 = (bf16[1,2048]{1,0:T(2,128)(2,1)S(1)}, bf16[1,2048]{1,0:T(2,128)(2,1)S(1)}, u32[]{:S(2)}, u32[]{:S(2)}) collective-permute-start(bf16[1,2048]{1,0:T(2,128)(2,1)S(1)} %get-tuple-element.51), channel_id=1, source_target_pairs={{0,16},{16,32},{32,48},{48,64},{64,80},{80,96},{96,112},{112,128},... | collective-permute-start | bytes 12296 | tf_op jit(solution)/shard_map/ppermute | solution.py:287
  168.7 1.9 %collective-permute-start.21 = (bf16[1,2048]{1,0:T(2,128)(2,1)S(1)}, bf16[1,2048]{1,0:T(2,128)(2,1)S(1)}, u32[]{:S(2)}, u32[]{:S(2)}) collective-permute-start(bf16[1,2048]{1,0:T(2,128)(2,1)S(1)} %get-tuple-element.52), channel_id=1, source_target_pairs={{16,0},{32,16},{48,32},{64,48},{80,64},{96,80},{112,96},{128,112},... | collective-permute-start | bytes 12296 | tf_op jit(solution)/shard_map/ppermute | solution.py:288
  172.0 4.4 %collective-permute-done.21 = bf16[1,2048]{1,0:T(2,128)(2,1)S(1)} collective-permute-done((bf16[1,2048]{1,0:T(2,128)(2,1)S(1)}, bf16[1,2048]{1,0:T(2,128)(2,1)S(1)}, u32[]{:S(2)}, u32[]{:S(2)}) %collective-permute-start.21) | collective-permute-done | bytes 4128 | tf_op jit(solution)/shard_map/ppermute | solution.py:288
  (103 shorter events, 22.1 us)
Async XLA Ops:
  7.2 170.5 %copy-start = (bf16[144,512]{1,0:T(8,128)(2,1)S(1)}, bf16[144,512]{1,0:T(8,128)(2,1)}, u32[]{:S(2)}) copy-start(bf16[144,512]{1,0:T(8,128)(2,1)} %param.30) | copy-start | bytes 442372
  7.2 43.5 %copy-start.6 = (bf16[1536,144]{0,1:T(8,128)(2,1)S(1)}, bf16[1536,144]{0,1:T(8,128)(2,1)}, u32[]{:S(2)}) copy-start(bf16[1536,144]{0,1:T(8,128)(2,1)} %param.24) | copy-start | bytes 1327108
  7.2 32.8 %copy-start.10 = (f32[1,2,1536]{2,1,0:T(2,128)S(1)}, f32[1,2,1536]{2,1,0:T(2,128)}, u32[]{:S(2)}) copy-start(f32[1,2,1536]{2,1,0:T(2,128)} %param.20) | copy-start | bytes 36868
  7.2 147.9 %all-gather.2.cloned.1.call-start = ((), (), s32[]{:S(2)}) async-start(), calls=%async_computation.2 | async-start | bytes 10027008 | tf_op jit(solution)/shard_map/all_gather | solution.py:318
  7.9 13.4 %collective-permute-start.1 = (bf16[144,1536]{1,0:T(8,128)(2,1)}, bf16[144,1536]{1,0:T(8,128)(2,1)S(1)}, u32[]{:S(2)}, u32[]{:S(2)}) collective-permute-start(bf16[144,1536]{1,0:T(8,128)(2,1)} %bitcast.89), channel_id=1, source_target_pairs={{0,4},{1,5},{2,6},{3,7},{4,8},{5,9},{6,10},{7,11},{8,12},{9,13},{1... | collective-permute-start | bytes 1327112 | tf_op jit(solution)/shard_map/ppermute | solution.py:50
  9.5 14.5 %collective-permute-start.2 = (bf16[144,1536]{1,0:T(8,128)(2,1)}, bf16[144,1536]{1,0:T(8,128)(2,1)S(1)}, u32[]{:S(2)}, u32[]{:S(2)}) collective-permute-start(bf16[144,1536]{1,0:T(8,128)(2,1)} %bitcast.90), channel_id=1, source_target_pairs={{0,12},{1,13},{2,14},{3,15},{4,0},{5,1},{6,2},{7,3},{8,4},{9,5},{1... | collective-permute-start | bytes 1327112 | tf_op jit(solution)/shard_map/ppermute | solution.py:50
  11.2 15.8 %collective-permute-start.3 = (bf16[144,1536]{1,0:T(8,128)(2,1)}, bf16[144,1536]{1,0:T(8,128)(2,1)S(1)}, u32[]{:S(2)}, u32[]{:S(2)}) collective-permute-start(bf16[144,1536]{1,0:T(8,128)(2,1)} %bitcast.91), channel_id=1, source_target_pairs={{0,2},{1,3},{2,0},{3,1},{4,6},{5,7},{6,4},{7,5},{8,10},{9,11},{10,... | collective-permute-start | bytes 1327112 | tf_op jit(solution)/shard_map/ppermute | solution.py:38
  18.7 23.2 %collective-permute-start = (bf16[128,1536]{1,0:T(8,128)(2,1)S(1)}, bf16[128,1536]{1,0:T(8,128)(2,1)}, u32[]{:S(2)}, u32[]{:S(2)}) collective-permute-start(bf16[128,1536]{1,0:T(8,128)(2,1)S(1)} %fusion.12.own_x), channel_id=1, source_target_pairs={{0,1},{1,0},{2,3},{3,2},{4,5},{5,4},{6,7},{7,6},{8,9},{9,8},{10,11... | collective-permute-start | bytes 1179656 | tf_op jit(solution)/shard_map/ppermute | solution.py:38
  21.4 11.2 %collective-permute-start.4 = (bf16[72,1536]{1,0:T(8,128)(2,1)S(1)}, bf16[72,1536]{1,0:T(8,128)(2,1)S(1)}, u32[]{:S(2)}, u32[]{:S(2)}) collective-permute-start(bf16[72,1536]{1,0:T(8,128)(2,1)S(1)} %slice.87), channel_id=1, source_target_pairs={{0,4},{1,5},{2,6},{3,7},{4,8},{5,9},{6,10},{7,11},{8,12},{9,13},{1... | collective-permute-start | bytes 663560 | tf_op jit(solution)/shard_map/ppermute | solution.py:50
  24.0 12.7 %collective-permute-start.5 = (bf16[72,1536]{1,0:T(8,128)(2,1)S(1)}, bf16[72,1536]{1,0:T(8,128)(2,1)S(1)}, u32[]{:S(2)}, u32[]{:S(2)}) collective-permute-start(bf16[72,1536]{1,0:T(8,128)(2,1)S(1)} %slice.88), channel_id=1, source_target_pairs={{0,12},{1,13},{2,14},{3,15},{4,0},{5,1},{6,2},{7,3},{8,4},{9,5},{1... | collective-permute-start | bytes 663560 | tf_op jit(solution)/shard_map/ppermute | solution.py:50
  27.1 22.3 %collective-permute-start.6 = (bf16[144,1536]{1,0:T(8,128)(2,1)S(1)}, bf16[144,1536]{1,0:T(8,128)(2,1)S(1)}, u32[]{:S(2)}, u32[]{:S(2)}) collective-permute-start(bf16[144,1536]{1,0:T(8,128)(2,1)S(1)} %collective-permute-done.3.refs_3_), channel_id=1, source_target_pairs={{0,4},{1,5},{2,6},{3,7},{4,8},{5,9},{6,10},{7,11},{8,12},{9,13},{1... | collective-permute-start | bytes 1327112 | tf_op jit(solution)/shard_map/ppermute | solution.py:50
  27.1 23.6 %collective-permute-start.7 = (bf16[144,1536]{1,0:T(8,128)(2,1)S(1)}, bf16[144,1536]{1,0:T(8,128)(2,1)}, u32[]{:S(2)}, u32[]{:S(2)}) collective-permute-start(bf16[144,1536]{1,0:T(8,128)(2,1)S(1)} %collective-permute-done.3.refs_3_), channel_id=1, source_target_pairs={{0,12},{1,13},{2,14},{3,15},{4,0},{5,1},{6,2},{7,3},{8,4},{9,5},{1... | collective-permute-start | bytes 1327112 | tf_op jit(solution)/shard_map/ppermute | solution.py:50
  36.7 14.0 %collective-permute-start.8 = (bf16[144,1536]{1,0:T(8,128)(2,1)S(1)}, bf16[144,1536]{1,0:T(8,128)(2,1)}, u32[]{:S(2)}, u32[]{:S(2)}) collective-permute-start(bf16[144,1536]{1,0:T(8,128)(2,1)S(1)} %constant_dynamic-update-slice_fusion.refs_4_), channel_id=1, source_target_pairs={{0,2},{1,3},{2,0},{3,1},{4,6},{5,7},{6,4},{7,5},{8,10},{9,11},{10,... | collective-permute-start | bytes 1327112 | tf_op jit(solution)/shard_map/ppermute | solution.py:38
  53.8 1.8 collective-permute-start.9
  55.7 83.6 %copy-start.2 = (bf16[1,128,1536]{2,1,0:T(8,128)(2,1)S(1)}, bf16[1,128,1536]{2,1,0:T(8,128)(2,1)}, u32[]{:S(2)}) copy-start(bf16[1,128,1536]{2,1,0:T(8,128)(2,1)} %param.16) | copy-start | bytes 1179652
  56.8 49.0 %all-to-all-start = ((bf16[16,192,128]{2,1,0:T(8,128)(2,1)}), bf16[16,192,128]{2,1,0:T(8,128)(2,1)S(1)}, u32[]{:S(2)}, u32[]{:S(2)}) async-start(bf16[16,192,128]{2,1,0:T(8,128)(2,1)} %pad.13), calls=%async_computation | async-start | bytes 1572864 | tf_op jit(solution)/shard_map/all_to_all | solution.py:351
  65.4 17.7 %collective-permute-start.10 = (bf16[192,1536]{1,0:T(8,128)(2,1)S(1)}, bf16[192,1536]{1,0:T(8,128)(2,1)S(1)}, u32[]{:S(2)}, u32[]{:S(2)}) collective-permute-start(bf16[192,1536]{1,0:T(8,128)(2,1)S(1)} %bitcast.83), channel_id=1, source_target_pairs={{0,4},{1,5},{2,6},{3,7},{4,8},{5,9},{6,10},{7,11},{8,12},{9,13},{1... | collective-permute-start | bytes 1769480 | tf_op jit(solution)/shard_map/ppermute | solution.py:50
  66.9 16.1 %collective-permute-start.11 = (bf16[192,1536]{1,0:T(8,128)(2,1)S(1)}, bf16[192,1536]{1,0:T(8,128)(2,1)S(1)}, u32[]{:S(2)}, u32[]{:S(2)}) collective-permute-start(bf16[192,1536]{1,0:T(8,128)(2,1)S(1)} %bitcast.84), channel_id=1, source_target_pairs={{0,12},{1,13},{2,14},{3,15},{4,0},{5,1},{6,2},{7,3},{8,4},{9,5},{1... | collective-permute-start | bytes 1769480 | tf_op jit(solution)/shard_map/ppermute | solution.py:50
  68.7 37.1 %collective-permute-start.12 = (bf16[192,1536]{1,0:T(8,128)(2,1)S(1)}, bf16[192,1536]{1,0:T(8,128)(2,1)}, u32[]{:S(2)}, u32[]{:S(2)}) collective-permute-start(bf16[192,1536]{1,0:T(8,128)(2,1)S(1)} %bitcast.85), channel_id=1, source_target_pairs={{0,2},{1,3},{2,0},{3,1},{4,6},{5,7},{6,4},{7,5},{8,10},{9,11},{10,... | collective-permute-start | bytes 1769480 | tf_op jit(solution)/shard_map/ppermute | solution.py:38
  105.9 18.3 %collective-permute-start.13 = (bf16[96,1536]{1,0:T(8,128)(2,1)S(1)}, bf16[96,1536]{1,0:T(8,128)(2,1)S(1)}, u32[]{:S(2)}, u32[]{:S(2)}) collective-permute-start(bf16[96,1536]{1,0:T(8,128)(2,1)S(1)} %slice.74), channel_id=1, source_target_pairs={{0,4},{1,5},{2,6},{3,7},{4,8},{5,9},{6,10},{7,11},{8,12},{9,13},{1... | collective-permute-start | bytes 884744 | tf_op jit(solution)/shard_map/ppermute | solution.py:50
  106.2 17.9 %collective-permute-start.14 = (bf16[96,1536]{1,0:T(8,128)(2,1)S(1)}, bf16[96,1536]{1,0:T(8,128)(2,1)S(1)}, u32[]{:S(2)}, u32[]{:S(2)}) collective-permute-start(bf16[96,1536]{1,0:T(8,128)(2,1)S(1)} %slice.75), channel_id=1, source_target_pairs={{0,12},{1,13},{2,14},{3,15},{4,0},{5,1},{6,2},{7,3},{8,4},{9,5},{1... | collective-permute-start | bytes 884744 | tf_op jit(solution)/shard_map/ppermute | solution.py:50
  109.9 32.0 %collective-permute-start.16 = (bf16[192,1536]{1,0:T(8,128)(2,1)}, bf16[192,1536]{1,0:T(8,128)(2,1)}, u32[]{:S(2)}, u32[]{:S(2)}) collective-permute-start(bf16[192,1536]{1,0:T(8,128)(2,1)} %collective-permute-done.12.refs_3_), channel_id=1, source_target_pairs={{0,4},{1,5},{2,6},{3,7},{4,8},{5,9},{6,10},{7,11},{8,12},{9,13},{1... | collective-permute-start | bytes 1769480 | tf_op jit(solution)/shard_map/ppermute | solution.py:50
  110.0 31.9 %collective-permute-start.17 = (bf16[192,1536]{1,0:T(8,128)(2,1)}, bf16[192,1536]{1,0:T(8,128)(2,1)}, u32[]{:S(2)}, u32[]{:S(2)}) collective-permute-start(bf16[192,1536]{1,0:T(8,128)(2,1)} %collective-permute-done.12.refs_3_), channel_id=1, source_target_pairs={{0,12},{1,13},{2,14},{3,15},{4,0},{5,1},{6,2},{7,3},{8,4},{9,5},{1... | collective-permute-start | bytes 1769480 | tf_op jit(solution)/shard_map/ppermute | solution.py:50
  124.1 15.1 %all-to-all-start.1 = ((bf16[16,64,128]{2,1,0:T(8,128)(2,1)}), bf16[16,64,128]{2,1,0:T(8,128)(2,1)S(1)}, u32[]{:S(2)}, u32[]{:S(2)}) async-start(bf16[16,64,128]{2,1,0:T(8,128)(2,1)} %attend.1), calls=%async_computation.1 | async-start | bytes 524288 | tf_op jit(solution)/shard_map/all_to_all | solution.py:358
  132.1 23.0 %copy-start.7 = (bf16[1536,64]{0,1:T(8,128)(2,1)S(1)}, bf16[1536,64]{0,1:T(8,128)(2,1)}, u32[]{:S(2)}) copy-start(bf16[1536,64]{0,1:T(8,128)(2,1)} %param.29) | copy-start | bytes 589828
  132.1 23.0 %copy-start.8 = (f32[1,2,1536]{2,1,0:T(2,128)S(1)}, f32[1,2,1536]{2,1,0:T(2,128)}, u32[]{:S(2)}) copy-start(f32[1,2,1536]{2,1,0:T(2,128)} %param.21) | copy-start | bytes 36868
  132.1 16.0 %collective-permute-start.18 = (bf16[192,1536]{1,0:T(8,128)(2,1)S(1)}, bf16[192,1536]{1,0:T(8,128)(2,1)}, u32[]{:S(2)}, u32[]{:S(2)}) collective-permute-start(bf16[192,1536]{1,0:T(8,128)(2,1)S(1)} %constant_dynamic-update-slice_fusion.2.refs_4_), channel_id=1, source_target_pairs={{0,2},{1,3},{2,0},{3,1},{4,6},{5,7},{6,4},{7,5},{8,10},{9,11},{10,... | collective-permute-start | bytes 1769480 | tf_op jit(solution)/shard_map/ppermute | solution.py:38
  141.8 6.3 %collective-permute-start.15 = (bf16[128,1536]{1,0:T(8,128)(2,1)S(1)}, bf16[128,1536]{1,0:T(8,128)(2,1)S(1)}, u32[]{:S(2)}, u32[]{:S(2)}) collective-permute-start(bf16[128,1536]{1,0:T(8,128)(2,1)S(1)} %get-tuple-element.28.own_x), channel_id=1, source_target_pairs={{0,1},{1,0},{2,3},{3,2},{4,5},{5,4},{6,7},{7,6},{8,9},{9,8},{10,11... | collective-permute-start | bytes 1179656 | tf_op jit(solution)/shard_map/ppermute | solution.py:38
  153.2 1.9 %collective-permute-start.19 = (bf16[8,192,128]{2,1,0:T(8,128)(2,1)}, bf16[8,192,128]{2,1,0:T(8,128)(2,1)S(1)}, u32[]{:S(2)}, u32[]{:S(2)}) collective-permute-start(bf16[8,192,128]{2,1,0:T(8,128)(2,1)} %get-tuple-element.33), channel_id=1, source_target_pairs={{0,1},{1,0},{2,3},{3,2},{4,5},{5,4},{6,7},{7,6},{8,9},{9,8},{10,11... | collective-permute-start | bytes 1179656 | tf_op jit(solution)/shard_map/ppermute | solution.py:38
  163.1 14.6 %copy-start.11 = (f32[512]{0:T(512)S(1)}, f32[512]{0:T(512)}, u32[]{:S(2)}) copy-start(f32[512]{0:T(512)} %param.31) | copy-start | bytes 6148
  163.9 8.1 %collective-permute-start.20 = (bf16[1,2048]{1,0:T(2,128)(2,1)S(1)}, bf16[1,2048]{1,0:T(2,128)(2,1)S(1)}, u32[]{:S(2)}, u32[]{:S(2)}) collective-permute-start(bf16[1,2048]{1,0:T(2,128)(2,1)S(1)} %get-tuple-element.51), channel_id=1, source_target_pairs={{0,16},{16,32},{32,48},{48,64},{64,80},{80,96},{96,112},{112,128},... | collective-permute-start | bytes 12296 | tf_op jit(solution)/shard_map/ppermute | solution.py:287
  168.7 7.7 %collective-permute-start.21 = (bf16[1,2048]{1,0:T(2,128)(2,1)S(1)}, bf16[1,2048]{1,0:T(2,128)(2,1)S(1)}, u32[]{:S(2)}, u32[]{:S(2)}) collective-permute-start(bf16[1,2048]{1,0:T(2,128)(2,1)S(1)} %get-tuple-element.52), channel_id=1, source_target_pairs={{16,0},{32,16},{48,32},{64,48},{80,64},{96,80},{112,96},{128,112},... | collective-permute-start | bytes 12296 | tf_op jit(solution)/shard_map/ppermute | solution.py:288
  (5 other events, 23.0 us)
Sparse Core Ops, SparseCore 0:
  10.7 118.6 all-gather.1

commit v4 on v2

--- a/solution.py
+++ b/solution.py
@@ -79,13 +79,15 @@
     weights, (own_out, peer_out) = refs[:-2], refs[-2:]
     rows = own_x.shape[0]
     both = jnp.concatenate([own_x[...], peer_x[...]], axis=0)
-    for k, weight in enumerate(weights):
-        part = lax.dot_general(
-            weight[...], both, (((1,), (1,)), ((), ())), preferred_element_type=F32
-        ).astype(BF16)
+    cols = own_out.shape[1]
+    stacked = jnp.concatenate([weight[...] for weight in weights], axis=0)
+    parts = lax.dot_general(
+        stacked, both, (((1,), (1,)), ((), ())), preferred_element_type=F32
+    ).astype(BF16)
+    for k in range(len(weights)):
         place = place_of(chip_ref[0], k)
-        own_out[place] = part[:, :rows]
-        peer_out[place] = part[:, rows:]
+        own_out[place] = parts[k * cols : (k + 1) * cols, :rows]
+        peer_out[place] = parts[k * cols : (k + 1) * cols, rows:]
 
 
 def project_qkv(chip, own_x, peer_x, weights):
@@ -204,11 +206,10 @@
     weights, out = refs[:-1], refs[-1]
     both = jnp.concatenate([own_x[...], peer_x[...]], axis=0)
     cols = out.shape[1]
-    for k, weight in enumerate(weights):
-        part = lax.dot_general(
-            weight[:cols], both, (((1,), (1,)), ((), ())), preferred_element_type=F32
-        )
-        out[place_of(chip_ref[0], k)] = gelu(part).astype(BF16)
+    stacked = jnp.concatenate([weight[:cols] for weight in weights], axis=0)
+    parts = lax.dot_general(stacked, both, (((1,), (1,)), ((), ())), preferred_element_type=F32)
+    for k in range(len(weights)):
+        out[place_of(chip_ref[0], k)] = gelu(parts[k * cols : (k + 1) * cols]).astype(BF16)
 
 
 def mlp_first(chip, own_x, peer_x, weights, cols):
@@ -240,12 +241,14 @@
             act[other, mid:] = peer[c, :, :mid]
     width = weights[0].shape[1]
     half = cols // 2
-    for k, weight in enumerate(weights):
-        part = jnp.dot(weight[late : late + half], act[:width], preferred_element_type=F32)
-        part += jnp.dot(weight[late + half :], act[width:], preferred_element_type=F32)
+    low = jnp.concatenate([weight[late : late + half] for weight in weights], axis=0)
+    parts = jnp.dot(low, act[:width], preferred_element_type=F32)
+    high = jnp.concatenate([weight[late + half :] for weight in weights], axis=0)
+    parts += jnp.dot(high, act[width:], preferred_element_type=F32)
+    for k in range(count):
         place = place_of(chip_ref[0], k)
-        own_out[place] = part[:, :mid]
-        peer_out[place] = part[:, mid:]
+        own_out[place] = parts[k * half : (k + 1) * half, :mid]
+        peer_out[place] = parts[k * half : (k + 1) * half, mid:]
 
 
 def mlp_second(chip, core, own_a, peer_a, own_b, peer_b, weights):
@@ -332,8 +335,9 @@
     part_b = jnp.concatenate(
         [mlp_in_t[early:], mlp_out_weight[:width].T, mlp_out_weight[width:].T], axis=0
     )
+    image_in = modulate(hidden[0], mods[0], mods[1])
+    part_a, part_b, image_in = lax.optimization_barrier((part_a, part_b, image_in))
     qkv_near = ring_first(qkv_t)
-    part_a, part_b, qkv_near = lax.optimization_barrier((part_a, part_b, qkv_near))
     qkv_next = ring_second(*qkv_near)
     qkv_far = ring_third(*qkv_next[:2])
     qkv_pieces = [qkv_t, *qkv_near, qkv_far[0], *qkv_next[2:], qkv_far[1]]
@@ -341,7 +345,6 @@
     part_a, qkv_low, qkv_high = lax.optimization_barrier((part_a, qkv_next[2], qkv_next[3]))
     near_a = ring_first(part_a)
 
-    image_in = modulate(hidden[0], mods[0], mods[1])
     peer_in = swap(image_in, "img", 1)
     head = jnp.minimum(blk, HEADS - 1)
     text_in = modulate(text_hidden[0], text_mod[0, 0], text_mod[0, 1])
@@ -359,25 +362,27 @@
     text_kv, peer_in = lax.optimization_barrier((text_kv, peer_in))
 
     mine, theirs = project_qkv(chip, image_in, peer_in, qkv_pieces)
-    theirs, near_a, part_b = lax.optimization_barrier((theirs, near_a, part_b))
+    theirs, near_a = lax.optimization_barrier((theirs, near_a))
+    next_a = ring_second(*near_a)
+    low_a, high_a, part_b = lax.optimization_barrier((next_a[0], next_a[1], part_b))
+    near_b = ring_first(part_b)
     other = swap(theirs, "img", 1)
     first = jnp.where(core[0] == 0, mine, other)
     second = jnp.where(core[0] == 0, other, mine)
     qkv = jnp.stack([first, second], axis=1).reshape(3, HEADS, HEAD, tok_rows)
     heads = qkv.transpose(1, 0, 2, 3).reshape(HEADS, 3 * HEAD, tok_rows)
     heads = jnp.pad(heads, ((0, blocks - HEADS), (0, 0), (0, 0)))
-    next_a = ring_second(*near_a)
-    near_b = ring_first(part_b)
     parts = lax.all_to_all(heads, "blk", 0, 0, tiled=True)
 
-    parts, next_a, near_b = lax.optimization_barrier((parts, next_a, near_b))
-    far_a = ring_third(*next_a[:2])
+    parts, low_a, high_a = lax.optimization_barrier((parts, low_a, high_a))
+    far_a = ring_third(low_a, high_a)
+    mixed = attend(counts, parts, text_kv)
+    mixed, far_a, near_b, last_a = lax.optimization_barrier((mixed, far_a, near_b, next_a[2:]))
     next_b = ring_second(*near_b)
-    mixed = attend(counts, parts, text_kv)
-    mixed, far_a, low_b, high_b = lax.optimization_barrier((mixed, far_a, next_b[0], next_b[1]))
+    mixed = lax.all_to_all(mixed, "blk", 0, 0, tiled=True)[:HEADS].reshape(width_attn, tok_rows)
+    mixed, low_b, high_b = lax.optimization_barrier((mixed, next_b[0], next_b[1]))
     far_b = ring_third(low_b, high_b)
-    mixed = lax.all_to_all(mixed, "blk", 0, 0, tiled=True)[:HEADS].reshape(width_attn, tok_rows)
-    pieces_a = [part_a, *near_a, far_a[0], *next_a[2:], far_a[1]]
+    pieces_a = [part_a, *near_a, far_a[0], *last_a, far_a[1]]
     pieces_b = [part_b, *near_b, far_b[0], *next_b[2:], far_b[1]]
 
     updated, mlp_in = middle(mixed, hidden[0], mods, out_weight)

time: 193 us -> 183 us (0.948)
  waiting for transfers between devices: 56.3 us -> 47.1 us
  local copies, waits for them, and re-layouts: 24.5 us -> 29.6 us
  Pallas kernels: 29.9 us -> 25.1 us
  other arithmetic: 9.05 us -> 5.04 us
    ppermute x12, waiting for transfers between devices: 19.2 us -> 7.79 us  [swap(): lax.ppermute(x, axis, [(i, i ^ bits) for i in range(lax.axis_size(axis))])]
    all_to_all x1, waiting for transfers between devices: 0.01 us -> 3.76 us  [per_device(): parts = lax.all_to_all(heads, 'blk', 0, 0, tiled=True)]
    all_to_all x1, waiting for transfers between devices: 2.73 us -> 0.01 us  [per_device(): lax.all_to_all(mixed, 'blk', 0, 0, tiled=True)[:HEADS]]
    pallas_call x2, Pallas kernels: 7.45 us -> 4.81 us  [mlp_first(): pl.pallas_call(first_body, out_shape=jax.ShapeDtypeStruct((count, cols, 2...]
    unnamed x61 -> x49, local copies, waits for them, and re-layouts: 12.4 us -> 11.9 us
  transfers between devices with their start and end apart: 34 -> 34, of which waited for: 12 -> 17; matrix products, arithmetic and copies ran while one was open for 10% -> 12% of each run, Pallas kernels for 13% -> 11%
where the time goes in v4:
time: 183 us; the launch traced here: 179 us
  starting transfers between devices  67.7 us (37%)
  waiting for transfers between devices  47.1 us (26%)
  local copies, waits for them, and re-layouts  29.6 us (16%)
  Pallas kernels  25.1 us (14%)
  other arithmetic  5.04 us (3%)
  between operations  2.66 us (1%)
  matrix products  2.04 us (1%)
    ppermute x18, waiting for transfers between devices, ring(): return lax.ppermute(x, axis, [(i, (i + step) % size) for i in range(size)])  34.3 us
    ppermute x18, starting transfers between devices, ring(): return lax.ppermute(x, axis, [(i, (i + step) % size) for i in range(size)])  30.5 us
    ppermute x12, starting transfers between devices, swap(): lax.ppermute(x, axis, [(i, i ^ bits) for i in range(lax.axis_size(axis))])  12.5 us
    unnamed x49, local copies, waits for them, and re-layouts  11.9 us
    pallas_call x1, Pallas kernels, attend(): pl.pallas_call(attend_body, out_shape=jax.ShapeDtypeStruct((blocks, HEAD,...  11.4 us
    all_to_all x1, starting transfers between devices, per_device(): parts = lax.all_to_all(heads, 'blk', 0, 0, tiled=True)  8.59 us
    all_to_all x1, starting transfers between devices, per_device(): lax.all_to_all(mixed, 'blk', 0, 0, tiled=True)[:HEADS]  8.12 us
    ppermute x12, waiting for transfers between devices, swap(): lax.ppermute(x, axis, [(i, i ^ bits) for i in range(lax.axis_size(axis))])  7.79 us
  transfers between devices with their start and end apart: 34, of which 17 were waited for; matrix products, arithmetic and copies ran while one was open for 12% of the time, Pallas kernels for 11%

profile of v4, /device:TPU:104, one launch (start us, length us, event | category | flops | bytes accessed | tf_op | source)
XLA Modules:
  0.0 179.2 jit_solution(16757233361516501913)
XLA Ops:
  4.0 2.3 %collective-permute-start.3 = (bf16[144,1536]{1,0:T(8,128)(2,1)}, bf16[144,1536]{1,0:T(8,128)(2,1)}, u32[]{:S(2)}, u32[]{:S(2)}) collective-permute-start(bf16[144,1536]{1,0:T(8,128)(2,1)} %bitcast.87), channel_id=1, source_target_pairs={{0,2},{1,3},{2,0},{3,1},{4,6},{5,7},{6,4},{7,5},{8,10},{9,11},{10,... | collective-permute-start | bytes 1327112 | tf_op jit(solution)/shard_map/ppermute | solution.py:38
  12.3 1.8 %collective-permute-done.1.refs_1_ = bf16[144,1536]{1,0:T(8,128)(2,1)S(1)} collective-permute-done((bf16[144,1536]{1,0:T(8,128)(2,1)}, bf16[144,1536]{1,0:T(8,128)(2,1)S(1)}, u32[]{:S(2)}, u32[]{:S(2)}) %collective-permute-start.1) | collective-permute-done | bytes 442400 | tf_op jit(solution)/shard_map/ppermute | solution.py:50
  14.4 2.3 %constant_dynamic-slice_fusion.1 = (bf16[1536,64]{1,0:T(8,128)(2,1)}, bf16[1536,64]{1,0:T(8,128)(2,1)}) fusion(bf16[1536,1536]{1,0:T(8,128)(2,1)} %param.25, s32[]{:T(128)S(6)} %select_n.75, s32[]{:T(128)S(6)} %select_n.76), kind=kLoop, calls=%fused_computation.70 | loop fusion | bytes 786440 | tf_op jit(solution)/shard_map/dynamic_slice | solution.py:353
  16.7 3.0 %collective-permute-start.5 = (bf16[72,1536]{1,0:T(8,128)(2,1)S(1)}, bf16[72,1536]{1,0:T(8,128)(2,1)S(1)}, u32[]{:S(2)}, u32[]{:S(2)}) collective-permute-start(bf16[72,1536]{1,0:T(8,128)(2,1)S(1)} %slice.114), channel_id=1, source_target_pairs={{0,12},{1,13},{2,14},{3,15},{4,0},{5,1},{6,2},{7,3},{8,4},{9,5},{1... | collective-permute-start | bytes 663560 | tf_op jit(solution)/shard_map/ppermute | solution.py:50
  19.8 3.2 %collective-permute-start.7 = (bf16[144,1536]{1,0:T(8,128)(2,1)}, bf16[144,1536]{1,0:T(8,128)(2,1)}, u32[]{:S(2)}, u32[]{:S(2)}) collective-permute-start(bf16[144,1536]{1,0:T(8,128)(2,1)} %collective-permute-done.3.refs_3_), channel_id=1, source_target_pairs={{0,12},{1,13},{2,14},{3,15},{4,0},{5,1},{6,2},{7,3},{8,4},{9,5},{1... | collective-permute-start | bytes 1327112 | tf_op jit(solution)/shard_map/ppermute | solution.py:50
  23.0 2.2 %collective-permute-done.5 = bf16[72,1536]{1,0:T(8,128)(2,1)S(1)} collective-permute-done((bf16[72,1536]{1,0:T(8,128)(2,1)S(1)}, bf16[72,1536]{1,0:T(8,128)(2,1)S(1)}, u32[]{:S(2)}, u32[]{:S(2)}) %collective-permute-start.5) | collective-permute-done | bytes 221216 | tf_op jit(solution)/shard_map/ppermute | solution.py:50
  25.2 2.5 %collective-permute-start.8 = (bf16[144,1536]{1,0:T(8,128)(2,1)S(1)}, bf16[144,1536]{1,0:T(8,128)(2,1)}, u32[]{:S(2)}, u32[]{:S(2)}) collective-permute-start(bf16[144,1536]{1,0:T(8,128)(2,1)S(1)} %constant_dynamic-update-slice_fusion.refs_4_), channel_id=1, source_target_pairs={{0,2},{1,3},{2,0},{3,1},{4,6},{5,7},{6,4},{7,5},{8,10},{9,11},{10,... | collective-permute-start | bytes 1327112 | tf_op jit(solution)/shard_map/ppermute | solution.py:38
  27.7 4.1 %collective-permute-done.6.refs_5_ = bf16[144,1536]{1,0:T(8,128)(2,1)} collective-permute-done((bf16[144,1536]{1,0:T(8,128)(2,1)}, bf16[144,1536]{1,0:T(8,128)(2,1)}, u32[]{:S(2)}, u32[]{:S(2)}) %collective-permute-start.6) | collective-permute-done | bytes 442400 | tf_op jit(solution)/shard_map/ppermute | solution.py:50
  34.0 2.6 %collective-permute-start.10 = (bf16[112,1536]{1,0:T(8,128)(2,1)S(1)}, bf16[112,1536]{1,0:T(8,128)(2,1)}, u32[]{:S(2)}, u32[]{:S(2)}) collective-permute-start(bf16[112,1536]{1,0:T(8,128)(2,1)S(1)} %slice.111.refs_0_), channel_id=1, source_target_pairs={{0,12},{1,13},{2,14},{3,15},{4,0},{5,1},{6,2},{7,3},{8,4},{9,5},{1... | collective-permute-start | bytes 1032200 | tf_op jit(solution)/shard_map/ppermute | solution.py:50
  36.6 2.4 %collective-permute-start.11 = (bf16[112,1536]{1,0:T(8,128)(2,1)S(1)}, bf16[112,1536]{1,0:T(8,128)(2,1)}, u32[]{:S(2)}, u32[]{:S(2)}) collective-permute-start(bf16[112,1536]{1,0:T(8,128)(2,1)S(1)} %slice.111.refs_0_), channel_id=1, source_target_pairs={{0,2},{1,3},{2,0},{3,1},{4,6},{5,7},{6,4},{7,5},{8,10},{9,11},{10,... | collective-permute-start | bytes 1032200 | tf_op jit(solution)/shard_map/ppermute | solution.py:38
  39.0 1.8 convolution_convert_fusion
  43.4 3.4 %project_qkv.1 = (bf16[8,144,128]{2,1,0:T(8,128)(2,1)S(1)}, bf16[8,144,128]{2,1,0:T(8,128)(2,1)}) custom-call(s32[1]{0:T(128)} %bitcast.2.chip_ref, bf16[128,1536]{1,0:T(8,128)(2,1)S(1)} %fusion.12.own_x, bf16[128,1536]{1,0:T(8,128)(2,1)} %collective-permute-done.peer_x, bf16[144,1536]{1,0:T(8,128)(2,1)S(1)} %bitcast.88, ...), custom_call_target="tpu_custom_call" | custom-call | flops 1000 | bytes 1000 | tf_op jit(solution)/shard_map/project_qkv/pallas_call | solution.py:97
  47.6 1.8 collective-permute-done.12
  51.5 8.6 %all-to-all-start = ((bf16[16,192,128]{2,1,0:T(8,128)(2,1)}), bf16[16,192,128]{2,1,0:T(8,128)(2,1)}, u32[]{:S(2)}, u32[]{:S(2)}) async-start(bf16[16,192,128]{2,1,0:T(8,128)(2,1)} %pad.13), calls=%async_computation | async-start | bytes 1572864 | tf_op jit(solution)/shard_map/all_to_all | solution.py:375
  62.1 3.3 %collective-permute-start.14 = (bf16[56,1536]{1,0:T(8,128)(2,1)S(1)}, bf16[56,1536]{1,0:T(8,128)(2,1)S(1)}, u32[]{:S(2)}, u32[]{:S(2)}) collective-permute-start(bf16[56,1536]{1,0:T(8,128)(2,1)S(1)} %slice.97), channel_id=1, source_target_pairs={{0,12},{1,13},{2,14},{3,15},{4,0},{5,1},{6,2},{7,3},{8,4},{9,5},{1... | collective-permute-start | bytes 516104 | tf_op jit(solution)/shard_map/ppermute | solution.py:50
  65.4 2.8 %collective-permute-done.13 = bf16[56,1536]{1,0:T(8,128)(2,1)S(1)} collective-permute-done((bf16[56,1536]{1,0:T(8,128)(2,1)S(1)}, bf16[56,1536]{1,0:T(8,128)(2,1)S(1)}, u32[]{:S(2)}, u32[]{:S(2)}) %collective-permute-start.13) | collective-permute-done | bytes 172064 | tf_op jit(solution)/shard_map/ppermute | solution.py:50
  69.4 2.8 %collective-permute-start.17 = (bf16[272,1536]{1,0:T(8,128)(2,1)S(1)}, bf16[272,1536]{1,0:T(8,128)(2,1)S(1)}, u32[]{:S(2)}, u32[]{:S(2)}) collective-permute-start(bf16[272,1536]{1,0:T(8,128)(2,1)S(1)} %pad_maximum_fusion.refs_0_), channel_id=1, source_target_pairs={{0,12},{1,13},{2,14},{3,15},{4,0},{5,1},{6,2},{7,3},{8,4},{9,5},{1... | collective-permute-start | bytes 2506760 | tf_op jit(solution)/shard_map/ppermute | solution.py:50
  73.4 3.2 %collective-permute-start.20 = (bf16[112,1536]{1,0:T(8,128)(2,1)}, bf16[112,1536]{1,0:T(8,128)(2,1)}, u32[]{:S(2)}, u32[]{:S(2)}) collective-permute-start(bf16[112,1536]{1,0:T(8,128)(2,1)} %collective-permute-done.11.refs_3_), channel_id=1, source_target_pairs={{0,12},{1,13},{2,14},{3,15},{4,0},{5,1},{6,2},{7,3},{8,4},{9,5},{1... | collective-permute-start | bytes 1032200 | tf_op jit(solution)/shard_map/ppermute | solution.py:50
  76.6 3.8 %all-to-all-done.parts = bf16[16,192,128]{2,1,0:T(8,128)(2,1)} async-done(((bf16[16,192,128]{2,1,0:T(8,128)(2,1)}), bf16[16,192,128]{2,1,0:T(8,128)(2,1)}, u32[]{:S(2)}, u32[]{:S(2)}) %all-to-all-start) | async-done | bytes 786464 | tf_op jit(solution)/shard_map/all_to_all | solution.py:375
  82.3 14.6 %collective-permute-done.19.refs_5_ = bf16[112,1536]{1,0:T(8,128)(2,1)} collective-permute-done((bf16[112,1536]{1,0:T(8,128)(2,1)}, bf16[112,1536]{1,0:T(8,128)(2,1)}, u32[]{:S(2)}, u32[]{:S(2)}) %collective-permute-start.19) | collective-permute-done | bytes 344096 | tf_op jit(solution)/shard_map/ppermute | solution.py:50
  98.7 11.4 %attend.1 = bf16[16,64,128]{2,1,0:T(8,128)(2,1)S(1)} custom-call(s32[1]{0:T(128)} %copy.54.count_ref, bf16[16,192,128]{2,1,0:T(8,128)(2,1)} %all-to-all-done.parts, bf16[128,256]{1,0:T(8,128)(2,1)S(1)} %pad.12.text), custom_call_target="tpu_custom_call" | custom-call | flops 1000 | bytes 1000 | tf_op jit(solution)/shard_map/attend/pallas_call | solution.py:154
  111.6 8.1 %all-to-all-start.1 = ((bf16[16,64,128]{2,1,0:T(8,128)(2,1)}), bf16[16,64,128]{2,1,0:T(8,128)(2,1)}, u32[]{:S(2)}, u32[]{:S(2)}) async-start(bf16[16,64,128]{2,1,0:T(8,128)(2,1)} %copy-done.3), calls=%async_computation.1 | async-start | bytes 524288 | tf_op jit(solution)/shard_map/all_to_all | solution.py:382
  121.3 3.2 %collective-permute-start.22 = (bf16[136,1536]{1,0:T(8,128)(2,1)}, bf16[136,1536]{1,0:T(8,128)(2,1)}, u32[]{:S(2)}, u32[]{:S(2)}) collective-permute-start(bf16[136,1536]{1,0:T(8,128)(2,1)} %slice.100), channel_id=1, source_target_pairs={{0,12},{1,13},{2,14},{3,15},{4,0},{5,1},{6,2},{7,3},{8,4},{9,5},{1... | collective-permute-start | bytes 1253384 | tf_op jit(solution)/shard_map/ppermute | solution.py:50
  124.5 3.2 %collective-permute-start.26 = (bf16[272,1536]{1,0:T(8,128)(2,1)}, bf16[272,1536]{1,0:T(8,128)(2,1)}, u32[]{:S(2)}, u32[]{:S(2)}) collective-permute-start(bf16[272,1536]{1,0:T(8,128)(2,1)} %collective-permute-done.18.refs_3_), channel_id=1, source_target_pairs={{0,12},{1,13},{2,14},{3,15},{4,0},{5,1},{6,2},{7,3},{8,4},{9,5},{1... | collective-permute-start | bytes 2506760 | tf_op jit(solution)/shard_map/ppermute | solution.py:50
  128.7 5.9 %collective-permute-done.21 = bf16[136,1536]{1,0:T(8,128)(2,1)} collective-permute-done((bf16[136,1536]{1,0:T(8,128)(2,1)}, bf16[136,1536]{1,0:T(8,128)(2,1)}, u32[]{:S(2)}, u32[]{:S(2)}) %collective-permute-start.21) | collective-permute-done | bytes 417824 | tf_op jit(solution)/shard_map/ppermute | solution.py:50
  137.1 2.5 %collective-permute-start.27 = (bf16[272,1536]{1,0:T(8,128)(2,1)S(1)}, bf16[272,1536]{1,0:T(8,128)(2,1)S(1)}, u32[]{:S(2)}, u32[]{:S(2)}) collective-permute-start(bf16[272,1536]{1,0:T(8,128)(2,1)S(1)} %constant_dynamic-update-slice_fusion.4.refs_4_), channel_id=1, source_target_pairs={{0,2},{1,3},{2,0},{3,1},{4,6},{5,7},{6,4},{7,5},{8,10},{9,11},{10,... | collective-permute-start | bytes 2506760 | tf_op jit(solution)/shard_map/ppermute | solution.py:38
  144.7 2.4 %mlp_first.2.own_a = bf16[8,112,256]{2,1,0:T(8,128)(2,1)S(1)} custom-call(s32[1]{0:T(128)} %bitcast.2.chip_ref, bf16[128,1536]{1,0:T(8,128)(2,1)S(1)} %get-tuple-element.58.own_x, bf16[128,1536]{1,0:T(8,128)(2,1)S(1)} %collective-permute-done.23.peer_x, bf16[112,1536]{1,0:T(8,128)(2,1)S(1)} %slice.111.refs_0_, ...), custom_call_target="tpu_custom_call" | custom-call | flops 1000 | bytes 1000 | tf_op jit(solution)/shard_map/mlp_first/pallas_call | solution.py:218
  148.5 2.7 %collective-permute-done.27.refs_7_ = bf16[272,1536]{1,0:T(8,128)(2,1)S(1)} collective-permute-done((bf16[272,1536]{1,0:T(8,128)(2,1)S(1)}, bf16[272,1536]{1,0:T(8,128)(2,1)S(1)}, u32[]{:S(2)}, u32[]{:S(2)}) %collective-permute-start.27) | collective-permute-done | bytes 835616 | tf_op jit(solution)/shard_map/ppermute | solution.py:38
  151.2 2.4 %mlp_first.3.own_b = bf16[8,80,256]{2,1,0:T(8,128)(2,1)S(1)} custom-call(s32[1]{0:T(128)} %bitcast.2.chip_ref, bf16[128,1536]{1,0:T(8,128)(2,1)S(1)} %get-tuple-element.58.own_x, bf16[128,1536]{1,0:T(8,128)(2,1)S(1)} %collective-permute-done.23.peer_x, bf16[272,1536]{1,0:T(8,128)(2,1)S(1)} %pad_maximum_fusion.refs_0_, ...), custom_call_target="tpu_custom_call" | custom-call | flops 1000 | bytes 1000 | tf_op jit(solution)/shard_map/mlp_first/pallas_call | solution.py:218
  155.3 4.0 %mlp_second.1 = (f32[8,96,128]{2,1,0:T(8,128)S(1)}, f32[8,96,128]{2,1,0:T(8,128)}) custom-call(s32[1]{0:T(128)} %bitcast.2.chip_ref, s32[1]{0:T(128)} %bitcast.1.core_ref, bf16[8,112,256]{2,1,0:T(8,128)(2,1)S(1)} %mlp_first.2.own_a, bf16[8,112,256]{2,1,0:T(8,128)(2,1)S(1)} %collective-permute-done.24.peer_a, bf16[8,80,256]{2,1,0:T(8,128)(2,1)S(1)} %mlp_first.3.own_b, ...), custom_call_target="tpu_custom_call" | custom-call | flops 1000 | bytes 1000 | tf_op jit(solution)/shard_map/mlp_second/pallas_call | solution.py:258
  167.3 2.5 %collective-permute-start.31 = (bf16[1,2048]{1,0:T(2,128)(2,1)S(1)}, bf16[1,2048]{1,0:T(2,128)(2,1)S(1)}, u32[]{:S(2)}, u32[]{:S(2)}) collective-permute-start(bf16[1,2048]{1,0:T(2,128)(2,1)S(1)} %get-tuple-element.88), channel_id=1, source_target_pairs={{16,0},{32,16},{48,32},{64,48},{80,64},{96,80},{112,96},{128,112},... | collective-permute-start | bytes 12296 | tf_op jit(solution)/shard_map/ppermute | solution.py:300
  169.8 5.5 %collective-permute-start.30 = (bf16[1,2048]{1,0:T(2,128)(2,1)S(1)}, bf16[1,2048]{1,0:T(2,128)(2,1)S(1)}, u32[]{:S(2)}, u32[]{:S(2)}) collective-permute-start(bf16[1,2048]{1,0:T(2,128)(2,1)S(1)} %get-tuple-element.87), channel_id=1, source_target_pairs={{0,16},{16,32},{32,48},{48,64},{64,80},{80,96},{96,112},{112,128},... | collective-permute-start | bytes 12296 | tf_op jit(solution)/shard_map/ppermute | solution.py:299
  (151 shorter events, 50.4 us)
Async XLA Ops:
  0.7 13.4 %collective-permute-start.1 = (bf16[144,1536]{1,0:T(8,128)(2,1)}, bf16[144,1536]{1,0:T(8,128)(2,1)S(1)}, u32[]{:S(2)}, u32[]{:S(2)}) collective-permute-start(bf16[144,1536]{1,0:T(8,128)(2,1)} %bitcast.85), channel_id=1, source_target_pairs={{0,4},{1,5},{2,6},{3,7},{4,8},{5,9},{6,10},{7,11},{8,12},{9,13},{1... | collective-permute-start | bytes 1327112 | tf_op jit(solution)/shard_map/ppermute | solution.py:50
  2.2 14.5 %collective-permute-start.2 = (bf16[144,1536]{1,0:T(8,128)(2,1)}, bf16[144,1536]{1,0:T(8,128)(2,1)S(1)}, u32[]{:S(2)}, u32[]{:S(2)}) collective-permute-start(bf16[144,1536]{1,0:T(8,128)(2,1)} %bitcast.86), channel_id=1, source_target_pairs={{0,12},{1,13},{2,14},{3,15},{4,0},{5,1},{6,2},{7,3},{8,4},{9,5},{1... | collective-permute-start | bytes 1327112 | tf_op jit(solution)/shard_map/ppermute | solution.py:50
  4.0 15.8 %collective-permute-start.3 = (bf16[144,1536]{1,0:T(8,128)(2,1)}, bf16[144,1536]{1,0:T(8,128)(2,1)}, u32[]{:S(2)}, u32[]{:S(2)}) collective-permute-start(bf16[144,1536]{1,0:T(8,128)(2,1)} %bitcast.87), channel_id=1, source_target_pairs={{0,2},{1,3},{2,0},{3,1},{4,6},{5,7},{6,4},{7,5},{8,10},{9,11},{10,... | collective-permute-start | bytes 1327112 | tf_op jit(solution)/shard_map/ppermute | solution.py:38
  11.6 30.8 %collective-permute-start = (bf16[128,1536]{1,0:T(8,128)(2,1)S(1)}, bf16[128,1536]{1,0:T(8,128)(2,1)}, u32[]{:S(2)}, u32[]{:S(2)}) collective-permute-start(bf16[128,1536]{1,0:T(8,128)(2,1)S(1)} %fusion.12.own_x), channel_id=1, source_target_pairs={{0,1},{1,0},{2,3},{3,2},{4,5},{5,4},{6,7},{7,6},{8,9},{9,8},{10,11... | collective-permute-start | bytes 1179656 | tf_op jit(solution)/shard_map/ppermute | solution.py:38
  14.1 8.9 %collective-permute-start.4 = (bf16[72,1536]{1,0:T(8,128)(2,1)S(1)}, bf16[72,1536]{1,0:T(8,128)(2,1)S(1)}, u32[]{:S(2)}, u32[]{:S(2)}) collective-permute-start(bf16[72,1536]{1,0:T(8,128)(2,1)S(1)} %slice.113), channel_id=1, source_target_pairs={{0,4},{1,5},{2,6},{3,7},{4,8},{5,9},{6,10},{7,11},{8,12},{9,13},{1... | collective-permute-start | bytes 663560 | tf_op jit(solution)/shard_map/ppermute | solution.py:50
  16.7 8.5 %collective-permute-start.5 = (bf16[72,1536]{1,0:T(8,128)(2,1)S(1)}, bf16[72,1536]{1,0:T(8,128)(2,1)S(1)}, u32[]{:S(2)}, u32[]{:S(2)}) collective-permute-start(bf16[72,1536]{1,0:T(8,128)(2,1)S(1)} %slice.114), channel_id=1, source_target_pairs={{0,12},{1,13},{2,14},{3,15},{4,0},{5,1},{6,2},{7,3},{8,4},{9,5},{1... | collective-permute-start | bytes 663560 | tf_op jit(solution)/shard_map/ppermute | solution.py:50
  19.8 12.0 %collective-permute-start.6 = (bf16[144,1536]{1,0:T(8,128)(2,1)}, bf16[144,1536]{1,0:T(8,128)(2,1)}, u32[]{:S(2)}, u32[]{:S(2)}) collective-permute-start(bf16[144,1536]{1,0:T(8,128)(2,1)} %collective-permute-done.3.refs_3_), channel_id=1, source_target_pairs={{0,4},{1,5},{2,6},{3,7},{4,8},{5,9},{6,10},{7,11},{8,12},{9,13},{1... | collective-permute-start | bytes 1327112 | tf_op jit(solution)/shard_map/ppermute | solution.py:50
  19.8 13.1 %collective-permute-start.7 = (bf16[144,1536]{1,0:T(8,128)(2,1)}, bf16[144,1536]{1,0:T(8,128)(2,1)}, u32[]{:S(2)}, u32[]{:S(2)}) collective-permute-start(bf16[144,1536]{1,0:T(8,128)(2,1)} %collective-permute-done.3.refs_3_), channel_id=1, source_target_pairs={{0,12},{1,13},{2,14},{3,15},{4,0},{5,1},{6,2},{7,3},{8,4},{9,5},{1... | collective-permute-start | bytes 1327112 | tf_op jit(solution)/shard_map/ppermute | solution.py:50
  25.2 17.2 %collective-permute-start.8 = (bf16[144,1536]{1,0:T(8,128)(2,1)S(1)}, bf16[144,1536]{1,0:T(8,128)(2,1)}, u32[]{:S(2)}, u32[]{:S(2)}) collective-permute-start(bf16[144,1536]{1,0:T(8,128)(2,1)S(1)} %constant_dynamic-update-slice_fusion.refs_4_), channel_id=1, source_target_pairs={{0,2},{1,3},{2,0},{3,1},{4,6},{5,7},{6,4},{7,5},{8,10},{9,11},{10,... | collective-permute-start | bytes 1327112 | tf_op jit(solution)/shard_map/ppermute | solution.py:38
  32.9 14.6 %collective-permute-start.9 = (bf16[112,1536]{1,0:T(8,128)(2,1)S(1)}, bf16[112,1536]{1,0:T(8,128)(2,1)}, u32[]{:S(2)}, u32[]{:S(2)}) collective-permute-start(bf16[112,1536]{1,0:T(8,128)(2,1)S(1)} %slice.111.refs_0_), channel_id=1, source_target_pairs={{0,4},{1,5},{2,6},{3,7},{4,8},{5,9},{6,10},{7,11},{8,12},{9,13},{1... | collective-permute-start | bytes 1032200 | tf_op jit(solution)/shard_map/ppermute | solution.py:50
  34.0 13.5 %collective-permute-start.10 = (bf16[112,1536]{1,0:T(8,128)(2,1)S(1)}, bf16[112,1536]{1,0:T(8,128)(2,1)}, u32[]{:S(2)}, u32[]{:S(2)}) collective-permute-start(bf16[112,1536]{1,0:T(8,128)(2,1)S(1)} %slice.111.refs_0_), channel_id=1, source_target_pairs={{0,12},{1,13},{2,14},{3,15},{4,0},{5,1},{6,2},{7,3},{8,4},{9,5},{1... | collective-permute-start | bytes 1032200 | tf_op jit(solution)/shard_map/ppermute | solution.py:50
  36.6 10.9 %collective-permute-start.11 = (bf16[112,1536]{1,0:T(8,128)(2,1)S(1)}, bf16[112,1536]{1,0:T(8,128)(2,1)}, u32[]{:S(2)}, u32[]{:S(2)}) collective-permute-start(bf16[112,1536]{1,0:T(8,128)(2,1)S(1)} %slice.111.refs_0_), channel_id=1, source_target_pairs={{0,2},{1,3},{2,0},{3,1},{4,6},{5,7},{6,4},{7,5},{8,10},{9,11},{10,... | collective-permute-start | bytes 1032200 | tf_op jit(solution)/shard_map/ppermute | solution.py:38
  47.5 1.9 %collective-permute-start.12 = (bf16[8,144,128]{2,1,0:T(8,128)(2,1)}, bf16[8,144,128]{2,1,0:T(8,128)(2,1)S(1)}, u32[]{:S(2)}, u32[]{:S(2)}) collective-permute-start(bf16[8,144,128]{2,1,0:T(8,128)(2,1)} %get-tuple-element.42), channel_id=1, source_target_pairs={{0,1},{1,0},{2,3},{3,2},{4,5},{5,4},{6,7},{7,6},{8,9},{9,8},{10,11... | collective-permute-start | bytes 884744 | tf_op jit(solution)/shard_map/ppermute | solution.py:38
  51.5 28.9 %all-to-all-start = ((bf16[16,192,128]{2,1,0:T(8,128)(2,1)}), bf16[16,192,128]{2,1,0:T(8,128)(2,1)}, u32[]{:S(2)}, u32[]{:S(2)}) async-start(bf16[16,192,128]{2,1,0:T(8,128)(2,1)} %pad.13), calls=%async_computation | async-start | bytes 1572864 | tf_op jit(solution)/shard_map/all_to_all | solution.py:375
  61.1 7.1 %collective-permute-start.13 = (bf16[56,1536]{1,0:T(8,128)(2,1)S(1)}, bf16[56,1536]{1,0:T(8,128)(2,1)S(1)}, u32[]{:S(2)}, u32[]{:S(2)}) collective-permute-start(bf16[56,1536]{1,0:T(8,128)(2,1)S(1)} %slice.96), channel_id=1, source_target_pairs={{0,4},{1,5},{2,6},{3,7},{4,8},{5,9},{6,10},{7,11},{8,12},{9,13},{1... | collective-permute-start | bytes 516104 | tf_op jit(solution)/shard_map/ppermute | solution.py:50
  62.1 6.4 %collective-permute-start.14 = (bf16[56,1536]{1,0:T(8,128)(2,1)S(1)}, bf16[56,1536]{1,0:T(8,128)(2,1)S(1)}, u32[]{:S(2)}, u32[]{:S(2)}) collective-permute-start(bf16[56,1536]{1,0:T(8,128)(2,1)S(1)} %slice.97), channel_id=1, source_target_pairs={{0,12},{1,13},{2,14},{3,15},{4,0},{5,1},{6,2},{7,3},{8,4},{9,5},{1... | collective-permute-start | bytes 516104 | tf_op jit(solution)/shard_map/ppermute | solution.py:50
  68.5 42.3 %collective-permute-start.16 = (bf16[272,1536]{1,0:T(8,128)(2,1)S(1)}, bf16[272,1536]{1,0:T(8,128)(2,1)S(1)}, u32[]{:S(2)}, u32[]{:S(2)}) collective-permute-start(bf16[272,1536]{1,0:T(8,128)(2,1)S(1)} %pad_maximum_fusion.refs_0_), channel_id=1, source_target_pairs={{0,4},{1,5},{2,6},{3,7},{4,8},{5,9},{6,10},{7,11},{8,12},{9,13},{1... | collective-permute-start | bytes 2506760 | tf_op jit(solution)/shard_map/ppermute | solution.py:50
  69.4 41.4 %collective-permute-start.17 = (bf16[272,1536]{1,0:T(8,128)(2,1)S(1)}, bf16[272,1536]{1,0:T(8,128)(2,1)S(1)}, u32[]{:S(2)}, u32[]{:S(2)}) collective-permute-start(bf16[272,1536]{1,0:T(8,128)(2,1)S(1)} %pad_maximum_fusion.refs_0_), channel_id=1, source_target_pairs={{0,12},{1,13},{2,14},{3,15},{4,0},{5,1},{6,2},{7,3},{8,4},{9,5},{1... | collective-permute-start | bytes 2506760 | tf_op jit(solution)/shard_map/ppermute | solution.py:50
  72.3 38.5 %collective-permute-start.18 = (bf16[272,1536]{1,0:T(8,128)(2,1)S(1)}, bf16[272,1536]{1,0:T(8,128)(2,1)}, u32[]{:S(2)}, u32[]{:S(2)}) collective-permute-start(bf16[272,1536]{1,0:T(8,128)(2,1)S(1)} %pad_maximum_fusion.refs_0_), channel_id=1, source_target_pairs={{0,2},{1,3},{2,0},{3,1},{4,6},{5,7},{6,4},{7,5},{8,10},{9,11},{10,... | collective-permute-start | bytes 2506760 | tf_op jit(solution)/shard_map/ppermute | solution.py:38
  73.4 23.5 %collective-permute-start.19 = (bf16[112,1536]{1,0:T(8,128)(2,1)}, bf16[112,1536]{1,0:T(8,128)(2,1)}, u32[]{:S(2)}, u32[]{:S(2)}) collective-permute-start(bf16[112,1536]{1,0:T(8,128)(2,1)} %collective-permute-done.11.refs_3_), channel_id=1, source_target_pairs={{0,4},{1,5},{2,6},{3,7},{4,8},{5,9},{6,10},{7,11},{8,12},{9,13},{1... | collective-permute-start | bytes 1032200 | tf_op jit(solution)/shard_map/ppermute | solution.py:50
  73.4 37.4 %collective-permute-start.20 = (bf16[112,1536]{1,0:T(8,128)(2,1)}, bf16[112,1536]{1,0:T(8,128)(2,1)}, u32[]{:S(2)}, u32[]{:S(2)}) collective-permute-start(bf16[112,1536]{1,0:T(8,128)(2,1)} %collective-permute-done.11.refs_3_), channel_id=1, source_target_pairs={{0,12},{1,13},{2,14},{3,15},{4,0},{5,1},{6,2},{7,3},{8,4},{9,5},{1... | collective-permute-start | bytes 1032200 | tf_op jit(solution)/shard_map/ppermute | solution.py:50
  96.9 13.9 %collective-permute-start.15 = (bf16[112,1536]{1,0:T(8,128)(2,1)S(1)}, bf16[112,1536]{1,0:T(8,128)(2,1)S(1)}, u32[]{:S(2)}, u32[]{:S(2)}) collective-permute-start(bf16[112,1536]{1,0:T(8,128)(2,1)S(1)} %constant_dynamic-update-slice_fusion.2.refs_4_), channel_id=1, source_target_pairs={{0,2},{1,3},{2,0},{3,1},{4,6},{5,7},{6,4},{7,5},{8,10},{9,11},{10,... | collective-permute-start | bytes 1032200 | tf_op jit(solution)/shard_map/ppermute | solution.py:38
  111.6 16.2 %all-to-all-start.1 = ((bf16[16,64,128]{2,1,0:T(8,128)(2,1)}), bf16[16,64,128]{2,1,0:T(8,128)(2,1)}, u32[]{:S(2)}, u32[]{:S(2)}) async-start(bf16[16,64,128]{2,1,0:T(8,128)(2,1)} %copy-done.3), calls=%async_computation.1 | async-start | bytes 524288 | tf_op jit(solution)/shard_map/all_to_all | solution.py:382
  120.5 14.1 %collective-permute-start.21 = (bf16[136,1536]{1,0:T(8,128)(2,1)}, bf16[136,1536]{1,0:T(8,128)(2,1)}, u32[]{:S(2)}, u32[]{:S(2)}) collective-permute-start(bf16[136,1536]{1,0:T(8,128)(2,1)} %slice.99), channel_id=1, source_target_pairs={{0,4},{1,5},{2,6},{3,7},{4,8},{5,9},{6,10},{7,11},{8,12},{9,13},{1... | collective-permute-start | bytes 1253384 | tf_op jit(solution)/shard_map/ppermute | solution.py:50
  121.3 13.6 %collective-permute-start.22 = (bf16[136,1536]{1,0:T(8,128)(2,1)}, bf16[136,1536]{1,0:T(8,128)(2,1)}, u32[]{:S(2)}, u32[]{:S(2)}) collective-permute-start(bf16[136,1536]{1,0:T(8,128)(2,1)} %slice.100), channel_id=1, source_target_pairs={{0,12},{1,13},{2,14},{3,15},{4,0},{5,1},{6,2},{7,3},{8,4},{9,5},{1... | collective-permute-start | bytes 1253384 | tf_op jit(solution)/shard_map/ppermute | solution.py:50
  124.5 23.9 %collective-permute-start.25 = (bf16[272,1536]{1,0:T(8,128)(2,1)}, bf16[272,1536]{1,0:T(8,128)(2,1)}, u32[]{:S(2)}, u32[]{:S(2)}) collective-permute-start(bf16[272,1536]{1,0:T(8,128)(2,1)} %collective-permute-done.18.refs_3_), channel_id=1, source_target_pairs={{0,4},{1,5},{2,6},{3,7},{4,8},{5,9},{6,10},{7,11},{8,12},{9,13},{1... | collective-permute-start | bytes 2506760 | tf_op jit(solution)/shard_map/ppermute | solution.py:50
  124.5 24.0 %collective-permute-start.26 = (bf16[272,1536]{1,0:T(8,128)(2,1)}, bf16[272,1536]{1,0:T(8,128)(2,1)}, u32[]{:S(2)}, u32[]{:S(2)}) collective-permute-start(bf16[272,1536]{1,0:T(8,128)(2,1)} %collective-permute-done.18.refs_3_), channel_id=1, source_target_pairs={{0,12},{1,13},{2,14},{3,15},{4,0},{5,1},{6,2},{7,3},{8,4},{9,5},{1... | collective-permute-start | bytes 2506760 | tf_op jit(solution)/shard_map/ppermute | solution.py:50
  137.1 14.1 %collective-permute-start.27 = (bf16[272,1536]{1,0:T(8,128)(2,1)S(1)}, bf16[272,1536]{1,0:T(8,128)(2,1)S(1)}, u32[]{:S(2)}, u32[]{:S(2)}) collective-permute-start(bf16[272,1536]{1,0:T(8,128)(2,1)S(1)} %constant_dynamic-update-slice_fusion.4.refs_4_), channel_id=1, source_target_pairs={{0,2},{1,3},{2,0},{3,1},{4,6},{5,7},{6,4},{7,5},{8,10},{9,11},{10,... | collective-permute-start | bytes 2506760 | tf_op jit(solution)/shard_map/ppermute | solution.py:38
  147.1 6.6 %collective-permute-start.24 = (bf16[8,112,256]{2,1,0:T(8,128)(2,1)S(1)}, bf16[8,112,256]{2,1,0:T(8,128)(2,1)S(1)}, u32[]{:S(2)}, u32[]{:S(2)}) collective-permute-start(bf16[8,112,256]{2,1,0:T(8,128)(2,1)S(1)} %mlp_first.2.own_a), channel_id=1, source_target_pairs={{0,1},{1,0},{2,3},{3,2},{4,5},{5,4},{6,7},{7,6},{8,9},{9,8},{10,11... | collective-permute-start | bytes 1376264 | tf_op jit(solution)/shard_map/ppermute | solution.py:38
  160.1 2.3 %collective-permute-start.29 = (f32[8,96,128]{2,1,0:T(8,128)}, f32[8,96,128]{2,1,0:T(8,128)S(1)}, u32[]{:S(2)}, u32[]{:S(2)}) collective-permute-start(f32[8,96,128]{2,1,0:T(8,128)} %get-tuple-element.67), channel_id=1, source_target_pairs={{0,1},{1,0},{2,3},{3,2},{4,5},{5,4},{6,7},{7,6},{8,9},{9,8},{10,11... | collective-permute-start | bytes 1179656 | tf_op jit(solution)/shard_map/ppermute | solution.py:38
  167.3 8.1 %collective-permute-start.31 = (bf16[1,2048]{1,0:T(2,128)(2,1)S(1)}, bf16[1,2048]{1,0:T(2,128)(2,1)S(1)}, u32[]{:S(2)}, u32[]{:S(2)}) collective-permute-start(bf16[1,2048]{1,0:T(2,128)(2,1)S(1)} %get-tuple-element.88), channel_id=1, source_target_pairs={{16,0},{32,16},{48,32},{64,48},{80,64},{96,80},{112,96},{128,112},... | collective-permute-start | bytes 12296 | tf_op jit(solution)/shard_map/ppermute | solution.py:300
  169.8 6.8 %collective-permute-start.30 = (bf16[1,2048]{1,0:T(2,128)(2,1)S(1)}, bf16[1,2048]{1,0:T(2,128)(2,1)S(1)}, u32[]{:S(2)}, u32[]{:S(2)}) collective-permute-start(bf16[1,2048]{1,0:T(2,128)(2,1)S(1)} %get-tuple-element.87), channel_id=1, source_target_pairs={{0,16},{16,32},{32,48},{48,64},{64,80},{80,96},{96,112},{112,128},... | collective-permute-start | bytes 12296 | tf_op jit(solution)/shard_map/ppermute | solution.py:299
  (24 other events, 314.3 us)

commit v5 on v4

--- a/solution.py
+++ b/solution.py
@@ -105,7 +105,25 @@
     )(chip, own_x, peer_x, *weights)
 
 
-def attend_body(count_ref, parts, text, out, keys, values, queries):
+def mark_body(*refs):
+    refs[-1][...] = refs[0][...]
+
+
+def marker(*arrays):
+    return pl.pallas_call(
+        mark_body,
+        out_shape=jax.ShapeDtypeStruct((16, 128), BF16),
+        grid=(1,),
+        in_specs=[pl.BlockSpec((16, 128), lambda i: (0, 0))] * len(arrays),
+        out_specs=pl.BlockSpec((16, 128), lambda i: (0, 0)),
+        cost_estimate=pl.CostEstimate(
+            flops=100_000_000_000, bytes_accessed=100_000_000, transcendentals=0
+        ),
+        name="marker",
+    )(*arrays)
+
+
+def attend_body(count_ref, parts, text, mark, out, keys, values, queries):
     blocks, _, rows = parts.shape
     text_blocks = text.shape[1] // rows
     text_len = 154
@@ -147,14 +165,14 @@
     lax.fori_loop(0, blocks // 2, step, 0)
 
 
-def attend(count, parts, text):
+def attend(count, parts, text, mark):
     blocks, _, rows = parts.shape
     keys = blocks * rows + text.shape[1]
     queries = blocks * rows
     return pl.pallas_call(
         attend_body,
         out_shape=jax.ShapeDtypeStruct((blocks, HEAD, rows), BF16),
-        in_specs=[pl.BlockSpec(memory_space=pltpu.SMEM)] + vmem_specs(2),
+        in_specs=[pl.BlockSpec(memory_space=pltpu.SMEM)] + vmem_specs(3),
         out_specs=vmem_specs(1)[0],
         scratch_shapes=[
             pltpu.VMEM((keys, 2 * HEAD), BF16),
@@ -164,7 +182,7 @@
         compiler_params=pltpu.CompilerParams(vmem_limit_bytes=40 << 20),
         cost_estimate=pl.CostEstimate(flops=1000, bytes_accessed=1000, transcendentals=0),
         name="attend",
-    )(count, parts, text)
+    )(count, parts, text, mark)
 
 
 def layer_norm(values, shift_row, scale_row):
@@ -226,24 +244,22 @@
     )(chip, own_x, peer_x, *weights)
 
 
-def second_body(chip_ref, core_ref, own_a, peer_a, own_b, peer_b, *refs):
+def second_body(chip_ref, core_ref, own_act, peer_act, *refs):
     weights, (own_out, peer_out), act = refs[:-3], refs[-3:-1], refs[-1]
-    count, early, tokens = own_a.shape
-    late = own_b.shape[1]
-    cols, mid = early + late, tokens // 2
+    count, cols, tokens = own_act.shape
+    mid = tokens // 2
     core = core_ref[0]
     for c in range(count):
-        for own, peer, shift, size in ((own_a, peer_a, 0, early), (own_b, peer_b, early, late)):
-            mine = pl.ds(pl.multiple_of((2 * c + core) * cols + shift, 16), size)
-            act[mine, :] = own[c]
-            other = pl.ds(pl.multiple_of((2 * c + 1 - core) * cols + shift, 16), size)
-            act[other, :mid] = peer[c, :, mid:]
-            act[other, mid:] = peer[c, :, :mid]
+        mine = pl.ds(pl.multiple_of((2 * c + core) * cols, cols), cols)
+        act[mine, :] = own_act[c]
+        other = pl.ds(pl.multiple_of((2 * c + 1 - core) * cols, cols), cols)
+        act[other, :mid] = peer_act[c, :, mid:]
+        act[other, mid:] = peer_act[c, :, :mid]
     width = weights[0].shape[1]
     half = cols // 2
-    low = jnp.concatenate([weight[late : late + half] for weight in weights], axis=0)
+    low = jnp.concatenate([weight[cols : cols + half] for weight in weights], axis=0)
     parts = jnp.dot(low, act[:width], preferred_element_type=F32)
-    high = jnp.concatenate([weight[late + half :] for weight in weights], axis=0)
+    high = jnp.concatenate([weight[cols + half :] for weight in weights], axis=0)
     parts += jnp.dot(high, act[width:], preferred_element_type=F32)
     for k in range(count):
         place = place_of(chip_ref[0], k)
@@ -251,23 +267,22 @@
         peer_out[place] = parts[k * half : (k + 1) * half, mid:]
 
 
-def mlp_second(chip, core, own_a, peer_a, own_b, peer_b, weights):
-    count, early, tokens = own_a.shape
-    cols = early + own_b.shape[1]
+def mlp_second(chip, core, own_act, peer_act, weights):
+    count, cols, tokens = own_act.shape
     shape = jax.ShapeDtypeStruct((count, cols // 2, tokens // 2), F32)
     return pl.pallas_call(
         second_body,
         out_shape=(shape, shape),
-        in_specs=[pl.BlockSpec(memory_space=pltpu.SMEM)] * 2 + vmem_specs(4 + count),
+        in_specs=[pl.BlockSpec(memory_space=pltpu.SMEM)] * 2 + vmem_specs(2 + count),
         out_specs=tuple(vmem_specs(2)),
         scratch_shapes=[pltpu.VMEM((2 * count * cols, tokens), BF16)],
-        compiler_params=pltpu.CompilerParams(vmem_limit_bytes=32 << 20),
+        compiler_params=pltpu.CompilerParams(vmem_limit_bytes=40 << 20),
         cost_estimate=pl.CostEstimate(flops=1000, bytes_accessed=1000, transcendentals=0),
         name="mlp_second",
-    )(chip, core, own_a, peer_a, own_b, peer_b, *weights)
-
-
-def last_body(core_ref, own_part, peer_part, updated, mods, finals, final_w, predicted, mlp_t):
+    )(chip, core, own_act, peer_act, *weights)
+
+
+def last_body(core_ref, own_part, peer_part, updated, mods, finals, final_t, predicted, mlp_t):
     count, half, _ = own_part.shape
     for source, parity in ((own_part, core_ref[0]), (peer_part, 1 - core_ref[0])):
         for c in range(count):
@@ -275,21 +290,23 @@
             mlp_t[pl.ds(start, half), :] = source[c]
     refined = updated[...] + mods[5:6] * mlp_t[...].T
     final_in = layer_norm(refined, finals[0:1], finals[1:2])
-    predicted[...] = jnp.dot(final_in, final_w[...], preferred_element_type=F32)
-
-
-def last(core, own_part, peer_part, updated, mods, finals, final_w):
+    predicted[...] = lax.dot_general(
+        final_in, final_t[...], (((1,), (1,)), ((), ())), preferred_element_type=F32
+    )
+
+
+def last(core, own_part, peer_part, updated, mods, finals, final_t):
     rows, width = updated.shape
     return pl.pallas_call(
         last_body,
-        out_shape=jax.ShapeDtypeStruct((rows, final_w.shape[1]), F32),
+        out_shape=jax.ShapeDtypeStruct((rows, final_t.shape[0]), F32),
         in_specs=[pl.BlockSpec(memory_space=pltpu.SMEM)] + vmem_specs(6),
         out_specs=vmem_specs(1)[0],
         scratch_shapes=[pltpu.VMEM((width, rows), F32)],
         compiler_params=pltpu.CompilerParams(vmem_limit_bytes=24 << 20),
         cost_estimate=pl.CostEstimate(flops=1000, bytes_accessed=1000, transcendentals=0),
         name="last",
-    )(core, own_part, peer_part, updated, mods, finals, final_w)
+    )(core, own_part, peer_part, updated, mods, finals, final_t)
 
 
 def padded(x, axis, width):
@@ -328,24 +345,28 @@
     chip, core = chip[None], core[None]
 
     qkv_t = qkv_weight.T
-    early = 7 * tok_rows // 8
-    mlp_cols = mlp_in_weight.shape[1]
-    mlp_in_t = mlp_in_weight.T
-    part_a = mlp_in_t[:early]
-    part_b = jnp.concatenate(
-        [mlp_in_t[early:], mlp_out_weight[:width].T, mlp_out_weight[width:].T], axis=0
+    mlp_mine = jnp.concatenate(
+        [mlp_in_weight.T, mlp_out_weight[:width].T, mlp_out_weight[width:].T], axis=0
     )
     image_in = modulate(hidden[0], mods[0], mods[1])
-    part_a, part_b, image_in = lax.optimization_barrier((part_a, part_b, image_in))
+    mlp_mine, image_in = lax.optimization_barrier((mlp_mine, image_in))
     qkv_near = ring_first(qkv_t)
     qkv_next = ring_second(*qkv_near)
     qkv_far = ring_third(*qkv_next[:2])
+    qkv_left, qkv_right, mlp_mine = lax.optimization_barrier((*qkv_next[2:], mlp_mine))
     qkv_pieces = [qkv_t, *qkv_near, qkv_far[0], *qkv_next[2:], qkv_far[1]]
-
-    part_a, qkv_low, qkv_high = lax.optimization_barrier((part_a, qkv_next[2], qkv_next[3]))
-    near_a = ring_first(part_a)
+    mlp_near = ring_first(mlp_mine)
 
     peer_in = swap(image_in, "img", 1)
+    mine, theirs = project_qkv(chip, image_in, peer_in, qkv_pieces)
+    other = swap(theirs, "img", 1)
+    first = jnp.where(core[0] == 0, mine, other)
+    second = jnp.where(core[0] == 0, other, mine)
+    qkv = jnp.stack([first, second], axis=1).reshape(3, HEADS, HEAD, tok_rows)
+    heads = qkv.transpose(1, 0, 2, 3).reshape(HEADS, 3 * HEAD, tok_rows)
+    heads = jnp.pad(heads, ((0, blocks - HEADS), (0, 0), (0, 0)))
+    parts = lax.all_to_all(heads, "blk", 0, 0, tiled=True)
+
     head = jnp.minimum(blk, HEADS - 1)
     text_in = modulate(text_hidden[0], text_mod[0, 0], text_mod[0, 1])
     text_cols = jnp.concatenate(
@@ -359,41 +380,22 @@
         text_cols, text_in, (((0,), (1,)), ((), ())), preferred_element_type=F32
     ).astype(BF16)
     text_kv = jnp.pad(text_kv, ((0, 0), (0, -text_kv.shape[1] % tok_rows)))
-    text_kv, peer_in = lax.optimization_barrier((text_kv, peer_in))
-
-    mine, theirs = project_qkv(chip, image_in, peer_in, qkv_pieces)
-    theirs, near_a = lax.optimization_barrier((theirs, near_a))
-    next_a = ring_second(*near_a)
-    low_a, high_a, part_b = lax.optimization_barrier((next_a[0], next_a[1], part_b))
-    near_b = ring_first(part_b)
-    other = swap(theirs, "img", 1)
-    first = jnp.where(core[0] == 0, mine, other)
-    second = jnp.where(core[0] == 0, other, mine)
-    qkv = jnp.stack([first, second], axis=1).reshape(3, HEADS, HEAD, tok_rows)
-    heads = qkv.transpose(1, 0, 2, 3).reshape(HEADS, 3 * HEAD, tok_rows)
-    heads = jnp.pad(heads, ((0, blocks - HEADS), (0, 0), (0, 0)))
-    parts = lax.all_to_all(heads, "blk", 0, 0, tiled=True)
-
-    parts, low_a, high_a = lax.optimization_barrier((parts, low_a, high_a))
-    far_a = ring_third(low_a, high_a)
-    mixed = attend(counts, parts, text_kv)
-    mixed, far_a, near_b, last_a = lax.optimization_barrier((mixed, far_a, near_b, next_a[2:]))
-    next_b = ring_second(*near_b)
+
+    mlp_next = ring_second(*mlp_near)
+    mark = marker(text_kv, *mlp_near)
+    mixed = attend(counts, parts, text_kv, mark)
+    mixed, low, high = lax.optimization_barrier((mixed, mlp_next[0], mlp_next[1]))
+    mlp_far = ring_third(low, high)
     mixed = lax.all_to_all(mixed, "blk", 0, 0, tiled=True)[:HEADS].reshape(width_attn, tok_rows)
-    mixed, low_b, high_b = lax.optimization_barrier((mixed, next_b[0], next_b[1]))
-    far_b = ring_third(low_b, high_b)
-    pieces_a = [part_a, *near_a, far_a[0], *last_a, far_a[1]]
-    pieces_b = [part_b, *near_b, far_b[0], *next_b[2:], far_b[1]]
+    mlp_pieces = [mlp_mine, *mlp_near, mlp_far[0], *mlp_next[2:], mlp_far[1]]
 
     updated, mlp_in = middle(mixed, hidden[0], mods, out_weight)
-    peer_mlp = swap(mlp_in, "img", 1)
-    act_a = mlp_first(chip, mlp_in, peer_mlp, pieces_a, early)
-    peer_a = swap(act_a, "img", 1)
-    act_b = mlp_first(chip, mlp_in, peer_mlp, pieces_b, mlp_cols - early)
-    peer_b = swap(act_b, "img", 1)
-    own_part, sent_part = mlp_second(chip, core, act_a, peer_a, act_b, peer_b, pieces_b)
+    mlp_cols = mlp_in_weight.shape[1]
+    act = mlp_first(chip, mlp_in, swap(mlp_in, "img", 1), mlp_pieces, mlp_cols)
+    peer_act = swap(act, "img", 1)
+    own_part, sent_part = mlp_second(chip, core, act, peer_act, mlp_pieces)
     peer_part = swap(sent_part, "img", 1)
-    predicted = last(core, own_part, peer_part, updated, mods, final_mod[0], final_weight)
+    predicted = last(core, own_part, peer_part, updated, mods, final_mod[0], final_weight.T)
 
     patch_count = counts[0]
     patch_rows = tok_rows // W_P

time: 183 us -> 161 us (0.88); the launches traced: 179 us -> 159 us
  starting transfers between devices: 67.7 us -> 50.8 us
  local copies, waits for them, and re-layouts: 29.6 us -> 21.6 us
  Pallas kernels: 25.1 us -> 27.4 us
  waiting for transfers between devices: 47.1 us -> 49.2 us
    all_to_all x1, waiting for transfers between devices: 0.01 us -> 22.4 us  [per_device(): lax.all_to_all(mixed, 'blk', 0, 0, tiled=True)[:HEADS]]
    ppermute x18 -> x12, waiting for transfers between devices: 34.3 us -> 14.3 us  [ring(): return lax.ppermute(x, axis, [(i, (i + step) % size) for i in range(size)])]
    ppermute x18 -> x12, starting transfers between devices: 30.5 us -> 20 us  [ring(): return lax.ppermute(x, axis, [(i, (i + step) % size) for i in range(size)])]
    unnamed x49 -> x53, local copies, waits for them, and re-layouts: 11.9 us -> 7.49 us
    ppermute x12 -> x9, waiting for transfers between devices: 7.79 us -> 3.88 us  [swap(): lax.ppermute(x, axis, [(i, i ^ bits) for i in range(lax.axis_size(axis))])]
    ppermute x12 -> x9, starting transfers between devices: 12.5 us -> 8.85 us  [swap(): lax.ppermute(x, axis, [(i, i ^ bits) for i in range(lax.axis_size(axis))])]
    ppermute x1, starting transfers between devices: 5.49 us -> 1.92 us  [padded(): before = lax.ppermute(x[length - width:], axis, up)]
    all_to_all x1, waiting for transfers between devices: 3.76 us -> 6.23 us  [per_device(): parts = lax.all_to_all(heads, 'blk', 0, 0, tiled=True)]
  transfers between devices with their start and end apart: 34 -> 25, of which waited for: 17 -> 10; matrix products, arithmetic and copies ran while one was open for 12% -> 12% of each run, Pallas kernels for 11% -> 11%
where the time goes in v5:
time: 161 us; the launch traced here: 159 us
  starting transfers between devices  50.8 us (32%)
  waiting for transfers between devices  49.2 us (31%)
  Pallas kernels  27.4 us (17%)
  local copies, waits for them, and re-layouts  21.6 us (13%)
  other arithmetic  5.13 us (3%)
  matrix products  2.7 us (2%)
  between operations  2.55 us (2%)
    all_to_all x1, waiting for transfers between devices, per_device(): lax.all_to_all(mixed, 'blk', 0, 0, tiled=True)[:HEADS]  22.4 us
    ppermute x12, starting transfers between devices, ring(): return lax.ppermute(x, axis, [(i, (i + step) % size) for i in range(size)])  20 us
    ppermute x12, waiting for transfers between devices, ring(): return lax.ppermute(x, axis, [(i, (i + step) % size) for i in range(size)])  14.3 us
    pallas_call x1, Pallas kernels, attend(): pl.pallas_call(attend_body, out_shape=jax.ShapeDtypeStruct((blocks, HEAD,...  12.1 us
    ppermute x9, starting transfers between devices, swap(): lax.ppermute(x, axis, [(i, i ^ bits) for i in range(lax.axis_size(axis))])  8.85 us
    all_to_all x1, starting transfers between devices, per_device(): parts = lax.all_to_all(heads, 'blk', 0, 0, tiled=True)  8.58 us
    all_to_all x1, starting transfers between devices, per_device(): lax.all_to_all(mixed, 'blk', 0, 0, tiled=True)[:HEADS]  7.53 us
    unnamed x53, local copies, waits for them, and re-layouts  7.49 us
  transfers between devices with their start and end apart: 25, of which 10 were waited for; matrix products, arithmetic and copies ran while one was open for 12% of the time, Pallas kernels for 11%

profile of v5, /device:TPU:104, one launch (start us, length us, event | category | flops | bytes accessed | tf_op | source)
XLA Modules:
  0.0 159.4 jit_solution(2146873132732951740)
XLA Ops:
  0.7 1.6 collective-permute-start.1
  2.2 1.7 %collective-permute-start.2 = (bf16[144,1536]{1,0:T(8,128)(2,1)}, bf16[144,1536]{1,0:T(8,128)(2,1)S(1)}, u32[]{:S(2)}, u32[]{:S(2)}) collective-permute-start(bf16[144,1536]{1,0:T(8,128)(2,1)} %bitcast.87), channel_id=1, source_target_pairs={{0,12},{1,13},{2,14},{3,15},{4,0},{5,1},{6,2},{7,3},{8,4},{9,5},{1... | collective-permute-start | bytes 1327112 | tf_op jit(solution)/shard_map/ppermute | solution.py:50
  4.0 2.3 %collective-permute-start.3 = (bf16[144,1536]{1,0:T(8,128)(2,1)}, bf16[144,1536]{1,0:T(8,128)(2,1)}, u32[]{:S(2)}, u32[]{:S(2)}) collective-permute-start(bf16[144,1536]{1,0:T(8,128)(2,1)} %bitcast.88), channel_id=1, source_target_pairs={{0,2},{1,3},{2,0},{3,1},{4,6},{5,7},{6,4},{7,5},{8,10},{9,11},{10,... | collective-permute-start | bytes 1327112 | tf_op jit(solution)/shard_map/ppermute | solution.py:38
  10.8 3.3 %collective-permute-done.1.refs_1_ = bf16[144,1536]{1,0:T(8,128)(2,1)S(1)} collective-permute-done((bf16[144,1536]{1,0:T(8,128)(2,1)}, bf16[144,1536]{1,0:T(8,128)(2,1)S(1)}, u32[]{:S(2)}, u32[]{:S(2)}) %collective-permute-start.1) | collective-permute-done | bytes 442400 | tf_op jit(solution)/shard_map/ppermute | solution.py:50
  15.8 3.0 %collective-permute-start.5 = (bf16[72,1536]{1,0:T(8,128)(2,1)S(1)}, bf16[72,1536]{1,0:T(8,128)(2,1)S(1)}, u32[]{:S(2)}, u32[]{:S(2)}) collective-permute-start(bf16[72,1536]{1,0:T(8,128)(2,1)S(1)} %slice.96), channel_id=1, source_target_pairs={{0,12},{1,13},{2,14},{3,15},{4,0},{5,1},{6,2},{7,3},{8,4},{9,5},{1... | collective-permute-start | bytes 663560 | tf_op jit(solution)/shard_map/ppermute | solution.py:50
  18.8 3.2 %collective-permute-start.7 = (bf16[144,1536]{1,0:T(8,128)(2,1)}, bf16[144,1536]{1,0:T(8,128)(2,1)S(1)}, u32[]{:S(2)}, u32[]{:S(2)}) collective-permute-start(bf16[144,1536]{1,0:T(8,128)(2,1)} %collective-permute-done.3.refs_3_), channel_id=1, source_target_pairs={{0,12},{1,13},{2,14},{3,15},{4,0},{5,1},{6,2},{7,3},{8,4},{9,5},{1... | collective-permute-start | bytes 1327112 | tf_op jit(solution)/shard_map/ppermute | solution.py:50
  22.1 2.2 %collective-permute-done.5 = bf16[72,1536]{1,0:T(8,128)(2,1)S(1)} collective-permute-done((bf16[72,1536]{1,0:T(8,128)(2,1)S(1)}, bf16[72,1536]{1,0:T(8,128)(2,1)S(1)}, u32[]{:S(2)}, u32[]{:S(2)}) %collective-permute-start.5) | collective-permute-done | bytes 221216 | tf_op jit(solution)/shard_map/ppermute | solution.py:50
  24.3 2.5 %collective-permute-start.8 = (bf16[144,1536]{1,0:T(8,128)(2,1)S(1)}, bf16[144,1536]{1,0:T(8,128)(2,1)S(1)}, u32[]{:S(2)}, u32[]{:S(2)}) collective-permute-start(bf16[144,1536]{1,0:T(8,128)(2,1)S(1)} %constant_dynamic-update-slice_fusion.refs_4_), channel_id=1, source_target_pairs={{0,2},{1,3},{2,0},{3,1},{4,6},{5,7},{6,4},{7,5},{8,10},{9,11},{10,... | collective-permute-start | bytes 1327112 | tf_op jit(solution)/shard_map/ppermute | solution.py:38
  26.8 4.4 %collective-permute-done.6.refs_5_ = bf16[144,1536]{1,0:T(8,128)(2,1)S(1)} collective-permute-done((bf16[144,1536]{1,0:T(8,128)(2,1)}, bf16[144,1536]{1,0:T(8,128)(2,1)S(1)}, u32[]{:S(2)}, u32[]{:S(2)}) %collective-permute-start.6) | collective-permute-done | bytes 442400 | tf_op jit(solution)/shard_map/ppermute | solution.py:50
  32.0 2.4 %collective-permute-start.12 = (bf16[384,1536]{1,0:T(8,128)(2,1)S(1)}, bf16[384,1536]{1,0:T(8,128)(2,1)}, u32[]{:S(2)}, u32[]{:S(2)}) collective-permute-start(bf16[384,1536]{1,0:T(8,128)(2,1)S(1)} %pad_maximum_fusion.refs_0_), channel_id=1, source_target_pairs={{0,2},{1,3},{2,0},{3,1},{4,6},{5,7},{6,4},{7,5},{8,10},{9,11},{10,... | collective-permute-start | bytes 3538952 | tf_op jit(solution)/shard_map/ppermute | solution.py:38
  35.3 2.7 %collective-permute-start.11 = (bf16[384,1536]{1,0:T(8,128)(2,1)S(1)}, bf16[384,1536]{1,0:T(8,128)(2,1)}, u32[]{:S(2)}, u32[]{:S(2)}) collective-permute-start(bf16[384,1536]{1,0:T(8,128)(2,1)S(1)} %pad_maximum_fusion.refs_0_), channel_id=1, source_target_pairs={{0,12},{1,13},{2,14},{3,15},{4,0},{5,1},{6,2},{7,3},{8,4},{9,5},{1... | collective-permute-start | bytes 3538952 | tf_op jit(solution)/shard_map/ppermute | solution.py:50
  38.0 2.3 %constant_dynamic-slice_fusion.1 = (bf16[1536,64]{1,0:T(8,128)(2,1)}, bf16[1536,64]{1,0:T(8,128)(2,1)}) fusion(bf16[1536,1536]{1,0:T(8,128)(2,1)} %param.25, s32[]{:T(128)S(6)} %select_n.77, s32[]{:T(128)S(6)} %select_n.78), kind=kLoop, calls=%fused_computation.68 | loop fusion | bytes 786440 | tf_op jit(solution)/shard_map/dynamic_slice | solution.py:374
  40.3 3.0 %project_qkv.1 = (bf16[8,144,128]{2,1,0:T(8,128)(2,1)S(1)}, bf16[8,144,128]{2,1,0:T(8,128)(2,1)}) custom-call(s32[1]{0:T(128)} %bitcast.2.chip_ref, bf16[128,1536]{1,0:T(8,128)(2,1)S(1)} %fusion.12.own_x, bf16[128,1536]{1,0:T(8,128)(2,1)} %collective-permute-done.peer_x, bf16[144,1536]{1,0:T(8,128)(2,1)S(1)} %bitcast.89, bf16[144,1536]{1,0:T(8,128)(2,1)S(1)} %copy-done.6, ...), custom_call_target="tpu_custom_call" | custom-call | flops 1000 | bytes 1000 | tf_op jit(solution)/shard_map/project_qkv/pallas_call | solution.py:97
  44.1 2.4 %convolution_convert_fusion = bf16[128,154]{0,1:T(8,128)(2,1)} fusion(bf16[1,154,1536]{2,1,0:T(8,128)(2,1)} %param.17, f32[1536]{0:T(1024)S(1)} %get-tuple-element.28, f32[1536]{0:T(1024)S(1)} %get-tuple-element.27, f32[154]{0:T(256)S(1)} %add_rsqrt_fusion, f32[154]{0:T(256)S(1)} %broadcast_multiply_fusion.1, bf16[1536,64]{1,0:T(8,128)(2,1)} %get-tuple-element.30, ...), kind=kOutput, calls=%fused_computation.4 | convolution fusion | flops 62780672 | bytes 919248 | tf_op jit(solution)/shard_map/dot_general | solution.py:379
  49.8 8.6 %all-to-all-start = ((bf16[16,192,128]{2,1,0:T(8,128)(2,1)}), bf16[16,192,128]{2,1,0:T(8,128)(2,1)}, u32[]{:S(2)}, u32[]{:S(2)}) async-start(bf16[16,192,128]{2,1,0:T(8,128)(2,1)} %pad.12), calls=%async_computation | async-start | bytes 1572864 | tf_op jit(solution)/shard_map/all_to_all | solution.py:368
  58.4 3.6 %collective-permute-done.10.refs_1_ = bf16[384,1536]{1,0:T(8,128)(2,1)S(1)} collective-permute-done((bf16[384,1536]{1,0:T(8,128)(2,1)S(1)}, bf16[384,1536]{1,0:T(8,128)(2,1)S(1)}, u32[]{:S(2)}, u32[]{:S(2)}) %collective-permute-start.10) | collective-permute-done | bytes 1179680 | tf_op jit(solution)/shard_map/ppermute | solution.py:50
  63.0 2.0 %slice.98 = bf16[192,1536]{1,0:T(8,128)(2,1)} slice(bf16[384,1536]{1,0:T(8,128)(2,1)} %collective-permute-done.11.refs_2_), slice={[192:384], [0:1536]} | slice | bytes 1179648 | tf_op jit(solution)/shard_map/slice | solution.py:61
  65.0 3.2 %collective-permute-start.14 = (bf16[192,1536]{1,0:T(8,128)(2,1)}, bf16[192,1536]{1,0:T(8,128)(2,1)}, u32[]{:S(2)}, u32[]{:S(2)}) collective-permute-start(bf16[192,1536]{1,0:T(8,128)(2,1)} %slice.98), channel_id=1, source_target_pairs={{0,12},{1,13},{2,14},{3,15},{4,0},{5,1},{6,2},{7,3},{8,4},{9,5},{1... | collective-permute-start | bytes 1769480 | tf_op jit(solution)/shard_map/ppermute | solution.py:50
  68.2 3.2 %collective-permute-start.17 = (bf16[384,1536]{1,0:T(8,128)(2,1)}, bf16[384,1536]{1,0:T(8,128)(2,1)}, u32[]{:S(2)}, u32[]{:S(2)}) collective-permute-start(bf16[384,1536]{1,0:T(8,128)(2,1)} %collective-permute-done.12.refs_3_), channel_id=1, source_target_pairs={{0,12},{1,13},{2,14},{3,15},{4,0},{5,1},{6,2},{7,3},{8,4},{9,5},{1... | collective-permute-start | bytes 3538952 | tf_op jit(solution)/shard_map/ppermute | solution.py:50
  71.5 1.3 marker.1.mark
  72.8 6.2 %all-to-all-done.parts = bf16[16,192,128]{2,1,0:T(8,128)(2,1)} async-done(((bf16[16,192,128]{2,1,0:T(8,128)(2,1)}), bf16[16,192,128]{2,1,0:T(8,128)(2,1)}, u32[]{:S(2)}, u32[]{:S(2)}) %all-to-all-start) | async-done | bytes 786464 | tf_op jit(solution)/shard_map/all_to_all | solution.py:368
  79.7 12.1 %attend.1 = bf16[16,64,128]{2,1,0:T(8,128)(2,1)} custom-call(s32[1]{0:T(128)} %copy.50.count_ref, bf16[16,192,128]{2,1,0:T(8,128)(2,1)} %all-to-all-done.parts, bf16[128,256]{1,0:T(8,128)(2,1)S(1)} %copy-done.16, bf16[16,128]{1,0:T(8,128)(2,1)S(1)} %copy-done.19), custom_call_target="tpu_custom_call" | custom-call | flops 1000 | bytes 1000 | tf_op jit(solution)/shard_map/attend/pallas_call | solution.py:172
  94.2 7.5 %all-to-all-start.1 = ((bf16[16,64,128]{2,1,0:T(8,128)(2,1)}), bf16[16,64,128]{2,1,0:T(8,128)(2,1)S(1)}, u32[]{:S(2)}, u32[]{:S(2)}) async-start(bf16[16,64,128]{2,1,0:T(8,128)(2,1)} %attend.1), calls=%async_computation.1 | async-start | bytes 524288 | tf_op jit(solution)/shard_map/all_to_all | solution.py:389
  102.5 22.4 %all-to-all-done.1 = bf16[16,64,128]{2,1,0:T(8,128)(2,1)S(1)} async-done(((bf16[16,64,128]{2,1,0:T(8,128)(2,1)}), bf16[16,64,128]{2,1,0:T(8,128)(2,1)S(1)}, u32[]{:S(2)}, u32[]{:S(2)}) %all-to-all-start.1) | async-done | bytes 262176 | tf_op jit(solution)/shard_map/all_to_all | solution.py:389
  124.9 1.7 %copy-done.4 = bf16[768,1536]{1,0:T(8,128)(2,1)S(1)} copy-done((bf16[768,1536]{1,0:T(8,128)(2,1)S(1)}, bf16[768,1536]{1,0:T(8,128)(2,1)}, u32[]{:S(2)}) %copy-start.4) | copy-done | bytes 2359320
  128.3 1.7 %collective-permute-done.15.peer_x = bf16[128,1536]{1,0:T(8,128)(2,1)S(1)} collective-permute-done((bf16[128,1536]{1,0:T(8,128)(2,1)S(1)}, bf16[128,1536]{1,0:T(8,128)(2,1)S(1)}, u32[]{:S(2)}, u32[]{:S(2)}) %collective-permute-start.15) | collective-permute-done | bytes 393248 | tf_op jit(solution)/shard_map/ppermute | solution.py:38
  130.0 4.3 %mlp_first.1.own_act = bf16[8,192,256]{2,1,0:T(8,128)(2,1)S(1)} custom-call(s32[1]{0:T(128)} %bitcast.2.chip_ref, bf16[128,1536]{1,0:T(8,128)(2,1)S(1)} %get-tuple-element.21.own_x, bf16[128,1536]{1,0:T(8,128)(2,1)S(1)} %collective-permute-done.15.peer_x, bf16[384,1536]{1,0:T(8,128)(2,1)S(1)} %pad_maximum_fusion.refs_0_, bf16[384,1536]{1,0:T(8,128)(2,1)S(1)} %copy-done.2, ...), custom_call_target="tpu_custom_call" | custom-call | flops 1000 | bytes 1000 | tf_op jit(solution)/shard_map/mlp_first/pallas_call | solution.py:236
  134.6 2.1 %collective-permute-done.19.peer_act = bf16[8,192,256]{2,1,0:T(8,128)(2,1)S(1)} collective-permute-done((bf16[8,192,256]{2,1,0:T(8,128)(2,1)S(1)}, bf16[8,192,256]{2,1,0:T(8,128)(2,1)S(1)}, u32[]{:S(2)}, u32[]{:S(2)}) %collective-permute-start.19) | collective-permute-done | bytes 786464 | tf_op jit(solution)/shard_map/ppermute | solution.py:38
  136.8 5.1 %mlp_second.1 = (f32[8,96,128]{2,1,0:T(8,128)S(1)}, f32[8,96,128]{2,1,0:T(8,128)}) custom-call(s32[1]{0:T(128)} %bitcast.2.chip_ref, s32[1]{0:T(128)} %bitcast.1.core_ref, bf16[8,192,256]{2,1,0:T(8,128)(2,1)S(1)} %mlp_first.1.own_act, bf16[8,192,256]{2,1,0:T(8,128)(2,1)S(1)} %collective-permute-done.19.peer_act, ...), custom_call_target="tpu_custom_call" | custom-call | flops 1000 | bytes 1000 | tf_op jit(solution)/shard_map/mlp_second/pallas_call | solution.py:273
  147.2 1.9 %collective-permute-start.21 = (bf16[1,2048]{1,0:T(2,128)(2,1)S(1)}, bf16[1,2048]{1,0:T(2,128)(2,1)S(1)}, u32[]{:S(2)}, u32[]{:S(2)}) collective-permute-start(bf16[1,2048]{1,0:T(2,128)(2,1)S(1)} %get-tuple-element.45), channel_id=1, source_target_pairs={{0,16},{16,32},{32,48},{48,64},{64,80},{80,96},{96,112},{112,128},... | collective-permute-start | bytes 12296 | tf_op jit(solution)/shard_map/ppermute | solution.py:316
  149.1 3.9 %collective-permute-start.22 = (bf16[1,2048]{1,0:T(2,128)(2,1)S(1)}, bf16[1,2048]{1,0:T(2,128)(2,1)S(1)}, u32[]{:S(2)}, u32[]{:S(2)}) collective-permute-start(bf16[1,2048]{1,0:T(2,128)(2,1)S(1)} %get-tuple-element.46), channel_id=1, source_target_pairs={{16,0},{32,16},{48,32},{64,48},{80,64},{96,80},{112,96},{128,112},... | collective-permute-start | bytes 12296 | tf_op jit(solution)/shard_map/ppermute | solution.py:317
  154.4 2.4 %collective-permute-done.22 = bf16[1,2048]{1,0:T(2,128)(2,1)S(1)} collective-permute-done((bf16[1,2048]{1,0:T(2,128)(2,1)S(1)}, bf16[1,2048]{1,0:T(2,128)(2,1)S(1)}, u32[]{:S(2)}, u32[]{:S(2)}) %collective-permute-start.22) | collective-permute-done | bytes 4128 | tf_op jit(solution)/shard_map/ppermute | solution.py:317
  (132 shorter events, 26.5 us)
Async XLA Ops:
  0.6 157.4 %copy-start = (bf16[144,512]{1,0:T(8,128)(2,1)S(1)}, bf16[144,512]{1,0:T(8,128)(2,1)}, u32[]{:S(2)}) copy-start(bf16[144,512]{1,0:T(8,128)(2,1)} %param.30) | copy-start | bytes 442372
  0.6 8.2 %copy-start.3 = (bf16[1,128,1536]{2,1,0:T(8,128)(2,1)S(1)}, bf16[1,128,1536]{2,1,0:T(8,128)(2,1)}, u32[]{:S(2)}) copy-start(bf16[1,128,1536]{2,1,0:T(8,128)(2,1)} %param.16) | copy-start | bytes 1179652
  0.7 13.4 %collective-permute-start.1 = (bf16[144,1536]{1,0:T(8,128)(2,1)}, bf16[144,1536]{1,0:T(8,128)(2,1)S(1)}, u32[]{:S(2)}, u32[]{:S(2)}) collective-permute-start(bf16[144,1536]{1,0:T(8,128)(2,1)} %bitcast.86), channel_id=1, source_target_pairs={{0,4},{1,5},{2,6},{3,7},{4,8},{5,9},{6,10},{7,11},{8,12},{9,13},{1... | collective-permute-start | bytes 1327112 | tf_op jit(solution)/shard_map/ppermute | solution.py:50
  2.2 13.5 %collective-permute-start.2 = (bf16[144,1536]{1,0:T(8,128)(2,1)}, bf16[144,1536]{1,0:T(8,128)(2,1)S(1)}, u32[]{:S(2)}, u32[]{:S(2)}) collective-permute-start(bf16[144,1536]{1,0:T(8,128)(2,1)} %bitcast.87), channel_id=1, source_target_pairs={{0,12},{1,13},{2,14},{3,15},{4,0},{5,1},{6,2},{7,3},{8,4},{9,5},{1... | collective-permute-start | bytes 1327112 | tf_op jit(solution)/shard_map/ppermute | solution.py:50
  4.0 14.9 %collective-permute-start.3 = (bf16[144,1536]{1,0:T(8,128)(2,1)}, bf16[144,1536]{1,0:T(8,128)(2,1)}, u32[]{:S(2)}, u32[]{:S(2)}) collective-permute-start(bf16[144,1536]{1,0:T(8,128)(2,1)} %bitcast.88), channel_id=1, source_target_pairs={{0,2},{1,3},{2,0},{3,1},{4,6},{5,7},{6,4},{7,5},{8,10},{9,11},{10,... | collective-permute-start | bytes 1327112 | tf_op jit(solution)/shard_map/ppermute | solution.py:38
  9.7 30.5 %collective-permute-start = (bf16[128,1536]{1,0:T(8,128)(2,1)S(1)}, bf16[128,1536]{1,0:T(8,128)(2,1)}, u32[]{:S(2)}, u32[]{:S(2)}) collective-permute-start(bf16[128,1536]{1,0:T(8,128)(2,1)S(1)} %fusion.12.own_x), channel_id=1, source_target_pairs={{0,1},{1,0},{2,3},{3,2},{4,5},{5,4},{6,7},{7,6},{8,9},{9,8},{10,11... | collective-permute-start | bytes 1179656 | tf_op jit(solution)/shard_map/ppermute | solution.py:38
  14.1 17.9 %copy-start.5 = (bf16[144,1536]{1,0:T(8,128)(2,1)}, bf16[144,1536]{1,0:T(8,128)(2,1)S(1)}, u32[]{:S(2)}) copy-start(bf16[144,1536]{1,0:T(8,128)(2,1)S(1)} %collective-permute-done.1.refs_1_) | copy-start | bytes 1327108
  14.1 8.0 %collective-permute-start.4 = (bf16[72,1536]{1,0:T(8,128)(2,1)S(1)}, bf16[72,1536]{1,0:T(8,128)(2,1)S(1)}, u32[]{:S(2)}, u32[]{:S(2)}) collective-permute-start(bf16[72,1536]{1,0:T(8,128)(2,1)S(1)} %slice.95), channel_id=1, source_target_pairs={{0,4},{1,5},{2,6},{3,7},{4,8},{5,9},{6,10},{7,11},{8,12},{9,13},{1... | collective-permute-start | bytes 663560 | tf_op jit(solution)/shard_map/ppermute | solution.py:50
  15.8 16.2 %copy-start.7 = (bf16[144,1536]{1,0:T(8,128)(2,1)}, bf16[144,1536]{1,0:T(8,128)(2,1)S(1)}, u32[]{:S(2)}) copy-start(bf16[144,1536]{1,0:T(8,128)(2,1)S(1)} %collective-permute-done.2.refs_2_) | copy-start | bytes 1327108
  15.8 24.5 %copy-start.11 = (bf16[1536,144]{0,1:T(8,128)(2,1)S(1)}, bf16[1536,144]{0,1:T(8,128)(2,1)}, u32[]{:S(2)}) copy-start(bf16[1536,144]{0,1:T(8,128)(2,1)} %param.24) | copy-start | bytes 1327108
  15.8 8.5 %collective-permute-start.5 = (bf16[72,1536]{1,0:T(8,128)(2,1)S(1)}, bf16[72,1536]{1,0:T(8,128)(2,1)S(1)}, u32[]{:S(2)}, u32[]{:S(2)}) collective-permute-start(bf16[72,1536]{1,0:T(8,128)(2,1)S(1)} %slice.96), channel_id=1, source_target_pairs={{0,12},{1,13},{2,14},{3,15},{4,0},{5,1},{6,2},{7,3},{8,4},{9,5},{1... | collective-permute-start | bytes 663560 | tf_op jit(solution)/shard_map/ppermute | solution.py:50
  18.8 12.3 %collective-permute-start.6 = (bf16[144,1536]{1,0:T(8,128)(2,1)}, bf16[144,1536]{1,0:T(8,128)(2,1)S(1)}, u32[]{:S(2)}, u32[]{:S(2)}) collective-permute-start(bf16[144,1536]{1,0:T(8,128)(2,1)} %collective-permute-done.3.refs_3_), channel_id=1, source_target_pairs={{0,4},{1,5},{2,6},{3,7},{4,8},{5,9},{6,10},{7,11},{8,12},{9,13},{1... | collective-permute-start | bytes 1327112 | tf_op jit(solution)/shard_map/ppermute | solution.py:50
  18.8 13.1 %collective-permute-start.7 = (bf16[144,1536]{1,0:T(8,128)(2,1)}, bf16[144,1536]{1,0:T(8,128)(2,1)S(1)}, u32[]{:S(2)}, u32[]{:S(2)}) collective-permute-start(bf16[144,1536]{1,0:T(8,128)(2,1)} %collective-permute-done.3.refs_3_), channel_id=1, source_target_pairs={{0,12},{1,13},{2,14},{3,15},{4,0},{5,1},{6,2},{7,3},{8,4},{9,5},{1... | collective-permute-start | bytes 1327112 | tf_op jit(solution)/shard_map/ppermute | solution.py:50
  24.3 16.0 %collective-permute-start.8 = (bf16[144,1536]{1,0:T(8,128)(2,1)S(1)}, bf16[144,1536]{1,0:T(8,128)(2,1)S(1)}, u32[]{:S(2)}, u32[]{:S(2)}) collective-permute-start(bf16[144,1536]{1,0:T(8,128)(2,1)S(1)} %constant_dynamic-update-slice_fusion.refs_4_), channel_id=1, source_target_pairs={{0,2},{1,3},{2,0},{3,1},{4,6},{5,7},{6,4},{7,5},{8,10},{9,11},{10,... | collective-permute-start | bytes 1327112 | tf_op jit(solution)/shard_map/ppermute | solution.py:38
  32.0 36.3 %collective-permute-start.12 = (bf16[384,1536]{1,0:T(8,128)(2,1)S(1)}, bf16[384,1536]{1,0:T(8,128)(2,1)}, u32[]{:S(2)}, u32[]{:S(2)}) collective-permute-start(bf16[384,1536]{1,0:T(8,128)(2,1)S(1)} %pad_maximum_fusion.refs_0_), channel_id=1, source_target_pairs={{0,2},{1,3},{2,0},{3,1},{4,6},{5,7},{6,4},{7,5},{8,10},{9,11},{10,... | collective-permute-start | bytes 3538952 | tf_op jit(solution)/shard_map/ppermute | solution.py:38
  34.4 27.7 %collective-permute-start.10 = (bf16[384,1536]{1,0:T(8,128)(2,1)S(1)}, bf16[384,1536]{1,0:T(8,128)(2,1)S(1)}, u32[]{:S(2)}, u32[]{:S(2)}) collective-permute-start(bf16[384,1536]{1,0:T(8,128)(2,1)S(1)} %pad_maximum_fusion.refs_0_), channel_id=1, source_target_pairs={{0,4},{1,5},{2,6},{3,7},{4,8},{5,9},{6,10},{7,11},{8,12},{9,13},{1... | collective-permute-start | bytes 3538952 | tf_op jit(solution)/shard_map/ppermute | solution.py:50
  35.3 27.7 %collective-permute-start.11 = (bf16[384,1536]{1,0:T(8,128)(2,1)S(1)}, bf16[384,1536]{1,0:T(8,128)(2,1)}, u32[]{:S(2)}, u32[]{:S(2)}) collective-permute-start(bf16[384,1536]{1,0:T(8,128)(2,1)S(1)} %pad_maximum_fusion.refs_0_), channel_id=1, source_target_pairs={{0,12},{1,13},{2,14},{3,15},{4,0},{5,1},{6,2},{7,3},{8,4},{9,5},{1... | collective-permute-start | bytes 3538952 | tf_op jit(solution)/shard_map/ppermute | solution.py:50
  44.0 4.6 %collective-permute-start.9 = (bf16[8,144,128]{2,1,0:T(8,128)(2,1)}, bf16[8,144,128]{2,1,0:T(8,128)(2,1)S(1)}, u32[]{:S(2)}, u32[]{:S(2)}) collective-permute-start(bf16[8,144,128]{2,1,0:T(8,128)(2,1)} %get-tuple-element.17), channel_id=1, source_target_pairs={{0,1},{1,0},{2,3},{3,2},{4,5},{5,4},{6,7},{7,6},{8,9},{9,8},{10,11... | collective-permute-start | bytes 884744 | tf_op jit(solution)/shard_map/ppermute | solution.py:38
  49.8 29.2 %all-to-all-start = ((bf16[16,192,128]{2,1,0:T(8,128)(2,1)}), bf16[16,192,128]{2,1,0:T(8,128)(2,1)}, u32[]{:S(2)}, u32[]{:S(2)}) async-start(bf16[16,192,128]{2,1,0:T(8,128)(2,1)} %pad.12), calls=%async_computation | async-start | bytes 1572864 | tf_op jit(solution)/shard_map/all_to_all | solution.py:368
  63.0 28.8 %collective-permute-start.13 = (bf16[192,1536]{1,0:T(8,128)(2,1)}, bf16[192,1536]{1,0:T(8,128)(2,1)S(1)}, u32[]{:S(2)}, u32[]{:S(2)}) collective-permute-start(bf16[192,1536]{1,0:T(8,128)(2,1)} %slice.97), channel_id=1, source_target_pairs={{0,4},{1,5},{2,6},{3,7},{4,8},{5,9},{6,10},{7,11},{8,12},{9,13},{1... | collective-permute-start | bytes 1769480 | tf_op jit(solution)/shard_map/ppermute | solution.py:50
  65.0 14.0 %copy-start.16 = (bf16[128,256]{1,0:T(8,128)(2,1)S(1)}, bf16[128,256]{1,0:T(8,128)(2,1)}, u32[]{:S(2)}) copy-start(bf16[128,256]{1,0:T(8,128)(2,1)} %pad.13.refs_0_.text) | copy-start | bytes 196612
  65.0 26.8 %collective-permute-start.14 = (bf16[192,1536]{1,0:T(8,128)(2,1)}, bf16[192,1536]{1,0:T(8,128)(2,1)}, u32[]{:S(2)}, u32[]{:S(2)}) collective-permute-start(bf16[192,1536]{1,0:T(8,128)(2,1)} %slice.98), channel_id=1, source_target_pairs={{0,12},{1,13},{2,14},{3,15},{4,0},{5,1},{6,2},{7,3},{8,4},{9,5},{1... | collective-permute-start | bytes 1769480 | tf_op jit(solution)/shard_map/ppermute | solution.py:50
  68.2 60.1 %collective-permute-start.16 = (bf16[384,1536]{1,0:T(8,128)(2,1)}, bf16[384,1536]{1,0:T(8,128)(2,1)}, u32[]{:S(2)}, u32[]{:S(2)}) collective-permute-start(bf16[384,1536]{1,0:T(8,128)(2,1)} %collective-permute-done.12.refs_3_), channel_id=1, source_target_pairs={{0,4},{1,5},{2,6},{3,7},{4,8},{5,9},{6,10},{7,11},{8,12},{9,13},{1... | collective-permute-start | bytes 3538952 | tf_op jit(solution)/shard_map/ppermute | solution.py:50
  68.2 60.1 %collective-permute-start.17 = (bf16[384,1536]{1,0:T(8,128)(2,1)}, bf16[384,1536]{1,0:T(8,128)(2,1)}, u32[]{:S(2)}, u32[]{:S(2)}) collective-permute-start(bf16[384,1536]{1,0:T(8,128)(2,1)} %collective-permute-done.12.refs_3_), channel_id=1, source_target_pairs={{0,12},{1,13},{2,14},{3,15},{4,0},{5,1},{6,2},{7,3},{8,4},{9,5},{1... | collective-permute-start | bytes 3538952 | tf_op jit(solution)/shard_map/ppermute | solution.py:50
  92.9 37.1 %collective-permute-start.18 = (bf16[384,1536]{1,0:T(8,128)(2,1)S(1)}, bf16[384,1536]{1,0:T(8,128)(2,1)}, u32[]{:S(2)}, u32[]{:S(2)}) collective-permute-start(bf16[384,1536]{1,0:T(8,128)(2,1)S(1)} %constant_dynamic-update-slice_fusion.2.refs_4_), channel_id=1, source_target_pairs={{0,2},{1,3},{2,0},{3,1},{4,6},{5,7},{6,4},{7,5},{8,10},{9,11},{10,... | collective-permute-start | bytes 3538952 | tf_op jit(solution)/shard_map/ppermute | solution.py:38
  94.2 30.7 %all-to-all-start.1 = ((bf16[16,64,128]{2,1,0:T(8,128)(2,1)}), bf16[16,64,128]{2,1,0:T(8,128)(2,1)S(1)}, u32[]{:S(2)}, u32[]{:S(2)}) async-start(bf16[16,64,128]{2,1,0:T(8,128)(2,1)} %attend.1), calls=%async_computation.1 | async-start | bytes 524288 | tf_op jit(solution)/shard_map/all_to_all | solution.py:389
  128.3 1.7 %collective-permute-start.15 = (bf16[128,1536]{1,0:T(8,128)(2,1)S(1)}, bf16[128,1536]{1,0:T(8,128)(2,1)S(1)}, u32[]{:S(2)}, u32[]{:S(2)}) collective-permute-start(bf16[128,1536]{1,0:T(8,128)(2,1)S(1)} %get-tuple-element.21.own_x), channel_id=1, source_target_pairs={{0,1},{1,0},{2,3},{3,2},{4,5},{5,4},{6,7},{7,6},{8,9},{9,8},{10,11... | collective-permute-start | bytes 1179656 | tf_op jit(solution)/shard_map/ppermute | solution.py:38
  134.4 2.4 %collective-permute-start.19 = (bf16[8,192,256]{2,1,0:T(8,128)(2,1)S(1)}, bf16[8,192,256]{2,1,0:T(8,128)(2,1)S(1)}, u32[]{:S(2)}, u32[]{:S(2)}) collective-permute-start(bf16[8,192,256]{2,1,0:T(8,128)(2,1)S(1)} %mlp_first.1.own_act), channel_id=1, source_target_pairs={{0,1},{1,0},{2,3},{3,2},{4,5},{5,4},{6,7},{7,6},{8,9},{9,8},{10,11... | collective-permute-start | bytes 2359304 | tf_op jit(solution)/shard_map/ppermute | solution.py:38
  136.8 7.8 %copy-start.18 = (f32[1,2,1536]{2,1,0:T(2,128)S(1)}, f32[1,2,1536]{2,1,0:T(2,128)}, u32[]{:S(2)}) copy-start(f32[1,2,1536]{2,1,0:T(2,128)} %param.21) | copy-start | bytes 36868
  142.6 1.9 %collective-permute-start.20 = (f32[8,96,128]{2,1,0:T(8,128)}, f32[8,96,128]{2,1,0:T(8,128)S(1)}, u32[]{:S(2)}, u32[]{:S(2)}) collective-permute-start(f32[8,96,128]{2,1,0:T(8,128)} %get-tuple-element.25), channel_id=1, source_target_pairs={{0,1},{1,0},{2,3},{3,2},{4,5},{5,4},{6,7},{7,6},{8,9},{9,8},{10,11... | collective-permute-start | bytes 1179656 | tf_op jit(solution)/shard_map/ppermute | solution.py:38
  147.2 7.2 %collective-permute-start.21 = (bf16[1,2048]{1,0:T(2,128)(2,1)S(1)}, bf16[1,2048]{1,0:T(2,128)(2,1)S(1)}, u32[]{:S(2)}, u32[]{:S(2)}) collective-permute-start(bf16[1,2048]{1,0:T(2,128)(2,1)S(1)} %get-tuple-element.45), channel_id=1, source_target_pairs={{0,16},{16,32},{32,48},{48,64},{64,80},{80,96},{96,112},{112,128},... | collective-permute-start | bytes 12296 | tf_op jit(solution)/shard_map/ppermute | solution.py:316
  149.1 7.7 %collective-permute-start.22 = (bf16[1,2048]{1,0:T(2,128)(2,1)S(1)}, bf16[1,2048]{1,0:T(2,128)(2,1)S(1)}, u32[]{:S(2)}, u32[]{:S(2)}) collective-permute-start(bf16[1,2048]{1,0:T(2,128)(2,1)S(1)} %get-tuple-element.46), channel_id=1, source_target_pairs={{16,0},{32,16},{48,32},{64,48},{80,64},{96,80},{112,96},{128,112},... | collective-permute-start | bytes 12296 | tf_op jit(solution)/shard_map/ppermute | solution.py:317
  (18 other events, 53.2 us)

commit v6 on v5

--- a/solution.py
+++ b/solution.py
@@ -64,18 +64,13 @@
     )
 
 
-def ring_third(low, high):
-    far = jnp.concatenate([low, high], axis=0)
-    return far, swap(far, "img", 2)
-
-
 def place_of(chip, k):
     dx, dy = OFFSETS[k]
     column = jnp.bitwise_and(chip // 2 + dx + 4, 3)
     return 2 * column + jnp.bitwise_xor(jnp.bitwise_and(chip, 1), dy)
 
 
-def qkv_body(chip_ref, own_x, peer_x, *refs):
+def qkv_body(chip_ref, ready, own_x, peer_x, *refs):
     weights, (own_out, peer_out) = refs[:-2], refs[-2:]
     rows = own_x.shape[0]
     both = jnp.concatenate([own_x[...], peer_x[...]], axis=0)
@@ -90,19 +85,47 @@
         peer_out[place] = parts[k * cols : (k + 1) * cols, rows:]
 
 
-def project_qkv(chip, own_x, peer_x, weights):
+def project_qkv(chip, ready, own_x, peer_x, weights):
     cols, rows = weights[0].shape[0], own_x.shape[0]
     shape = jax.ShapeDtypeStruct((len(weights), cols, rows), BF16)
     flops = 4 * len(weights) * cols * rows * own_x.shape[1]
     return pl.pallas_call(
         qkv_body,
         out_shape=(shape, shape),
-        in_specs=[pl.BlockSpec(memory_space=pltpu.SMEM)] + vmem_specs(2 + len(weights)),
+        in_specs=[pl.BlockSpec(memory_space=pltpu.SMEM)] + vmem_specs(3 + len(weights)),
         out_specs=tuple(vmem_specs(2)),
         compiler_params=pltpu.CompilerParams(vmem_limit_bytes=32 << 20),
         cost_estimate=pl.CostEstimate(flops=1000, bytes_accessed=1000, transcendentals=0),
         name="project_qkv",
-    )(chip, own_x, peer_x, *weights)
+    )(chip, ready, own_x, peer_x, *weights)
+
+
+def heads_body(core_ref, mine, other, out):
+    count, cols, _ = mine.shape
+    step = 16
+    per_shard, per_head = cols // step, HEAD // step
+    section = HEADS * per_head
+    for source, parity in ((mine, core_ref[0]), (other, 1 - core_ref[0])):
+        for c in range(count):
+            for j in range(per_shard):
+                piece = (2 * c + parity) * per_shard + j
+                kind = (piece >= section).astype(jnp.int32) + (piece >= 2 * section).astype(jnp.int32)
+                rest = piece - kind * section
+                head = rest // per_head
+                start = pl.multiple_of(kind * HEAD + (rest - head * per_head) * step, step)
+                out[head, pl.ds(start, step), :] = source[c, j * step : (j + 1) * step]
+    out[HEADS:] = jnp.zeros((out.shape[0] - HEADS,) + out.shape[1:], BF16)
+
+
+def place_heads(core, mine, other, blocks):
+    return pl.pallas_call(
+        heads_body,
+        out_shape=jax.ShapeDtypeStruct((blocks, 3 * HEAD, mine.shape[2]), BF16),
+        in_specs=[pl.BlockSpec(memory_space=pltpu.SMEM)] + vmem_specs(2),
+        out_specs=vmem_specs(1)[0],
+        cost_estimate=pl.CostEstimate(flops=1000, bytes_accessed=1000, transcendentals=0),
+        name="place_heads",
+    )(core, mine, other)
 
 
 def mark_body(*refs):
@@ -128,38 +151,40 @@
     text_blocks = text.shape[1] // rows
     text_len = 154
     tile = 2 * rows
-    lane = lax.broadcasted_iota(jnp.int32, (8, rows), 1)
-    row = lax.broadcasted_iota(jnp.int32, (8, rows), 0)
+    lane = lax.broadcasted_iota(jnp.int32, (HEAD, rows), 1)
+    row = lax.broadcasted_iota(jnp.int32, (HEAD, rows), 0)
     top = row == 0
-    zeros = jnp.zeros((HEAD - 8, rows), F32)
-
-    def place_keys(index, key_part, limit):
+    zeros = jnp.zeros((HEAD, rows), F32)
+    ones = jnp.where(top, 1.0, 0.0).astype(F32)
+
+    def place(index, key_part, value_part, limit):
+        cols = slice(index * rows, (index + 1) * rows)
+        keys[:HEAD, cols] = key_part
         bias = jnp.where(jnp.logical_and(top, lane >= limit), masked_score, 0.0)
-        full = jnp.concatenate([key_part.astype(F32), bias, zeros], axis=0)
-        keys[pl.ds(index * rows, rows), :] = full.T.astype(BF16)
-
-    ones = jnp.concatenate([jnp.where(top, 1.0, 0.0).astype(F32), zeros], axis=0)
+        keys[HEAD:, cols] = bias.astype(BF16)
+        full = jnp.concatenate([value_part.astype(F32), zeros], axis=0)
+        values[cols, :] = full.T.astype(BF16)
+
     for b in range(blocks):
         part = parts[b]
-        place_keys(b, part[HEAD : 2 * HEAD], count_ref[0] - b * rows)
-        values[:, b * rows : (b + 1) * rows] = part[2 * HEAD :]
+        place(b, part[HEAD : 2 * HEAD], part[2 * HEAD :], count_ref[0] - b * rows)
         scaled = part[:HEAD].astype(F32) * 0.125
-        queries[:, b * rows : (b + 1) * rows] = jnp.concatenate([scaled, ones], axis=0).astype(BF16)
+        full = jnp.concatenate([scaled, ones], axis=0)
+        queries[b * rows : (b + 1) * rows, :] = full.T.astype(BF16)
     for t in range(text_blocks):
         cols = slice(t * rows, (t + 1) * rows)
-        place_keys(blocks + t, text[:HEAD, cols], text_len - t * rows)
-        values[:, (blocks + t) * rows : (blocks + t + 1) * rows] = text[HEAD:, cols]
+        place(blocks + t, text[:HEAD, cols], text[HEAD:, cols], text_len - t * rows)
 
     def step(t, carry):
         first = pl.multiple_of(t * tile, tile)
-        scores = jnp.dot(keys[...], queries[:, pl.ds(first, tile)], preferred_element_type=F32)
-        top_score = jnp.max(scores, axis=0, keepdims=True)
+        scores = jnp.dot(queries[pl.ds(first, tile), :], keys[...], preferred_element_type=F32)
+        top_score = jnp.max(scores, axis=1, keepdims=True)
         numer = jnp.exp(scores - top_score)
-        total = jnp.sum(numer, axis=0, keepdims=True)
-        mixed = jnp.dot(values[...], numer.astype(BF16), preferred_element_type=F32) / total
-        mixed = mixed.astype(BF16)
-        out[2 * t] = mixed[:, :rows]
-        out[2 * t + 1] = mixed[:, rows:]
+        total = jnp.sum(numer, axis=1, keepdims=True)
+        mixed = jnp.dot(numer.astype(BF16), values[...], preferred_element_type=F32) / total
+        turned = mixed.T[:HEAD].astype(BF16)
+        out[2 * t] = turned[:, :rows]
+        out[2 * t + 1] = turned[:, rows:]
         return carry
 
     lax.fori_loop(0, blocks // 2, step, 0)
@@ -175,9 +200,9 @@
         in_specs=[pl.BlockSpec(memory_space=pltpu.SMEM)] + vmem_specs(3),
         out_specs=vmem_specs(1)[0],
         scratch_shapes=[
+            pltpu.VMEM((2 * HEAD, keys), BF16),
             pltpu.VMEM((keys, 2 * HEAD), BF16),
-            pltpu.VMEM((HEAD, keys), BF16),
-            pltpu.VMEM((2 * HEAD, queries), BF16),
+            pltpu.VMEM((queries, 2 * HEAD), BF16),
         ],
         compiler_params=pltpu.CompilerParams(vmem_limit_bytes=40 << 20),
         cost_estimate=pl.CostEstimate(flops=1000, bytes_accessed=1000, transcendentals=0),
@@ -196,7 +221,7 @@
     return 0.5 * v * (1.0 + jnp.tanh(0.7978845608028654 * (v + 0.044715 * v * v * v)))
 
 
-def middle_body(mixed, hidden, mods, out_w, updated, mlp_in):
+def middle_body(mixed, hidden, mods, out_w, mark, updated, mlp_in):
     attended = mixed[...].astype(F32).T.astype(BF16)
     projected = jnp.dot(attended, out_w[...], preferred_element_type=F32)
     now = hidden[...].astype(F32) + mods[2:3] * projected
@@ -204,7 +229,7 @@
     mlp_in[...] = layer_norm(now, mods[3:4], mods[4:5])
 
 
-def middle(mixed, hidden, mods, out_w):
+def middle(mixed, hidden, mods, out_w, mark):
     rows, width = hidden.shape
     return pl.pallas_call(
         middle_body,
@@ -212,33 +237,45 @@
             jax.ShapeDtypeStruct((rows, width), F32),
             jax.ShapeDtypeStruct((rows, width), BF16),
         ),
-        in_specs=vmem_specs(4),
+        in_specs=vmem_specs(5),
         out_specs=tuple(vmem_specs(2)),
         compiler_params=pltpu.CompilerParams(vmem_limit_bytes=24 << 20),
         cost_estimate=pl.CostEstimate(flops=1000, bytes_accessed=1000, transcendentals=0),
         name="middle",
-    )(mixed, hidden, mods, out_w)
+    )(mixed, hidden, mods, out_w, mark)
 
 
 def first_body(chip_ref, own_x, peer_x, *refs):
     weights, out = refs[:-1], refs[-1]
     both = jnp.concatenate([own_x[...], peer_x[...]], axis=0)
     cols = out.shape[1]
-    stacked = jnp.concatenate([weight[:cols] for weight in weights], axis=0)
+    stacked = jnp.concatenate([weight[...] for weight in weights], axis=0)
     parts = lax.dot_general(stacked, both, (((1,), (1,)), ((), ())), preferred_element_type=F32)
     for k in range(len(weights)):
         out[place_of(chip_ref[0], k)] = gelu(parts[k * cols : (k + 1) * cols]).astype(BF16)
 
 
+def whole(x):
+    return pl.BlockSpec(x.shape, lambda i: (0,) * x.ndim)
+
+
+def half_of(x, cols, index):
+    position = index if x.shape[0] > cols else 0
+    return pl.BlockSpec((cols, x.shape[1]), lambda i: (position, 0))
+
+
 def mlp_first(chip, own_x, peer_x, weights, cols):
     rows = own_x.shape[0]
     count = len(weights)
+    shape = (count, cols, 2 * rows)
     return pl.pallas_call(
         first_body,
-        out_shape=jax.ShapeDtypeStruct((count, cols, 2 * rows), BF16),
-        in_specs=[pl.BlockSpec(memory_space=pltpu.SMEM)] + vmem_specs(2 + count),
-        out_specs=vmem_specs(1)[0],
-        compiler_params=pltpu.CompilerParams(vmem_limit_bytes=32 << 20),
+        out_shape=jax.ShapeDtypeStruct(shape, BF16),
+        grid=(1,),
+        in_specs=[pl.BlockSpec(memory_space=pltpu.SMEM), whole(own_x), whole(peer_x)]
+        + [half_of(x, cols, 0) for x in weights],
+        out_specs=pl.BlockSpec(shape, lambda i: (0, 0, 0)),
+        compiler_params=pltpu.CompilerParams(vmem_limit_bytes=40 << 20),
         cost_estimate=pl.CostEstimate(flops=1000, bytes_accessed=1000, transcendentals=0),
         name="mlp_first",
     )(chip, own_x, peer_x, *weights)
@@ -257,9 +294,9 @@
         act[other, mid:] = peer_act[c, :, :mid]
     width = weights[0].shape[1]
     half = cols // 2
-    low = jnp.concatenate([weight[cols : cols + half] for weight in weights], axis=0)
+    low = jnp.concatenate([weight[:half] for weight in weights], axis=0)
     parts = jnp.dot(low, act[:width], preferred_element_type=F32)
-    high = jnp.concatenate([weight[cols + half :] for weight in weights], axis=0)
+    high = jnp.concatenate([weight[half:] for weight in weights], axis=0)
     parts += jnp.dot(high, act[width:], preferred_element_type=F32)
     for k in range(count):
         place = place_of(chip_ref[0], k)
@@ -269,12 +306,15 @@
 
 def mlp_second(chip, core, own_act, peer_act, weights):
     count, cols, tokens = own_act.shape
-    shape = jax.ShapeDtypeStruct((count, cols // 2, tokens // 2), F32)
+    shape = (count, cols // 2, tokens // 2)
     return pl.pallas_call(
         second_body,
-        out_shape=(shape, shape),
-        in_specs=[pl.BlockSpec(memory_space=pltpu.SMEM)] * 2 + vmem_specs(2 + count),
-        out_specs=tuple(vmem_specs(2)),
+        out_shape=(jax.ShapeDtypeStruct(shape, F32), jax.ShapeDtypeStruct(shape, F32)),
+        grid=(1,),
+        in_specs=[pl.BlockSpec(memory_space=pltpu.SMEM)] * 2
+        + [whole(own_act), whole(peer_act)]
+        + [half_of(x, cols, 1) for x in weights],
+        out_specs=(pl.BlockSpec(shape, lambda i: (0, 0, 0)),) * 2,
         scratch_shapes=[pltpu.VMEM((2 * count * cols, tokens), BF16)],
         compiler_params=pltpu.CompilerParams(vmem_limit_bytes=40 << 20),
         cost_estimate=pl.CostEstimate(flops=1000, bytes_accessed=1000, transcendentals=0),
@@ -352,22 +392,22 @@
     mlp_mine, image_in = lax.optimization_barrier((mlp_mine, image_in))
     qkv_near = ring_first(qkv_t)
     qkv_next = ring_second(*qkv_near)
-    qkv_far = ring_third(*qkv_next[:2])
-    qkv_left, qkv_right, mlp_mine = lax.optimization_barrier((*qkv_next[2:], mlp_mine))
+    far = jnp.concatenate(qkv_next[:2], axis=0)
+    side_left, side_right, mlp_mine = lax.optimization_barrier((*qkv_next[2:], mlp_mine))
+    qkv_far = far, swap(far, "img", 2)
     qkv_pieces = [qkv_t, *qkv_near, qkv_far[0], *qkv_next[2:], qkv_far[1]]
     mlp_near = ring_first(mlp_mine)
 
     peer_in = swap(image_in, "img", 1)
-    mine, theirs = project_qkv(chip, image_in, peer_in, qkv_pieces)
+    ready, peer_in = lax.optimization_barrier((marker(qkv_far[1]), peer_in))
+    mine, theirs = project_qkv(chip, ready, image_in, peer_in, qkv_pieces)
     other = swap(theirs, "img", 1)
-    first = jnp.where(core[0] == 0, mine, other)
-    second = jnp.where(core[0] == 0, other, mine)
-    qkv = jnp.stack([first, second], axis=1).reshape(3, HEADS, HEAD, tok_rows)
-    heads = qkv.transpose(1, 0, 2, 3).reshape(HEADS, 3 * HEAD, tok_rows)
-    heads = jnp.pad(heads, ((0, blocks - HEADS), (0, 0), (0, 0)))
+    heads = place_heads(core, mine, other, blocks)
     parts = lax.all_to_all(heads, "blk", 0, 0, tiled=True)
 
     head = jnp.minimum(blk, HEADS - 1)
+    right, head = lax.optimization_barrier((mlp_near[1], head))
+    mlp_near = (mlp_near[0], right, mlp_near[2])
     text_in = modulate(text_hidden[0], text_mod[0, 0], text_mod[0, 1])
     text_cols = jnp.concatenate(
         [
@@ -382,18 +422,24 @@
     text_kv = jnp.pad(text_kv, ((0, 0), (0, -text_kv.shape[1] % tok_rows)))
 
     mlp_next = ring_second(*mlp_near)
-    mark = marker(text_kv, *mlp_near)
+    mark = marker(*mlp_near)
+    parts, low, high, mark, text_kv = lax.optimization_barrier(
+        (parts, mlp_next[0], mlp_next[1], mark, text_kv)
+    )
+    peer_low, peer_high = swap(low, "img", 2), swap(high, "img", 2)
     mixed = attend(counts, parts, text_kv, mark)
-    mixed, low, high = lax.optimization_barrier((mixed, mlp_next[0], mlp_next[1]))
-    mlp_far = ring_third(low, high)
     mixed = lax.all_to_all(mixed, "blk", 0, 0, tiled=True)[:HEADS].reshape(width_attn, tok_rows)
-    mlp_pieces = [mlp_mine, *mlp_near, mlp_far[0], *mlp_next[2:], mlp_far[1]]
-
-    updated, mlp_in = middle(mixed, hidden[0], mods, out_weight)
+    near_pieces, next_pieces = [mlp_mine, *mlp_near], list(mlp_next[2:])
+
+    updated, mlp_in = middle(mixed, hidden[0], mods, out_weight, marker(peer_low, peer_high, *next_pieces))
     mlp_cols = mlp_in_weight.shape[1]
-    act = mlp_first(chip, mlp_in, swap(mlp_in, "img", 1), mlp_pieces, mlp_cols)
+    peer_mlp = swap(mlp_in, "img", 1)
+    first_pieces = near_pieces + [low] + next_pieces + [peer_low]
+    act = mlp_first(chip, mlp_in, peer_mlp, first_pieces, mlp_cols)
     peer_act = swap(act, "img", 1)
-    own_part, sent_part = mlp_second(chip, core, act, peer_act, mlp_pieces)
+    own_part, sent_part = mlp_second(
+        chip, core, act, peer_act, near_pieces + [high] + next_pieces + [peer_high]
+    )
     peer_part = swap(sent_part, "img", 1)
     predicted = last(core, own_part, peer_part, updated, mods, final_mod[0], final_weight.T)
 

time: 161 us -> 159 us (0.988)
  the two profiles are of different devices: /device:TPU:104 before, /device:TPU:24 now
where the time goes in v6:
time: 159 us; the launch traced here: 158 us
  starting transfers between devices  54.2 us (34%)
  waiting for transfers between devices  40.7 us (26%)
  Pallas kernels  30 us (19%)
  local copies, waits for them, and re-layouts  23.7 us (15%)
  other arithmetic  6.07 us (4%)
  between operations  2.67 us (2%)
    ppermute x12, waiting for transfers between devices, ring(): return lax.ppermute(x, axis, [(i, (i + step) % size) for i in range(size)])  22.5 us
    ppermute x12, starting transfers between devices, ring(): return lax.ppermute(x, axis, [(i, (i + step) % size) for i in range(size)])  20 us
    unnamed x70, local copies, waits for them, and re-layouts  14 us
    pallas_call x1, Pallas kernels, attend(): pl.pallas_call(attend_body, out_shape=jax.ShapeDtypeStruct((blocks, HEAD,...  11.3 us
    ppermute x10, starting transfers between devices, swap(): lax.ppermute(x, axis, [(i, i ^ bits) for i in range(lax.axis_size(axis))])  10.3 us
    all_to_all x1, starting transfers between devices, per_device(): parts = lax.all_to_all(heads, 'blk', 0, 0, tiled=True)  9.94 us
    all_to_all x1, waiting for transfers between devices, per_device(): lax.all_to_all(mixed, 'blk', 0, 0, tiled=True)[:HEADS]  9.73 us
    all_to_all x1, starting transfers between devices, per_device(): lax.all_to_all(mixed, 'blk', 0, 0, tiled=True)[:HEADS]  8.13 us
  transfers between devices with their start and end apart: 26, of which 13 were waited for; matrix products, arithmetic and copies ran while one was open for 9% of the time, Pallas kernels for 12%

profile of v6, /device:TPU:24, one launch (start us, length us, event | category | flops | bytes accessed | tf_op | source)
XLA Modules:
  0.0 158.0 jit_solution(4500564059905742348)
XLA Ops:
  0.7 1.3 collective-permute-start.6
  2.0 1.5 collective-permute-start
  3.5 1.7 %collective-permute-start.2 = (bf16[144,1536]{1,0:T(8,128)(2,1)}, bf16[144,1536]{1,0:T(8,128)(2,1)S(1)}, u32[]{:S(2)}, u32[]{:S(2)}) collective-permute-start(bf16[144,1536]{1,0:T(8,128)(2,1)} %bitcast.80), channel_id=1, source_target_pairs={{0,12},{1,13},{2,14},{3,15},{4,0},{5,1},{6,2},{7,3},{8,4},{9,5},{1... | collective-permute-start | bytes 1327112 | tf_op jit(solution)/shard_map/ppermute | solution.py:50
  8.5 6.5 %collective-permute-done.refs_1_ = bf16[144,1536]{1,0:T(8,128)(2,1)S(1)} collective-permute-done((bf16[144,1536]{1,0:T(8,128)(2,1)}, bf16[144,1536]{1,0:T(8,128)(2,1)S(1)}, u32[]{:S(2)}, u32[]{:S(2)}) %collective-permute-start) | collective-permute-done | bytes 442400 | tf_op jit(solution)/shard_map/ppermute | solution.py:50
  16.3 3.0 %collective-permute-start.3 = (bf16[72,1536]{1,0:T(8,128)(2,1)S(1)}, bf16[72,1536]{1,0:T(8,128)(2,1)S(1)}, u32[]{:S(2)}, u32[]{:S(2)}) collective-permute-start(bf16[72,1536]{1,0:T(8,128)(2,1)S(1)} %slice.96), channel_id=1, source_target_pairs={{0,12},{1,13},{2,14},{3,15},{4,0},{5,1},{6,2},{7,3},{8,4},{9,5},{1... | collective-permute-start | bytes 663560 | tf_op jit(solution)/shard_map/ppermute | solution.py:50
  19.3 3.2 %collective-permute-start.8 = (bf16[144,1536]{1,0:T(8,128)(2,1)S(1)}, bf16[144,1536]{1,0:T(8,128)(2,1)S(1)}, u32[]{:S(2)}, u32[]{:S(2)}) collective-permute-start(bf16[144,1536]{1,0:T(8,128)(2,1)S(1)} %collective-permute-done.6.refs_3_), channel_id=1, source_target_pairs={{0,12},{1,13},{2,14},{3,15},{4,0},{5,1},{6,2},{7,3},{8,4},{9,5},{1... | collective-permute-start | bytes 1327112 | tf_op jit(solution)/shard_map/ppermute | solution.py:50
  25.1 2.4 %collective-permute-start.4 = (bf16[144,1536]{1,0:T(8,128)(2,1)S(1)}, bf16[144,1536]{1,0:T(8,128)(2,1)}, u32[]{:S(2)}, u32[]{:S(2)}) collective-permute-start(bf16[144,1536]{1,0:T(8,128)(2,1)S(1)} %constant_dynamic-update-slice_fusion.refs_4_), channel_id=1, source_target_pairs={{0,2},{1,3},{2,0},{3,1},{4,6},{5,7},{6,4},{7,5},{8,10},{9,11},{10,... | collective-permute-start | bytes 1327112 | tf_op jit(solution)/shard_map/ppermute | solution.py:38
  30.0 2.8 %collective-permute-done.7.refs_5_ = bf16[144,1536]{1,0:T(8,128)(2,1)S(1)} collective-permute-done((bf16[144,1536]{1,0:T(8,128)(2,1)S(1)}, bf16[144,1536]{1,0:T(8,128)(2,1)S(1)}, u32[]{:S(2)}, u32[]{:S(2)}) %collective-permute-start.7) | collective-permute-done | bytes 442400 | tf_op jit(solution)/shard_map/ppermute | solution.py:50
  34.8 3.7 %collective-permute-start.12 = (bf16[384,1536]{1,0:T(8,128)(2,1)S(1)}, bf16[384,1536]{1,0:T(8,128)(2,1)S(1)}, u32[]{:S(2)}, u32[]{:S(2)}) collective-permute-start(bf16[384,1536]{1,0:T(8,128)(2,1)S(1)} %pad_maximum_fusion.refs_0_), channel_id=1, source_target_pairs={{0,12},{1,13},{2,14},{3,15},{4,0},{5,1},{6,2},{7,3},{8,4},{9,5},{1... | collective-permute-start | bytes 3538952 | tf_op jit(solution)/shard_map/ppermute | solution.py:50
  38.5 2.3 %collective-permute-start.14 = (bf16[384,1536]{1,0:T(8,128)(2,1)S(1)}, bf16[384,1536]{1,0:T(8,128)(2,1)}, u32[]{:S(2)}, u32[]{:S(2)}) collective-permute-start(bf16[384,1536]{1,0:T(8,128)(2,1)S(1)} %pad_maximum_fusion.refs_0_), channel_id=1, source_target_pairs={{0,2},{1,3},{2,0},{3,1},{4,6},{5,7},{6,4},{7,5},{8,10},{9,11},{10,... | collective-permute-start | bytes 3538952 | tf_op jit(solution)/shard_map/ppermute | solution.py:38
  48.9 2.3 %project_qkv.1 = (bf16[8,144,128]{2,1,0:T(8,128)(2,1)S(1)}, bf16[8,144,128]{2,1,0:T(8,128)(2,1)S(1)}) custom-call(s32[1]{0:T(128)} %bitcast.2.chip_ref, bf16[16,128]{1,0:T(8,128)(2,1)S(1)} %copy-done.24, bf16[128,1536]{1,0:T(8,128)(2,1)S(1)} %fusion.12.own_x, bf16[128,1536]{1,0:T(8,128)(2,1)} %collective-permute-done.5.peer_x, ...), custom_call_target="tpu_custom_call" | custom-call | flops 1000 | bytes 1000 | tf_op jit(solution)/shard_map/project_qkv/pallas_call | solution.py:92
  51.9 1.5 collective-permute-done.9.other
  54.2 3.3 %place_heads.1 = bf16[16,192,128]{2,1,0:T(8,128)(2,1)} custom-call(s32[1]{0:T(128)} %bitcast.1.core_ref, bf16[8,144,128]{2,1,0:T(8,128)(2,1)} %copy-done.19, bf16[8,144,128]{2,1,0:T(8,128)(2,1)} %copy-done.27), custom_call_target="tpu_custom_call" | custom-call | flops 1000 | bytes 1000 | tf_op jit(solution)/shard_map/place_heads/pallas_call | solution.py:121
  57.5 9.9 %all-to-all-start = ((bf16[16,192,128]{2,1,0:T(8,128)(2,1)}), bf16[16,192,128]{2,1,0:T(8,128)(2,1)S(1)}, u32[]{:S(2)}, u32[]{:S(2)}) async-start(bf16[16,192,128]{2,1,0:T(8,128)(2,1)} %place_heads.1), calls=%async_computation | async-start | bytes 1572864 | tf_op jit(solution)/shard_map/all_to_all | solution.py:406
  68.5 3.2 %collective-permute-start.13 = (bf16[192,1536]{1,0:T(8,128)(2,1)}, bf16[192,1536]{1,0:T(8,128)(2,1)}, u32[]{:S(2)}, u32[]{:S(2)}) collective-permute-start(bf16[192,1536]{1,0:T(8,128)(2,1)} %slice.81), channel_id=1, source_target_pairs={{0,12},{1,13},{2,14},{3,15},{4,0},{5,1},{6,2},{7,3},{8,4},{9,5},{1... | collective-permute-start | bytes 1769480 | tf_op jit(solution)/shard_map/ppermute | solution.py:50
  71.7 1.9 %slice.97 = bf16[192,1536]{1,0:T(8,128)(2,1)} slice(bf16[384,1536]{1,0:T(8,128)(2,1)} %collective-permute-done.10.refs_0_.refs_1_), slice={[0:192], [0:1536]} | slice | bytes 1179648 | tf_op jit(solution)/shard_map/slice | solution.py:60
  73.7 3.3 %collective-permute-start.18 = (bf16[384,1536]{1,0:T(8,128)(2,1)}, bf16[384,1536]{1,0:T(8,128)(2,1)}, u32[]{:S(2)}, u32[]{:S(2)}) collective-permute-start(bf16[384,1536]{1,0:T(8,128)(2,1)} %collective-permute-done.14.refs_2_.refs_3_), channel_id=1, source_target_pairs={{0,12},{1,13},{2,14},{3,15},{4,0},{5,1},{6,2},{7,3},{8,4},{9,5},{1... | collective-permute-start | bytes 3538952 | tf_op jit(solution)/shard_map/ppermute | solution.py:50
  78.2 1.5 constant_dynamic-slice_fusion.1
  80.4 5.4 %collective-permute-done.13.refs_4_ = bf16[192,1536]{1,0:T(8,128)(2,1)} collective-permute-done((bf16[192,1536]{1,0:T(8,128)(2,1)}, bf16[192,1536]{1,0:T(8,128)(2,1)}, u32[]{:S(2)}, u32[]{:S(2)}) %collective-permute-start.13) | collective-permute-done | bytes 589856 | tf_op jit(solution)/shard_map/ppermute | solution.py:50
  85.8 5.6 %collective-permute-done.11.refs_4_ = bf16[192,1536]{1,0:T(8,128)(2,1)} collective-permute-done((bf16[192,1536]{1,0:T(8,128)(2,1)}, bf16[192,1536]{1,0:T(8,128)(2,1)}, u32[]{:S(2)}, u32[]{:S(2)}) %collective-permute-start.11) | collective-permute-done | bytes 589856 | tf_op jit(solution)/shard_map/ppermute | solution.py:50
  92.7 2.3 %collective-permute-start.16 = (bf16[192,1536]{1,0:T(8,128)(2,1)}, bf16[192,1536]{1,0:T(8,128)(2,1)S(1)}, u32[]{:S(2)}, u32[]{:S(2)}) collective-permute-start(bf16[192,1536]{1,0:T(8,128)(2,1)} %collective-permute-done.13.refs_4_), channel_id=1, source_target_pairs={{0,2},{1,3},{2,0},{3,1},{4,6},{5,7},{6,4},{7,5},{8,10},{9,11},{10,... | collective-permute-start | bytes 1769480 | tf_op jit(solution)/shard_map/ppermute | solution.py:38
  95.6 11.3 %attend.1 = bf16[16,64,128]{2,1,0:T(8,128)(2,1)} custom-call(s32[1]{0:T(128)} %copy.45.count_ref, bf16[16,192,128]{2,1,0:T(8,128)(2,1)S(1)} %all-to-all-done.parts, bf16[128,256]{1,0:T(8,128)(2,1)S(1)} %pad.8.text, bf16[16,128]{1,0:T(8,128)(2,1)S(1)} %copy-done.22), custom_call_target="tpu_custom_call" | custom-call | flops 1000 | bytes 1000 | tf_op jit(solution)/shard_map/attend/pallas_call | solution.py:197
  106.9 8.1 %all-to-all-start.1 = ((bf16[16,64,128]{2,1,0:T(8,128)(2,1)}), bf16[16,64,128]{2,1,0:T(8,128)(2,1)S(1)}, u32[]{:S(2)}, u32[]{:S(2)}) async-start(bf16[16,64,128]{2,1,0:T(8,128)(2,1)} %attend.1), calls=%async_computation.1 | async-start | bytes 524288 | tf_op jit(solution)/shard_map/all_to_all | solution.py:431
  115.1 9.7 %all-to-all-done.1 = bf16[16,64,128]{2,1,0:T(8,128)(2,1)S(1)} async-done(((bf16[16,64,128]{2,1,0:T(8,128)(2,1)}), bf16[16,64,128]{2,1,0:T(8,128)(2,1)S(1)}, u32[]{:S(2)}, u32[]{:S(2)}) %all-to-all-start.1) | async-done | bytes 262176 | tf_op jit(solution)/shard_map/all_to_all | solution.py:431
  127.1 1.7 %copy-done.5 = bf16[768,1536]{1,0:T(8,128)(2,1)S(1)} copy-done((bf16[768,1536]{1,0:T(8,128)(2,1)S(1)}, bf16[768,1536]{1,0:T(8,128)(2,1)}, u32[]{:S(2)}) %copy-start.5) | copy-done | bytes 2359320
  130.3 1.7 %collective-permute-done.19.peer_x = bf16[128,1536]{1,0:T(8,128)(2,1)S(1)} collective-permute-done((bf16[128,1536]{1,0:T(8,128)(2,1)S(1)}, bf16[128,1536]{1,0:T(8,128)(2,1)S(1)}, u32[]{:S(2)}, u32[]{:S(2)}) %collective-permute-start.19) | collective-permute-done | bytes 393248 | tf_op jit(solution)/shard_map/ppermute | solution.py:38
  132.1 3.6 %mlp_first.1.own_act = bf16[8,192,256]{2,1,0:T(8,128)(2,1)S(1)} custom-call(s32[1]{0:T(128)} %bitcast.2.chip_ref, bf16[128,1536]{1,0:T(8,128)(2,1)S(1)} %get-tuple-element.35.own_x, bf16[128,1536]{1,0:T(8,128)(2,1)S(1)} %collective-permute-done.19.peer_x, bf16[384,1536]{1,0:T(8,128)(2,1)S(1)} %pad_maximum_fusion.refs_0_, ...), custom_call_target="tpu_custom_call" | custom-call | flops 1000 | bytes 1000 | tf_op jit(solution)/shard_map/mlp_first/pallas_call | solution.py:271
  136.1 2.2 %collective-permute-done.20.peer_act = bf16[8,192,256]{2,1,0:T(8,128)(2,1)S(1)} collective-permute-done((bf16[8,192,256]{2,1,0:T(8,128)(2,1)S(1)}, bf16[8,192,256]{2,1,0:T(8,128)(2,1)S(1)}, u32[]{:S(2)}, u32[]{:S(2)}) %collective-permute-start.20) | collective-permute-done | bytes 786464 | tf_op jit(solution)/shard_map/ppermute | solution.py:38
  138.3 4.1 %mlp_second.1 = (f32[8,96,128]{2,1,0:T(8,128)S(1)}, f32[8,96,128]{2,1,0:T(8,128)}) custom-call(s32[1]{0:T(128)} %bitcast.2.chip_ref, s32[1]{0:T(128)} %bitcast.1.core_ref, bf16[8,192,256]{2,1,0:T(8,128)(2,1)S(1)} %mlp_first.1.own_act, bf16[8,192,256]{2,1,0:T(8,128)(2,1)S(1)} %collective-permute-done.20.peer_act, ...), custom_call_target="tpu_custom_call" | custom-call | flops 1000 | bytes 1000 | tf_op jit(solution)/shard_map/mlp_second/pallas_call | solution.py:310
  145.9 3.0 %collective-permute-start.22 = (bf16[1,2048]{1,0:T(2,128)(2,1)S(1)}, bf16[1,2048]{1,0:T(2,128)(2,1)S(1)}, u32[]{:S(2)}, u32[]{:S(2)}) collective-permute-start(bf16[1,2048]{1,0:T(2,128)(2,1)S(1)} %get-tuple-element.55), channel_id=1, source_target_pairs={{0,16},{16,32},{32,48},{48,64},{64,80},{80,96},{96,112},{112,128},... | collective-permute-start | bytes 12296 | tf_op jit(solution)/shard_map/ppermute | solution.py:356
  149.0 2.8 %collective-permute-start.23 = (bf16[1,2048]{1,0:T(2,128)(2,1)S(1)}, bf16[1,2048]{1,0:T(2,128)(2,1)S(1)}, u32[]{:S(2)}, u32[]{:S(2)}) collective-permute-start(bf16[1,2048]{1,0:T(2,128)(2,1)S(1)} %get-tuple-element.56), channel_id=1, source_target_pairs={{16,0},{32,16},{48,32},{64,48},{80,64},{96,80},{112,96},{128,112},... | collective-permute-start | bytes 12296 | tf_op jit(solution)/shard_map/ppermute | solution.py:357
  153.2 2.2 %collective-permute-done.23 = bf16[1,2048]{1,0:T(2,128)(2,1)S(1)} collective-permute-done((bf16[1,2048]{1,0:T(2,128)(2,1)S(1)}, bf16[1,2048]{1,0:T(2,128)(2,1)S(1)}, u32[]{:S(2)}, u32[]{:S(2)}) %collective-permute-start.23) | collective-permute-done | bytes 4128 | tf_op jit(solution)/shard_map/ppermute | solution.py:357
  (148 shorter events, 36.1 us)
Async XLA Ops:
  0.6 156.1 %copy-start = (bf16[144,512]{1,0:T(8,128)(2,1)S(1)}, bf16[144,512]{1,0:T(8,128)(2,1)}, u32[]{:S(2)}) copy-start(bf16[144,512]{1,0:T(8,128)(2,1)} %param.30) | copy-start | bytes 442372
  0.7 18.6 %collective-permute-start.6 = (bf16[144,1536]{1,0:T(8,128)(2,1)}, bf16[144,1536]{1,0:T(8,128)(2,1)S(1)}, u32[]{:S(2)}, u32[]{:S(2)}) collective-permute-start(bf16[144,1536]{1,0:T(8,128)(2,1)} %bitcast.78), channel_id=1, source_target_pairs={{0,2},{1,3},{2,0},{3,1},{4,6},{5,7},{6,4},{7,5},{8,10},{9,11},{10,... | collective-permute-start | bytes 1327112 | tf_op jit(solution)/shard_map/ppermute | solution.py:38
  2.0 13.0 %collective-permute-start = (bf16[144,1536]{1,0:T(8,128)(2,1)}, bf16[144,1536]{1,0:T(8,128)(2,1)S(1)}, u32[]{:S(2)}, u32[]{:S(2)}) collective-permute-start(bf16[144,1536]{1,0:T(8,128)(2,1)} %bitcast.79), channel_id=1, source_target_pairs={{0,4},{1,5},{2,6},{3,7},{4,8},{5,9},{6,10},{7,11},{8,12},{9,13},{1... | collective-permute-start | bytes 1327112 | tf_op jit(solution)/shard_map/ppermute | solution.py:50
  3.5 12.7 %collective-permute-start.2 = (bf16[144,1536]{1,0:T(8,128)(2,1)}, bf16[144,1536]{1,0:T(8,128)(2,1)S(1)}, u32[]{:S(2)}, u32[]{:S(2)}) collective-permute-start(bf16[144,1536]{1,0:T(8,128)(2,1)} %bitcast.80), channel_id=1, source_target_pairs={{0,12},{1,13},{2,14},{3,15},{4,0},{5,1},{6,2},{7,3},{8,4},{9,5},{1... | collective-permute-start | bytes 1327112 | tf_op jit(solution)/shard_map/ppermute | solution.py:50
  15.7 7.5 %collective-permute-start.1 = (bf16[72,1536]{1,0:T(8,128)(2,1)}, bf16[72,1536]{1,0:T(8,128)(2,1)}, u32[]{:S(2)}, u32[]{:S(2)}) collective-permute-start(bf16[72,1536]{1,0:T(8,128)(2,1)} %slice.95), channel_id=1, source_target_pairs={{0,4},{1,5},{2,6},{3,7},{4,8},{5,9},{6,10},{7,11},{8,12},{9,13},{1... | collective-permute-start | bytes 663560 | tf_op jit(solution)/shard_map/ppermute | solution.py:50
  16.1 26.0 %collective-permute-start.5 = (bf16[128,1536]{1,0:T(8,128)(2,1)S(1)}, bf16[128,1536]{1,0:T(8,128)(2,1)}, u32[]{:S(2)}, u32[]{:S(2)}) collective-permute-start(bf16[128,1536]{1,0:T(8,128)(2,1)S(1)} %fusion.12.own_x), channel_id=1, source_target_pairs={{0,1},{1,0},{2,3},{3,2},{4,5},{5,4},{6,7},{7,6},{8,9},{9,8},{10,11... | collective-permute-start | bytes 1179656 | tf_op jit(solution)/shard_map/ppermute | solution.py:38
  16.2 16.5 %copy-start.6 = (bf16[144,1536]{1,0:T(8,128)(2,1)}, bf16[144,1536]{1,0:T(8,128)(2,1)S(1)}, u32[]{:S(2)}) copy-start(bf16[144,1536]{1,0:T(8,128)(2,1)S(1)} %collective-permute-done.2.refs_2_) | copy-start | bytes 1327108
  16.3 8.8 %collective-permute-start.3 = (bf16[72,1536]{1,0:T(8,128)(2,1)S(1)}, bf16[72,1536]{1,0:T(8,128)(2,1)S(1)}, u32[]{:S(2)}, u32[]{:S(2)}) collective-permute-start(bf16[72,1536]{1,0:T(8,128)(2,1)S(1)} %slice.96), channel_id=1, source_target_pairs={{0,12},{1,13},{2,14},{3,15},{4,0},{5,1},{6,2},{7,3},{8,4},{9,5},{1... | collective-permute-start | bytes 663560 | tf_op jit(solution)/shard_map/ppermute | solution.py:50
  19.3 13.5 %copy-start.13 = (bf16[144,1536]{1,0:T(8,128)(2,1)}, bf16[144,1536]{1,0:T(8,128)(2,1)S(1)}, u32[]{:S(2)}) copy-start(bf16[144,1536]{1,0:T(8,128)(2,1)S(1)} %collective-permute-done.6.refs_3_) | copy-start | bytes 1327108
  19.3 13.5 %collective-permute-start.7 = (bf16[144,1536]{1,0:T(8,128)(2,1)S(1)}, bf16[144,1536]{1,0:T(8,128)(2,1)S(1)}, u32[]{:S(2)}, u32[]{:S(2)}) collective-permute-start(bf16[144,1536]{1,0:T(8,128)(2,1)S(1)} %collective-permute-done.6.refs_3_), channel_id=1, source_target_pairs={{0,4},{1,5},{2,6},{3,7},{4,8},{5,9},{6,10},{7,11},{8,12},{9,13},{1... | collective-permute-start | bytes 1327112 | tf_op jit(solution)/shard_map/ppermute | solution.py:50
  19.3 14.8 %collective-permute-start.8 = (bf16[144,1536]{1,0:T(8,128)(2,1)S(1)}, bf16[144,1536]{1,0:T(8,128)(2,1)S(1)}, u32[]{:S(2)}, u32[]{:S(2)}) collective-permute-start(bf16[144,1536]{1,0:T(8,128)(2,1)S(1)} %collective-permute-done.6.refs_3_), channel_id=1, source_target_pairs={{0,12},{1,13},{2,14},{3,15},{4,0},{5,1},{6,2},{7,3},{8,4},{9,5},{1... | collective-permute-start | bytes 1327112 | tf_op jit(solution)/shard_map/ppermute | solution.py:50
  25.1 13.5 %copy-start.8 = (bf16[144,1536]{1,0:T(8,128)(2,1)}, bf16[144,1536]{1,0:T(8,128)(2,1)S(1)}, u32[]{:S(2)}) copy-start(bf16[144,1536]{1,0:T(8,128)(2,1)S(1)} %constant_dynamic-update-slice_fusion.refs_4_) | copy-start | bytes 1327108
  25.1 15.8 %collective-permute-start.4 = (bf16[144,1536]{1,0:T(8,128)(2,1)S(1)}, bf16[144,1536]{1,0:T(8,128)(2,1)}, u32[]{:S(2)}, u32[]{:S(2)}) collective-permute-start(bf16[144,1536]{1,0:T(8,128)(2,1)S(1)} %constant_dynamic-update-slice_fusion.refs_4_), channel_id=1, source_target_pairs={{0,2},{1,3},{2,0},{3,1},{4,6},{5,7},{6,4},{7,5},{8,10},{9,11},{10,... | collective-permute-start | bytes 1327112 | tf_op jit(solution)/shard_map/ppermute | solution.py:38
  34.8 32.6 %collective-permute-start.12 = (bf16[384,1536]{1,0:T(8,128)(2,1)S(1)}, bf16[384,1536]{1,0:T(8,128)(2,1)S(1)}, u32[]{:S(2)}, u32[]{:S(2)}) collective-permute-start(bf16[384,1536]{1,0:T(8,128)(2,1)S(1)} %pad_maximum_fusion.refs_0_), channel_id=1, source_target_pairs={{0,12},{1,13},{2,14},{3,15},{4,0},{5,1},{6,2},{7,3},{8,4},{9,5},{1... | collective-permute-start | bytes 3538952 | tf_op jit(solution)/shard_map/ppermute | solution.py:50
  38.5 35.1 %collective-permute-start.14 = (bf16[384,1536]{1,0:T(8,128)(2,1)S(1)}, bf16[384,1536]{1,0:T(8,128)(2,1)}, u32[]{:S(2)}, u32[]{:S(2)}) collective-permute-start(bf16[384,1536]{1,0:T(8,128)(2,1)S(1)} %pad_maximum_fusion.refs_0_), channel_id=1, source_target_pairs={{0,2},{1,3},{2,0},{3,1},{4,6},{5,7},{6,4},{7,5},{8,10},{9,11},{10,... | collective-permute-start | bytes 3538952 | tf_op jit(solution)/shard_map/ppermute | solution.py:38
  40.8 30.9 %collective-permute-start.10 = (bf16[384,1536]{1,0:T(8,128)(2,1)S(1)}, bf16[384,1536]{1,0:T(8,128)(2,1)}, u32[]{:S(2)}, u32[]{:S(2)}) collective-permute-start(bf16[384,1536]{1,0:T(8,128)(2,1)S(1)} %pad_maximum_fusion.refs_0_), channel_id=1, source_target_pairs={{0,4},{1,5},{2,6},{3,7},{4,8},{5,9},{6,10},{7,11},{8,12},{9,13},{1... | collective-permute-start | bytes 3538952 | tf_op jit(solution)/shard_map/ppermute | solution.py:50
  51.9 1.6 %collective-permute-start.9 = (bf16[8,144,128]{2,1,0:T(8,128)(2,1)S(1)}, bf16[8,144,128]{2,1,0:T(8,128)(2,1)S(1)}, u32[]{:S(2)}, u32[]{:S(2)}) collective-permute-start(bf16[8,144,128]{2,1,0:T(8,128)(2,1)S(1)} %get-tuple-element.25), channel_id=1, source_target_pairs={{0,1},{1,0},{2,3},{3,2},{4,5},{5,4},{6,7},{7,6},{8,9},{9,8},{10,11... | collective-permute-start | bytes 884744 | tf_op jit(solution)/shard_map/ppermute | solution.py:38
  57.5 33.9 %all-to-all-start = ((bf16[16,192,128]{2,1,0:T(8,128)(2,1)}), bf16[16,192,128]{2,1,0:T(8,128)(2,1)S(1)}, u32[]{:S(2)}, u32[]{:S(2)}) async-start(bf16[16,192,128]{2,1,0:T(8,128)(2,1)} %place_heads.1), calls=%async_computation | async-start | bytes 1572864 | tf_op jit(solution)/shard_map/all_to_all | solution.py:406
  68.5 17.3 %collective-permute-start.13 = (bf16[192,1536]{1,0:T(8,128)(2,1)}, bf16[192,1536]{1,0:T(8,128)(2,1)}, u32[]{:S(2)}, u32[]{:S(2)}) collective-permute-start(bf16[192,1536]{1,0:T(8,128)(2,1)} %slice.81), channel_id=1, source_target_pairs={{0,12},{1,13},{2,14},{3,15},{4,0},{5,1},{6,2},{7,3},{8,4},{9,5},{1... | collective-permute-start | bytes 1769480 | tf_op jit(solution)/shard_map/ppermute | solution.py:50
  73.7 17.8 %collective-permute-start.11 = (bf16[192,1536]{1,0:T(8,128)(2,1)}, bf16[192,1536]{1,0:T(8,128)(2,1)}, u32[]{:S(2)}, u32[]{:S(2)}) collective-permute-start(bf16[192,1536]{1,0:T(8,128)(2,1)} %slice.97), channel_id=1, source_target_pairs={{0,4},{1,5},{2,6},{3,7},{4,8},{5,9},{6,10},{7,11},{8,12},{9,13},{1... | collective-permute-start | bytes 1769480 | tf_op jit(solution)/shard_map/ppermute | solution.py:50
  73.7 51.2 %collective-permute-start.17 = (bf16[384,1536]{1,0:T(8,128)(2,1)}, bf16[384,1536]{1,0:T(8,128)(2,1)}, u32[]{:S(2)}, u32[]{:S(2)}) collective-permute-start(bf16[384,1536]{1,0:T(8,128)(2,1)} %collective-permute-done.14.refs_2_.refs_3_), channel_id=1, source_target_pairs={{0,4},{1,5},{2,6},{3,7},{4,8},{5,9},{6,10},{7,11},{8,12},{9,13},{1... | collective-permute-start | bytes 3538952 | tf_op jit(solution)/shard_map/ppermute | solution.py:50
  73.7 51.2 %collective-permute-start.18 = (bf16[384,1536]{1,0:T(8,128)(2,1)}, bf16[384,1536]{1,0:T(8,128)(2,1)}, u32[]{:S(2)}, u32[]{:S(2)}) collective-permute-start(bf16[384,1536]{1,0:T(8,128)(2,1)} %collective-permute-done.14.refs_2_.refs_3_), channel_id=1, source_target_pairs={{0,12},{1,13},{2,14},{3,15},{4,0},{5,1},{6,2},{7,3},{8,4},{9,5},{1... | collective-permute-start | bytes 3538952 | tf_op jit(solution)/shard_map/ppermute | solution.py:50
  79.7 15.9 %copy-start.22 = (bf16[16,128]{1,0:T(8,128)(2,1)S(1)}, bf16[16,128]{1,0:T(8,128)(2,1)}, u32[]{:S(2)}) copy-start(bf16[16,128]{1,0:T(8,128)(2,1)} %marker.4.mark) | copy-start | bytes 12292
  80.2 34.8 %copy-start.29 = (f32[1,6,1536]{2,0,1:T(1,128)S(1)}, f32[1,6,1536]{2,0,1:T(1,128)}, u32[]{:S(2)}) copy-start(f32[1,6,1536]{2,0,1:T(1,128)} %param.19) | copy-start | bytes 110596
  91.5 33.4 %collective-permute-start.15 = (bf16[192,1536]{1,0:T(8,128)(2,1)}, bf16[192,1536]{1,0:T(8,128)(2,1)}, u32[]{:S(2)}, u32[]{:S(2)}) collective-permute-start(bf16[192,1536]{1,0:T(8,128)(2,1)} %collective-permute-done.11.refs_4_), channel_id=1, source_target_pairs={{0,2},{1,3},{2,0},{3,1},{4,6},{5,7},{6,4},{7,5},{8,10},{9,11},{10,... | collective-permute-start | bytes 1769480 | tf_op jit(solution)/shard_map/ppermute | solution.py:38
  92.7 32.2 %collective-permute-start.16 = (bf16[192,1536]{1,0:T(8,128)(2,1)}, bf16[192,1536]{1,0:T(8,128)(2,1)S(1)}, u32[]{:S(2)}, u32[]{:S(2)}) collective-permute-start(bf16[192,1536]{1,0:T(8,128)(2,1)} %collective-permute-done.13.refs_4_), channel_id=1, source_target_pairs={{0,2},{1,3},{2,0},{3,1},{4,6},{5,7},{6,4},{7,5},{8,10},{9,11},{10,... | collective-permute-start | bytes 1769480 | tf_op jit(solution)/shard_map/ppermute | solution.py:38
  106.9 17.9 %all-to-all-start.1 = ((bf16[16,64,128]{2,1,0:T(8,128)(2,1)}), bf16[16,64,128]{2,1,0:T(8,128)(2,1)S(1)}, u32[]{:S(2)}, u32[]{:S(2)}) async-start(bf16[16,64,128]{2,1,0:T(8,128)(2,1)} %attend.1), calls=%async_computation.1 | async-start | bytes 524288 | tf_op jit(solution)/shard_map/all_to_all | solution.py:431
  130.2 1.8 %collective-permute-start.19 = (bf16[128,1536]{1,0:T(8,128)(2,1)S(1)}, bf16[128,1536]{1,0:T(8,128)(2,1)S(1)}, u32[]{:S(2)}, u32[]{:S(2)}) collective-permute-start(bf16[128,1536]{1,0:T(8,128)(2,1)S(1)} %get-tuple-element.35.own_x), channel_id=1, source_target_pairs={{0,1},{1,0},{2,3},{3,2},{4,5},{5,4},{6,7},{7,6},{8,9},{9,8},{10,11... | collective-permute-start | bytes 1179656 | tf_op jit(solution)/shard_map/ppermute | solution.py:38
  135.7 2.6 %collective-permute-start.20 = (bf16[8,192,256]{2,1,0:T(8,128)(2,1)S(1)}, bf16[8,192,256]{2,1,0:T(8,128)(2,1)S(1)}, u32[]{:S(2)}, u32[]{:S(2)}) collective-permute-start(bf16[8,192,256]{2,1,0:T(8,128)(2,1)S(1)} %mlp_first.1.own_act), channel_id=1, source_target_pairs={{0,1},{1,0},{2,3},{3,2},{4,5},{5,4},{6,7},{7,6},{8,9},{9,8},{10,11... | collective-permute-start | bytes 2359304 | tf_op jit(solution)/shard_map/ppermute | solution.py:38
  142.4 1.9 %collective-permute-start.21 = (f32[8,96,128]{2,1,0:T(8,128)}, f32[8,96,128]{2,1,0:T(8,128)S(1)}, u32[]{:S(2)}, u32[]{:S(2)}) collective-permute-start(f32[8,96,128]{2,1,0:T(8,128)} %get-tuple-element.37), channel_id=1, source_target_pairs={{0,1},{1,0},{2,3},{3,2},{4,5},{5,4},{6,7},{7,6},{8,9},{9,8},{10,11... | collective-permute-start | bytes 1179656 | tf_op jit(solution)/shard_map/ppermute | solution.py:38
  145.9 7.2 %collective-permute-start.22 = (bf16[1,2048]{1,0:T(2,128)(2,1)S(1)}, bf16[1,2048]{1,0:T(2,128)(2,1)S(1)}, u32[]{:S(2)}, u32[]{:S(2)}) collective-permute-start(bf16[1,2048]{1,0:T(2,128)(2,1)S(1)} %get-tuple-element.55), channel_id=1, source_target_pairs={{0,16},{16,32},{32,48},{48,64},{64,80},{80,96},{96,112},{112,128},... | collective-permute-start | bytes 12296 | tf_op jit(solution)/shard_map/ppermute | solution.py:356
  149.0 6.4 %collective-permute-start.23 = (bf16[1,2048]{1,0:T(2,128)(2,1)S(1)}, bf16[1,2048]{1,0:T(2,128)(2,1)S(1)}, u32[]{:S(2)}, u32[]{:S(2)}) collective-permute-start(bf16[1,2048]{1,0:T(2,128)(2,1)S(1)} %get-tuple-element.56), channel_id=1, source_target_pairs={{16,0},{32,16},{48,32},{64,48},{80,64},{96,80},{112,96},{128,112},... | collective-permute-start | bytes 12296 | tf_op jit(solution)/shard_map/ppermute | solution.py:357
  (28 other events, 86.4 us)

commit v7 on v6

--- a/solution.py
+++ b/solution.py
@@ -40,6 +40,10 @@
 
 def vmem_specs(count):
     return [pl.BlockSpec(memory_space=pltpu.VMEM)] * count
+
+
+def whole(x):
+    return pl.BlockSpec(x.shape, lambda i: (0,) * x.ndim)
 
 
 OFFSETS = ((0, 0), (-1, 0), (1, 0), (0, 1), (2, 0), (-1, 1), (1, 1), (2, 1))
@@ -87,17 +91,18 @@
 
 def project_qkv(chip, ready, own_x, peer_x, weights):
     cols, rows = weights[0].shape[0], own_x.shape[0]
-    shape = jax.ShapeDtypeStruct((len(weights), cols, rows), BF16)
-    flops = 4 * len(weights) * cols * rows * own_x.shape[1]
+    shape = (len(weights), cols, rows)
+    inputs = (ready, own_x, peer_x, *weights)
     return pl.pallas_call(
         qkv_body,
-        out_shape=(shape, shape),
-        in_specs=[pl.BlockSpec(memory_space=pltpu.SMEM)] + vmem_specs(3 + len(weights)),
-        out_specs=tuple(vmem_specs(2)),
-        compiler_params=pltpu.CompilerParams(vmem_limit_bytes=32 << 20),
+        out_shape=(jax.ShapeDtypeStruct(shape, BF16),) * 2,
+        grid=(1,),
+        in_specs=[pl.BlockSpec(memory_space=pltpu.SMEM)] + [whole(x) for x in inputs],
+        out_specs=(pl.BlockSpec(shape, lambda i: (0, 0, 0)),) * 2,
+        compiler_params=pltpu.CompilerParams(vmem_limit_bytes=20 << 20),
         cost_estimate=pl.CostEstimate(flops=1000, bytes_accessed=1000, transcendentals=0),
         name="project_qkv",
-    )(chip, ready, own_x, peer_x, *weights)
+    )(chip, *inputs)
 
 
 def heads_body(core_ref, mine, other, out):
@@ -105,24 +110,37 @@
     step = 16
     per_shard, per_head = cols // step, HEAD // step
     section = HEADS * per_head
-    for source, parity in ((mine, core_ref[0]), (other, 1 - core_ref[0])):
+
+    def copy(sources):
         for c in range(count):
-            for j in range(per_shard):
-                piece = (2 * c + parity) * per_shard + j
-                kind = (piece >= section).astype(jnp.int32) + (piece >= 2 * section).astype(jnp.int32)
-                rest = piece - kind * section
-                head = rest // per_head
-                start = pl.multiple_of(kind * HEAD + (rest - head * per_head) * step, step)
-                out[head, pl.ds(start, step), :] = source[c, j * step : (j + 1) * step]
+            for parity, source in enumerate(sources):
+                for j in range(per_shard):
+                    piece = (2 * c + parity) * per_shard + j
+                    kind, rest = piece // section, piece % section
+                    start = kind * HEAD + rest % per_head * step
+                    rows = source[c, j * step : (j + 1) * step]
+                    out[rest // per_head, start : start + step] = rows
+
+    @pl.when(core_ref[0] == 0)
+    def _():
+        copy((mine, other))
+
+    @pl.when(core_ref[0] != 0)
+    def _():
+        copy((other, mine))
+
     out[HEADS:] = jnp.zeros((out.shape[0] - HEADS,) + out.shape[1:], BF16)
 
 
 def place_heads(core, mine, other, blocks):
+    shape = (blocks, 3 * HEAD, mine.shape[2])
     return pl.pallas_call(
         heads_body,
-        out_shape=jax.ShapeDtypeStruct((blocks, 3 * HEAD, mine.shape[2]), BF16),
-        in_specs=[pl.BlockSpec(memory_space=pltpu.SMEM)] + vmem_specs(2),
-        out_specs=vmem_specs(1)[0],
+        out_shape=jax.ShapeDtypeStruct(shape, BF16),
+        grid=(1,),
+        in_specs=[pl.BlockSpec(memory_space=pltpu.SMEM), whole(mine), whole(other)],
+        out_specs=pl.BlockSpec(shape, lambda i: (0, 0, 0)),
+        compiler_params=pltpu.CompilerParams(vmem_limit_bytes=6 << 20),
         cost_estimate=pl.CostEstimate(flops=1000, bytes_accessed=1000, transcendentals=0),
         name="place_heads",
     )(core, mine, other)
@@ -139,6 +157,7 @@
         grid=(1,),
         in_specs=[pl.BlockSpec((16, 128), lambda i: (0, 0))] * len(arrays),
         out_specs=pl.BlockSpec((16, 128), lambda i: (0, 0)),
+        compiler_params=pltpu.CompilerParams(vmem_limit_bytes=1 << 20),
         cost_estimate=pl.CostEstimate(
             flops=100_000_000_000, bytes_accessed=100_000_000, transcendentals=0
         ),
@@ -204,7 +223,7 @@
             pltpu.VMEM((keys, 2 * HEAD), BF16),
             pltpu.VMEM((queries, 2 * HEAD), BF16),
         ],
-        compiler_params=pltpu.CompilerParams(vmem_limit_bytes=40 << 20),
+        compiler_params=pltpu.CompilerParams(vmem_limit_bytes=20 << 20),
         cost_estimate=pl.CostEstimate(flops=1000, bytes_accessed=1000, transcendentals=0),
         name="attend",
     )(count, parts, text, mark)
@@ -239,7 +258,7 @@
         ),
         in_specs=vmem_specs(5),
         out_specs=tuple(vmem_specs(2)),
-        compiler_params=pltpu.CompilerParams(vmem_limit_bytes=24 << 20),
+        compiler_params=pltpu.CompilerParams(vmem_limit_bytes=14 << 20),
         cost_estimate=pl.CostEstimate(flops=1000, bytes_accessed=1000, transcendentals=0),
         name="middle",
     )(mixed, hidden, mods, out_w, mark)
@@ -255,10 +274,6 @@
         out[place_of(chip_ref[0], k)] = gelu(parts[k * cols : (k + 1) * cols]).astype(BF16)
 
 
-def whole(x):
-    return pl.BlockSpec(x.shape, lambda i: (0,) * x.ndim)
-
-
 def half_of(x, cols, index):
     position = index if x.shape[0] > cols else 0
     return pl.BlockSpec((cols, x.shape[1]), lambda i: (position, 0))
@@ -275,7 +290,7 @@
         in_specs=[pl.BlockSpec(memory_space=pltpu.SMEM), whole(own_x), whole(peer_x)]
         + [half_of(x, cols, 0) for x in weights],
         out_specs=pl.BlockSpec(shape, lambda i: (0, 0, 0)),
-        compiler_params=pltpu.CompilerParams(vmem_limit_bytes=40 << 20),
+        compiler_params=pltpu.CompilerParams(vmem_limit_bytes=28 << 20),
         cost_estimate=pl.CostEstimate(flops=1000, bytes_accessed=1000, transcendentals=0),
         name="mlp_first",
     )(chip, own_x, peer_x, *weights)
@@ -316,7 +331,7 @@
         + [half_of(x, cols, 1) for x in weights],
         out_specs=(pl.BlockSpec(shape, lambda i: (0, 0, 0)),) * 2,
         scratch_shapes=[pltpu.VMEM((2 * count * cols, tokens), BF16)],
-        compiler_params=pltpu.CompilerParams(vmem_limit_bytes=40 << 20),
+        compiler_params=pltpu.CompilerParams(vmem_limit_bytes=28 << 20),
         cost_estimate=pl.CostEstimate(flops=1000, bytes_accessed=1000, transcendentals=0),
         name="mlp_second",
     )(chip, core, own_act, peer_act, *weights)
@@ -343,7 +358,7 @@
         in_specs=[pl.BlockSpec(memory_space=pltpu.SMEM)] + vmem_specs(6),
         out_specs=vmem_specs(1)[0],
         scratch_shapes=[pltpu.VMEM((width, rows), F32)],
-        compiler_params=pltpu.CompilerParams(vmem_limit_bytes=24 << 20),
+        compiler_params=pltpu.CompilerParams(vmem_limit_bytes=8 << 20),
         cost_estimate=pl.CostEstimate(flops=1000, bytes_accessed=1000, transcendentals=0),
         name="last",
     )(core, own_part, peer_part, updated, mods, finals, final_t)
@@ -423,11 +438,10 @@
 
     mlp_next = ring_second(*mlp_near)
     mark = marker(*mlp_near)
-    parts, low, high, mark, text_kv = lax.optimization_barrier(
-        (parts, mlp_next[0], mlp_next[1], mark, text_kv)
-    )
+    parts, mark, text_kv = lax.optimization_barrier((parts, mark, text_kv))
+    mixed = attend(counts, parts, text_kv, mark)
+    mixed, low, high = lax.optimization_barrier((mixed, mlp_next[0], mlp_next[1]))
     peer_low, peer_high = swap(low, "img", 2), swap(high, "img", 2)
-    mixed = attend(counts, parts, text_kv, mark)
     mixed = lax.all_to_all(mixed, "blk", 0, 0, tiled=True)[:HEADS].reshape(width_attn, tok_rows)
     near_pieces, next_pieces = [mlp_mine, *mlp_near], list(mlp_next[2:])
 

time: 159 us -> 160 us (level)
  the two profiles are of different devices: /device:TPU:24 before, /device:TPU:104 now
where the time goes in v7:
time: 160 us; the launch traced here: 159 us
  starting transfers between devices  56.8 us (36%)
  waiting for transfers between devices  53.7 us (34%)
  Pallas kernels  24.3 us (15%)
  local copies, waits for them, and re-layouts  15 us (9%)
  other arithmetic  6.07 us (4%)
  between operations  2.66 us (2%)
    ppermute x12, waiting for transfers between devices, ring(): return lax.ppermute(x, axis, [(i, (i + step) % size) for i in range(size)])  23.7 us
    ppermute x12, starting transfers between devices, ring(): return lax.ppermute(x, axis, [(i, (i + step) % size) for i in range(size)])  20.4 us
    all_to_all x1, waiting for transfers between devices, per_device(): lax.all_to_all(mixed, 'blk', 0, 0, tiled=True)[:HEADS]  13.6 us
    ppermute x10, waiting for transfers between devices, swap(): lax.ppermute(x, axis, [(i, i ^ bits) for i in range(lax.axis_size(axis))])  12.1 us
    pallas_call x1, Pallas kernels, attend(): pl.pallas_call(attend_body, out_shape=jax.ShapeDtypeStruct((blocks, HEAD,...  11.3 us
    ppermute x10, starting transfers between devices, swap(): lax.ppermute(x, axis, [(i, i ^ bits) for i in range(lax.axis_size(axis))])  9.1 us
    all_to_all x1, starting transfers between devices, per_device(): parts = lax.all_to_all(heads, 'blk', 0, 0, tiled=True)  8.59 us
    all_to_all x1, starting transfers between devices, per_device(): lax.all_to_all(mixed, 'blk', 0, 0, tiled=True)[:HEADS]  8.58 us
  transfers between devices with their start and end apart: 26, of which 12 were waited for; matrix products, arithmetic and copies ran while one was open for 9% of the time, Pallas kernels for 9%

profile of v7, /device:TPU:104, one launch (start us, length us, event | category | flops | bytes accessed | tf_op | source)
XLA Modules:
  0.0 159.4 jit_solution(13465695334261931781)
XLA Ops:
  0.7 2.4 %collective-permute-start.6 = (bf16[144,1536]{1,0:T(8,128)(2,1)}, bf16[144,1536]{1,0:T(8,128)(2,1)S(1)}, u32[]{:S(2)}, u32[]{:S(2)}) collective-permute-start(bf16[144,1536]{1,0:T(8,128)(2,1)} %bitcast.78), channel_id=1, source_target_pairs={{0,2},{1,3},{2,0},{3,1},{4,6},{5,7},{6,4},{7,5},{8,10},{9,11},{10,... | collective-permute-start | bytes 1327112 | tf_op jit(solution)/shard_map/ppermute | solution.py:38
  3.0 1.5 collective-permute-start
  4.5 1.7 %collective-permute-start.2 = (bf16[144,1536]{1,0:T(8,128)(2,1)}, bf16[144,1536]{1,0:T(8,128)(2,1)S(1)}, u32[]{:S(2)}, u32[]{:S(2)}) collective-permute-start(bf16[144,1536]{1,0:T(8,128)(2,1)} %bitcast.80), channel_id=1, source_target_pairs={{0,12},{1,13},{2,14},{3,15},{4,0},{5,1},{6,2},{7,3},{8,4},{9,5},{1... | collective-permute-start | bytes 1327112 | tf_op jit(solution)/shard_map/ppermute | solution.py:54
  9.6 6.5 %collective-permute-done.refs_1_ = bf16[144,1536]{1,0:T(8,128)(2,1)S(1)} collective-permute-done((bf16[144,1536]{1,0:T(8,128)(2,1)}, bf16[144,1536]{1,0:T(8,128)(2,1)S(1)}, u32[]{:S(2)}, u32[]{:S(2)}) %collective-permute-start) | collective-permute-done | bytes 442400 | tf_op jit(solution)/shard_map/ppermute | solution.py:54
  18.0 3.0 %collective-permute-start.3 = (bf16[72,1536]{1,0:T(8,128)(2,1)S(1)}, bf16[72,1536]{1,0:T(8,128)(2,1)S(1)}, u32[]{:S(2)}, u32[]{:S(2)}) collective-permute-start(bf16[72,1536]{1,0:T(8,128)(2,1)S(1)} %slice.96), channel_id=1, source_target_pairs={{0,12},{1,13},{2,14},{3,15},{4,0},{5,1},{6,2},{7,3},{8,4},{9,5},{1... | collective-permute-start | bytes 663560 | tf_op jit(solution)/shard_map/ppermute | solution.py:54
  21.0 3.2 %collective-permute-start.8 = (bf16[144,1536]{1,0:T(8,128)(2,1)S(1)}, bf16[144,1536]{1,0:T(8,128)(2,1)S(1)}, u32[]{:S(2)}, u32[]{:S(2)}) collective-permute-start(bf16[144,1536]{1,0:T(8,128)(2,1)S(1)} %collective-permute-done.6.refs_3_), channel_id=1, source_target_pairs={{0,12},{1,13},{2,14},{3,15},{4,0},{5,1},{6,2},{7,3},{8,4},{9,5},{1... | collective-permute-start | bytes 1327112 | tf_op jit(solution)/shard_map/ppermute | solution.py:54
  25.2 1.5 collective-permute-done.3
  26.8 1.3 collective-permute-start.4
  30.6 3.9 %collective-permute-done.7.refs_5_ = bf16[144,1536]{1,0:T(8,128)(2,1)S(1)} collective-permute-done((bf16[144,1536]{1,0:T(8,128)(2,1)S(1)}, bf16[144,1536]{1,0:T(8,128)(2,1)S(1)}, u32[]{:S(2)}, u32[]{:S(2)}) %collective-permute-start.7) | collective-permute-done | bytes 442400 | tf_op jit(solution)/shard_map/ppermute | solution.py:54
  34.5 1.3 collective-permute-done.8.refs_6_
  35.8 3.7 %collective-permute-start.11 = (bf16[384,1536]{1,0:T(8,128)(2,1)S(1)}, bf16[384,1536]{1,0:T(8,128)(2,1)S(1)}, u32[]{:S(2)}, u32[]{:S(2)}) collective-permute-start(bf16[384,1536]{1,0:T(8,128)(2,1)S(1)} %pad_maximum_fusion.refs_0_), channel_id=1, source_target_pairs={{0,12},{1,13},{2,14},{3,15},{4,0},{5,1},{6,2},{7,3},{8,4},{9,5},{1... | collective-permute-start | bytes 3538952 | tf_op jit(solution)/shard_map/ppermute | solution.py:54
  40.8 2.1 %project_qkv.1 = (bf16[8,144,128]{2,1,0:T(8,128)(2,1)S(1)}, bf16[8,144,128]{2,1,0:T(8,128)(2,1)S(1)}) custom-call(s32[1]{0:T(128)} %bitcast.2.chip_ref, bf16[16,128]{1,0:T(8,128)(2,1)S(1)} %marker.3.ready, bf16[128,1536]{1,0:T(8,128)(2,1)S(1)} %fusion.12.own_x, bf16[128,1536]{1,0:T(8,128)(2,1)} %collective-permute-done.5.peer_x, ...), custom_call_target="tpu_custom_call" | custom-call | flops 1000 | bytes 1000 | tf_op jit(solution)/shard_map/project_qkv/pallas_call | solution.py:96
  43.1 1.5 collective-permute-done.9.other
  45.6 8.6 %all-to-all-start = ((bf16[16,192,128]{2,1,0:T(8,128)(2,1)}), bf16[16,192,128]{2,1,0:T(8,128)(2,1)S(1)}, u32[]{:S(2)}, u32[]{:S(2)}) async-start(bf16[16,192,128]{2,1,0:T(8,128)(2,1)} %copy-done.3), calls=%async_computation | async-start | bytes 1572864 | tf_op jit(solution)/shard_map/all_to_all | solution.py:421
  54.2 10.4 %collective-permute-done.11.refs_1_.refs_2_ = bf16[384,1536]{1,0:T(8,128)(2,1)S(1)} collective-permute-done((bf16[384,1536]{1,0:T(8,128)(2,1)S(1)}, bf16[384,1536]{1,0:T(8,128)(2,1)S(1)}, u32[]{:S(2)}, u32[]{:S(2)}) %collective-permute-start.11) | collective-permute-done | bytes 1179680 | tf_op jit(solution)/shard_map/ppermute | solution.py:54
  65.5 3.7 %collective-permute-start.14 = (bf16[192,1536]{1,0:T(8,128)(2,1)}, bf16[192,1536]{1,0:T(8,128)(2,1)}, u32[]{:S(2)}, u32[]{:S(2)}) collective-permute-start(bf16[192,1536]{1,0:T(8,128)(2,1)} %slice.83), channel_id=1, source_target_pairs={{0,12},{1,13},{2,14},{3,15},{4,0},{5,1},{6,2},{7,3},{8,4},{9,5},{1... | collective-permute-start | bytes 1769480 | tf_op jit(solution)/shard_map/ppermute | solution.py:54
  69.2 2.0 %slice.97 = bf16[192,1536]{1,0:T(8,128)(2,1)} slice(bf16[384,1536]{1,0:T(8,128)(2,1)} %collective-permute-done.10.refs_0_.refs_1_), slice={[0:192], [0:1536]} | slice | bytes 1179648 | tf_op jit(solution)/shard_map/slice | solution.py:64
  71.1 5.2 %collective-permute-done.12.refs_2_.refs_3_ = bf16[384,1536]{1,0:T(8,128)(2,1)} collective-permute-done((bf16[384,1536]{1,0:T(8,128)(2,1)S(1)}, bf16[384,1536]{1,0:T(8,128)(2,1)}, u32[]{:S(2)}, u32[]{:S(2)}) %collective-permute-start.12) | collective-permute-done | bytes 1179680 | tf_op jit(solution)/shard_map/ppermute | solution.py:38
  76.3 3.2 %collective-permute-start.18 = (bf16[384,1536]{1,0:T(8,128)(2,1)}, bf16[384,1536]{1,0:T(8,128)(2,1)}, u32[]{:S(2)}, u32[]{:S(2)}) collective-permute-start(bf16[384,1536]{1,0:T(8,128)(2,1)} %collective-permute-done.12.refs_2_.refs_3_), channel_id=1, source_target_pairs={{0,12},{1,13},{2,14},{3,15},{4,0},{5,1},{6,2},{7,3},{8,4},{9,5},{1... | collective-permute-start | bytes 3538952 | tf_op jit(solution)/shard_map/ppermute | solution.py:54
  80.3 1.5 constant_dynamic-slice_fusion.1
  82.4 11.3 %attend.1 = bf16[16,64,128]{2,1,0:T(8,128)(2,1)} custom-call(s32[1]{0:T(128)} %copy.45.count_ref, bf16[16,192,128]{2,1,0:T(8,128)(2,1)S(1)} %all-to-all-done.parts, bf16[128,256]{1,0:T(8,128)(2,1)S(1)} %pad.8.text, bf16[16,128]{1,0:T(8,128)(2,1)S(1)} %marker.4.mark), custom_call_target="tpu_custom_call" | custom-call | flops 1000 | bytes 1000 | tf_op jit(solution)/shard_map/attend/pallas_call | solution.py:216
  95.0 2.3 %collective-permute-start.16 = (bf16[192,1536]{1,0:T(8,128)(2,1)}, bf16[192,1536]{1,0:T(8,128)(2,1)S(1)}, u32[]{:S(2)}, u32[]{:S(2)}) collective-permute-start(bf16[192,1536]{1,0:T(8,128)(2,1)} %collective-permute-done.14.refs_4_), channel_id=1, source_target_pairs={{0,2},{1,3},{2,0},{3,1},{4,6},{5,7},{6,4},{7,5},{8,10},{9,11},{10,... | collective-permute-start | bytes 1769480 | tf_op jit(solution)/shard_map/ppermute | solution.py:38
  97.2 8.6 %all-to-all-start.1 = ((bf16[16,64,128]{2,1,0:T(8,128)(2,1)}), bf16[16,64,128]{2,1,0:T(8,128)(2,1)S(1)}, u32[]{:S(2)}, u32[]{:S(2)}) async-start(bf16[16,64,128]{2,1,0:T(8,128)(2,1)} %attend.1), calls=%async_computation.1 | async-start | bytes 524288 | tf_op jit(solution)/shard_map/all_to_all | solution.py:445
  105.9 13.6 %all-to-all-done.1 = bf16[16,64,128]{2,1,0:T(8,128)(2,1)S(1)} async-done(((bf16[16,64,128]{2,1,0:T(8,128)(2,1)}), bf16[16,64,128]{2,1,0:T(8,128)(2,1)S(1)}, u32[]{:S(2)}, u32[]{:S(2)}) %all-to-all-start.1) | async-done | bytes 262176 | tf_op jit(solution)/shard_map/all_to_all | solution.py:445
  119.5 1.5 collective-permute-done.16.refs_1_.refs_7_
  123.8 1.7 %collective-permute-done.19.peer_x = bf16[128,1536]{1,0:T(8,128)(2,1)S(1)} collective-permute-done((bf16[128,1536]{1,0:T(8,128)(2,1)S(1)}, bf16[128,1536]{1,0:T(8,128)(2,1)S(1)}, u32[]{:S(2)}, u32[]{:S(2)}) %collective-permute-start.19) | collective-permute-done | bytes 393248 | tf_op jit(solution)/shard_map/ppermute | solution.py:38
  125.5 3.6 %mlp_first.1.own_act = bf16[8,192,256]{2,1,0:T(8,128)(2,1)S(1)} custom-call(s32[1]{0:T(128)} %bitcast.2.chip_ref, bf16[128,1536]{1,0:T(8,128)(2,1)S(1)} %get-tuple-element.37.own_x, bf16[128,1536]{1,0:T(8,128)(2,1)S(1)} %collective-permute-done.19.peer_x, bf16[384,1536]{1,0:T(8,128)(2,1)S(1)} %pad_maximum_fusion.refs_0_, ...), custom_call_target="tpu_custom_call" | custom-call | flops 1000 | bytes 1000 | tf_op jit(solution)/shard_map/mlp_first/pallas_call | solution.py:286
  129.4 2.2 %collective-permute-done.20.peer_act = bf16[8,192,256]{2,1,0:T(8,128)(2,1)S(1)} collective-permute-done((bf16[8,192,256]{2,1,0:T(8,128)(2,1)S(1)}, bf16[8,192,256]{2,1,0:T(8,128)(2,1)S(1)}, u32[]{:S(2)}, u32[]{:S(2)}) %collective-permute-start.20) | collective-permute-done | bytes 786464 | tf_op jit(solution)/shard_map/ppermute | solution.py:38
  131.5 4.1 %mlp_second.1 = (f32[8,96,128]{2,1,0:T(8,128)S(1)}, f32[8,96,128]{2,1,0:T(8,128)}) custom-call(s32[1]{0:T(128)} %bitcast.2.chip_ref, s32[1]{0:T(128)} %bitcast.1.core_ref, bf16[8,192,256]{2,1,0:T(8,128)(2,1)S(1)} %mlp_first.1.own_act, bf16[8,192,256]{2,1,0:T(8,128)(2,1)S(1)} %collective-permute-done.20.peer_act, ...), custom_call_target="tpu_custom_call" | custom-call | flops 1000 | bytes 1000 | tf_op jit(solution)/shard_map/mlp_second/pallas_call | solution.py:325
  140.9 8.2 %collective-permute-start.22 = (bf16[1,2048]{1,0:T(2,128)(2,1)S(1)}, bf16[1,2048]{1,0:T(2,128)(2,1)S(1)}, u32[]{:S(2)}, u32[]{:S(2)}) collective-permute-start(bf16[1,2048]{1,0:T(2,128)(2,1)S(1)} %get-tuple-element.57), channel_id=1, source_target_pairs={{0,16},{16,32},{32,48},{48,64},{64,80},{80,96},{96,112},{112,128},... | collective-permute-start | bytes 12296 | tf_op jit(solution)/shard_map/ppermute | solution.py:371
  149.1 1.9 %collective-permute-start.23 = (bf16[1,2048]{1,0:T(2,128)(2,1)S(1)}, bf16[1,2048]{1,0:T(2,128)(2,1)S(1)}, u32[]{:S(2)}, u32[]{:S(2)}) collective-permute-start(bf16[1,2048]{1,0:T(2,128)(2,1)S(1)} %get-tuple-element.58), channel_id=1, source_target_pairs={{16,0},{32,16},{48,32},{64,48},{80,64},{96,80},{112,96},{128,112},... | collective-permute-start | bytes 12296 | tf_op jit(solution)/shard_map/ppermute | solution.py:372
  152.4 4.4 %collective-permute-done.23 = bf16[1,2048]{1,0:T(2,128)(2,1)S(1)} collective-permute-done((bf16[1,2048]{1,0:T(2,128)(2,1)S(1)}, bf16[1,2048]{1,0:T(2,128)(2,1)S(1)}, u32[]{:S(2)}, u32[]{:S(2)}) %collective-permute-start.23) | collective-permute-done | bytes 4128 | tf_op jit(solution)/shard_map/ppermute | solution.py:372
  (128 shorter events, 25.2 us)
Async XLA Ops:
  0.6 157.5 %copy-start = (bf16[144,512]{1,0:T(8,128)(2,1)S(1)}, bf16[144,512]{1,0:T(8,128)(2,1)}, u32[]{:S(2)}) copy-start(bf16[144,512]{1,0:T(8,128)(2,1)} %param.30) | copy-start | bytes 442372
  0.7 20.4 %collective-permute-start.6 = (bf16[144,1536]{1,0:T(8,128)(2,1)}, bf16[144,1536]{1,0:T(8,128)(2,1)S(1)}, u32[]{:S(2)}, u32[]{:S(2)}) collective-permute-start(bf16[144,1536]{1,0:T(8,128)(2,1)} %bitcast.78), channel_id=1, source_target_pairs={{0,2},{1,3},{2,0},{3,1},{4,6},{5,7},{6,4},{7,5},{8,10},{9,11},{10,... | collective-permute-start | bytes 1327112 | tf_op jit(solution)/shard_map/ppermute | solution.py:38
  3.0 13.0 %collective-permute-start = (bf16[144,1536]{1,0:T(8,128)(2,1)}, bf16[144,1536]{1,0:T(8,128)(2,1)S(1)}, u32[]{:S(2)}, u32[]{:S(2)}) collective-permute-start(bf16[144,1536]{1,0:T(8,128)(2,1)} %bitcast.79), channel_id=1, source_target_pairs={{0,4},{1,5},{2,6},{3,7},{4,8},{5,9},{6,10},{7,11},{8,12},{9,13},{1... | collective-permute-start | bytes 1327112 | tf_op jit(solution)/shard_map/ppermute | solution.py:54
  4.5 13.4 %collective-permute-start.2 = (bf16[144,1536]{1,0:T(8,128)(2,1)}, bf16[144,1536]{1,0:T(8,128)(2,1)S(1)}, u32[]{:S(2)}, u32[]{:S(2)}) collective-permute-start(bf16[144,1536]{1,0:T(8,128)(2,1)} %bitcast.80), channel_id=1, source_target_pairs={{0,12},{1,13},{2,14},{3,15},{4,0},{5,1},{6,2},{7,3},{8,4},{9,5},{1... | collective-permute-start | bytes 1327112 | tf_op jit(solution)/shard_map/ppermute | solution.py:54
  16.8 7.5 %collective-permute-start.1 = (bf16[72,1536]{1,0:T(8,128)(2,1)}, bf16[72,1536]{1,0:T(8,128)(2,1)}, u32[]{:S(2)}, u32[]{:S(2)}) collective-permute-start(bf16[72,1536]{1,0:T(8,128)(2,1)} %slice.95), channel_id=1, source_target_pairs={{0,4},{1,5},{2,6},{3,7},{4,8},{5,9},{6,10},{7,11},{8,12},{9,13},{1... | collective-permute-start | bytes 663560 | tf_op jit(solution)/shard_map/ppermute | solution.py:54
  17.2 23.6 %collective-permute-start.5 = (bf16[128,1536]{1,0:T(8,128)(2,1)S(1)}, bf16[128,1536]{1,0:T(8,128)(2,1)}, u32[]{:S(2)}, u32[]{:S(2)}) collective-permute-start(bf16[128,1536]{1,0:T(8,128)(2,1)S(1)} %fusion.12.own_x), channel_id=1, source_target_pairs={{0,1},{1,0},{2,3},{3,2},{4,5},{5,4},{6,7},{7,6},{8,9},{9,8},{10,11... | collective-permute-start | bytes 1179656 | tf_op jit(solution)/shard_map/ppermute | solution.py:38
  17.9 16.6 %copy-start.5 = (bf16[144,1536]{1,0:T(8,128)(2,1)}, bf16[144,1536]{1,0:T(8,128)(2,1)S(1)}, u32[]{:S(2)}) copy-start(bf16[144,1536]{1,0:T(8,128)(2,1)S(1)} %collective-permute-done.2.refs_2_) | copy-start | bytes 1327108
  18.0 8.8 %collective-permute-start.3 = (bf16[72,1536]{1,0:T(8,128)(2,1)S(1)}, bf16[72,1536]{1,0:T(8,128)(2,1)S(1)}, u32[]{:S(2)}, u32[]{:S(2)}) collective-permute-start(bf16[72,1536]{1,0:T(8,128)(2,1)S(1)} %slice.96), channel_id=1, source_target_pairs={{0,12},{1,13},{2,14},{3,15},{4,0},{5,1},{6,2},{7,3},{8,4},{9,5},{1... | collective-permute-start | bytes 663560 | tf_op jit(solution)/shard_map/ppermute | solution.py:54
  21.0 13.5 %copy-start.10 = (bf16[144,1536]{1,0:T(8,128)(2,1)}, bf16[144,1536]{1,0:T(8,128)(2,1)S(1)}, u32[]{:S(2)}) copy-start(bf16[144,1536]{1,0:T(8,128)(2,1)S(1)} %collective-permute-done.6.refs_3_) | copy-start | bytes 1327108
  21.0 13.5 %collective-permute-start.7 = (bf16[144,1536]{1,0:T(8,128)(2,1)S(1)}, bf16[144,1536]{1,0:T(8,128)(2,1)S(1)}, u32[]{:S(2)}, u32[]{:S(2)}) collective-permute-start(bf16[144,1536]{1,0:T(8,128)(2,1)S(1)} %collective-permute-done.6.refs_3_), channel_id=1, source_target_pairs={{0,4},{1,5},{2,6},{3,7},{4,8},{5,9},{6,10},{7,11},{8,12},{9,13},{1... | collective-permute-start | bytes 1327112 | tf_op jit(solution)/shard_map/ppermute | solution.py:54
  21.0 14.8 %collective-permute-start.8 = (bf16[144,1536]{1,0:T(8,128)(2,1)S(1)}, bf16[144,1536]{1,0:T(8,128)(2,1)S(1)}, u32[]{:S(2)}, u32[]{:S(2)}) collective-permute-start(bf16[144,1536]{1,0:T(8,128)(2,1)S(1)} %collective-permute-done.6.refs_3_), channel_id=1, source_target_pairs={{0,12},{1,13},{2,14},{3,15},{4,0},{5,1},{6,2},{7,3},{8,4},{9,5},{1... | collective-permute-start | bytes 1327112 | tf_op jit(solution)/shard_map/ppermute | solution.py:54
  26.8 14.0 %collective-permute-start.4 = (bf16[144,1536]{1,0:T(8,128)(2,1)S(1)}, bf16[144,1536]{1,0:T(8,128)(2,1)S(1)}, u32[]{:S(2)}, u32[]{:S(2)}) collective-permute-start(bf16[144,1536]{1,0:T(8,128)(2,1)S(1)} %constant_dynamic-update-slice_fusion.refs_4_), channel_id=1, source_target_pairs={{0,2},{1,3},{2,0},{3,1},{4,6},{5,7},{6,4},{7,5},{8,10},{9,11},{10,... | collective-permute-start | bytes 1327112 | tf_op jit(solution)/shard_map/ppermute | solution.py:38
  30.6 10.2 %copy-start.9 = (bf16[1536,144]{0,1:T(8,128)(2,1)S(1)}, bf16[1536,144]{0,1:T(8,128)(2,1)}, u32[]{:S(2)}) copy-start(bf16[1536,144]{0,1:T(8,128)(2,1)} %param.24) | copy-start | bytes 1327108
  35.8 28.8 %collective-permute-start.11 = (bf16[384,1536]{1,0:T(8,128)(2,1)S(1)}, bf16[384,1536]{1,0:T(8,128)(2,1)S(1)}, u32[]{:S(2)}, u32[]{:S(2)}) collective-permute-start(bf16[384,1536]{1,0:T(8,128)(2,1)S(1)} %pad_maximum_fusion.refs_0_), channel_id=1, source_target_pairs={{0,12},{1,13},{2,14},{3,15},{4,0},{5,1},{6,2},{7,3},{8,4},{9,5},{1... | collective-permute-start | bytes 3538952 | tf_op jit(solution)/shard_map/ppermute | solution.py:54
  39.5 36.8 %collective-permute-start.12 = (bf16[384,1536]{1,0:T(8,128)(2,1)S(1)}, bf16[384,1536]{1,0:T(8,128)(2,1)}, u32[]{:S(2)}, u32[]{:S(2)}) collective-permute-start(bf16[384,1536]{1,0:T(8,128)(2,1)S(1)} %pad_maximum_fusion.refs_0_), channel_id=1, source_target_pairs={{0,2},{1,3},{2,0},{3,1},{4,6},{5,7},{6,4},{7,5},{8,10},{9,11},{10,... | collective-permute-start | bytes 3538952 | tf_op jit(solution)/shard_map/ppermute | solution.py:38
  40.8 28.4 %collective-permute-start.10 = (bf16[384,1536]{1,0:T(8,128)(2,1)S(1)}, bf16[384,1536]{1,0:T(8,128)(2,1)}, u32[]{:S(2)}, u32[]{:S(2)}) collective-permute-start(bf16[384,1536]{1,0:T(8,128)(2,1)S(1)} %pad_maximum_fusion.refs_0_), channel_id=1, source_target_pairs={{0,4},{1,5},{2,6},{3,7},{4,8},{5,9},{6,10},{7,11},{8,12},{9,13},{1... | collective-permute-start | bytes 3538952 | tf_op jit(solution)/shard_map/ppermute | solution.py:54
  42.9 1.7 %collective-permute-start.9 = (bf16[8,144,128]{2,1,0:T(8,128)(2,1)S(1)}, bf16[8,144,128]{2,1,0:T(8,128)(2,1)S(1)}, u32[]{:S(2)}, u32[]{:S(2)}) collective-permute-start(bf16[8,144,128]{2,1,0:T(8,128)(2,1)S(1)} %get-tuple-element.26), channel_id=1, source_target_pairs={{0,1},{1,0},{2,3},{3,2},{4,5},{5,4},{6,7},{7,6},{8,9},{9,8},{10,11... | collective-permute-start | bytes 884744 | tf_op jit(solution)/shard_map/ppermute | solution.py:38
  45.6 36.8 %all-to-all-start = ((bf16[16,192,128]{2,1,0:T(8,128)(2,1)}), bf16[16,192,128]{2,1,0:T(8,128)(2,1)S(1)}, u32[]{:S(2)}, u32[]{:S(2)}) async-start(bf16[16,192,128]{2,1,0:T(8,128)(2,1)} %copy-done.3), calls=%async_computation | async-start | bytes 1572864 | tf_op jit(solution)/shard_map/all_to_all | solution.py:421
  65.5 28.2 %collective-permute-start.14 = (bf16[192,1536]{1,0:T(8,128)(2,1)}, bf16[192,1536]{1,0:T(8,128)(2,1)}, u32[]{:S(2)}, u32[]{:S(2)}) collective-permute-start(bf16[192,1536]{1,0:T(8,128)(2,1)} %slice.83), channel_id=1, source_target_pairs={{0,12},{1,13},{2,14},{3,15},{4,0},{5,1},{6,2},{7,3},{8,4},{9,5},{1... | collective-permute-start | bytes 1769480 | tf_op jit(solution)/shard_map/ppermute | solution.py:54
  71.1 22.6 %collective-permute-start.13 = (bf16[192,1536]{1,0:T(8,128)(2,1)}, bf16[192,1536]{1,0:T(8,128)(2,1)}, u32[]{:S(2)}, u32[]{:S(2)}) collective-permute-start(bf16[192,1536]{1,0:T(8,128)(2,1)} %slice.97), channel_id=1, source_target_pairs={{0,4},{1,5},{2,6},{3,7},{4,8},{5,9},{6,10},{7,11},{8,12},{9,13},{1... | collective-permute-start | bytes 1769480 | tf_op jit(solution)/shard_map/ppermute | solution.py:54
  76.3 43.1 %collective-permute-start.17 = (bf16[384,1536]{1,0:T(8,128)(2,1)}, bf16[384,1536]{1,0:T(8,128)(2,1)}, u32[]{:S(2)}, u32[]{:S(2)}) collective-permute-start(bf16[384,1536]{1,0:T(8,128)(2,1)} %collective-permute-done.12.refs_2_.refs_3_), channel_id=1, source_target_pairs={{0,4},{1,5},{2,6},{3,7},{4,8},{5,9},{6,10},{7,11},{8,12},{9,13},{1... | collective-permute-start | bytes 3538952 | tf_op jit(solution)/shard_map/ppermute | solution.py:54
  76.3 43.1 %collective-permute-start.18 = (bf16[384,1536]{1,0:T(8,128)(2,1)}, bf16[384,1536]{1,0:T(8,128)(2,1)}, u32[]{:S(2)}, u32[]{:S(2)}) collective-permute-start(bf16[384,1536]{1,0:T(8,128)(2,1)} %collective-permute-done.12.refs_2_.refs_3_), channel_id=1, source_target_pairs={{0,12},{1,13},{2,14},{3,15},{4,0},{5,1},{6,2},{7,3},{8,4},{9,5},{1... | collective-permute-start | bytes 3538952 | tf_op jit(solution)/shard_map/ppermute | solution.py:54
  82.3 23.6 %copy-start.19 = (f32[1,6,1536]{2,0,1:T(1,128)S(1)}, f32[1,6,1536]{2,0,1:T(1,128)}, u32[]{:S(2)}) copy-start(f32[1,6,1536]{2,0,1:T(1,128)} %param.19) | copy-start | bytes 110596
  93.7 25.7 %collective-permute-start.15 = (bf16[192,1536]{1,0:T(8,128)(2,1)}, bf16[192,1536]{1,0:T(8,128)(2,1)}, u32[]{:S(2)}, u32[]{:S(2)}) collective-permute-start(bf16[192,1536]{1,0:T(8,128)(2,1)} %collective-permute-done.13.refs_4_), channel_id=1, source_target_pairs={{0,2},{1,3},{2,0},{3,1},{4,6},{5,7},{6,4},{7,5},{8,10},{9,11},{10,... | collective-permute-start | bytes 1769480 | tf_op jit(solution)/shard_map/ppermute | solution.py:38
  95.0 26.0 %collective-permute-start.16 = (bf16[192,1536]{1,0:T(8,128)(2,1)}, bf16[192,1536]{1,0:T(8,128)(2,1)S(1)}, u32[]{:S(2)}, u32[]{:S(2)}) collective-permute-start(bf16[192,1536]{1,0:T(8,128)(2,1)} %collective-permute-done.14.refs_4_), channel_id=1, source_target_pairs={{0,2},{1,3},{2,0},{3,1},{4,6},{5,7},{6,4},{7,5},{8,10},{9,11},{10,... | collective-permute-start | bytes 1769480 | tf_op jit(solution)/shard_map/ppermute | solution.py:38
  97.2 22.2 %all-to-all-start.1 = ((bf16[16,64,128]{2,1,0:T(8,128)(2,1)}), bf16[16,64,128]{2,1,0:T(8,128)(2,1)S(1)}, u32[]{:S(2)}, u32[]{:S(2)}) async-start(bf16[16,64,128]{2,1,0:T(8,128)(2,1)} %attend.1), calls=%async_computation.1 | async-start | bytes 524288 | tf_op jit(solution)/shard_map/all_to_all | solution.py:445
  123.7 1.8 %collective-permute-start.19 = (bf16[128,1536]{1,0:T(8,128)(2,1)S(1)}, bf16[128,1536]{1,0:T(8,128)(2,1)S(1)}, u32[]{:S(2)}, u32[]{:S(2)}) collective-permute-start(bf16[128,1536]{1,0:T(8,128)(2,1)S(1)} %get-tuple-element.37.own_x), channel_id=1, source_target_pairs={{0,1},{1,0},{2,3},{3,2},{4,5},{5,4},{6,7},{7,6},{8,9},{9,8},{10,11... | collective-permute-start | bytes 1179656 | tf_op jit(solution)/shard_map/ppermute | solution.py:38
  129.1 9.2 %copy-start.14 = (bf16[1536,64]{0,1:T(8,128)(2,1)S(1)}, bf16[1536,64]{0,1:T(8,128)(2,1)}, u32[]{:S(2)}) copy-start(bf16[1536,64]{0,1:T(8,128)(2,1)} %param.29) | copy-start | bytes 589828
  129.1 2.4 %collective-permute-start.20 = (bf16[8,192,256]{2,1,0:T(8,128)(2,1)S(1)}, bf16[8,192,256]{2,1,0:T(8,128)(2,1)S(1)}, u32[]{:S(2)}, u32[]{:S(2)}) collective-permute-start(bf16[8,192,256]{2,1,0:T(8,128)(2,1)S(1)} %mlp_first.1.own_act), channel_id=1, source_target_pairs={{0,1},{1,0},{2,3},{3,2},{4,5},{5,4},{6,7},{7,6},{8,9},{9,8},{10,11... | collective-permute-start | bytes 2359304 | tf_op jit(solution)/shard_map/ppermute | solution.py:38
  136.4 1.9 %collective-permute-start.21 = (f32[8,96,128]{2,1,0:T(8,128)}, f32[8,96,128]{2,1,0:T(8,128)S(1)}, u32[]{:S(2)}, u32[]{:S(2)}) collective-permute-start(f32[8,96,128]{2,1,0:T(8,128)} %get-tuple-element.39), channel_id=1, source_target_pairs={{0,1},{1,0},{2,3},{3,2},{4,5},{5,4},{6,7},{7,6},{8,9},{9,8},{10,11... | collective-permute-start | bytes 1179656 | tf_op jit(solution)/shard_map/ppermute | solution.py:38
  140.9 11.5 %collective-permute-start.22 = (bf16[1,2048]{1,0:T(2,128)(2,1)S(1)}, bf16[1,2048]{1,0:T(2,128)(2,1)S(1)}, u32[]{:S(2)}, u32[]{:S(2)}) collective-permute-start(bf16[1,2048]{1,0:T(2,128)(2,1)S(1)} %get-tuple-element.57), channel_id=1, source_target_pairs={{0,16},{16,32},{32,48},{48,64},{64,80},{80,96},{96,112},{112,128},... | collective-permute-start | bytes 12296 | tf_op jit(solution)/shard_map/ppermute | solution.py:371
  149.1 7.7 %collective-permute-start.23 = (bf16[1,2048]{1,0:T(2,128)(2,1)S(1)}, bf16[1,2048]{1,0:T(2,128)(2,1)S(1)}, u32[]{:S(2)}, u32[]{:S(2)}) collective-permute-start(bf16[1,2048]{1,0:T(2,128)(2,1)S(1)} %get-tuple-element.58), channel_id=1, source_target_pairs={{16,0},{32,16},{48,32},{64,48},{80,64},{96,80},{112,96},{128,112},... | collective-permute-start | bytes 12296 | tf_op jit(solution)/shard_map/ppermute | solution.py:372
  (18 other events, 63.9 us)

commit v8 on v7

--- a/solution.py
+++ b/solution.py
@@ -21,12 +21,12 @@
 BF16 = jnp.bfloat16
 
 
-def modulate(inputs, shift_row, scale_row):
+def modulate(inputs, shift_row, gain_row):
     values = inputs.astype(F32)
     center = jnp.mean(values, axis=-1, keepdims=True)
     spread = jnp.mean(jnp.square(values - center), axis=-1, keepdims=True)
     normed = (values - center) * lax.rsqrt(spread + norm_eps)
-    return (normed * (1.0 + scale_row) + shift_row).astype(BF16)
+    return (normed * gain_row + shift_row).astype(BF16)
 
 
 def plan(step_value):
@@ -54,8 +54,8 @@
     return lax.ppermute(x, axis, [(i, (i + step) % size) for i in range(size)])
 
 
-def ring_first(x):
-    return ring(x, "img", 4), ring(x, "img", -4), swap(x, "img", 2)
+def ring_first(x, side):
+    return ring(x, "img", 4), ring(x, "img", -4), swap(side, "img", 2)
 
 
 def ring_second(left, right, across):
@@ -337,7 +337,10 @@
     )(chip, core, own_act, peer_act, *weights)
 
 
-def last_body(core_ref, own_part, peer_part, updated, mods, finals, final_t, predicted, mlp_t):
+def last_body(
+    core_ref, live_ref, gap_ref, own_part, peer_part, updated, mods, finals, final_t, latent,
+    velocity, next_latent, scaled, top, bottom, mlp_t,
+):
     count, half, _ = own_part.shape
     for source, parity in ((own_part, core_ref[0]), (peer_part, 1 - core_ref[0])):
         for c in range(count):
@@ -345,32 +348,89 @@
             mlp_t[pl.ds(start, half), :] = source[c]
     refined = updated[...] + mods[5:6] * mlp_t[...].T
     final_in = layer_norm(refined, finals[0:1], finals[1:2])
-    predicted[...] = lax.dot_general(
+    predicted = lax.dot_general(
         final_in, final_t[...], (((1,), (1,)), ((), ())), preferred_element_type=F32
     )
-
-
-def last(core, own_part, peer_part, updated, mods, finals, final_t):
+    live = jnp.full(predicted.shape, live_ref[0], jnp.int32) != 0
+    moved = latent[...] + gap_ref[0] * predicted
+    inner = (moved / vae_scale + vae_offset).astype(F32)
+    velocity[...] = jnp.where(live, predicted, 0.0)
+    next_latent[...] = jnp.where(live, moved, 0.0)
+    inner = jnp.where(live, inner, 0.0).astype(BF16)
+    scaled[...] = inner
+    lanes = inner.shape[1] // 2
+    top[...] = inner[:W_P, :lanes]
+    bottom[...] = inner[inner.shape[0] - W_P :, lanes:]
+
+
+def last(core, live, gap, own_part, peer_part, updated, mods, finals, final_t, latent):
     rows, width = updated.shape
+    cols = final_t.shape[0]
+    smem = pl.BlockSpec(memory_space=pltpu.SMEM)
     return pl.pallas_call(
         last_body,
-        out_shape=jax.ShapeDtypeStruct((rows, final_t.shape[0]), F32),
-        in_specs=[pl.BlockSpec(memory_space=pltpu.SMEM)] + vmem_specs(6),
-        out_specs=vmem_specs(1)[0],
+        out_shape=(
+            jax.ShapeDtypeStruct((rows, cols), F32),
+            jax.ShapeDtypeStruct((rows, cols), F32),
+            jax.ShapeDtypeStruct((rows, cols), BF16),
+            jax.ShapeDtypeStruct((W_P, cols // 2), BF16),
+            jax.ShapeDtypeStruct((W_P, cols // 2), BF16),
+        ),
+        in_specs=[smem] * 3 + vmem_specs(7),
+        out_specs=tuple(vmem_specs(5)),
         scratch_shapes=[pltpu.VMEM((width, rows), F32)],
         compiler_params=pltpu.CompilerParams(vmem_limit_bytes=8 << 20),
         cost_estimate=pl.CostEstimate(flops=1000, bytes_accessed=1000, transcendentals=0),
         name="last",
-    )(core, own_part, peer_part, updated, mods, finals, final_t)
-
-
-def padded(x, axis, width):
-    size, length = lax.axis_size(axis), x.shape[0]
-    up = [(i, i + 1) for i in range(size - 1)]
-    down = [(j, i) for i, j in up]
-    before = lax.ppermute(x[length - width :], axis, up)
-    after = lax.ppermute(x[:width], axis, down)
-    return jnp.concatenate([before, x, after], axis=0)
+    )(core, live, gap, own_part, peer_part, updated, mods, finals, final_t, latent)
+
+
+def conv_body(live_ref, scaled, before, after, weights, bias, out):
+    lanes = before.shape[1]
+    lines = [before[...]]
+    for r in range(scaled.shape[0] // W_P):
+        rows = scaled[r * W_P : (r + 1) * W_P]
+        lines += [rows[:, :lanes], rows[:, lanes:]]
+    lines.append(after[...])
+    grid = jnp.concatenate([line.astype(F32) for line in lines], axis=1).astype(BF16)
+    pixels = 2 * W_P
+    pixel = lax.broadcasted_iota(jnp.int32, (pixels, W_P), 0)
+    patch = lax.broadcasted_iota(jnp.int32, (pixels, W_P), 1)
+    half, odd = pixel // 2, pixel % 2
+    shifted = []
+    for parity, offset in ((0, -1), (0, 0), (1, 0), (1, 1)):
+        pick = jnp.logical_and(odd == parity, patch == half + offset)
+        pick = jnp.where(pick, 1.0, 0.0).astype(BF16)
+        shifted.append(jnp.dot(pick, grid, preferred_element_type=F32).astype(BF16))
+    live = live_ref[0] != 0
+    for line in range(out.shape[0]):
+        total = jnp.zeros((pixels, out.shape[2]), F32)
+        for k in range(4):
+            window = shifted[k][:, line * lanes : (line + 3) * lanes]
+            total += jnp.dot(window, weights[k], preferred_element_type=F32)
+        total = jnp.where(live, total + bias[...], 0.0)
+        out[line] = total.astype(BF16)
+
+
+def convolve(live, scaled, before, after, weights, bias):
+    lines = 2 * scaled.shape[0] // W_P
+    shape = (lines, 2 * W_P, weights.shape[2])
+    return pl.pallas_call(
+        conv_body,
+        out_shape=jax.ShapeDtypeStruct(shape, BF16),
+        in_specs=[pl.BlockSpec(memory_space=pltpu.SMEM)] + vmem_specs(5),
+        out_specs=vmem_specs(1)[0],
+        compiler_params=pltpu.CompilerParams(vmem_limit_bytes=12 << 20),
+        cost_estimate=pl.CostEstimate(flops=1000, bytes_accessed=1000, transcendentals=0),
+        name="convolve",
+    )(live, scaled, before, after, weights, bias)
+
+
+def conv_weights(conv_weight):
+    taps = conv_weight.reshape(3, 3, CH, -1)
+    none = jnp.zeros_like(taps[:, 0])
+    pairs = ((none, taps[:, 0]), (taps[:, 1], taps[:, 2]), (taps[:, 0], taps[:, 1]), (taps[:, 2], none))
+    return jnp.stack([jnp.stack(pair, axis=1).reshape(6 * CH, -1) for pair in pairs])
 
 
 def per_device(
@@ -403,27 +463,27 @@
     mlp_mine = jnp.concatenate(
         [mlp_in_weight.T, mlp_out_weight[:width].T, mlp_out_weight[width:].T], axis=0
     )
-    image_in = modulate(hidden[0], mods[0], mods[1])
+    gain, qkv_side = lax.optimization_barrier((1.0 + mods[1], qkv_t))
+    image_in = modulate(hidden[0], mods[0], gain)
     mlp_mine, image_in = lax.optimization_barrier((mlp_mine, image_in))
-    qkv_near = ring_first(qkv_t)
+    qkv_near = ring_first(qkv_t, qkv_side)
     qkv_next = ring_second(*qkv_near)
     far = jnp.concatenate(qkv_next[:2], axis=0)
     side_left, side_right, mlp_mine = lax.optimization_barrier((*qkv_next[2:], mlp_mine))
     qkv_far = far, swap(far, "img", 2)
     qkv_pieces = [qkv_t, *qkv_near, qkv_far[0], *qkv_next[2:], qkv_far[1]]
-    mlp_near = ring_first(mlp_mine)
+    mlp_near = ring_first(mlp_mine, mlp_mine)
 
     peer_in = swap(image_in, "img", 1)
     ready, peer_in = lax.optimization_barrier((marker(qkv_far[1]), peer_in))
     mine, theirs = project_qkv(chip, ready, image_in, peer_in, qkv_pieces)
     other = swap(theirs, "img", 1)
     heads = place_heads(core, mine, other, blocks)
-    parts = lax.all_to_all(heads, "blk", 0, 0, tiled=True)
-
     head = jnp.minimum(blk, HEADS - 1)
     right, head = lax.optimization_barrier((mlp_near[1], head))
     mlp_near = (mlp_near[0], right, mlp_near[2])
-    text_in = modulate(text_hidden[0], text_mod[0, 0], text_mod[0, 1])
+    parts = lax.all_to_all(heads, "blk", 0, 0, tiled=True)
+    text_in = modulate(text_hidden[0], text_mod[0, 0], 1.0 + text_mod[0, 1])
     text_cols = jnp.concatenate(
         [
             lax.dynamic_slice(text_weight, (0, start + head * HEAD), (width, HEAD))
@@ -445,6 +505,13 @@
     mixed = lax.all_to_all(mixed, "blk", 0, 0, tiled=True)[:HEADS].reshape(width_attn, tok_rows)
     near_pieces, next_pieces = [mlp_mine, *mlp_near], list(mlp_next[2:])
 
+    latent_p = latent[0].reshape(-1, 2, W_P, 2 * CH).transpose(0, 2, 1, 3)
+    latent_p = latent_p.reshape(tok_rows, 4 * CH)
+    conv_w = conv_weights(conv_weight)
+    live = (blk * tok_rows < counts).astype(jnp.int32)
+    step_value = step_index.astype(F32)
+    gap = plan(step_value + 1.0) - plan(step_value)
+    mixed, latent_p, conv_w = lax.optimization_barrier((mixed, latent_p, conv_w))
     updated, mlp_in = middle(mixed, hidden[0], mods, out_weight, marker(peer_low, peer_high, *next_pieces))
     mlp_cols = mlp_in_weight.shape[1]
     peer_mlp = swap(mlp_in, "img", 1)
@@ -455,38 +522,18 @@
         chip, core, act, peer_act, near_pieces + [high] + next_pieces + [peer_high]
     )
     peer_part = swap(sent_part, "img", 1)
-    predicted = last(core, own_part, peer_part, updated, mods, final_mod[0], final_weight.T)
-
-    patch_count = counts[0]
-    patch_rows = tok_rows // W_P
-    lat_rows = 2 * patch_rows
-    vel_lat = (
-        predicted.reshape(patch_rows, W_P, 2, 2, CH)
-        .transpose(0, 2, 1, 3, 4)
-        .reshape(lat_rows, 2 * W_P * CH)
-    )
-    global_rows = blk * lat_rows + jnp.arange(lat_rows, dtype=jnp.int32)
-    live_rows = (global_rows < 2 * (patch_count // W_P))[:, None]
-    velocity = jnp.where(live_rows, vel_lat, 0.0)
-    step_value = step_index[0].astype(F32)
-    sigma_gap = plan(step_value + 1.0) - plan(step_value)
-    next_lat = jnp.where(live_rows, latent[0] + sigma_gap * vel_lat, 0.0)
-    scaled = jnp.where(live_rows, next_lat / vae_scale + vae_offset, 0.0).astype(BF16)
-    framed = padded(scaled, "blk", 1)
-    padded_grid = jnp.pad(framed.reshape(lat_rows + 2, 2 * W_P, CH), ((0, 0), (1, 1), (0, 0)))
-    columns = jnp.concatenate(
-        [
-            padded_grid[row_off : row_off + lat_rows, col_off : col_off + 2 * W_P, :]
-            for row_off in range(3)
-            for col_off in range(3)
-        ],
-        axis=-1,
-    ).reshape(lat_rows * 2 * W_P, 9 * CH)
-    feature = jnp.dot(columns, conv_weight, preferred_element_type=F32) + conv_bias
-    feature = jnp.where(live_rows[:, :, None], feature.reshape(lat_rows, 2 * W_P, -1), 0.0).astype(
-        BF16
-    )
-    return (velocity[None], next_lat[None], feature[None])
+    velocity, next_lat, scaled, top, bottom = last(
+        core, live, gap, own_part, peer_part, updated, mods, final_mod[0], final_weight.T, latent_p
+    )
+    size = blocks
+    before = lax.ppermute(bottom, "blk", [(i, i + 1) for i in range(size - 1)])
+    after = lax.ppermute(top, "blk", [(i + 1, i) for i in range(size - 1)])
+    feature = convolve(live, scaled, before, after, conv_w, conv_bias[None])
+
+    def by_rows(x):
+        return x.reshape(-1, W_P, 2, 2 * CH).transpose(0, 2, 1, 3).reshape(latent[0].shape)
+
+    return (by_rows(velocity)[None], by_rows(next_lat)[None], feature[None])
 
 
 def solution(mesh):

time: 160 us -> 167 us (1.044)
  waiting for transfers between devices: 53.7 us -> 37.5 us
  local copies, waits for them, and re-layouts: 15 us -> 30.4 us
  starting transfers between devices: 56.8 us -> 59 us
  Pallas kernels: 24.3 us -> 26.5 us
    all_to_all x1, waiting for transfers between devices: 13.6 us -> 4.7 us  [per_device(): lax.all_to_all(mixed, 'blk', 0, 0, tiled=True)[:HEADS]]
    unnamed x50 -> x62, local copies, waits for them, and re-layouts: 4.73 us -> 10.7 us
    another operation x0 -> x6, local copies, waits for them, and re-layouts: none -> 5.25 us  [the longest x3 2.27 us: conv_weights(): jnp.stack(pair, axis=1).reshape(6 * CH, -1)]
    ppermute x10, waiting for transfers between devices: 12.1 us -> 8.67 us  [swap(): lax.ppermute(x, axis, [(i, i ^ bits) for i in range(lax.axis_size(axis))])]
    ppermute x12, waiting for transfers between devices: 23.7 us -> 20.4 us  [ring(): return lax.ppermute(x, axis, [(i, (i + step) % size) for i in range(size)])]
    ppermute x10, starting transfers between devices: 9.1 us -> 11.1 us  [swap(): lax.ppermute(x, axis, [(i, i ^ bits) for i in range(lax.axis_size(axis))])]
    slice x2, local copies, waits for them, and re-layouts: 2.67 us -> 0.88 us  [ring_second(): left[:half]]
    pallas_call x1 -> x2, Pallas kernels: 0.76 us -> 2.53 us  [the longest x1 1.7 us: convolve(): pl.pallas_call(conv_body, out_shape=jax.ShapeDtypeStruct(shape, BF16), in...]
  transfers between devices with their start and end apart: 26 -> 26, of which waited for: 12 -> 13; matrix products, arithmetic and copies ran while one was open for 9% -> 18% of each run, Pallas kernels for 9% -> 9%
where the time goes in v8:
time: 167 us; the launch traced here: 165 us
  starting transfers between devices  59 us (35%)
  waiting for transfers between devices  37.5 us (22%)
  local copies, waits for them, and re-layouts  30.4 us (18%)
  Pallas kernels  26.5 us (16%)
  other arithmetic  7.62 us (5%)
  between operations  2.53 us (2%)
  matrix products  1.79 us (1%)
    ppermute x12, waiting for transfers between devices, ring(): return lax.ppermute(x, axis, [(i, (i + step) % size) for i in range(size)])  20.4 us
    ppermute x12, starting transfers between devices, ring(): return lax.ppermute(x, axis, [(i, (i + step) % size) for i in range(size)])  20.2 us
    pallas_call x1, Pallas kernels, attend(): pl.pallas_call(attend_body, out_shape=jax.ShapeDtypeStruct((blocks, HEAD,...  11.7 us
    ppermute x10, starting transfers between devices, swap(): lax.ppermute(x, axis, [(i, i ^ bits) for i in range(lax.axis_size(axis))])  11.1 us
    unnamed x62, local copies, waits for them, and re-layouts  10.7 us
    all_to_all x1, starting transfers between devices, per_device(): lax.all_to_all(mixed, 'blk', 0, 0, tiled=True)[:HEADS]  9.74 us
    ppermute x10, waiting for transfers between devices, swap(): lax.ppermute(x, axis, [(i, i ^ bits) for i in range(lax.axis_size(axis))])  8.67 us
    all_to_all x1, starting transfers between devices, per_device(): parts = lax.all_to_all(heads, 'blk', 0, 0, tiled=True)  8.57 us
  transfers between devices with their start and end apart: 26, of which 13 were waited for; matrix products, arithmetic and copies ran while one was open for 18% of the time, Pallas kernels for 9%

profile of v8, /device:TPU:104, one launch (start us, length us, event | category | flops | bytes accessed | tf_op | source)
XLA Modules:
  0.0 165.3 jit_solution(11620583824545225384)
XLA Ops:
  0.6 1.6 collective-permute-start
  2.2 1.7 %collective-permute-start.2 = (bf16[144,1536]{1,0:T(8,128)(2,1)}, bf16[144,1536]{1,0:T(8,128)(2,1)S(1)}, u32[]{:S(2)}, u32[]{:S(2)}) collective-permute-start(bf16[144,1536]{1,0:T(8,128)(2,1)} %bitcast.63), channel_id=1, source_target_pairs={{0,12},{1,13},{2,14},{3,15},{4,0},{5,1},{6,2},{7,3},{8,4},{9,5},{1... | collective-permute-start | bytes 1327112 | tf_op jit(solution)/shard_map/ppermute | solution.py:54
  4.7 2.4 %collective-permute-start.6 = (bf16[144,1536]{1,0:T(8,128)(2,1)}, bf16[144,1536]{1,0:T(8,128)(2,1)S(1)}, u32[]{:S(2)}, u32[]{:S(2)}) collective-permute-start(bf16[144,1536]{1,0:T(8,128)(2,1)} %bitcast.64), channel_id=1, source_target_pairs={{0,2},{1,3},{2,0},{3,1},{4,6},{5,7},{6,4},{7,5},{8,10},{9,11},{10,... | collective-permute-start | bytes 1327112 | tf_op jit(solution)/shard_map/ppermute | solution.py:38
  12.4 1.6 collective-permute-done.refs_1_
  15.8 2.7 %collective-permute-start.3 = (bf16[72,1536]{1,0:T(8,128)(2,1)S(1)}, bf16[72,1536]{1,0:T(8,128)(2,1)S(1)}, u32[]{:S(2)}, u32[]{:S(2)}) collective-permute-start(bf16[72,1536]{1,0:T(8,128)(2,1)S(1)} %slice.61), channel_id=1, source_target_pairs={{0,12},{1,13},{2,14},{3,15},{4,0},{5,1},{6,2},{7,3},{8,4},{9,5},{1... | collective-permute-start | bytes 663560 | tf_op jit(solution)/shard_map/ppermute | solution.py:54
  18.4 3.2 %collective-permute-start.8 = (bf16[144,1536]{1,0:T(8,128)(2,1)S(1)}, bf16[144,1536]{1,0:T(8,128)(2,1)S(1)}, u32[]{:S(2)}, u32[]{:S(2)}) collective-permute-start(bf16[144,1536]{1,0:T(8,128)(2,1)S(1)} %collective-permute-done.6.refs_3_), channel_id=1, source_target_pairs={{0,12},{1,13},{2,14},{3,15},{4,0},{5,1},{6,2},{7,3},{8,4},{9,5},{1... | collective-permute-start | bytes 1327112 | tf_op jit(solution)/shard_map/ppermute | solution.py:54
  21.7 2.5 %collective-permute-done.3 = bf16[72,1536]{1,0:T(8,128)(2,1)S(1)} collective-permute-done((bf16[72,1536]{1,0:T(8,128)(2,1)S(1)}, bf16[72,1536]{1,0:T(8,128)(2,1)S(1)}, u32[]{:S(2)}, u32[]{:S(2)}) %collective-permute-start.3) | collective-permute-done | bytes 221216 | tf_op jit(solution)/shard_map/ppermute | solution.py:54
  24.2 2.4 %collective-permute-start.4 = (bf16[144,1536]{1,0:T(8,128)(2,1)S(1)}, bf16[144,1536]{1,0:T(8,128)(2,1)S(1)}, u32[]{:S(2)}, u32[]{:S(2)}) collective-permute-start(bf16[144,1536]{1,0:T(8,128)(2,1)S(1)} %constant_dynamic-update-slice_fusion.refs_4_), channel_id=1, source_target_pairs={{0,2},{1,3},{2,0},{3,1},{4,6},{5,7},{6,4},{7,5},{8,10},{9,11},{10,... | collective-permute-start | bytes 1327112 | tf_op jit(solution)/shard_map/ppermute | solution.py:38
  27.0 4.8 %collective-permute-done.7.refs_5_ = bf16[144,1536]{1,0:T(8,128)(2,1)S(1)} collective-permute-done((bf16[144,1536]{1,0:T(8,128)(2,1)S(1)}, bf16[144,1536]{1,0:T(8,128)(2,1)S(1)}, u32[]{:S(2)}, u32[]{:S(2)}) %collective-permute-start.7) | collective-permute-done | bytes 442400 | tf_op jit(solution)/shard_map/ppermute | solution.py:54
  33.2 3.7 %collective-permute-start.11 = (bf16[384,1536]{1,0:T(8,128)(2,1)S(1)}, bf16[384,1536]{1,0:T(8,128)(2,1)S(1)}, u32[]{:S(2)}, u32[]{:S(2)}) collective-permute-start(bf16[384,1536]{1,0:T(8,128)(2,1)S(1)} %pad_maximum_fusion.refs_0_), channel_id=1, source_target_pairs={{0,12},{1,13},{2,14},{3,15},{4,0},{5,1},{6,2},{7,3},{8,4},{9,5},{1... | collective-permute-start | bytes 3538952 | tf_op jit(solution)/shard_map/ppermute | solution.py:54
  36.9 2.3 %collective-permute-start.12 = (bf16[384,1536]{1,0:T(8,128)(2,1)S(1)}, bf16[384,1536]{1,0:T(8,128)(2,1)}, u32[]{:S(2)}, u32[]{:S(2)}) collective-permute-start(bf16[384,1536]{1,0:T(8,128)(2,1)S(1)} %pad_maximum_fusion.refs_0_), channel_id=1, source_target_pairs={{0,2},{1,3},{2,0},{3,1},{4,6},{5,7},{6,4},{7,5},{8,10},{9,11},{10,... | collective-permute-start | bytes 3538952 | tf_op jit(solution)/shard_map/ppermute | solution.py:38
  39.3 2.2 %project_qkv.1 = (bf16[8,144,128]{2,1,0:T(8,128)(2,1)S(1)}, bf16[8,144,128]{2,1,0:T(8,128)(2,1)S(1)}) custom-call(s32[1]{0:T(128)} %bitcast.2.chip_ref, bf16[16,128]{1,0:T(8,128)(2,1)S(1)} %marker.3.ready, bf16[128,1536]{1,0:T(8,128)(2,1)} %fusion.12.own_x, bf16[128,1536]{1,0:T(8,128)(2,1)} %collective-permute-done.5.peer_x, bf16[144,1536]{1,0:T(8,128)(2,1)S(1)} %bitcast.65, ...), custom_call_target="tpu_custom_call" | custom-call | flops 1000 | bytes 1000 | tf_op jit(solution)/shard_map/project_qkv/pallas_call | solution.py:96
  44.2 8.6 %all-to-all-start = ((bf16[16,192,128]{2,1,0:T(8,128)(2,1)}), bf16[16,192,128]{2,1,0:T(8,128)(2,1)}, u32[]{:S(2)}, u32[]{:S(2)}) async-start(bf16[16,192,128]{2,1,0:T(8,128)(2,1)} %copy-done.2), calls=%async_computation | async-start | bytes 1572864 | tf_op jit(solution)/shard_map/all_to_all | solution.py:485
  52.7 9.2 %collective-permute-done.11.refs_1_.refs_2_ = bf16[384,1536]{1,0:T(8,128)(2,1)S(1)} collective-permute-done((bf16[384,1536]{1,0:T(8,128)(2,1)S(1)}, bf16[384,1536]{1,0:T(8,128)(2,1)S(1)}, u32[]{:S(2)}, u32[]{:S(2)}) %collective-permute-start.11) | collective-permute-done | bytes 1179680 | tf_op jit(solution)/shard_map/ppermute | solution.py:54
  62.8 3.7 %collective-permute-start.14 = (bf16[192,1536]{1,0:T(8,128)(2,1)}, bf16[192,1536]{1,0:T(8,128)(2,1)}, u32[]{:S(2)}, u32[]{:S(2)}) collective-permute-start(bf16[192,1536]{1,0:T(8,128)(2,1)} %slice.56), channel_id=1, source_target_pairs={{0,12},{1,13},{2,14},{3,15},{4,0},{5,1},{6,2},{7,3},{8,4},{9,5},{1... | collective-permute-start | bytes 1769480 | tf_op jit(solution)/shard_map/ppermute | solution.py:54
  68.2 4.3 %collective-permute-done.12.refs_2_.refs_3_ = bf16[384,1536]{1,0:T(8,128)(2,1)} collective-permute-done((bf16[384,1536]{1,0:T(8,128)(2,1)S(1)}, bf16[384,1536]{1,0:T(8,128)(2,1)}, u32[]{:S(2)}, u32[]{:S(2)}) %collective-permute-start.12) | collective-permute-done | bytes 1179680 | tf_op jit(solution)/shard_map/ppermute | solution.py:38
  72.5 3.2 %collective-permute-start.18 = (bf16[384,1536]{1,0:T(8,128)(2,1)}, bf16[384,1536]{1,0:T(8,128)(2,1)}, u32[]{:S(2)}, u32[]{:S(2)}) collective-permute-start(bf16[384,1536]{1,0:T(8,128)(2,1)} %collective-permute-done.12.refs_2_.refs_3_), channel_id=1, source_target_pairs={{0,12},{1,13},{2,14},{3,15},{4,0},{5,1},{6,2},{7,3},{8,4},{9,5},{1... | collective-permute-start | bytes 3538952 | tf_op jit(solution)/shard_map/ppermute | solution.py:54
  78.0 1.8 %convolution_convert_fusion = bf16[128,154]{0,1:T(8,128)(2,1)} fusion(bf16[1,154,1536]{2,1,0:T(8,128)(2,1)S(1)} %copy-done.24, f32[1536]{0:T(1024)S(1)} %copy-done.27, f32[1536]{0:T(1024)S(1)} %get-tuple-element.61, f32[154]{0:T(256)} %add_rsqrt_fusion, f32[154]{0:T(256)S(1)} %copy-done.29, bf16[1536,64]{1,0:T(8,128)(2,1)S(1)} %get-tuple-element.64, ...), kind=kOutput, calls=%fused_computation.3 | convolution fusion | flops 62780672 | bytes 919248 | tf_op jit(solution)/shard_map/dot_general | solution.py:494
  83.6 11.7 %attend.1 = bf16[16,64,128]{2,1,0:T(8,128)(2,1)S(1)} custom-call(s32[1]{0:T(128)S(6)} %copy.45.count_ref, bf16[16,192,128]{2,1,0:T(8,128)(2,1)} %all-to-all-done.parts, bf16[128,256]{1,0:T(8,128)(2,1)S(1)} %copy-done.19, bf16[16,128]{1,0:T(8,128)(2,1)S(1)} %marker.4.mark), custom_call_target="tpu_custom_call" | custom-call | flops 1000 | bytes 1000 | tf_op jit(solution)/shard_map/attend/pallas_call | solution.py:216
  96.0 2.3 %collective-permute-start.15 = (bf16[192,1536]{1,0:T(8,128)(2,1)}, bf16[192,1536]{1,0:T(8,128)(2,1)}, u32[]{:S(2)}, u32[]{:S(2)}) collective-permute-start(bf16[192,1536]{1,0:T(8,128)(2,1)} %collective-permute-done.13.refs_4_), channel_id=1, source_target_pairs={{0,2},{1,3},{2,0},{3,1},{4,6},{5,7},{6,4},{7,5},{8,10},{9,11},{10,... | collective-permute-start | bytes 1769480 | tf_op jit(solution)/shard_map/ppermute | solution.py:38
  100.9 9.7 %all-to-all-start.1 = ((bf16[16,64,128]{2,1,0:T(8,128)(2,1)}), bf16[16,64,128]{2,1,0:T(8,128)(2,1)}, u32[]{:S(2)}, u32[]{:S(2)}) async-start(bf16[16,64,128]{2,1,0:T(8,128)(2,1)} %copy-done.5), calls=%async_computation.1 | async-start | bytes 524288 | tf_op jit(solution)/shard_map/all_to_all | solution.py:505
  114.3 1.6 copy.34
  118.5 1.7 %pad_maximum_fusion.1.weights = bf16[4,96,512]{2,1,0:T(8,128)(2,1)} fusion(bf16[1,96,512]{2,1,0:T(8,128)(2,1)} %bitcast.77, bf16[1,96,512]{2,1,0:T(8,128)(2,1)S(1)} %bitcast.79, bf16[1,96,512]{2,1,0:T(8,128)(2,1)S(1)} %bitcast.78, bf16[1,96,512]{2,1,0:T(8,128)(2,1)} %bitcast.76), kind=kLoop, calls=%fused_computation.26 | loop fusion | flops 589824 | bytes 786432 | tf_op jit(solution)/shard_map/stack | solution.py:433
  120.2 4.7 %all-to-all-done.1 = bf16[16,64,128]{2,1,0:T(8,128)(2,1)} async-done(((bf16[16,64,128]{2,1,0:T(8,128)(2,1)}), bf16[16,64,128]{2,1,0:T(8,128)(2,1)}, u32[]{:S(2)}, u32[]{:S(2)}) %all-to-all-start.1) | async-done | bytes 262176 | tf_op jit(solution)/shard_map/all_to_all | solution.py:505
  129.4 1.7 %collective-permute-done.19.peer_x = bf16[128,1536]{1,0:T(8,128)(2,1)S(1)} collective-permute-done((bf16[128,1536]{1,0:T(8,128)(2,1)S(1)}, bf16[128,1536]{1,0:T(8,128)(2,1)S(1)}, u32[]{:S(2)}, u32[]{:S(2)}) %collective-permute-start.19) | collective-permute-done | bytes 393248 | tf_op jit(solution)/shard_map/ppermute | solution.py:38
  131.1 3.4 %mlp_first.1.own_act = bf16[8,192,256]{2,1,0:T(8,128)(2,1)S(1)} custom-call(s32[1]{0:T(128)} %bitcast.2.chip_ref, bf16[128,1536]{1,0:T(8,128)(2,1)S(1)} %get-tuple-element.50.own_x, bf16[128,1536]{1,0:T(8,128)(2,1)S(1)} %collective-permute-done.19.peer_x, bf16[384,1536]{1,0:T(8,128)(2,1)S(1)} %pad_maximum_fusion.refs_0_, ...), custom_call_target="tpu_custom_call" | custom-call | flops 1000 | bytes 1000 | tf_op jit(solution)/shard_map/mlp_first/pallas_call | solution.py:286
  134.8 2.1 %collective-permute-done.20.peer_act = bf16[8,192,256]{2,1,0:T(8,128)(2,1)S(1)} collective-permute-done((bf16[8,192,256]{2,1,0:T(8,128)(2,1)S(1)}, bf16[8,192,256]{2,1,0:T(8,128)(2,1)S(1)}, u32[]{:S(2)}, u32[]{:S(2)}) %collective-permute-start.20) | collective-permute-done | bytes 786464 | tf_op jit(solution)/shard_map/ppermute | solution.py:38
  136.9 4.1 %mlp_second.1 = (f32[8,96,128]{2,1,0:T(8,128)S(1)}, f32[8,96,128]{2,1,0:T(8,128)}) custom-call(s32[1]{0:T(128)} %bitcast.2.chip_ref, s32[1]{0:T(128)} %bitcast.core_ref, bf16[8,192,256]{2,1,0:T(8,128)(2,1)S(1)} %mlp_first.1.own_act, bf16[8,192,256]{2,1,0:T(8,128)(2,1)S(1)} %collective-permute-done.20.peer_act, ...), custom_call_target="tpu_custom_call" | custom-call | flops 1000 | bytes 1000 | tf_op jit(solution)/shard_map/mlp_second/pallas_call | solution.py:325
  148.4 7.4 %collective-permute-start.22 = (bf16[64,32]{1,0:T(8,128)(2,1)S(1)}, bf16[64,32]{1,0:T(8,128)(2,1)S(1)}, u32[]{:S(2)}, u32[]{:S(2)}) collective-permute-start(bf16[64,32]{1,0:T(8,128)(2,1)S(1)} %get-tuple-element.58), channel_id=1, source_target_pairs={{0,16},{16,32},{32,48},{48,64},{64,80},{80,96},{96,112},{112,128},... | collective-permute-start | bytes 12296 | tf_op jit(solution)/shard_map/ppermute | solution.py:529
  155.8 1.9 %collective-permute-start.23 = (bf16[64,32]{1,0:T(8,128)(2,1)S(1)}, bf16[64,32]{1,0:T(8,128)(2,1)S(1)}, u32[]{:S(2)}, u32[]{:S(2)}) collective-permute-start(bf16[64,32]{1,0:T(8,128)(2,1)S(1)} %get-tuple-element.59), channel_id=1, source_target_pairs={{16,0},{32,16},{48,32},{64,48},{80,64},{96,80},{112,96},{128,112},... | collective-permute-start | bytes 12296 | tf_op jit(solution)/shard_map/ppermute | solution.py:530
  159.8 3.7 %collective-permute-done.23.after = bf16[64,32]{1,0:T(8,128)(2,1)S(1)} collective-permute-done((bf16[64,32]{1,0:T(8,128)(2,1)S(1)}, bf16[64,32]{1,0:T(8,128)(2,1)S(1)}, u32[]{:S(2)}, u32[]{:S(2)}) %collective-permute-start.23) | collective-permute-done | bytes 4128 | tf_op jit(solution)/shard_map/ppermute | solution.py:530
  163.6 1.7 %convolve.1 = bf16[4,128,512]{2,1,0:T(8,128)(2,1)} custom-call(s32[1]{0:T(128)S(6)} %convert_element_type.26.live_ref, bf16[128,64]{1,0:T(8,128)(2,1)S(1)} %get-tuple-element.57.scaled, bf16[64,32]{1,0:T(8,128)(2,1)S(1)} %collective-permute-done.22.before, bf16[64,32]{1,0:T(8,128)(2,1)S(1)} %collective-permute-done.23.after, ...), custom_call_target="tpu_custom_call" | custom-call | flops 1000 | bytes 1000 | tf_op jit(solution)/shard_map/convolve/pallas_call | solution.py:418
  (134 shorter events, 42.9 us)
Async XLA Ops:
  0.6 13.4 %collective-permute-start = (bf16[144,1536]{1,0:T(8,128)(2,1)}, bf16[144,1536]{1,0:T(8,128)(2,1)S(1)}, u32[]{:S(2)}, u32[]{:S(2)}) collective-permute-start(bf16[144,1536]{1,0:T(8,128)(2,1)} %bitcast.62), channel_id=1, source_target_pairs={{0,4},{1,5},{2,6},{3,7},{4,8},{5,9},{6,10},{7,11},{8,12},{9,13},{1... | collective-permute-start | bytes 1327112 | tf_op jit(solution)/shard_map/ppermute | solution.py:54
  2.2 13.5 %collective-permute-start.2 = (bf16[144,1536]{1,0:T(8,128)(2,1)}, bf16[144,1536]{1,0:T(8,128)(2,1)S(1)}, u32[]{:S(2)}, u32[]{:S(2)}) collective-permute-start(bf16[144,1536]{1,0:T(8,128)(2,1)} %bitcast.63), channel_id=1, source_target_pairs={{0,12},{1,13},{2,14},{3,15},{4,0},{5,1},{6,2},{7,3},{8,4},{9,5},{1... | collective-permute-start | bytes 1327112 | tf_op jit(solution)/shard_map/ppermute | solution.py:54
  4.7 13.7 %collective-permute-start.6 = (bf16[144,1536]{1,0:T(8,128)(2,1)}, bf16[144,1536]{1,0:T(8,128)(2,1)S(1)}, u32[]{:S(2)}, u32[]{:S(2)}) collective-permute-start(bf16[144,1536]{1,0:T(8,128)(2,1)} %bitcast.64), channel_id=1, source_target_pairs={{0,2},{1,3},{2,0},{3,1},{4,6},{5,7},{6,4},{7,5},{8,10},{9,11},{10,... | collective-permute-start | bytes 1327112 | tf_op jit(solution)/shard_map/ppermute | solution.py:38
  14.1 7.6 %collective-permute-start.1 = (bf16[72,1536]{1,0:T(8,128)(2,1)S(1)}, bf16[72,1536]{1,0:T(8,128)(2,1)S(1)}, u32[]{:S(2)}, u32[]{:S(2)}) collective-permute-start(bf16[72,1536]{1,0:T(8,128)(2,1)S(1)} %slice.60), channel_id=1, source_target_pairs={{0,4},{1,5},{2,6},{3,7},{4,8},{5,9},{6,10},{7,11},{8,12},{9,13},{1... | collective-permute-start | bytes 663560 | tf_op jit(solution)/shard_map/ppermute | solution.py:54
  14.9 24.3 %collective-permute-start.5 = (bf16[128,1536]{1,0:T(8,128)(2,1)}, bf16[128,1536]{1,0:T(8,128)(2,1)}, u32[]{:S(2)}, u32[]{:S(2)}) collective-permute-start(bf16[128,1536]{1,0:T(8,128)(2,1)} %fusion.12.own_x), channel_id=1, source_target_pairs={{0,1},{1,0},{2,3},{3,2},{4,5},{5,4},{6,7},{7,6},{8,9},{9,8},{10,11... | collective-permute-start | bytes 1179656 | tf_op jit(solution)/shard_map/ppermute | solution.py:38
  15.7 16.1 %copy-start.8 = (bf16[144,1536]{1,0:T(8,128)(2,1)}, bf16[144,1536]{1,0:T(8,128)(2,1)S(1)}, u32[]{:S(2)}) copy-start(bf16[144,1536]{1,0:T(8,128)(2,1)S(1)} %collective-permute-done.2.refs_2_) | copy-start | bytes 1327108
  15.8 8.4 %collective-permute-start.3 = (bf16[72,1536]{1,0:T(8,128)(2,1)S(1)}, bf16[72,1536]{1,0:T(8,128)(2,1)S(1)}, u32[]{:S(2)}, u32[]{:S(2)}) collective-permute-start(bf16[72,1536]{1,0:T(8,128)(2,1)S(1)} %slice.61), channel_id=1, source_target_pairs={{0,12},{1,13},{2,14},{3,15},{4,0},{5,1},{6,2},{7,3},{8,4},{9,5},{1... | collective-permute-start | bytes 663560 | tf_op jit(solution)/shard_map/ppermute | solution.py:54
  18.4 13.5 %copy-start.13 = (bf16[144,1536]{1,0:T(8,128)(2,1)}, bf16[144,1536]{1,0:T(8,128)(2,1)S(1)}, u32[]{:S(2)}) copy-start(bf16[144,1536]{1,0:T(8,128)(2,1)S(1)} %collective-permute-done.6.refs_3_) | copy-start | bytes 1327108
  18.4 13.5 %collective-permute-start.7 = (bf16[144,1536]{1,0:T(8,128)(2,1)S(1)}, bf16[144,1536]{1,0:T(8,128)(2,1)S(1)}, u32[]{:S(2)}, u32[]{:S(2)}) collective-permute-start(bf16[144,1536]{1,0:T(8,128)(2,1)S(1)} %collective-permute-done.6.refs_3_), channel_id=1, source_target_pairs={{0,4},{1,5},{2,6},{3,7},{4,8},{5,9},{6,10},{7,11},{8,12},{9,13},{1... | collective-permute-start | bytes 1327112 | tf_op jit(solution)/shard_map/ppermute | solution.py:54
  18.4 14.8 %collective-permute-start.8 = (bf16[144,1536]{1,0:T(8,128)(2,1)S(1)}, bf16[144,1536]{1,0:T(8,128)(2,1)S(1)}, u32[]{:S(2)}, u32[]{:S(2)}) collective-permute-start(bf16[144,1536]{1,0:T(8,128)(2,1)S(1)} %collective-permute-done.6.refs_3_), channel_id=1, source_target_pairs={{0,12},{1,13},{2,14},{3,15},{4,0},{5,1},{6,2},{7,3},{8,4},{9,5},{1... | collective-permute-start | bytes 1327112 | tf_op jit(solution)/shard_map/ppermute | solution.py:54
  24.2 15.0 %collective-permute-start.4 = (bf16[144,1536]{1,0:T(8,128)(2,1)S(1)}, bf16[144,1536]{1,0:T(8,128)(2,1)S(1)}, u32[]{:S(2)}, u32[]{:S(2)}) collective-permute-start(bf16[144,1536]{1,0:T(8,128)(2,1)S(1)} %constant_dynamic-update-slice_fusion.refs_4_), channel_id=1, source_target_pairs={{0,2},{1,3},{2,0},{3,1},{4,6},{5,7},{6,4},{7,5},{8,10},{9,11},{10,... | collective-permute-start | bytes 1327112 | tf_op jit(solution)/shard_map/ppermute | solution.py:38
  26.7 12.5 %copy-start.28 = (f32[154]{0:T(256)}, f32[154]{0:T(256)S(1)}, u32[]{:S(2)}) copy-start(f32[154]{0:T(256)S(1)} %broadcast_multiply_fusion) | copy-start | bytes 1852
  27.0 12.2 %copy-start.12 = (bf16[1536,144]{0,1:T(8,128)(2,1)S(1)}, bf16[1536,144]{0,1:T(8,128)(2,1)}, u32[]{:S(2)}) copy-start(bf16[1536,144]{0,1:T(8,128)(2,1)} %param.24) | copy-start | bytes 1327108
  33.2 28.7 %collective-permute-start.11 = (bf16[384,1536]{1,0:T(8,128)(2,1)S(1)}, bf16[384,1536]{1,0:T(8,128)(2,1)S(1)}, u32[]{:S(2)}, u32[]{:S(2)}) collective-permute-start(bf16[384,1536]{1,0:T(8,128)(2,1)S(1)} %pad_maximum_fusion.refs_0_), channel_id=1, source_target_pairs={{0,12},{1,13},{2,14},{3,15},{4,0},{5,1},{6,2},{7,3},{8,4},{9,5},{1... | collective-permute-start | bytes 3538952 | tf_op jit(solution)/shard_map/ppermute | solution.py:54
  36.9 35.6 %collective-permute-start.12 = (bf16[384,1536]{1,0:T(8,128)(2,1)S(1)}, bf16[384,1536]{1,0:T(8,128)(2,1)}, u32[]{:S(2)}, u32[]{:S(2)}) collective-permute-start(bf16[384,1536]{1,0:T(8,128)(2,1)S(1)} %pad_maximum_fusion.refs_0_), channel_id=1, source_target_pairs={{0,2},{1,3},{2,0},{3,1},{4,6},{5,7},{6,4},{7,5},{8,10},{9,11},{10,... | collective-permute-start | bytes 3538952 | tf_op jit(solution)/shard_map/ppermute | solution.py:38
  39.2 28.2 %collective-permute-start.10 = (bf16[384,1536]{1,0:T(8,128)(2,1)S(1)}, bf16[384,1536]{1,0:T(8,128)(2,1)S(1)}, u32[]{:S(2)}, u32[]{:S(2)}) collective-permute-start(bf16[384,1536]{1,0:T(8,128)(2,1)S(1)} %pad_maximum_fusion.refs_0_), channel_id=1, source_target_pairs={{0,4},{1,5},{2,6},{3,7},{4,8},{5,9},{6,10},{7,11},{8,12},{9,13},{1... | collective-permute-start | bytes 3538952 | tf_op jit(solution)/shard_map/ppermute | solution.py:54
  41.5 1.7 %collective-permute-start.9 = (bf16[8,144,128]{2,1,0:T(8,128)(2,1)S(1)}, bf16[8,144,128]{2,1,0:T(8,128)(2,1)S(1)}, u32[]{:S(2)}, u32[]{:S(2)}) collective-permute-start(bf16[8,144,128]{2,1,0:T(8,128)(2,1)S(1)} %get-tuple-element.38), channel_id=1, source_target_pairs={{0,1},{1,0},{2,3},{3,2},{4,5},{5,4},{6,7},{7,6},{8,9},{9,8},{10,11... | collective-permute-start | bytes 884744 | tf_op jit(solution)/shard_map/ppermute | solution.py:38
  44.2 38.6 %all-to-all-start = ((bf16[16,192,128]{2,1,0:T(8,128)(2,1)}), bf16[16,192,128]{2,1,0:T(8,128)(2,1)}, u32[]{:S(2)}, u32[]{:S(2)}) async-start(bf16[16,192,128]{2,1,0:T(8,128)(2,1)} %copy-done.2), calls=%async_computation | async-start | bytes 1572864 | tf_op jit(solution)/shard_map/all_to_all | solution.py:485
  62.8 33.2 %collective-permute-start.14 = (bf16[192,1536]{1,0:T(8,128)(2,1)}, bf16[192,1536]{1,0:T(8,128)(2,1)}, u32[]{:S(2)}, u32[]{:S(2)}) collective-permute-start(bf16[192,1536]{1,0:T(8,128)(2,1)} %slice.56), channel_id=1, source_target_pairs={{0,12},{1,13},{2,14},{3,15},{4,0},{5,1},{6,2},{7,3},{8,4},{9,5},{1... | collective-permute-start | bytes 1769480 | tf_op jit(solution)/shard_map/ppermute | solution.py:54
  68.2 27.8 %collective-permute-start.13 = (bf16[192,1536]{1,0:T(8,128)(2,1)}, bf16[192,1536]{1,0:T(8,128)(2,1)}, u32[]{:S(2)}, u32[]{:S(2)}) collective-permute-start(bf16[192,1536]{1,0:T(8,128)(2,1)} %slice.62), channel_id=1, source_target_pairs={{0,4},{1,5},{2,6},{3,7},{4,8},{5,9},{6,10},{7,11},{8,12},{9,13},{1... | collective-permute-start | bytes 1769480 | tf_op jit(solution)/shard_map/ppermute | solution.py:54
  72.5 53.4 %collective-permute-start.17 = (bf16[384,1536]{1,0:T(8,128)(2,1)}, bf16[384,1536]{1,0:T(8,128)(2,1)}, u32[]{:S(2)}, u32[]{:S(2)}) collective-permute-start(bf16[384,1536]{1,0:T(8,128)(2,1)} %collective-permute-done.12.refs_2_.refs_3_), channel_id=1, source_target_pairs={{0,4},{1,5},{2,6},{3,7},{4,8},{5,9},{6,10},{7,11},{8,12},{9,13},{1... | collective-permute-start | bytes 3538952 | tf_op jit(solution)/shard_map/ppermute | solution.py:54
  72.5 53.4 %collective-permute-start.18 = (bf16[384,1536]{1,0:T(8,128)(2,1)}, bf16[384,1536]{1,0:T(8,128)(2,1)}, u32[]{:S(2)}, u32[]{:S(2)}) collective-permute-start(bf16[384,1536]{1,0:T(8,128)(2,1)} %collective-permute-done.12.refs_2_.refs_3_), channel_id=1, source_target_pairs={{0,12},{1,13},{2,14},{3,15},{4,0},{5,1},{6,2},{7,3},{8,4},{9,5},{1... | collective-permute-start | bytes 3538952 | tf_op jit(solution)/shard_map/ppermute | solution.py:54
  96.0 29.9 %collective-permute-start.15 = (bf16[192,1536]{1,0:T(8,128)(2,1)}, bf16[192,1536]{1,0:T(8,128)(2,1)}, u32[]{:S(2)}, u32[]{:S(2)}) collective-permute-start(bf16[192,1536]{1,0:T(8,128)(2,1)} %collective-permute-done.13.refs_4_), channel_id=1, source_target_pairs={{0,2},{1,3},{2,0},{3,1},{4,6},{5,7},{6,4},{7,5},{8,10},{9,11},{10,... | collective-permute-start | bytes 1769480 | tf_op jit(solution)/shard_map/ppermute | solution.py:38
  98.3 27.6 %collective-permute-start.16 = (bf16[192,1536]{1,0:T(8,128)(2,1)}, bf16[192,1536]{1,0:T(8,128)(2,1)}, u32[]{:S(2)}, u32[]{:S(2)}) collective-permute-start(bf16[192,1536]{1,0:T(8,128)(2,1)} %collective-permute-done.14.refs_4_), channel_id=1, source_target_pairs={{0,2},{1,3},{2,0},{3,1},{4,6},{5,7},{6,4},{7,5},{8,10},{9,11},{10,... | collective-permute-start | bytes 1769480 | tf_op jit(solution)/shard_map/ppermute | solution.py:38
  100.9 24.0 %all-to-all-start.1 = ((bf16[16,64,128]{2,1,0:T(8,128)(2,1)}), bf16[16,64,128]{2,1,0:T(8,128)(2,1)}, u32[]{:S(2)}, u32[]{:S(2)}) async-start(bf16[16,64,128]{2,1,0:T(8,128)(2,1)} %copy-done.5), calls=%async_computation.1 | async-start | bytes 524288 | tf_op jit(solution)/shard_map/all_to_all | solution.py:505
  129.4 1.7 %collective-permute-start.19 = (bf16[128,1536]{1,0:T(8,128)(2,1)S(1)}, bf16[128,1536]{1,0:T(8,128)(2,1)S(1)}, u32[]{:S(2)}, u32[]{:S(2)}) collective-permute-start(bf16[128,1536]{1,0:T(8,128)(2,1)S(1)} %get-tuple-element.50.own_x), channel_id=1, source_target_pairs={{0,1},{1,0},{2,3},{3,2},{4,5},{5,4},{6,7},{7,6},{8,9},{9,8},{10,11... | collective-permute-start | bytes 1179656 | tf_op jit(solution)/shard_map/ppermute | solution.py:38
  134.5 2.4 %collective-permute-start.20 = (bf16[8,192,256]{2,1,0:T(8,128)(2,1)S(1)}, bf16[8,192,256]{2,1,0:T(8,128)(2,1)S(1)}, u32[]{:S(2)}, u32[]{:S(2)}) collective-permute-start(bf16[8,192,256]{2,1,0:T(8,128)(2,1)S(1)} %mlp_first.1.own_act), channel_id=1, source_target_pairs={{0,1},{1,0},{2,3},{3,2},{4,5},{5,4},{6,7},{7,6},{8,9},{9,8},{10,11... | collective-permute-start | bytes 2359304 | tf_op jit(solution)/shard_map/ppermute | solution.py:38
  141.8 1.9 %collective-permute-start.21 = (f32[8,96,128]{2,1,0:T(8,128)}, f32[8,96,128]{2,1,0:T(8,128)S(1)}, u32[]{:S(2)}, u32[]{:S(2)}) collective-permute-start(f32[8,96,128]{2,1,0:T(8,128)} %get-tuple-element.52), channel_id=1, source_target_pairs={{0,1},{1,0},{2,3},{3,2},{4,5},{5,4},{6,7},{7,6},{8,9},{9,8},{10,11... | collective-permute-start | bytes 1179656 | tf_op jit(solution)/shard_map/ppermute | solution.py:38
  147.5 16.0 %copy-start.4 = (bf16[4,96,512]{2,1,0:T(8,128)(2,1)S(1)}, bf16[4,96,512]{2,1,0:T(8,128)(2,1)}, u32[]{:S(2)}) copy-start(bf16[4,96,512]{2,1,0:T(8,128)(2,1)} %pad_maximum_fusion.1.weights) | copy-start | bytes 1179652
  147.5 16.0 %copy-start.22 = (f32[512]{0:T(512)S(1)}, f32[512]{0:T(512)}, u32[]{:S(2)}) copy-start(f32[512]{0:T(512)} %param.31) | copy-start | bytes 6148
  148.4 11.4 %collective-permute-start.22 = (bf16[64,32]{1,0:T(8,128)(2,1)S(1)}, bf16[64,32]{1,0:T(8,128)(2,1)S(1)}, u32[]{:S(2)}, u32[]{:S(2)}) collective-permute-start(bf16[64,32]{1,0:T(8,128)(2,1)S(1)} %get-tuple-element.58), channel_id=1, source_target_pairs={{0,16},{16,32},{32,48},{48,64},{64,80},{80,96},{96,112},{112,128},... | collective-permute-start | bytes 12296 | tf_op jit(solution)/shard_map/ppermute | solution.py:529
  155.8 7.7 %collective-permute-start.23 = (bf16[64,32]{1,0:T(8,128)(2,1)S(1)}, bf16[64,32]{1,0:T(8,128)(2,1)S(1)}, u32[]{:S(2)}, u32[]{:S(2)}) collective-permute-start(bf16[64,32]{1,0:T(8,128)(2,1)S(1)} %get-tuple-element.59), channel_id=1, source_target_pairs={{16,0},{32,16},{48,32},{64,48},{80,64},{96,80},{112,96},{128,112},... | collective-permute-start | bytes 12296 | tf_op jit(solution)/shard_map/ppermute | solution.py:530
  (24 other events, 79.8 us)

commit v9 on v8

--- a/solution.py
+++ b/solution.py
@@ -146,6 +146,43 @@
     )(core, mine, other)
 
 
+def text_body(head_ref, hidden, mods, key_w, value_w, out, turned):
+    odd = head_ref[0] % 2 != 0
+    rows = hidden.shape[0]
+    states = layer_norm(hidden[...].astype(F32), mods[0:1], mods[1:2])
+    turned[...] = jnp.zeros_like(turned)
+    for part, weight in enumerate((key_w, value_w)):
+        turned[:rows, :] = jnp.dot(states, weight[...], preferred_element_type=F32)
+        both = turned[...].T
+        chosen = jnp.where(odd, both[HEAD:], both[:HEAD])
+        out[part * HEAD : (part + 1) * HEAD, :] = chosen.astype(BF16)
+
+
+def text_keys(head, hidden, mods, weight, rows):
+    width = hidden.shape[1]
+    pair = 2 * HEAD
+    values_at = HEADS * HEAD // pair
+    return pl.pallas_call(
+        text_body,
+        out_shape=jax.ShapeDtypeStruct((pair, rows), BF16),
+        grid_spec=pltpu.PrefetchScalarGridSpec(
+            num_scalar_prefetch=1,
+            grid=(1,),
+            in_specs=[
+                pl.BlockSpec(hidden.shape, lambda i, h: (0, 0)),
+                pl.BlockSpec(mods.shape, lambda i, h: (0, 0)),
+                pl.BlockSpec((width, pair), lambda i, h: (0, h[0] // 2)),
+                pl.BlockSpec((width, pair), lambda i, h: (0, values_at + h[0] // 2)),
+            ],
+            out_specs=pl.BlockSpec((pair, rows), lambda i, h: (0, 0)),
+            scratch_shapes=[pltpu.VMEM((rows, pair), F32)],
+        ),
+        compiler_params=pltpu.CompilerParams(vmem_limit_bytes=10 << 20),
+        cost_estimate=pl.CostEstimate(flops=1000, bytes_accessed=1000, transcendentals=0),
+        name="text_keys",
+    )(head, hidden, mods, weight, weight)
+
+
 def mark_body(*refs):
     refs[-1][...] = refs[0][...]
 
@@ -250,18 +287,20 @@
 
 def middle(mixed, hidden, mods, out_w, mark):
     rows, width = hidden.shape
+    inputs = (mixed, hidden, mods, out_w, mark)
     return pl.pallas_call(
         middle_body,
         out_shape=(
             jax.ShapeDtypeStruct((rows, width), F32),
             jax.ShapeDtypeStruct((rows, width), BF16),
         ),
-        in_specs=vmem_specs(5),
-        out_specs=tuple(vmem_specs(2)),
+        grid=(1,),
+        in_specs=[whole(x) for x in inputs],
+        out_specs=(pl.BlockSpec((rows, width), lambda i: (0, 0)),) * 2,
         compiler_params=pltpu.CompilerParams(vmem_limit_bytes=14 << 20),
         cost_estimate=pl.CostEstimate(flops=1000, bytes_accessed=1000, transcendentals=0),
         name="middle",
-    )(mixed, hidden, mods, out_w, mark)
+    )(*inputs)
 
 
 def first_body(chip_ref, own_x, peer_x, *refs):
@@ -367,6 +406,8 @@
     rows, width = updated.shape
     cols = final_t.shape[0]
     smem = pl.BlockSpec(memory_space=pltpu.SMEM)
+    inputs = (own_part, peer_part, updated, mods, finals, final_t, latent)
+    shapes = ((rows, cols), (rows, cols), (rows, cols), (W_P, cols // 2), (W_P, cols // 2))
     return pl.pallas_call(
         last_body,
         out_shape=(
@@ -376,13 +417,14 @@
             jax.ShapeDtypeStruct((W_P, cols // 2), BF16),
             jax.ShapeDtypeStruct((W_P, cols // 2), BF16),
         ),
-        in_specs=[smem] * 3 + vmem_specs(7),
-        out_specs=tuple(vmem_specs(5)),
+        grid=(1,),
+        in_specs=[smem] * 3 + [whole(x) for x in inputs],
+        out_specs=tuple(pl.BlockSpec(x, lambda i: (0, 0)) for x in shapes),
         scratch_shapes=[pltpu.VMEM((width, rows), F32)],
-        compiler_params=pltpu.CompilerParams(vmem_limit_bytes=8 << 20),
+        compiler_params=pltpu.CompilerParams(vmem_limit_bytes=12 << 20),
         cost_estimate=pl.CostEstimate(flops=1000, bytes_accessed=1000, transcendentals=0),
         name="last",
-    )(core, live, gap, own_part, peer_part, updated, mods, finals, final_t, latent)
+    )(core, live, gap, *inputs)
 
 
 def conv_body(live_ref, scaled, before, after, weights, bias, out):
@@ -415,15 +457,17 @@
 def convolve(live, scaled, before, after, weights, bias):
     lines = 2 * scaled.shape[0] // W_P
     shape = (lines, 2 * W_P, weights.shape[2])
+    inputs = (scaled, before, after, weights, bias)
     return pl.pallas_call(
         conv_body,
         out_shape=jax.ShapeDtypeStruct(shape, BF16),
-        in_specs=[pl.BlockSpec(memory_space=pltpu.SMEM)] + vmem_specs(5),
-        out_specs=vmem_specs(1)[0],
+        grid=(1,),
+        in_specs=[pl.BlockSpec(memory_space=pltpu.SMEM)] + [whole(x) for x in inputs],
+        out_specs=pl.BlockSpec(shape, lambda i: (0, 0, 0)),
         compiler_params=pltpu.CompilerParams(vmem_limit_bytes=12 << 20),
         cost_estimate=pl.CostEstimate(flops=1000, bytes_accessed=1000, transcendentals=0),
         name="convolve",
-    )(live, scaled, before, after, weights, bias)
+    )(live, *inputs)
 
 
 def conv_weights(conv_weight):
@@ -483,18 +527,8 @@
     right, head = lax.optimization_barrier((mlp_near[1], head))
     mlp_near = (mlp_near[0], right, mlp_near[2])
     parts = lax.all_to_all(heads, "blk", 0, 0, tiled=True)
-    text_in = modulate(text_hidden[0], text_mod[0, 0], 1.0 + text_mod[0, 1])
-    text_cols = jnp.concatenate(
-        [
-            lax.dynamic_slice(text_weight, (0, start + head * HEAD), (width, HEAD))
-            for start in (0, width_attn)
-        ],
-        axis=1,
-    )
-    text_kv = lax.dot_general(
-        text_cols, text_in, (((0,), (1,)), ((), ())), preferred_element_type=F32
-    ).astype(BF16)
-    text_kv = jnp.pad(text_kv, ((0, 0), (0, -text_kv.shape[1] % tok_rows)))
+    text_rows = tok_rows * pl.cdiv(text_hidden.shape[1], tok_rows)
+    text_kv = text_keys(head[None], text_hidden[0], text_mod[0], text_weight, text_rows)
 
     mlp_next = ring_second(*mlp_near)
     mark = marker(*mlp_near)

time: 167 us -> 155 us (0.928)
  local copies, waits for them, and re-layouts: 30.4 us -> 19 us
  waiting for transfers between devices: 37.5 us -> 45.1 us
  starting transfers between devices: 59 us -> 53 us
  other arithmetic: 7.62 us -> 3.52 us
  Pallas kernels: 26.5 us -> 30 us
  matrix products: 1.79 us -> 0 us
    all_to_all x1, waiting for transfers between devices: 4.7 us -> 17.9 us  [per_device(): lax.all_to_all(mixed, 'blk', 0, 0, tiled=True)[:HEADS]]
    ppermute x1, starting transfers between devices: 7.43 us -> 1.91 us  [per_device(): before = lax.ppermute(bottom, 'blk', [(i, i + 1) for i in range(size - 1)])]
    ppermute x12, waiting for transfers between devices: 20.4 us -> 15.5 us  [ring(): return lax.ppermute(x, axis, [(i, (i + step) % size) for i in range(size)])]
    all_to_all x1, waiting for transfers between devices: 0.01 us -> 3.67 us  [per_device(): parts = lax.all_to_all(heads, 'blk', 0, 0, tiled=True)]
    ppermute x10, waiting for transfers between devices: 8.67 us -> 6.3 us  [swap(): lax.ppermute(x, axis, [(i, i ^ bits) for i in range(lax.axis_size(axis))])]
    all_to_all x1, starting transfers between devices: 9.74 us -> 7.48 us  [per_device(): lax.all_to_all(mixed, 'blk', 0, 0, tiled=True)[:HEADS]]
    ppermute x1, starting transfers between devices: 1.92 us -> 3.92 us  [per_device(): after = lax.ppermute(top, 'blk', [(i + 1, i) for i in range(size - 1)])]
    ppermute x1, waiting for transfers between devices: 3.74 us -> 1.74 us  [per_device(): after = lax.ppermute(top, 'blk', [(i + 1, i) for i in range(size - 1)])]
  transfers between devices with their start and end apart: 26 -> 26, of which waited for: 13 -> 13; matrix products, arithmetic and copies ran while one was open for 18% -> 9% of each run, Pallas kernels for 9% -> 12%
where the time goes in v9:
time: 155 us; the launch traced here: 153 us
  starting transfers between devices  53 us (34%)
  waiting for transfers between devices  45.1 us (29%)
  Pallas kernels  30 us (19%)
  local copies, waits for them, and re-layouts  19 us (12%)
  other arithmetic  3.52 us (2%)
  between operations  2.46 us (2%)
    ppermute x12, starting transfers between devices, ring(): return lax.ppermute(x, axis, [(i, (i + step) % size) for i in range(size)])  20 us
    all_to_all x1, waiting for transfers between devices, per_device(): lax.all_to_all(mixed, 'blk', 0, 0, tiled=True)[:HEADS]  17.9 us
    ppermute x12, waiting for transfers between devices, ring(): return lax.ppermute(x, axis, [(i, (i + step) % size) for i in range(size)])  15.5 us
    pallas_call x1, Pallas kernels, attend(): pl.pallas_call(attend_body, out_shape=jax.ShapeDtypeStruct((blocks, HEAD,...  12.4 us
    ppermute x10, starting transfers between devices, swap(): lax.ppermute(x, axis, [(i, i ^ bits) for i in range(lax.axis_size(axis))])  11 us
    unnamed x52, local copies, waits for them, and re-layouts  9.69 us
    all_to_all x1, starting transfers between devices, per_device(): parts = lax.all_to_all(heads, 'blk', 0, 0, tiled=True)  8.7 us
    all_to_all x1, starting transfers between devices, per_device(): lax.all_to_all(mixed, 'blk', 0, 0, tiled=True)[:HEADS]  7.48 us
  transfers between devices with their start and end apart: 26, of which 13 were waited for; matrix products, arithmetic and copies ran while one was open for 9% of the time, Pallas kernels for 12%

profile of v9, /device:TPU:104, one launch (start us, length us, event | category | flops | bytes accessed | tf_op | source)
XLA Modules:
  0.0 153.1 jit_solution(15349374128224662677)
XLA Ops:
  0.7 1.6 %collective-permute-start = (bf16[144,1536]{1,0:T(8,128)(2,1)}, bf16[144,1536]{1,0:T(8,128)(2,1)S(1)}, u32[]{:S(2)}, u32[]{:S(2)}) collective-permute-start(bf16[144,1536]{1,0:T(8,128)(2,1)} %bitcast.47), channel_id=1, source_target_pairs={{0,4},{1,5},{2,6},{3,7},{4,8},{5,9},{6,10},{7,11},{8,12},{9,13},{1... | collective-permute-start | bytes 1327112 | tf_op jit(solution)/shard_map/ppermute | solution.py:54
  2.2 1.7 %collective-permute-start.2 = (bf16[144,1536]{1,0:T(8,128)(2,1)}, bf16[144,1536]{1,0:T(8,128)(2,1)S(1)}, u32[]{:S(2)}, u32[]{:S(2)}) collective-permute-start(bf16[144,1536]{1,0:T(8,128)(2,1)} %bitcast.48), channel_id=1, source_target_pairs={{0,12},{1,13},{2,14},{3,15},{4,0},{5,1},{6,2},{7,3},{8,4},{9,5},{1... | collective-permute-start | bytes 1327112 | tf_op jit(solution)/shard_map/ppermute | solution.py:54
  4.7 2.4 %collective-permute-start.6 = (bf16[144,1536]{1,0:T(8,128)(2,1)}, bf16[144,1536]{1,0:T(8,128)(2,1)S(1)}, u32[]{:S(2)}, u32[]{:S(2)}) collective-permute-start(bf16[144,1536]{1,0:T(8,128)(2,1)} %bitcast.49), channel_id=1, source_target_pairs={{0,2},{1,3},{2,0},{3,1},{4,6},{5,7},{6,4},{7,5},{8,10},{9,11},{10,... | collective-permute-start | bytes 1327112 | tf_op jit(solution)/shard_map/ppermute | solution.py:38
  9.7 4.4 %collective-permute-done.refs_1_ = bf16[144,1536]{1,0:T(8,128)(2,1)S(1)} collective-permute-done((bf16[144,1536]{1,0:T(8,128)(2,1)}, bf16[144,1536]{1,0:T(8,128)(2,1)S(1)}, u32[]{:S(2)}, u32[]{:S(2)}) %collective-permute-start) | collective-permute-done | bytes 442400 | tf_op jit(solution)/shard_map/ppermute | solution.py:54
  14.5 3.0 %collective-permute-start.3 = (bf16[72,1536]{1,0:T(8,128)(2,1)S(1)}, bf16[72,1536]{1,0:T(8,128)(2,1)S(1)}, u32[]{:S(2)}, u32[]{:S(2)}) collective-permute-start(bf16[72,1536]{1,0:T(8,128)(2,1)S(1)} %slice.53), channel_id=1, source_target_pairs={{0,12},{1,13},{2,14},{3,15},{4,0},{5,1},{6,2},{7,3},{8,4},{9,5},{1... | collective-permute-start | bytes 663560 | tf_op jit(solution)/shard_map/ppermute | solution.py:54
  18.1 3.0 %collective-permute-start.8 = (bf16[144,1536]{1,0:T(8,128)(2,1)S(1)}, bf16[144,1536]{1,0:T(8,128)(2,1)}, u32[]{:S(2)}, u32[]{:S(2)}) collective-permute-start(bf16[144,1536]{1,0:T(8,128)(2,1)S(1)} %collective-permute-done.6.refs_3_), channel_id=1, source_target_pairs={{0,12},{1,13},{2,14},{3,15},{4,0},{5,1},{6,2},{7,3},{8,4},{9,5},{1... | collective-permute-start | bytes 1327112 | tf_op jit(solution)/shard_map/ppermute | solution.py:54
  21.1 2.2 %collective-permute-done.1 = bf16[72,1536]{1,0:T(8,128)(2,1)S(1)} collective-permute-done((bf16[72,1536]{1,0:T(8,128)(2,1)S(1)}, bf16[72,1536]{1,0:T(8,128)(2,1)S(1)}, u32[]{:S(2)}, u32[]{:S(2)}) %collective-permute-start.1) | collective-permute-done | bytes 221216 | tf_op jit(solution)/shard_map/ppermute | solution.py:54
  24.7 2.3 %collective-permute-start.4 = (bf16[144,1536]{1,0:T(8,128)(2,1)}, bf16[144,1536]{1,0:T(8,128)(2,1)}, u32[]{:S(2)}, u32[]{:S(2)}) collective-permute-start(bf16[144,1536]{1,0:T(8,128)(2,1)} %constant_dynamic-update-slice_fusion.refs_4_), channel_id=1, source_target_pairs={{0,2},{1,3},{2,0},{3,1},{4,6},{5,7},{6,4},{7,5},{8,10},{9,11},{10,... | collective-permute-start | bytes 1327112 | tf_op jit(solution)/shard_map/ppermute | solution.py:38
  27.4 3.8 %collective-permute-done.7.refs_5_ = bf16[144,1536]{1,0:T(8,128)(2,1)} collective-permute-done((bf16[144,1536]{1,0:T(8,128)(2,1)S(1)}, bf16[144,1536]{1,0:T(8,128)(2,1)}, u32[]{:S(2)}, u32[]{:S(2)}) %collective-permute-start.7) | collective-permute-done | bytes 442400 | tf_op jit(solution)/shard_map/ppermute | solution.py:54
  31.3 3.0 %collective-permute-start.11 = (bf16[384,1536]{1,0:T(8,128)(2,1)S(1)}, bf16[384,1536]{1,0:T(8,128)(2,1)S(1)}, u32[]{:S(2)}, u32[]{:S(2)}) collective-permute-start(bf16[384,1536]{1,0:T(8,128)(2,1)S(1)} %pad_maximum_fusion.refs_0_), channel_id=1, source_target_pairs={{0,12},{1,13},{2,14},{3,15},{4,0},{5,1},{6,2},{7,3},{8,4},{9,5},{1... | collective-permute-start | bytes 3538952 | tf_op jit(solution)/shard_map/ppermute | solution.py:54
  34.3 2.3 %collective-permute-start.12 = (bf16[384,1536]{1,0:T(8,128)(2,1)S(1)}, bf16[384,1536]{1,0:T(8,128)(2,1)}, u32[]{:S(2)}, u32[]{:S(2)}) collective-permute-start(bf16[384,1536]{1,0:T(8,128)(2,1)S(1)} %pad_maximum_fusion.refs_0_), channel_id=1, source_target_pairs={{0,2},{1,3},{2,0},{3,1},{4,6},{5,7},{6,4},{7,5},{8,10},{9,11},{10,... | collective-permute-start | bytes 3538952 | tf_op jit(solution)/shard_map/ppermute | solution.py:38
  37.3 3.4 %project_qkv.1 = (bf16[8,144,128]{2,1,0:T(8,128)(2,1)S(1)}, bf16[8,144,128]{2,1,0:T(8,128)(2,1)}) custom-call(s32[1]{0:T(128)} %bitcast.2.chip_ref, bf16[16,128]{1,0:T(8,128)(2,1)S(1)} %marker.3.ready, bf16[128,1536]{1,0:T(8,128)(2,1)S(1)} %fusion.5.own_x, bf16[128,1536]{1,0:T(8,128)(2,1)} %collective-permute-done.5.peer_x, bf16[144,1536]{1,0:T(8,128)(2,1)S(1)} %bitcast.50, ...), custom_call_target="tpu_custom_call" | custom-call | flops 1000 | bytes 1000 | tf_op jit(solution)/shard_map/project_qkv/pallas_call | solution.py:96
  42.1 1.1 collective-permute-done.9.other
  45.1 8.7 %all-to-all-start = ((bf16[16,192,128]{2,1,0:T(8,128)(2,1)}), bf16[16,192,128]{2,1,0:T(8,128)(2,1)}, u32[]{:S(2)}, u32[]{:S(2)}) async-start(bf16[16,192,128]{2,1,0:T(8,128)(2,1)} %copy-done.2), calls=%async_computation | async-start | bytes 1572864 | tf_op jit(solution)/shard_map/all_to_all | solution.py:529
  53.8 4.2 %collective-permute-done.11.refs_1_.refs_2_ = bf16[384,1536]{1,0:T(8,128)(2,1)S(1)} collective-permute-done((bf16[384,1536]{1,0:T(8,128)(2,1)S(1)}, bf16[384,1536]{1,0:T(8,128)(2,1)S(1)}, u32[]{:S(2)}, u32[]{:S(2)}) %collective-permute-start.11) | collective-permute-done | bytes 1179680 | tf_op jit(solution)/shard_map/ppermute | solution.py:54
  58.9 3.7 %collective-permute-start.14 = (bf16[192,1536]{1,0:T(8,128)(2,1)}, bf16[192,1536]{1,0:T(8,128)(2,1)S(1)}, u32[]{:S(2)}, u32[]{:S(2)}) collective-permute-start(bf16[192,1536]{1,0:T(8,128)(2,1)} %slice.48), channel_id=1, source_target_pairs={{0,12},{1,13},{2,14},{3,15},{4,0},{5,1},{6,2},{7,3},{8,4},{9,5},{1... | collective-permute-start | bytes 1769480 | tf_op jit(solution)/shard_map/ppermute | solution.py:54
  63.6 1.9 %slice.54 = bf16[192,1536]{1,0:T(8,128)(2,1)} slice(bf16[384,1536]{1,0:T(8,128)(2,1)} %collective-permute-done.10.refs_0_.refs_1_), slice={[0:192], [0:1536]} | slice | bytes 1179648 | tf_op jit(solution)/shard_map/slice | solution.py:64
  65.6 3.2 %collective-permute-start.18 = (bf16[384,1536]{1,0:T(8,128)(2,1)}, bf16[384,1536]{1,0:T(8,128)(2,1)}, u32[]{:S(2)}, u32[]{:S(2)}) collective-permute-start(bf16[384,1536]{1,0:T(8,128)(2,1)} %collective-permute-done.12.refs_2_.refs_3_), channel_id=1, source_target_pairs={{0,12},{1,13},{2,14},{3,15},{4,0},{5,1},{6,2},{7,3},{8,4},{9,5},{1... | collective-permute-start | bytes 3538952 | tf_op jit(solution)/shard_map/ppermute | solution.py:54
  70.4 3.7 %all-to-all-done.parts = bf16[16,192,128]{2,1,0:T(8,128)(2,1)} async-done(((bf16[16,192,128]{2,1,0:T(8,128)(2,1)}), bf16[16,192,128]{2,1,0:T(8,128)(2,1)}, u32[]{:S(2)}, u32[]{:S(2)}) %all-to-all-start) | async-done | bytes 786464 | tf_op jit(solution)/shard_map/all_to_all | solution.py:529
  74.1 12.4 %attend.1 = bf16[16,64,128]{2,1,0:T(8,128)(2,1)} custom-call(s32[1]{0:T(128)S(6)} %copy.32.count_ref, bf16[16,192,128]{2,1,0:T(8,128)(2,1)} %all-to-all-done.parts, bf16[128,256]{1,0:T(8,128)(2,1)S(1)} %text_keys.1.text, bf16[16,128]{1,0:T(8,128)(2,1)S(1)} %marker.4.mark), custom_call_target="tpu_custom_call" | custom-call | flops 1000 | bytes 1000 | tf_op jit(solution)/shard_map/attend/pallas_call | solution.py:253
  86.6 1.2 collective-permute-start.15
  87.8 2.3 %collective-permute-start.16 = (bf16[192,1536]{1,0:T(8,128)(2,1)S(1)}, bf16[192,1536]{1,0:T(8,128)(2,1)}, u32[]{:S(2)}, u32[]{:S(2)}) collective-permute-start(bf16[192,1536]{1,0:T(8,128)(2,1)S(1)} %collective-permute-done.14.refs_4_), channel_id=1, source_target_pairs={{0,2},{1,3},{2,0},{3,1},{4,6},{5,7},{6,4},{7,5},{8,10},{9,11},{10,... | collective-permute-start | bytes 1769480 | tf_op jit(solution)/shard_map/ppermute | solution.py:38
  90.9 7.5 %all-to-all-start.1 = ((bf16[16,64,128]{2,1,0:T(8,128)(2,1)}), bf16[16,64,128]{2,1,0:T(8,128)(2,1)}, u32[]{:S(2)}, u32[]{:S(2)}) async-start(bf16[16,64,128]{2,1,0:T(8,128)(2,1)} %attend.1), calls=%async_computation.1 | async-start | bytes 524288 | tf_op jit(solution)/shard_map/all_to_all | solution.py:539
  101.0 17.9 %all-to-all-done.1 = bf16[16,64,128]{2,1,0:T(8,128)(2,1)} async-done(((bf16[16,64,128]{2,1,0:T(8,128)(2,1)}), bf16[16,64,128]{2,1,0:T(8,128)(2,1)}, u32[]{:S(2)}, u32[]{:S(2)}) %all-to-all-start.1) | async-done | bytes 262176 | tf_op jit(solution)/shard_map/all_to_all | solution.py:539
  123.3 1.7 %collective-permute-done.19.peer_x = bf16[128,1536]{1,0:T(8,128)(2,1)S(1)} collective-permute-done((bf16[128,1536]{1,0:T(8,128)(2,1)S(1)}, bf16[128,1536]{1,0:T(8,128)(2,1)S(1)}, u32[]{:S(2)}, u32[]{:S(2)}) %collective-permute-start.19) | collective-permute-done | bytes 393248 | tf_op jit(solution)/shard_map/ppermute | solution.py:38
  125.0 3.6 %mlp_first.1.own_act = bf16[8,192,256]{2,1,0:T(8,128)(2,1)S(1)} custom-call(s32[1]{0:T(128)} %bitcast.2.chip_ref, bf16[128,1536]{1,0:T(8,128)(2,1)S(1)} %get-tuple-element.50.own_x, bf16[128,1536]{1,0:T(8,128)(2,1)S(1)} %collective-permute-done.19.peer_x, bf16[384,1536]{1,0:T(8,128)(2,1)S(1)} %pad_maximum_fusion.refs_0_, ...), custom_call_target="tpu_custom_call" | custom-call | flops 1000 | bytes 1000 | tf_op jit(solution)/shard_map/mlp_first/pallas_call | solution.py:325
  128.9 2.1 %collective-permute-done.20.peer_act = bf16[8,192,256]{2,1,0:T(8,128)(2,1)S(1)} collective-permute-done((bf16[8,192,256]{2,1,0:T(8,128)(2,1)S(1)}, bf16[8,192,256]{2,1,0:T(8,128)(2,1)S(1)}, u32[]{:S(2)}, u32[]{:S(2)}) %collective-permute-start.20) | collective-permute-done | bytes 786464 | tf_op jit(solution)/shard_map/ppermute | solution.py:38
  131.0 4.1 %mlp_second.1 = (f32[8,96,128]{2,1,0:T(8,128)S(1)}, f32[8,96,128]{2,1,0:T(8,128)}) custom-call(s32[1]{0:T(128)} %bitcast.2.chip_ref, s32[1]{0:T(128)} %bitcast.core_ref, bf16[8,192,256]{2,1,0:T(8,128)(2,1)S(1)} %mlp_first.1.own_act, bf16[8,192,256]{2,1,0:T(8,128)(2,1)S(1)} %collective-permute-done.20.peer_act, ...), custom_call_target="tpu_custom_call" | custom-call | flops 1000 | bytes 1000 | tf_op jit(solution)/shard_map/mlp_second/pallas_call | solution.py:364
  141.7 1.9 %collective-permute-start.22 = (bf16[64,32]{1,0:T(8,128)(2,1)S(1)}, bf16[64,32]{1,0:T(8,128)(2,1)S(1)}, u32[]{:S(2)}, u32[]{:S(2)}) collective-permute-start(bf16[64,32]{1,0:T(8,128)(2,1)S(1)} %get-tuple-element.58), channel_id=1, source_target_pairs={{0,16},{16,32},{32,48},{48,64},{64,80},{80,96},{96,112},{112,128},... | collective-permute-start | bytes 12296 | tf_op jit(solution)/shard_map/ppermute | solution.py:563
  143.6 3.9 %collective-permute-start.23 = (bf16[64,32]{1,0:T(8,128)(2,1)S(1)}, bf16[64,32]{1,0:T(8,128)(2,1)S(1)}, u32[]{:S(2)}, u32[]{:S(2)}) collective-permute-start(bf16[64,32]{1,0:T(8,128)(2,1)S(1)} %get-tuple-element.59), channel_id=1, source_target_pairs={{16,0},{32,16},{48,32},{64,48},{80,64},{96,80},{112,96},{128,112},... | collective-permute-start | bytes 12296 | tf_op jit(solution)/shard_map/ppermute | solution.py:564
  149.6 1.7 %collective-permute-done.23.after = bf16[64,32]{1,0:T(8,128)(2,1)S(1)} collective-permute-done((bf16[64,32]{1,0:T(8,128)(2,1)S(1)}, bf16[64,32]{1,0:T(8,128)(2,1)S(1)}, u32[]{:S(2)}, u32[]{:S(2)}) %collective-permute-start.23) | collective-permute-done | bytes 4128 | tf_op jit(solution)/shard_map/ppermute | solution.py:564
  151.4 1.7 %convolve.1 = bf16[4,128,512]{2,1,0:T(8,128)(2,1)} custom-call(s32[1]{0:T(128)S(6)} %convert_element_type.12.live_ref, bf16[128,64]{1,0:T(8,128)(2,1)S(1)} %get-tuple-element.57.scaled, bf16[64,32]{1,0:T(8,128)(2,1)S(1)} %collective-permute-done.22.before, bf16[64,32]{1,0:T(8,128)(2,1)S(1)} %collective-permute-done.23.after, ...), custom_call_target="tpu_custom_call" | custom-call | flops 1000 | bytes 1000 | tf_op jit(solution)/shard_map/convolve/pallas_call | solution.py:461
  (116 shorter events, 28.8 us)
Async XLA Ops:
  0.7 13.4 %collective-permute-start = (bf16[144,1536]{1,0:T(8,128)(2,1)}, bf16[144,1536]{1,0:T(8,128)(2,1)S(1)}, u32[]{:S(2)}, u32[]{:S(2)}) collective-permute-start(bf16[144,1536]{1,0:T(8,128)(2,1)} %bitcast.47), channel_id=1, source_target_pairs={{0,4},{1,5},{2,6},{3,7},{4,8},{5,9},{6,10},{7,11},{8,12},{9,13},{1... | collective-permute-start | bytes 1327112 | tf_op jit(solution)/shard_map/ppermute | solution.py:54
  2.2 12.2 %collective-permute-start.2 = (bf16[144,1536]{1,0:T(8,128)(2,1)}, bf16[144,1536]{1,0:T(8,128)(2,1)S(1)}, u32[]{:S(2)}, u32[]{:S(2)}) collective-permute-start(bf16[144,1536]{1,0:T(8,128)(2,1)} %bitcast.48), channel_id=1, source_target_pairs={{0,12},{1,13},{2,14},{3,15},{4,0},{5,1},{6,2},{7,3},{8,4},{9,5},{1... | collective-permute-start | bytes 1327112 | tf_op jit(solution)/shard_map/ppermute | solution.py:54
  4.7 13.1 %collective-permute-start.6 = (bf16[144,1536]{1,0:T(8,128)(2,1)}, bf16[144,1536]{1,0:T(8,128)(2,1)S(1)}, u32[]{:S(2)}, u32[]{:S(2)}) collective-permute-start(bf16[144,1536]{1,0:T(8,128)(2,1)} %bitcast.49), channel_id=1, source_target_pairs={{0,2},{1,3},{2,0},{3,1},{4,6},{5,7},{6,4},{7,5},{8,10},{9,11},{10,... | collective-permute-start | bytes 1327112 | tf_op jit(solution)/shard_map/ppermute | solution.py:38
  14.1 9.2 %collective-permute-start.1 = (bf16[72,1536]{1,0:T(8,128)(2,1)S(1)}, bf16[72,1536]{1,0:T(8,128)(2,1)S(1)}, u32[]{:S(2)}, u32[]{:S(2)}) collective-permute-start(bf16[72,1536]{1,0:T(8,128)(2,1)S(1)} %slice.52), channel_id=1, source_target_pairs={{0,4},{1,5},{2,6},{3,7},{4,8},{5,9},{6,10},{7,11},{8,12},{9,13},{1... | collective-permute-start | bytes 663560 | tf_op jit(solution)/shard_map/ppermute | solution.py:54
  14.4 16.8 %copy-start.4 = (bf16[144,1536]{1,0:T(8,128)(2,1)}, bf16[144,1536]{1,0:T(8,128)(2,1)S(1)}, u32[]{:S(2)}) copy-start(bf16[144,1536]{1,0:T(8,128)(2,1)S(1)} %collective-permute-done.2.refs_2_) | copy-start | bytes 1327108
  14.5 9.5 %collective-permute-start.3 = (bf16[72,1536]{1,0:T(8,128)(2,1)S(1)}, bf16[72,1536]{1,0:T(8,128)(2,1)S(1)}, u32[]{:S(2)}, u32[]{:S(2)}) collective-permute-start(bf16[72,1536]{1,0:T(8,128)(2,1)S(1)} %slice.53), channel_id=1, source_target_pairs={{0,12},{1,13},{2,14},{3,15},{4,0},{5,1},{6,2},{7,3},{8,4},{9,5},{1... | collective-permute-start | bytes 663560 | tf_op jit(solution)/shard_map/ppermute | solution.py:54
  17.9 13.4 %copy-start.10 = (bf16[144,1536]{1,0:T(8,128)(2,1)}, bf16[144,1536]{1,0:T(8,128)(2,1)S(1)}, u32[]{:S(2)}) copy-start(bf16[144,1536]{1,0:T(8,128)(2,1)S(1)} %collective-permute-done.6.refs_3_) | copy-start | bytes 1327108
  17.9 13.4 %collective-permute-start.7 = (bf16[144,1536]{1,0:T(8,128)(2,1)S(1)}, bf16[144,1536]{1,0:T(8,128)(2,1)}, u32[]{:S(2)}, u32[]{:S(2)}) collective-permute-start(bf16[144,1536]{1,0:T(8,128)(2,1)S(1)} %collective-permute-done.6.refs_3_), channel_id=1, source_target_pairs={{0,4},{1,5},{2,6},{3,7},{4,8},{5,9},{6,10},{7,11},{8,12},{9,13},{1... | collective-permute-start | bytes 1327112 | tf_op jit(solution)/shard_map/ppermute | solution.py:54
  18.1 13.1 %collective-permute-start.8 = (bf16[144,1536]{1,0:T(8,128)(2,1)S(1)}, bf16[144,1536]{1,0:T(8,128)(2,1)}, u32[]{:S(2)}, u32[]{:S(2)}) collective-permute-start(bf16[144,1536]{1,0:T(8,128)(2,1)S(1)} %collective-permute-done.6.refs_3_), channel_id=1, source_target_pairs={{0,12},{1,13},{2,14},{3,15},{4,0},{5,1},{6,2},{7,3},{8,4},{9,5},{1... | collective-permute-start | bytes 1327112 | tf_op jit(solution)/shard_map/ppermute | solution.py:54
  24.7 11.9 %collective-permute-start.4 = (bf16[144,1536]{1,0:T(8,128)(2,1)}, bf16[144,1536]{1,0:T(8,128)(2,1)}, u32[]{:S(2)}, u32[]{:S(2)}) collective-permute-start(bf16[144,1536]{1,0:T(8,128)(2,1)} %constant_dynamic-update-slice_fusion.refs_4_), channel_id=1, source_target_pairs={{0,2},{1,3},{2,0},{3,1},{4,6},{5,7},{6,4},{7,5},{8,10},{9,11},{10,... | collective-permute-start | bytes 1327112 | tf_op jit(solution)/shard_map/ppermute | solution.py:38
  27.3 10.0 %collective-permute-start.5 = (bf16[128,1536]{1,0:T(8,128)(2,1)S(1)}, bf16[128,1536]{1,0:T(8,128)(2,1)}, u32[]{:S(2)}, u32[]{:S(2)}) collective-permute-start(bf16[128,1536]{1,0:T(8,128)(2,1)S(1)} %fusion.5.own_x), channel_id=1, source_target_pairs={{0,1},{1,0},{2,3},{3,2},{4,5},{5,4},{6,7},{7,6},{8,9},{9,8},{10,11... | collective-permute-start | bytes 1179656 | tf_op jit(solution)/shard_map/ppermute | solution.py:38
  31.3 26.7 %collective-permute-start.11 = (bf16[384,1536]{1,0:T(8,128)(2,1)S(1)}, bf16[384,1536]{1,0:T(8,128)(2,1)S(1)}, u32[]{:S(2)}, u32[]{:S(2)}) collective-permute-start(bf16[384,1536]{1,0:T(8,128)(2,1)S(1)} %pad_maximum_fusion.refs_0_), channel_id=1, source_target_pairs={{0,12},{1,13},{2,14},{3,15},{4,0},{5,1},{6,2},{7,3},{8,4},{9,5},{1... | collective-permute-start | bytes 3538952 | tf_op jit(solution)/shard_map/ppermute | solution.py:54
  34.3 31.2 %collective-permute-start.12 = (bf16[384,1536]{1,0:T(8,128)(2,1)S(1)}, bf16[384,1536]{1,0:T(8,128)(2,1)}, u32[]{:S(2)}, u32[]{:S(2)}) collective-permute-start(bf16[384,1536]{1,0:T(8,128)(2,1)S(1)} %pad_maximum_fusion.refs_0_), channel_id=1, source_target_pairs={{0,2},{1,3},{2,0},{3,1},{4,6},{5,7},{6,4},{7,5},{8,10},{9,11},{10,... | collective-permute-start | bytes 3538952 | tf_op jit(solution)/shard_map/ppermute | solution.py:38
  36.6 26.9 %collective-permute-start.10 = (bf16[384,1536]{1,0:T(8,128)(2,1)S(1)}, bf16[384,1536]{1,0:T(8,128)(2,1)}, u32[]{:S(2)}, u32[]{:S(2)}) collective-permute-start(bf16[384,1536]{1,0:T(8,128)(2,1)S(1)} %pad_maximum_fusion.refs_0_), channel_id=1, source_target_pairs={{0,4},{1,5},{2,6},{3,7},{4,8},{5,9},{6,10},{7,11},{8,12},{9,13},{1... | collective-permute-start | bytes 3538952 | tf_op jit(solution)/shard_map/ppermute | solution.py:54
  41.4 1.8 %collective-permute-start.9 = (bf16[8,144,128]{2,1,0:T(8,128)(2,1)}, bf16[8,144,128]{2,1,0:T(8,128)(2,1)S(1)}, u32[]{:S(2)}, u32[]{:S(2)}) collective-permute-start(bf16[8,144,128]{2,1,0:T(8,128)(2,1)} %get-tuple-element.38), channel_id=1, source_target_pairs={{0,1},{1,0},{2,3},{3,2},{4,5},{5,4},{6,7},{7,6},{8,9},{9,8},{10,11... | collective-permute-start | bytes 884744 | tf_op jit(solution)/shard_map/ppermute | solution.py:38
  45.1 24.4 %slice-start = ((s8[4718592]{0:T(1024)(128)(4,1)}), s8[524288]{0:T(1024)(128)(4,1)S(1)}, s32[]{:S(2)}) async-start(s8[4718592]{0:T(1024)(128)(4,1)} %bitcast.42), calls=%async_computation.2 | async-start | bytes 1048576
  45.1 29.0 %all-to-all-start = ((bf16[16,192,128]{2,1,0:T(8,128)(2,1)}), bf16[16,192,128]{2,1,0:T(8,128)(2,1)}, u32[]{:S(2)}, u32[]{:S(2)}) async-start(bf16[16,192,128]{2,1,0:T(8,128)(2,1)} %copy-done.2), calls=%async_computation | async-start | bytes 1572864 | tf_op jit(solution)/shard_map/all_to_all | solution.py:529
  58.9 27.6 %collective-permute-start.14 = (bf16[192,1536]{1,0:T(8,128)(2,1)}, bf16[192,1536]{1,0:T(8,128)(2,1)S(1)}, u32[]{:S(2)}, u32[]{:S(2)}) collective-permute-start(bf16[192,1536]{1,0:T(8,128)(2,1)} %slice.48), channel_id=1, source_target_pairs={{0,12},{1,13},{2,14},{3,15},{4,0},{5,1},{6,2},{7,3},{8,4},{9,5},{1... | collective-permute-start | bytes 1769480 | tf_op jit(solution)/shard_map/ppermute | solution.py:54
  65.5 21.1 %collective-permute-start.13 = (bf16[192,1536]{1,0:T(8,128)(2,1)}, bf16[192,1536]{1,0:T(8,128)(2,1)}, u32[]{:S(2)}, u32[]{:S(2)}) collective-permute-start(bf16[192,1536]{1,0:T(8,128)(2,1)} %slice.54), channel_id=1, source_target_pairs={{0,4},{1,5},{2,6},{3,7},{4,8},{5,9},{6,10},{7,11},{8,12},{9,13},{1... | collective-permute-start | bytes 1769480 | tf_op jit(solution)/shard_map/ppermute | solution.py:54
  65.5 54.3 %collective-permute-start.17 = (bf16[384,1536]{1,0:T(8,128)(2,1)}, bf16[384,1536]{1,0:T(8,128)(2,1)}, u32[]{:S(2)}, u32[]{:S(2)}) collective-permute-start(bf16[384,1536]{1,0:T(8,128)(2,1)} %collective-permute-done.12.refs_2_.refs_3_), channel_id=1, source_target_pairs={{0,4},{1,5},{2,6},{3,7},{4,8},{5,9},{6,10},{7,11},{8,12},{9,13},{1... | collective-permute-start | bytes 3538952 | tf_op jit(solution)/shard_map/ppermute | solution.py:54
  65.6 54.2 %collective-permute-start.18 = (bf16[384,1536]{1,0:T(8,128)(2,1)}, bf16[384,1536]{1,0:T(8,128)(2,1)}, u32[]{:S(2)}, u32[]{:S(2)}) collective-permute-start(bf16[384,1536]{1,0:T(8,128)(2,1)} %collective-permute-done.12.refs_2_.refs_3_), channel_id=1, source_target_pairs={{0,12},{1,13},{2,14},{3,15},{4,0},{5,1},{6,2},{7,3},{8,4},{9,5},{1... | collective-permute-start | bytes 3538952 | tf_op jit(solution)/shard_map/ppermute | solution.py:54
  70.4 27.9 %copy-start.20 = (bf16[144,512]{1,0:T(8,128)(2,1)S(1)}, bf16[144,512]{1,0:T(8,128)(2,1)}, u32[]{:S(2)}) copy-start(bf16[144,512]{1,0:T(8,128)(2,1)} %param.30) | copy-start | bytes 442372
  70.4 29.2 %copy-start.22 = (f32[1,4,2048]{2,1,0:T(4,128)S(1)}, f32[1,4,2048]{2,1,0:T(4,128)}, u32[]{:S(2)}) copy-start(f32[1,4,2048]{2,1,0:T(4,128)} %param.18) | copy-start | bytes 98308
  86.6 33.3 %collective-permute-start.15 = (bf16[192,1536]{1,0:T(8,128)(2,1)}, bf16[192,1536]{1,0:T(8,128)(2,1)}, u32[]{:S(2)}, u32[]{:S(2)}) collective-permute-start(bf16[192,1536]{1,0:T(8,128)(2,1)} %collective-permute-done.13.refs_4_), channel_id=1, source_target_pairs={{0,2},{1,3},{2,0},{3,1},{4,6},{5,7},{6,4},{7,5},{8,10},{9,11},{10,... | collective-permute-start | bytes 1769480 | tf_op jit(solution)/shard_map/ppermute | solution.py:38
  87.8 32.0 %collective-permute-start.16 = (bf16[192,1536]{1,0:T(8,128)(2,1)S(1)}, bf16[192,1536]{1,0:T(8,128)(2,1)}, u32[]{:S(2)}, u32[]{:S(2)}) collective-permute-start(bf16[192,1536]{1,0:T(8,128)(2,1)S(1)} %collective-permute-done.14.refs_4_), channel_id=1, source_target_pairs={{0,2},{1,3},{2,0},{3,1},{4,6},{5,7},{6,4},{7,5},{8,10},{9,11},{10,... | collective-permute-start | bytes 1769480 | tf_op jit(solution)/shard_map/ppermute | solution.py:38
  90.9 28.0 %all-to-all-start.1 = ((bf16[16,64,128]{2,1,0:T(8,128)(2,1)}), bf16[16,64,128]{2,1,0:T(8,128)(2,1)}, u32[]{:S(2)}, u32[]{:S(2)}) async-start(bf16[16,64,128]{2,1,0:T(8,128)(2,1)} %attend.1), calls=%async_computation.1 | async-start | bytes 524288 | tf_op jit(solution)/shard_map/all_to_all | solution.py:539
  123.3 1.7 %collective-permute-start.19 = (bf16[128,1536]{1,0:T(8,128)(2,1)S(1)}, bf16[128,1536]{1,0:T(8,128)(2,1)S(1)}, u32[]{:S(2)}, u32[]{:S(2)}) collective-permute-start(bf16[128,1536]{1,0:T(8,128)(2,1)S(1)} %get-tuple-element.50.own_x), channel_id=1, source_target_pairs={{0,1},{1,0},{2,3},{3,2},{4,5},{5,4},{6,7},{7,6},{8,9},{9,8},{10,11... | collective-permute-start | bytes 1179656 | tf_op jit(solution)/shard_map/ppermute | solution.py:38
  128.7 2.4 %collective-permute-start.20 = (bf16[8,192,256]{2,1,0:T(8,128)(2,1)S(1)}, bf16[8,192,256]{2,1,0:T(8,128)(2,1)S(1)}, u32[]{:S(2)}, u32[]{:S(2)}) collective-permute-start(bf16[8,192,256]{2,1,0:T(8,128)(2,1)S(1)} %mlp_first.1.own_act), channel_id=1, source_target_pairs={{0,1},{1,0},{2,3},{3,2},{4,5},{5,4},{6,7},{7,6},{8,9},{9,8},{10,11... | collective-permute-start | bytes 2359304 | tf_op jit(solution)/shard_map/ppermute | solution.py:38
  135.9 1.9 %collective-permute-start.21 = (f32[8,96,128]{2,1,0:T(8,128)}, f32[8,96,128]{2,1,0:T(8,128)S(1)}, u32[]{:S(2)}, u32[]{:S(2)}) collective-permute-start(f32[8,96,128]{2,1,0:T(8,128)} %get-tuple-element.52), channel_id=1, source_target_pairs={{0,1},{1,0},{2,3},{3,2},{4,5},{5,4},{6,7},{7,6},{8,9},{9,8},{10,11... | collective-permute-start | bytes 1179656 | tf_op jit(solution)/shard_map/ppermute | solution.py:38
  140.9 10.5 %copy-start.19 = (f32[512]{0:T(512)S(1)}, f32[512]{0:T(512)}, u32[]{:S(2)}) copy-start(f32[512]{0:T(512)} %param.31) | copy-start | bytes 6148
  141.7 7.9 %collective-permute-start.22 = (bf16[64,32]{1,0:T(8,128)(2,1)S(1)}, bf16[64,32]{1,0:T(8,128)(2,1)S(1)}, u32[]{:S(2)}, u32[]{:S(2)}) collective-permute-start(bf16[64,32]{1,0:T(8,128)(2,1)S(1)} %get-tuple-element.58), channel_id=1, source_target_pairs={{0,16},{16,32},{32,48},{48,64},{64,80},{80,96},{96,112},{112,128},... | collective-permute-start | bytes 12296 | tf_op jit(solution)/shard_map/ppermute | solution.py:563
  143.6 7.7 %collective-permute-start.23 = (bf16[64,32]{1,0:T(8,128)(2,1)S(1)}, bf16[64,32]{1,0:T(8,128)(2,1)S(1)}, u32[]{:S(2)}, u32[]{:S(2)}) collective-permute-start(bf16[64,32]{1,0:T(8,128)(2,1)S(1)} %get-tuple-element.59), channel_id=1, source_target_pairs={{16,0},{32,16},{48,32},{64,48},{80,64},{96,80},{112,96},{128,112},... | collective-permute-start | bytes 12296 | tf_op jit(solution)/shard_map/ppermute | solution.py:564
  (19 other events, 71.0 us)

commit v10 on v9

--- a/solution.py
+++ b/solution.py
@@ -336,7 +336,8 @@
 
 
 def second_body(chip_ref, core_ref, own_act, peer_act, *refs):
-    weights, (own_out, peer_out), act = refs[:-3], refs[-3:-1], refs[-1]
+    weights, (far_low, far_high) = refs[:-5], refs[-5:-3]
+    (own_out, peer_out), act = refs[-3:-1], refs[-1]
     count, cols, tokens = own_act.shape
     mid = tokens // 2
     core = core_ref[0]
@@ -348,9 +349,9 @@
         act[other, mid:] = peer_act[c, :, :mid]
     width = weights[0].shape[1]
     half = cols // 2
-    low = jnp.concatenate([weight[:half] for weight in weights], axis=0)
+    low = jnp.concatenate([weight[:half] for weight in weights] + [far_low[...]], axis=0)
     parts = jnp.dot(low, act[:width], preferred_element_type=F32)
-    high = jnp.concatenate([weight[half:] for weight in weights], axis=0)
+    high = jnp.concatenate([weight[half:] for weight in weights] + [far_high[...]], axis=0)
     parts += jnp.dot(high, act[width:], preferred_element_type=F32)
     for k in range(count):
         place = place_of(chip_ref[0], k)
@@ -358,7 +359,7 @@
         peer_out[place] = parts[k * half : (k + 1) * half, mid:]
 
 
-def mlp_second(chip, core, own_act, peer_act, weights):
+def mlp_second(chip, core, own_act, peer_act, weights, far):
     count, cols, tokens = own_act.shape
     shape = (count, cols // 2, tokens // 2)
     return pl.pallas_call(
@@ -367,13 +368,14 @@
         grid=(1,),
         in_specs=[pl.BlockSpec(memory_space=pltpu.SMEM)] * 2
         + [whole(own_act), whole(peer_act)]
-        + [half_of(x, cols, 1) for x in weights],
+        + [half_of(x, cols, 1) for x in weights]
+        + [whole(x) for x in far],
         out_specs=(pl.BlockSpec(shape, lambda i: (0, 0, 0)),) * 2,
         scratch_shapes=[pltpu.VMEM((2 * count * cols, tokens), BF16)],
         compiler_params=pltpu.CompilerParams(vmem_limit_bytes=28 << 20),
         cost_estimate=pl.CostEstimate(flops=1000, bytes_accessed=1000, transcendentals=0),
         name="mlp_second",
-    )(chip, core, own_act, peer_act, *weights)
+    )(chip, core, own_act, peer_act, *weights, *far)
 
 
 def last_body(
@@ -535,7 +537,12 @@
     parts, mark, text_kv = lax.optimization_barrier((parts, mark, text_kv))
     mixed = attend(counts, parts, text_kv, mark)
     mixed, low, high = lax.optimization_barrier((mixed, mlp_next[0], mlp_next[1]))
-    peer_low, peer_high = swap(low, "img", 2), swap(high, "img", 2)
+    peer_low = swap(low, "img", 2)
+    quarter = mlp_next[2].shape[0] // 4
+    far = (
+        ring(mlp_next[2][2 * quarter : 3 * quarter], "img", 4),
+        ring(mlp_next[3][3 * quarter :], "img", -4),
+    )
     mixed = lax.all_to_all(mixed, "blk", 0, 0, tiled=True)[:HEADS].reshape(width_attn, tok_rows)
     near_pieces, next_pieces = [mlp_mine, *mlp_near], list(mlp_next[2:])
 
@@ -546,14 +553,14 @@
     step_value = step_index.astype(F32)
     gap = plan(step_value + 1.0) - plan(step_value)
     mixed, latent_p, conv_w = lax.optimization_barrier((mixed, latent_p, conv_w))
-    updated, mlp_in = middle(mixed, hidden[0], mods, out_weight, marker(peer_low, peer_high, *next_pieces))
+    updated, mlp_in = middle(mixed, hidden[0], mods, out_weight, marker(peer_low, *next_pieces, *far))
     mlp_cols = mlp_in_weight.shape[1]
     peer_mlp = swap(mlp_in, "img", 1)
     first_pieces = near_pieces + [low] + next_pieces + [peer_low]
     act = mlp_first(chip, mlp_in, peer_mlp, first_pieces, mlp_cols)
     peer_act = swap(act, "img", 1)
     own_part, sent_part = mlp_second(
-        chip, core, act, peer_act, near_pieces + [high] + next_pieces + [peer_high]
+        chip, core, act, peer_act, near_pieces + [high] + next_pieces, far
     )
     peer_part = swap(sent_part, "img", 1)
     velocity, next_lat, scaled, top, bottom = last(

time: 155 us -> 155 us (level)
  waiting for transfers between devices: 45.1 us -> 38.8 us
  local copies, waits for them, and re-layouts: 19 us -> 22.4 us
  starting transfers between devices: 53 us -> 56.4 us
    all_to_all x1, waiting for transfers between devices: 17.9 us -> 0.01 us  [per_device(): lax.all_to_all(mixed, 'blk', 0, 0, tiled=True)[:HEADS]]
    ppermute x12 -> x14, waiting for transfers between devices: 15.5 us -> 25.1 us  [ring(): return lax.ppermute(x, axis, [(i, (i + step) % size) for i in range(size)])]
    ppermute x1, starting transfers between devices: 1.91 us -> 5.81 us  [per_device(): before = lax.ppermute(bottom, 'blk', [(i, i + 1) for i in range(size - 1)])]
    slice x0 -> x2, local copies, waits for them, and re-layouts: none -> 3.39 us  [the longest x1 1.7 us: per_device(): mlp_next[3][3 * quarter:]]
    ppermute x12 -> x14, starting transfers between devices: 20 us -> 23.2 us  [ring(): return lax.ppermute(x, axis, [(i, (i + step) % size) for i in range(size)])]
    ppermute x10 -> x9, starting transfers between devices: 11 us -> 8.65 us  [swap(): lax.ppermute(x, axis, [(i, i ^ bits) for i in range(lax.axis_size(axis))])]
    ppermute x1, starting transfers between devices: 3.92 us -> 1.92 us  [per_device(): after = lax.ppermute(top, 'blk', [(i + 1, i) for i in range(size - 1)])]
    ppermute x1, waiting for transfers between devices: 1.74 us -> 3.74 us  [per_device(): after = lax.ppermute(top, 'blk', [(i + 1, i) for i in range(size - 1)])]
  transfers between devices with their start and end apart: 26 -> 27, of which waited for: 13 -> 15; matrix products, arithmetic and copies ran while one was open for 9% -> 11% of each run, Pallas kernels for 12% -> 12%
where the time goes in v10:
time: 155 us; the launch traced here: 153 us
  starting transfers between devices  56.4 us (36%)
  waiting for transfers between devices  38.8 us (25%)
  Pallas kernels  30 us (19%)
  local copies, waits for them, and re-layouts  22.4 us (14%)
  other arithmetic  2.58 us (2%)
  between operations  2.45 us (2%)
    ppermute x14, waiting for transfers between devices, ring(): return lax.ppermute(x, axis, [(i, (i + step) % size) for i in range(size)])  25.1 us
    ppermute x14, starting transfers between devices, ring(): return lax.ppermute(x, axis, [(i, (i + step) % size) for i in range(size)])  23.2 us
    pallas_call x1, Pallas kernels, attend(): pl.pallas_call(attend_body, out_shape=jax.ShapeDtypeStruct((blocks, HEAD,...  12.5 us
    unnamed x56, local copies, waits for them, and re-layouts  9.65 us
    all_to_all x1, starting transfers between devices, per_device(): parts = lax.all_to_all(heads, 'blk', 0, 0, tiled=True)  8.72 us
    ppermute x9, starting transfers between devices, swap(): lax.ppermute(x, axis, [(i, i ^ bits) for i in range(lax.axis_size(axis))])  8.65 us
    all_to_all x1, starting transfers between devices, per_device(): lax.all_to_all(mixed, 'blk', 0, 0, tiled=True)[:HEADS]  8.08 us
    ppermute x9, waiting for transfers between devices, swap(): lax.ppermute(x, axis, [(i, i ^ bits) for i in range(lax.axis_size(axis))])  6.32 us
  transfers between devices with their start and end apart: 27, of which 15 were waited for; matrix products, arithmetic and copies ran while one was open for 11% of the time, Pallas kernels for 12%

profile of v10, /device:TPU:104, one launch (start us, length us, event | category | flops | bytes accessed | tf_op | source)
XLA Modules:
  0.0 152.6 jit_solution(15579061422208346638)
XLA Ops:
  2.2 1.7 %collective-permute-start.2 = (bf16[144,1536]{1,0:T(8,128)(2,1)}, bf16[144,1536]{1,0:T(8,128)(2,1)S(1)}, u32[]{:S(2)}, u32[]{:S(2)}) collective-permute-start(bf16[144,1536]{1,0:T(8,128)(2,1)} %bitcast.48), channel_id=1, source_target_pairs={{0,12},{1,13},{2,14},{3,15},{4,0},{5,1},{6,2},{7,3},{8,4},{9,5},{1... | collective-permute-start | bytes 1327112 | tf_op jit(solution)/shard_map/ppermute | solution.py:54
  4.7 2.4 %collective-permute-start.6 = (bf16[144,1536]{1,0:T(8,128)(2,1)}, bf16[144,1536]{1,0:T(8,128)(2,1)S(1)}, u32[]{:S(2)}, u32[]{:S(2)}) collective-permute-start(bf16[144,1536]{1,0:T(8,128)(2,1)} %bitcast.49), channel_id=1, source_target_pairs={{0,2},{1,3},{2,0},{3,1},{4,6},{5,7},{6,4},{7,5},{8,10},{9,11},{10,... | collective-permute-start | bytes 1327112 | tf_op jit(solution)/shard_map/ppermute | solution.py:38
  9.7 4.4 %collective-permute-done.refs_1_ = bf16[144,1536]{1,0:T(8,128)(2,1)S(1)} collective-permute-done((bf16[144,1536]{1,0:T(8,128)(2,1)}, bf16[144,1536]{1,0:T(8,128)(2,1)S(1)}, u32[]{:S(2)}, u32[]{:S(2)}) %collective-permute-start) | collective-permute-done | bytes 442400 | tf_op jit(solution)/shard_map/ppermute | solution.py:54
  14.5 3.0 %collective-permute-start.3 = (bf16[72,1536]{1,0:T(8,128)(2,1)S(1)}, bf16[72,1536]{1,0:T(8,128)(2,1)S(1)}, u32[]{:S(2)}, u32[]{:S(2)}) collective-permute-start(bf16[72,1536]{1,0:T(8,128)(2,1)S(1)} %slice.61), channel_id=1, source_target_pairs={{0,12},{1,13},{2,14},{3,15},{4,0},{5,1},{6,2},{7,3},{8,4},{9,5},{1... | collective-permute-start | bytes 663560 | tf_op jit(solution)/shard_map/ppermute | solution.py:54
  18.1 3.0 %collective-permute-start.8 = (bf16[144,1536]{1,0:T(8,128)(2,1)S(1)}, bf16[144,1536]{1,0:T(8,128)(2,1)}, u32[]{:S(2)}, u32[]{:S(2)}) collective-permute-start(bf16[144,1536]{1,0:T(8,128)(2,1)S(1)} %collective-permute-done.6.refs_3_), channel_id=1, source_target_pairs={{0,12},{1,13},{2,14},{3,15},{4,0},{5,1},{6,2},{7,3},{8,4},{9,5},{1... | collective-permute-start | bytes 1327112 | tf_op jit(solution)/shard_map/ppermute | solution.py:54
  21.1 2.2 %collective-permute-done.1 = bf16[72,1536]{1,0:T(8,128)(2,1)S(1)} collective-permute-done((bf16[72,1536]{1,0:T(8,128)(2,1)S(1)}, bf16[72,1536]{1,0:T(8,128)(2,1)S(1)}, u32[]{:S(2)}, u32[]{:S(2)}) %collective-permute-start.1) | collective-permute-done | bytes 221216 | tf_op jit(solution)/shard_map/ppermute | solution.py:54
  24.7 2.3 %collective-permute-start.4 = (bf16[144,1536]{1,0:T(8,128)(2,1)}, bf16[144,1536]{1,0:T(8,128)(2,1)}, u32[]{:S(2)}, u32[]{:S(2)}) collective-permute-start(bf16[144,1536]{1,0:T(8,128)(2,1)} %constant_dynamic-update-slice_fusion.refs_4_), channel_id=1, source_target_pairs={{0,2},{1,3},{2,0},{3,1},{4,6},{5,7},{6,4},{7,5},{8,10},{9,11},{10,... | collective-permute-start | bytes 1327112 | tf_op jit(solution)/shard_map/ppermute | solution.py:38
  27.4 3.8 %collective-permute-done.7.refs_5_ = bf16[144,1536]{1,0:T(8,128)(2,1)} collective-permute-done((bf16[144,1536]{1,0:T(8,128)(2,1)S(1)}, bf16[144,1536]{1,0:T(8,128)(2,1)}, u32[]{:S(2)}, u32[]{:S(2)}) %collective-permute-start.7) | collective-permute-done | bytes 442400 | tf_op jit(solution)/shard_map/ppermute | solution.py:54
  31.3 3.0 %collective-permute-start.11 = (bf16[384,1536]{1,0:T(8,128)(2,1)S(1)}, bf16[384,1536]{1,0:T(8,128)(2,1)S(1)}, u32[]{:S(2)}, u32[]{:S(2)}) collective-permute-start(bf16[384,1536]{1,0:T(8,128)(2,1)S(1)} %pad_maximum_fusion.refs_0_), channel_id=1, source_target_pairs={{0,12},{1,13},{2,14},{3,15},{4,0},{5,1},{6,2},{7,3},{8,4},{9,5},{1... | collective-permute-start | bytes 3538952 | tf_op jit(solution)/shard_map/ppermute | solution.py:54
  34.3 2.3 %collective-permute-start.12 = (bf16[384,1536]{1,0:T(8,128)(2,1)S(1)}, bf16[384,1536]{1,0:T(8,128)(2,1)}, u32[]{:S(2)}, u32[]{:S(2)}) collective-permute-start(bf16[384,1536]{1,0:T(8,128)(2,1)S(1)} %pad_maximum_fusion.refs_0_), channel_id=1, source_target_pairs={{0,2},{1,3},{2,0},{3,1},{4,6},{5,7},{6,4},{7,5},{8,10},{9,11},{10,... | collective-permute-start | bytes 3538952 | tf_op jit(solution)/shard_map/ppermute | solution.py:38
  37.3 3.4 %project_qkv.1 = (bf16[8,144,128]{2,1,0:T(8,128)(2,1)S(1)}, bf16[8,144,128]{2,1,0:T(8,128)(2,1)}) custom-call(s32[1]{0:T(128)} %bitcast.2.chip_ref, bf16[16,128]{1,0:T(8,128)(2,1)S(1)} %marker.3.ready, bf16[128,1536]{1,0:T(8,128)(2,1)S(1)} %fusion.5.own_x, bf16[128,1536]{1,0:T(8,128)(2,1)} %collective-permute-done.5.peer_x, bf16[144,1536]{1,0:T(8,128)(2,1)S(1)} %bitcast.50, ...), custom_call_target="tpu_custom_call" | custom-call | flops 1000 | bytes 1000 | tf_op jit(solution)/shard_map/project_qkv/pallas_call | solution.py:96
  45.1 8.7 %all-to-all-start = ((bf16[16,192,128]{2,1,0:T(8,128)(2,1)}), bf16[16,192,128]{2,1,0:T(8,128)(2,1)}, u32[]{:S(2)}, u32[]{:S(2)}) async-start(bf16[16,192,128]{2,1,0:T(8,128)(2,1)} %copy-done.2), calls=%async_computation | async-start | bytes 1572864 | tf_op jit(solution)/shard_map/all_to_all | solution.py:531
  53.9 4.2 %collective-permute-done.11.refs_1_.refs_2_ = bf16[384,1536]{1,0:T(8,128)(2,1)S(1)} collective-permute-done((bf16[384,1536]{1,0:T(8,128)(2,1)S(1)}, bf16[384,1536]{1,0:T(8,128)(2,1)S(1)}, u32[]{:S(2)}, u32[]{:S(2)}) %collective-permute-start.11) | collective-permute-done | bytes 1179680 | tf_op jit(solution)/shard_map/ppermute | solution.py:54
  58.9 3.7 %collective-permute-start.14 = (bf16[192,1536]{1,0:T(8,128)(2,1)}, bf16[192,1536]{1,0:T(8,128)(2,1)S(1)}, u32[]{:S(2)}, u32[]{:S(2)}) collective-permute-start(bf16[192,1536]{1,0:T(8,128)(2,1)} %slice.54), channel_id=1, source_target_pairs={{0,12},{1,13},{2,14},{3,15},{4,0},{5,1},{6,2},{7,3},{8,4},{9,5},{1... | collective-permute-start | bytes 1769480 | tf_op jit(solution)/shard_map/ppermute | solution.py:54
  63.6 1.9 %slice.62 = bf16[192,1536]{1,0:T(8,128)(2,1)} slice(bf16[384,1536]{1,0:T(8,128)(2,1)} %collective-permute-done.10.refs_0_.refs_1_), slice={[0:192], [0:1536]} | slice | bytes 1179648 | tf_op jit(solution)/shard_map/slice | solution.py:64
  65.6 3.2 %collective-permute-start.17 = (bf16[384,1536]{1,0:T(8,128)(2,1)}, bf16[384,1536]{1,0:T(8,128)(2,1)}, u32[]{:S(2)}, u32[]{:S(2)}) collective-permute-start(bf16[384,1536]{1,0:T(8,128)(2,1)} %collective-permute-done.12.refs_2_.refs_3_), channel_id=1, source_target_pairs={{0,12},{1,13},{2,14},{3,15},{4,0},{5,1},{6,2},{7,3},{8,4},{9,5},{1... | collective-permute-start | bytes 3538952 | tf_op jit(solution)/shard_map/ppermute | solution.py:54
  70.4 3.7 %all-to-all-done.parts = bf16[16,192,128]{2,1,0:T(8,128)(2,1)} async-done(((bf16[16,192,128]{2,1,0:T(8,128)(2,1)}), bf16[16,192,128]{2,1,0:T(8,128)(2,1)}, u32[]{:S(2)}, u32[]{:S(2)}) %all-to-all-start) | async-done | bytes 786464 | tf_op jit(solution)/shard_map/all_to_all | solution.py:531
  74.1 12.5 %attend.1 = bf16[16,64,128]{2,1,0:T(8,128)(2,1)} custom-call(s32[1]{0:T(128)S(6)} %copy.32.count_ref, bf16[16,192,128]{2,1,0:T(8,128)(2,1)} %all-to-all-done.parts, bf16[128,256]{1,0:T(8,128)(2,1)S(1)} %text_keys.1.text, bf16[16,128]{1,0:T(8,128)(2,1)S(1)} %marker.4.mark), custom_call_target="tpu_custom_call" | custom-call | flops 1000 | bytes 1000 | tf_op jit(solution)/shard_map/attend/pallas_call | solution.py:253
  88.6 8.1 %all-to-all-start.1 = ((bf16[16,64,128]{2,1,0:T(8,128)(2,1)}), bf16[16,64,128]{2,1,0:T(8,128)(2,1)}, u32[]{:S(2)}, u32[]{:S(2)}) async-start(bf16[16,64,128]{2,1,0:T(8,128)(2,1)} %attend.1), calls=%async_computation.1 | async-start | bytes 524288 | tf_op jit(solution)/shard_map/all_to_all | solution.py:546
  98.3 6.1 %collective-permute-done.16.refs_1_.refs_5_ = bf16[384,1536]{1,0:T(8,128)(2,1)} collective-permute-done((bf16[384,1536]{1,0:T(8,128)(2,1)}, bf16[384,1536]{1,0:T(8,128)(2,1)}, u32[]{:S(2)}, u32[]{:S(2)}) %collective-permute-start.16) | collective-permute-done | bytes 1179680 | tf_op jit(solution)/shard_map/ppermute | solution.py:54
  104.4 1.7 %slice.66 = bf16[96,1536]{1,0:T(8,128)(2,1)} slice(bf16[384,1536]{1,0:T(8,128)(2,1)} %collective-permute-done.16.refs_1_.refs_5_), slice={[192:288], [0:1536]} | slice | bytes 589824 | tf_op jit(solution)/shard_map/slice | solution.py:543
  106.1 1.7 %slice.67 = bf16[96,1536]{1,0:T(8,128)(2,1)} slice(bf16[384,1536]{1,0:T(8,128)(2,1)} %collective-permute-done.17.refs_2_.refs_6_), slice={[288:384], [0:1536]} | slice | bytes 589824 | tf_op jit(solution)/shard_map/slice | solution.py:544
  107.8 3.2 %collective-permute-start.19 = (bf16[96,1536]{1,0:T(8,128)(2,1)}, bf16[96,1536]{1,0:T(8,128)(2,1)}, u32[]{:S(2)}, u32[]{:S(2)}) collective-permute-start(bf16[96,1536]{1,0:T(8,128)(2,1)} %slice.67), channel_id=1, source_target_pairs={{0,12},{1,13},{2,14},{3,15},{4,0},{5,1},{6,2},{7,3},{8,4},{9,5},{1... | collective-permute-start | bytes 884744 | tf_op jit(solution)/shard_map/ppermute | solution.py:54
  112.1 2.2 %collective-permute-done.18.refs_3_.refs_7_ = bf16[96,1536]{1,0:T(8,128)(2,1)} collective-permute-done((bf16[96,1536]{1,0:T(8,128)(2,1)}, bf16[96,1536]{1,0:T(8,128)(2,1)}, u32[]{:S(2)}, u32[]{:S(2)}) %collective-permute-start.18) | collective-permute-done | bytes 294944 | tf_op jit(solution)/shard_map/ppermute | solution.py:54
  118.9 1.7 %collective-permute-done.20.peer_x = bf16[128,1536]{1,0:T(8,128)(2,1)S(1)} collective-permute-done((bf16[128,1536]{1,0:T(8,128)(2,1)S(1)}, bf16[128,1536]{1,0:T(8,128)(2,1)S(1)}, u32[]{:S(2)}, u32[]{:S(2)}) %collective-permute-start.20) | collective-permute-done | bytes 393248 | tf_op jit(solution)/shard_map/ppermute | solution.py:38
  120.7 3.6 %mlp_first.1.own_act = bf16[8,192,256]{2,1,0:T(8,128)(2,1)S(1)} custom-call(s32[1]{0:T(128)} %bitcast.2.chip_ref, bf16[128,1536]{1,0:T(8,128)(2,1)S(1)} %get-tuple-element.49.own_x, bf16[128,1536]{1,0:T(8,128)(2,1)S(1)} %collective-permute-done.20.peer_x, bf16[384,1536]{1,0:T(8,128)(2,1)S(1)} %pad_maximum_fusion.refs_0_, ...), custom_call_target="tpu_custom_call" | custom-call | flops 1000 | bytes 1000 | tf_op jit(solution)/shard_map/mlp_first/pallas_call | solution.py:325
  124.5 2.1 %collective-permute-done.21.peer_act = bf16[8,192,256]{2,1,0:T(8,128)(2,1)S(1)} collective-permute-done((bf16[8,192,256]{2,1,0:T(8,128)(2,1)S(1)}, bf16[8,192,256]{2,1,0:T(8,128)(2,1)S(1)}, u32[]{:S(2)}, u32[]{:S(2)}) %collective-permute-start.21) | collective-permute-done | bytes 786464 | tf_op jit(solution)/shard_map/ppermute | solution.py:38
  126.7 4.1 %mlp_second.1 = (f32[8,96,128]{2,1,0:T(8,128)S(1)}, f32[8,96,128]{2,1,0:T(8,128)}) custom-call(s32[1]{0:T(128)} %bitcast.2.chip_ref, s32[1]{0:T(128)} %bitcast.core_ref, bf16[8,192,256]{2,1,0:T(8,128)(2,1)S(1)} %mlp_first.1.own_act, bf16[8,192,256]{2,1,0:T(8,128)(2,1)S(1)} %collective-permute-done.21.peer_act, ...), custom_call_target="tpu_custom_call" | custom-call | flops 1000 | bytes 1000 | tf_op jit(solution)/shard_map/mlp_second/pallas_call | solution.py:365
  137.3 5.8 %collective-permute-start.23 = (bf16[64,32]{1,0:T(8,128)(2,1)S(1)}, bf16[64,32]{1,0:T(8,128)(2,1)S(1)}, u32[]{:S(2)}, u32[]{:S(2)}) collective-permute-start(bf16[64,32]{1,0:T(8,128)(2,1)S(1)} %get-tuple-element.58), channel_id=1, source_target_pairs={{0,16},{16,32},{32,48},{48,64},{64,80},{80,96},{96,112},{112,128},... | collective-permute-start | bytes 12296 | tf_op jit(solution)/shard_map/ppermute | solution.py:570
  143.2 1.9 %collective-permute-start.24 = (bf16[64,32]{1,0:T(8,128)(2,1)S(1)}, bf16[64,32]{1,0:T(8,128)(2,1)S(1)}, u32[]{:S(2)}, u32[]{:S(2)}) collective-permute-start(bf16[64,32]{1,0:T(8,128)(2,1)S(1)} %get-tuple-element.59), channel_id=1, source_target_pairs={{16,0},{32,16},{48,32},{64,48},{80,64},{96,80},{112,96},{128,112},... | collective-permute-start | bytes 12296 | tf_op jit(solution)/shard_map/ppermute | solution.py:571
  147.2 3.7 %collective-permute-done.24.after = bf16[64,32]{1,0:T(8,128)(2,1)S(1)} collective-permute-done((bf16[64,32]{1,0:T(8,128)(2,1)S(1)}, bf16[64,32]{1,0:T(8,128)(2,1)S(1)}, u32[]{:S(2)}, u32[]{:S(2)}) %collective-permute-start.24) | collective-permute-done | bytes 4128 | tf_op jit(solution)/shard_map/ppermute | solution.py:571
  150.9 1.7 %convolve.1 = bf16[4,128,512]{2,1,0:T(8,128)(2,1)} custom-call(s32[1]{0:T(128)S(6)} %convert_element_type.12.live_ref, bf16[128,64]{1,0:T(8,128)(2,1)S(1)} %get-tuple-element.57.scaled, bf16[64,32]{1,0:T(8,128)(2,1)S(1)} %collective-permute-done.23.before, bf16[64,32]{1,0:T(8,128)(2,1)S(1)} %collective-permute-done.24.after, ...), custom_call_target="tpu_custom_call" | custom-call | flops 1000 | bytes 1000 | tf_op jit(solution)/shard_map/convolve/pallas_call | solution.py:463
  (124 shorter events, 33.0 us)
Async XLA Ops:
  0.7 13.4 %collective-permute-start = (bf16[144,1536]{1,0:T(8,128)(2,1)}, bf16[144,1536]{1,0:T(8,128)(2,1)S(1)}, u32[]{:S(2)}, u32[]{:S(2)}) collective-permute-start(bf16[144,1536]{1,0:T(8,128)(2,1)} %bitcast.47), channel_id=1, source_target_pairs={{0,4},{1,5},{2,6},{3,7},{4,8},{5,9},{6,10},{7,11},{8,12},{9,13},{1... | collective-permute-start | bytes 1327112 | tf_op jit(solution)/shard_map/ppermute | solution.py:54
  2.2 12.2 %collective-permute-start.2 = (bf16[144,1536]{1,0:T(8,128)(2,1)}, bf16[144,1536]{1,0:T(8,128)(2,1)S(1)}, u32[]{:S(2)}, u32[]{:S(2)}) collective-permute-start(bf16[144,1536]{1,0:T(8,128)(2,1)} %bitcast.48), channel_id=1, source_target_pairs={{0,12},{1,13},{2,14},{3,15},{4,0},{5,1},{6,2},{7,3},{8,4},{9,5},{1... | collective-permute-start | bytes 1327112 | tf_op jit(solution)/shard_map/ppermute | solution.py:54
  4.7 13.1 %collective-permute-start.6 = (bf16[144,1536]{1,0:T(8,128)(2,1)}, bf16[144,1536]{1,0:T(8,128)(2,1)S(1)}, u32[]{:S(2)}, u32[]{:S(2)}) collective-permute-start(bf16[144,1536]{1,0:T(8,128)(2,1)} %bitcast.49), channel_id=1, source_target_pairs={{0,2},{1,3},{2,0},{3,1},{4,6},{5,7},{6,4},{7,5},{8,10},{9,11},{10,... | collective-permute-start | bytes 1327112 | tf_op jit(solution)/shard_map/ppermute | solution.py:38
  14.1 9.2 %collective-permute-start.1 = (bf16[72,1536]{1,0:T(8,128)(2,1)S(1)}, bf16[72,1536]{1,0:T(8,128)(2,1)S(1)}, u32[]{:S(2)}, u32[]{:S(2)}) collective-permute-start(bf16[72,1536]{1,0:T(8,128)(2,1)S(1)} %slice.60), channel_id=1, source_target_pairs={{0,4},{1,5},{2,6},{3,7},{4,8},{5,9},{6,10},{7,11},{8,12},{9,13},{1... | collective-permute-start | bytes 663560 | tf_op jit(solution)/shard_map/ppermute | solution.py:54
  14.4 16.8 %copy-start.4 = (bf16[144,1536]{1,0:T(8,128)(2,1)}, bf16[144,1536]{1,0:T(8,128)(2,1)S(1)}, u32[]{:S(2)}) copy-start(bf16[144,1536]{1,0:T(8,128)(2,1)S(1)} %collective-permute-done.2.refs_2_) | copy-start | bytes 1327108
  14.5 9.5 %collective-permute-start.3 = (bf16[72,1536]{1,0:T(8,128)(2,1)S(1)}, bf16[72,1536]{1,0:T(8,128)(2,1)S(1)}, u32[]{:S(2)}, u32[]{:S(2)}) collective-permute-start(bf16[72,1536]{1,0:T(8,128)(2,1)S(1)} %slice.61), channel_id=1, source_target_pairs={{0,12},{1,13},{2,14},{3,15},{4,0},{5,1},{6,2},{7,3},{8,4},{9,5},{1... | collective-permute-start | bytes 663560 | tf_op jit(solution)/shard_map/ppermute | solution.py:54
  17.9 13.4 %collective-permute-start.7 = (bf16[144,1536]{1,0:T(8,128)(2,1)S(1)}, bf16[144,1536]{1,0:T(8,128)(2,1)}, u32[]{:S(2)}, u32[]{:S(2)}) collective-permute-start(bf16[144,1536]{1,0:T(8,128)(2,1)S(1)} %collective-permute-done.6.refs_3_), channel_id=1, source_target_pairs={{0,4},{1,5},{2,6},{3,7},{4,8},{5,9},{6,10},{7,11},{8,12},{9,13},{1... | collective-permute-start | bytes 1327112 | tf_op jit(solution)/shard_map/ppermute | solution.py:54
  18.1 13.1 %collective-permute-start.8 = (bf16[144,1536]{1,0:T(8,128)(2,1)S(1)}, bf16[144,1536]{1,0:T(8,128)(2,1)}, u32[]{:S(2)}, u32[]{:S(2)}) collective-permute-start(bf16[144,1536]{1,0:T(8,128)(2,1)S(1)} %collective-permute-done.6.refs_3_), channel_id=1, source_target_pairs={{0,12},{1,13},{2,14},{3,15},{4,0},{5,1},{6,2},{7,3},{8,4},{9,5},{1... | collective-permute-start | bytes 1327112 | tf_op jit(solution)/shard_map/ppermute | solution.py:54
  24.7 11.9 %collective-permute-start.4 = (bf16[144,1536]{1,0:T(8,128)(2,1)}, bf16[144,1536]{1,0:T(8,128)(2,1)}, u32[]{:S(2)}, u32[]{:S(2)}) collective-permute-start(bf16[144,1536]{1,0:T(8,128)(2,1)} %constant_dynamic-update-slice_fusion.refs_4_), channel_id=1, source_target_pairs={{0,2},{1,3},{2,0},{3,1},{4,6},{5,7},{6,4},{7,5},{8,10},{9,11},{10,... | collective-permute-start | bytes 1327112 | tf_op jit(solution)/shard_map/ppermute | solution.py:38
  27.3 10.0 %collective-permute-start.5 = (bf16[128,1536]{1,0:T(8,128)(2,1)S(1)}, bf16[128,1536]{1,0:T(8,128)(2,1)}, u32[]{:S(2)}, u32[]{:S(2)}) collective-permute-start(bf16[128,1536]{1,0:T(8,128)(2,1)S(1)} %fusion.5.own_x), channel_id=1, source_target_pairs={{0,1},{1,0},{2,3},{3,2},{4,5},{5,4},{6,7},{7,6},{8,9},{9,8},{10,11... | collective-permute-start | bytes 1179656 | tf_op jit(solution)/shard_map/ppermute | solution.py:38
  31.3 26.7 %collective-permute-start.11 = (bf16[384,1536]{1,0:T(8,128)(2,1)S(1)}, bf16[384,1536]{1,0:T(8,128)(2,1)S(1)}, u32[]{:S(2)}, u32[]{:S(2)}) collective-permute-start(bf16[384,1536]{1,0:T(8,128)(2,1)S(1)} %pad_maximum_fusion.refs_0_), channel_id=1, source_target_pairs={{0,12},{1,13},{2,14},{3,15},{4,0},{5,1},{6,2},{7,3},{8,4},{9,5},{1... | collective-permute-start | bytes 3538952 | tf_op jit(solution)/shard_map/ppermute | solution.py:54
  34.3 31.2 %collective-permute-start.12 = (bf16[384,1536]{1,0:T(8,128)(2,1)S(1)}, bf16[384,1536]{1,0:T(8,128)(2,1)}, u32[]{:S(2)}, u32[]{:S(2)}) collective-permute-start(bf16[384,1536]{1,0:T(8,128)(2,1)S(1)} %pad_maximum_fusion.refs_0_), channel_id=1, source_target_pairs={{0,2},{1,3},{2,0},{3,1},{4,6},{5,7},{6,4},{7,5},{8,10},{9,11},{10,... | collective-permute-start | bytes 3538952 | tf_op jit(solution)/shard_map/ppermute | solution.py:38
  36.6 26.9 %collective-permute-start.10 = (bf16[384,1536]{1,0:T(8,128)(2,1)S(1)}, bf16[384,1536]{1,0:T(8,128)(2,1)}, u32[]{:S(2)}, u32[]{:S(2)}) collective-permute-start(bf16[384,1536]{1,0:T(8,128)(2,1)S(1)} %pad_maximum_fusion.refs_0_), channel_id=1, source_target_pairs={{0,4},{1,5},{2,6},{3,7},{4,8},{5,9},{6,10},{7,11},{8,12},{9,13},{1... | collective-permute-start | bytes 3538952 | tf_op jit(solution)/shard_map/ppermute | solution.py:54
  41.4 1.8 %collective-permute-start.9 = (bf16[8,144,128]{2,1,0:T(8,128)(2,1)}, bf16[8,144,128]{2,1,0:T(8,128)(2,1)S(1)}, u32[]{:S(2)}, u32[]{:S(2)}) collective-permute-start(bf16[8,144,128]{2,1,0:T(8,128)(2,1)} %get-tuple-element.38), channel_id=1, source_target_pairs={{0,1},{1,0},{2,3},{3,2},{4,5},{5,4},{6,7},{7,6},{8,9},{9,8},{10,11... | collective-permute-start | bytes 884744 | tf_op jit(solution)/shard_map/ppermute | solution.py:38
  45.1 24.4 %slice-start = ((s8[4718592]{0:T(1024)(128)(4,1)}), s8[524288]{0:T(1024)(128)(4,1)S(1)}, s32[]{:S(2)}) async-start(s8[4718592]{0:T(1024)(128)(4,1)} %bitcast.42), calls=%async_computation.2 | async-start | bytes 1048576
  45.1 29.0 %all-to-all-start = ((bf16[16,192,128]{2,1,0:T(8,128)(2,1)}), bf16[16,192,128]{2,1,0:T(8,128)(2,1)}, u32[]{:S(2)}, u32[]{:S(2)}) async-start(bf16[16,192,128]{2,1,0:T(8,128)(2,1)} %copy-done.2), calls=%async_computation | async-start | bytes 1572864 | tf_op jit(solution)/shard_map/all_to_all | solution.py:531
  58.9 27.6 %collective-permute-start.14 = (bf16[192,1536]{1,0:T(8,128)(2,1)}, bf16[192,1536]{1,0:T(8,128)(2,1)S(1)}, u32[]{:S(2)}, u32[]{:S(2)}) collective-permute-start(bf16[192,1536]{1,0:T(8,128)(2,1)} %slice.54), channel_id=1, source_target_pairs={{0,12},{1,13},{2,14},{3,15},{4,0},{5,1},{6,2},{7,3},{8,4},{9,5},{1... | collective-permute-start | bytes 1769480 | tf_op jit(solution)/shard_map/ppermute | solution.py:54
  65.5 21.1 %collective-permute-start.13 = (bf16[192,1536]{1,0:T(8,128)(2,1)}, bf16[192,1536]{1,0:T(8,128)(2,1)}, u32[]{:S(2)}, u32[]{:S(2)}) collective-permute-start(bf16[192,1536]{1,0:T(8,128)(2,1)} %slice.62), channel_id=1, source_target_pairs={{0,4},{1,5},{2,6},{3,7},{4,8},{5,9},{6,10},{7,11},{8,12},{9,13},{1... | collective-permute-start | bytes 1769480 | tf_op jit(solution)/shard_map/ppermute | solution.py:54
  65.5 38.8 %collective-permute-start.16 = (bf16[384,1536]{1,0:T(8,128)(2,1)}, bf16[384,1536]{1,0:T(8,128)(2,1)}, u32[]{:S(2)}, u32[]{:S(2)}) collective-permute-start(bf16[384,1536]{1,0:T(8,128)(2,1)} %collective-permute-done.12.refs_2_.refs_3_), channel_id=1, source_target_pairs={{0,4},{1,5},{2,6},{3,7},{4,8},{5,9},{6,10},{7,11},{8,12},{9,13},{1... | collective-permute-start | bytes 3538952 | tf_op jit(solution)/shard_map/ppermute | solution.py:54
  65.6 40.5 %collective-permute-start.17 = (bf16[384,1536]{1,0:T(8,128)(2,1)}, bf16[384,1536]{1,0:T(8,128)(2,1)}, u32[]{:S(2)}, u32[]{:S(2)}) collective-permute-start(bf16[384,1536]{1,0:T(8,128)(2,1)} %collective-permute-done.12.refs_2_.refs_3_), channel_id=1, source_target_pairs={{0,12},{1,13},{2,14},{3,15},{4,0},{5,1},{6,2},{7,3},{8,4},{9,5},{1... | collective-permute-start | bytes 3538952 | tf_op jit(solution)/shard_map/ppermute | solution.py:54
  70.4 26.2 %copy-start.20 = (bf16[144,512]{1,0:T(8,128)(2,1)S(1)}, bf16[144,512]{1,0:T(8,128)(2,1)}, u32[]{:S(2)}) copy-start(bf16[144,512]{1,0:T(8,128)(2,1)} %param.30) | copy-start | bytes 442372
  70.4 27.5 %copy-start.24 = (f32[1,4,2048]{2,1,0:T(4,128)S(1)}, f32[1,4,2048]{2,1,0:T(4,128)}, u32[]{:S(2)}) copy-start(f32[1,4,2048]{2,1,0:T(4,128)} %param.18) | copy-start | bytes 98308
  86.6 25.5 %collective-permute-start.15 = (bf16[192,1536]{1,0:T(8,128)(2,1)}, bf16[192,1536]{1,0:T(8,128)(2,1)}, u32[]{:S(2)}, u32[]{:S(2)}) collective-permute-start(bf16[192,1536]{1,0:T(8,128)(2,1)} %collective-permute-done.13.refs_4_), channel_id=1, source_target_pairs={{0,2},{1,3},{2,0},{3,1},{4,6},{5,7},{6,4},{7,5},{8,10},{9,11},{10,... | collective-permute-start | bytes 1769480 | tf_op jit(solution)/shard_map/ppermute | solution.py:38
  88.6 22.5 %all-to-all-start.1 = ((bf16[16,64,128]{2,1,0:T(8,128)(2,1)}), bf16[16,64,128]{2,1,0:T(8,128)(2,1)}, u32[]{:S(2)}, u32[]{:S(2)}) async-start(bf16[16,64,128]{2,1,0:T(8,128)(2,1)} %attend.1), calls=%async_computation.1 | async-start | bytes 524288 | tf_op jit(solution)/shard_map/all_to_all | solution.py:546
  106.1 8.2 %collective-permute-start.18 = (bf16[96,1536]{1,0:T(8,128)(2,1)}, bf16[96,1536]{1,0:T(8,128)(2,1)}, u32[]{:S(2)}, u32[]{:S(2)}) collective-permute-start(bf16[96,1536]{1,0:T(8,128)(2,1)} %slice.66), channel_id=1, source_target_pairs={{0,4},{1,5},{2,6},{3,7},{4,8},{5,9},{6,10},{7,11},{8,12},{9,13},{1... | collective-permute-start | bytes 884744 | tf_op jit(solution)/shard_map/ppermute | solution.py:54
  107.8 7.8 %collective-permute-start.19 = (bf16[96,1536]{1,0:T(8,128)(2,1)}, bf16[96,1536]{1,0:T(8,128)(2,1)}, u32[]{:S(2)}, u32[]{:S(2)}) collective-permute-start(bf16[96,1536]{1,0:T(8,128)(2,1)} %slice.67), channel_id=1, source_target_pairs={{0,12},{1,13},{2,14},{3,15},{4,0},{5,1},{6,2},{7,3},{8,4},{9,5},{1... | collective-permute-start | bytes 884744 | tf_op jit(solution)/shard_map/ppermute | solution.py:54
  118.9 1.7 %collective-permute-start.20 = (bf16[128,1536]{1,0:T(8,128)(2,1)S(1)}, bf16[128,1536]{1,0:T(8,128)(2,1)S(1)}, u32[]{:S(2)}, u32[]{:S(2)}) collective-permute-start(bf16[128,1536]{1,0:T(8,128)(2,1)S(1)} %get-tuple-element.49.own_x), channel_id=1, source_target_pairs={{0,1},{1,0},{2,3},{3,2},{4,5},{5,4},{6,7},{7,6},{8,9},{9,8},{10,11... | collective-permute-start | bytes 1179656 | tf_op jit(solution)/shard_map/ppermute | solution.py:38
  124.3 2.4 %collective-permute-start.21 = (bf16[8,192,256]{2,1,0:T(8,128)(2,1)S(1)}, bf16[8,192,256]{2,1,0:T(8,128)(2,1)S(1)}, u32[]{:S(2)}, u32[]{:S(2)}) collective-permute-start(bf16[8,192,256]{2,1,0:T(8,128)(2,1)S(1)} %mlp_first.1.own_act), channel_id=1, source_target_pairs={{0,1},{1,0},{2,3},{3,2},{4,5},{5,4},{6,7},{7,6},{8,9},{9,8},{10,11... | collective-permute-start | bytes 2359304 | tf_op jit(solution)/shard_map/ppermute | solution.py:38
  131.5 1.9 %collective-permute-start.22 = (f32[8,96,128]{2,1,0:T(8,128)}, f32[8,96,128]{2,1,0:T(8,128)S(1)}, u32[]{:S(2)}, u32[]{:S(2)}) collective-permute-start(f32[8,96,128]{2,1,0:T(8,128)} %get-tuple-element.52), channel_id=1, source_target_pairs={{0,1},{1,0},{2,3},{3,2},{4,5},{5,4},{6,7},{7,6},{8,9},{9,8},{10,11... | collective-permute-start | bytes 1179656 | tf_op jit(solution)/shard_map/ppermute | solution.py:38
  136.5 14.4 %copy-start.19 = (f32[512]{0:T(512)S(1)}, f32[512]{0:T(512)}, u32[]{:S(2)}) copy-start(f32[512]{0:T(512)} %param.31) | copy-start | bytes 6148
  137.3 9.8 %collective-permute-start.23 = (bf16[64,32]{1,0:T(8,128)(2,1)S(1)}, bf16[64,32]{1,0:T(8,128)(2,1)S(1)}, u32[]{:S(2)}, u32[]{:S(2)}) collective-permute-start(bf16[64,32]{1,0:T(8,128)(2,1)S(1)} %get-tuple-element.58), channel_id=1, source_target_pairs={{0,16},{16,32},{32,48},{48,64},{64,80},{80,96},{96,112},{112,128},... | collective-permute-start | bytes 12296 | tf_op jit(solution)/shard_map/ppermute | solution.py:570
  143.2 7.7 %collective-permute-start.24 = (bf16[64,32]{1,0:T(8,128)(2,1)S(1)}, bf16[64,32]{1,0:T(8,128)(2,1)S(1)}, u32[]{:S(2)}, u32[]{:S(2)}) collective-permute-start(bf16[64,32]{1,0:T(8,128)(2,1)S(1)} %get-tuple-element.59), channel_id=1, source_target_pairs={{16,0},{32,16},{48,32},{64,48},{80,64},{96,80},{112,96},{128,112},... | collective-permute-start | bytes 12296 | tf_op jit(solution)/shard_map/ppermute | solution.py:571
  (22 other events, 113.1 us)

commit v11 on v10

--- a/solution.py
+++ b/solution.py
@@ -95,7 +95,7 @@
     inputs = (ready, own_x, peer_x, *weights)
     return pl.pallas_call(
         qkv_body,
-        out_shape=(jax.ShapeDtypeStruct(shape, BF16),) * 2,
+        out_shape=(pltpu.HBM(shape, BF16), jax.ShapeDtypeStruct(shape, BF16)),
         grid=(1,),
         in_specs=[pl.BlockSpec(memory_space=pltpu.SMEM)] + [whole(x) for x in inputs],
         out_specs=(pl.BlockSpec(shape, lambda i: (0, 0, 0)),) * 2,
@@ -134,9 +134,10 @@
 
 def place_heads(core, mine, other, blocks):
     shape = (blocks, 3 * HEAD, mine.shape[2])
+    mine = pltpu.with_memory_space_constraint(mine, pltpu.HBM)
     return pl.pallas_call(
         heads_body,
-        out_shape=jax.ShapeDtypeStruct(shape, BF16),
+        out_shape=pltpu.HBM(shape, BF16),
         grid=(1,),
         in_specs=[pl.BlockSpec(memory_space=pltpu.SMEM), whole(mine), whole(other)],
         out_specs=pl.BlockSpec(shape, lambda i: (0, 0, 0)),
@@ -291,7 +292,7 @@
     return pl.pallas_call(
         middle_body,
         out_shape=(
-            jax.ShapeDtypeStruct((rows, width), F32),
+            pltpu.HBM((rows, width), F32),
             jax.ShapeDtypeStruct((rows, width), BF16),
         ),
         grid=(1,),
@@ -364,7 +365,7 @@
     shape = (count, cols // 2, tokens // 2)
     return pl.pallas_call(
         second_body,
-        out_shape=(jax.ShapeDtypeStruct(shape, F32), jax.ShapeDtypeStruct(shape, F32)),
+        out_shape=(pltpu.HBM(shape, F32), jax.ShapeDtypeStruct(shape, F32)),
         grid=(1,),
         in_specs=[pl.BlockSpec(memory_space=pltpu.SMEM)] * 2
         + [whole(own_act), whole(peer_act)]
@@ -408,6 +409,9 @@
     rows, width = updated.shape
     cols = final_t.shape[0]
     smem = pl.BlockSpec(memory_space=pltpu.SMEM)
+    updated, final_t, own_part = (
+        pltpu.with_memory_space_constraint(x, pltpu.HBM) for x in (updated, final_t, own_part)
+    )
     inputs = (own_part, peer_part, updated, mods, finals, final_t, latent)
     shapes = ((rows, cols), (rows, cols), (rows, cols), (W_P, cols // 2), (W_P, cols // 2))
     return pl.pallas_call(

time: 155 us -> 152 us (0.981)
  local copies, waits for them, and re-layouts: 22.4 us -> 15.2 us
  Pallas kernels: 30 us -> 34 us
    unnamed x56 -> x40, local copies, waits for them, and re-layouts: 9.65 us -> 2.39 us
    pallas_call x4, Pallas kernels: 8.32 us -> 11 us  [the longest x1 4.22 us: mlp_second(): pl.pallas_call(second_body, out_shape=(pltpu.HBM(shape, F32), jax.ShapeDt...]
  transfers between devices with their start and end apart: 27 -> 27, of which waited for: 15 -> 15; matrix products, arithmetic and copies ran while one was open for 11% -> 11% of each run, Pallas kernels for 12% -> 13%
where the time goes in v11:
time: 152 us; the launch traced here: 150 us
  starting transfers between devices  57.7 us (38%)
  waiting for transfers between devices  38.1 us (25%)
  Pallas kernels  34 us (22%)
  local copies, waits for them, and re-layouts  15.2 us (10%)
  other arithmetic  2.58 us (2%)
  between operations  2.41 us (2%)
    ppermute x14, waiting for transfers between devices, ring(): return lax.ppermute(x, axis, [(i, (i + step) % size) for i in range(size)])  25 us
    ppermute x14, starting transfers between devices, ring(): return lax.ppermute(x, axis, [(i, (i + step) % size) for i in range(size)])  23.2 us
    pallas_call x1, Pallas kernels, attend(): pl.pallas_call(attend_body, out_shape=jax.ShapeDtypeStruct((blocks, HEAD,...  12.5 us
    all_to_all x1, starting transfers between devices, per_device(): lax.all_to_all(mixed, 'blk', 0, 0, tiled=True)[:HEADS]  9.29 us
    all_to_all x1, starting transfers between devices, per_device(): parts = lax.all_to_all(heads, 'blk', 0, 0, tiled=True)  8.72 us
    ppermute x9, starting transfers between devices, swap(): lax.ppermute(x, axis, [(i, i ^ bits) for i in range(lax.axis_size(axis))])  8.69 us
    ppermute x9, waiting for transfers between devices, swap(): lax.ppermute(x, axis, [(i, i ^ bits) for i in range(lax.axis_size(axis))])  6.3 us
    ppermute x1, starting transfers between devices, per_device(): before = lax.ppermute(bottom, 'blk', [(i, i + 1) for i in range(size - 1)])  5.83 us
  transfers between devices with their start and end apart: 27, of which 15 were waited for; matrix products, arithmetic and copies ran while one was open for 11% of the time, Pallas kernels for 13%

profile of v11, /device:TPU:104, one launch (start us, length us, event | category | flops | bytes accessed | tf_op | source)
XLA Modules:
  0.0 149.9 jit_solution(16046172962850768465)
XLA Ops:
  2.2 1.7 %collective-permute-start.2 = (bf16[144,1536]{1,0:T(8,128)(2,1)}, bf16[144,1536]{1,0:T(8,128)(2,1)S(1)}, u32[]{:S(2)}, u32[]{:S(2)}) collective-permute-start(bf16[144,1536]{1,0:T(8,128)(2,1)} %bitcast.48), channel_id=1, source_target_pairs={{0,12},{1,13},{2,14},{3,15},{4,0},{5,1},{6,2},{7,3},{8,4},{9,5},{1... | collective-permute-start | bytes 1327112 | tf_op jit(solution)/shard_map/ppermute | solution.py:54
  4.7 2.4 %collective-permute-start.6 = (bf16[144,1536]{1,0:T(8,128)(2,1)}, bf16[144,1536]{1,0:T(8,128)(2,1)S(1)}, u32[]{:S(2)}, u32[]{:S(2)}) collective-permute-start(bf16[144,1536]{1,0:T(8,128)(2,1)} %bitcast.49), channel_id=1, source_target_pairs={{0,2},{1,3},{2,0},{3,1},{4,6},{5,7},{6,4},{7,5},{8,10},{9,11},{10,... | collective-permute-start | bytes 1327112 | tf_op jit(solution)/shard_map/ppermute | solution.py:38
  9.7 4.4 %collective-permute-done.refs_1_ = bf16[144,1536]{1,0:T(8,128)(2,1)S(1)} collective-permute-done((bf16[144,1536]{1,0:T(8,128)(2,1)}, bf16[144,1536]{1,0:T(8,128)(2,1)S(1)}, u32[]{:S(2)}, u32[]{:S(2)}) %collective-permute-start) | collective-permute-done | bytes 442400 | tf_op jit(solution)/shard_map/ppermute | solution.py:54
  14.5 3.0 %collective-permute-start.3 = (bf16[72,1536]{1,0:T(8,128)(2,1)S(1)}, bf16[72,1536]{1,0:T(8,128)(2,1)S(1)}, u32[]{:S(2)}, u32[]{:S(2)}) collective-permute-start(bf16[72,1536]{1,0:T(8,128)(2,1)S(1)} %slice.61), channel_id=1, source_target_pairs={{0,12},{1,13},{2,14},{3,15},{4,0},{5,1},{6,2},{7,3},{8,4},{9,5},{1... | collective-permute-start | bytes 663560 | tf_op jit(solution)/shard_map/ppermute | solution.py:54
  18.1 3.0 %collective-permute-start.8 = (bf16[144,1536]{1,0:T(8,128)(2,1)S(1)}, bf16[144,1536]{1,0:T(8,128)(2,1)}, u32[]{:S(2)}, u32[]{:S(2)}) collective-permute-start(bf16[144,1536]{1,0:T(8,128)(2,1)S(1)} %collective-permute-done.6.refs_3_), channel_id=1, source_target_pairs={{0,12},{1,13},{2,14},{3,15},{4,0},{5,1},{6,2},{7,3},{8,4},{9,5},{1... | collective-permute-start | bytes 1327112 | tf_op jit(solution)/shard_map/ppermute | solution.py:54
  21.1 2.2 %collective-permute-done.1 = bf16[72,1536]{1,0:T(8,128)(2,1)S(1)} collective-permute-done((bf16[72,1536]{1,0:T(8,128)(2,1)S(1)}, bf16[72,1536]{1,0:T(8,128)(2,1)S(1)}, u32[]{:S(2)}, u32[]{:S(2)}) %collective-permute-start.1) | collective-permute-done | bytes 221216 | tf_op jit(solution)/shard_map/ppermute | solution.py:54
  24.7 2.3 %collective-permute-start.4 = (bf16[144,1536]{1,0:T(8,128)(2,1)}, bf16[144,1536]{1,0:T(8,128)(2,1)}, u32[]{:S(2)}, u32[]{:S(2)}) collective-permute-start(bf16[144,1536]{1,0:T(8,128)(2,1)} %constant_dynamic-update-slice_fusion.refs_4_), channel_id=1, source_target_pairs={{0,2},{1,3},{2,0},{3,1},{4,6},{5,7},{6,4},{7,5},{8,10},{9,11},{10,... | collective-permute-start | bytes 1327112 | tf_op jit(solution)/shard_map/ppermute | solution.py:38
  27.4 3.8 %collective-permute-done.7.refs_5_ = bf16[144,1536]{1,0:T(8,128)(2,1)} collective-permute-done((bf16[144,1536]{1,0:T(8,128)(2,1)S(1)}, bf16[144,1536]{1,0:T(8,128)(2,1)}, u32[]{:S(2)}, u32[]{:S(2)}) %collective-permute-start.7) | collective-permute-done | bytes 442400 | tf_op jit(solution)/shard_map/ppermute | solution.py:54
  31.3 3.0 %collective-permute-start.11 = (bf16[384,1536]{1,0:T(8,128)(2,1)S(1)}, bf16[384,1536]{1,0:T(8,128)(2,1)S(1)}, u32[]{:S(2)}, u32[]{:S(2)}) collective-permute-start(bf16[384,1536]{1,0:T(8,128)(2,1)S(1)} %pad_maximum_fusion.refs_0_), channel_id=1, source_target_pairs={{0,12},{1,13},{2,14},{3,15},{4,0},{5,1},{6,2},{7,3},{8,4},{9,5},{1... | collective-permute-start | bytes 3538952 | tf_op jit(solution)/shard_map/ppermute | solution.py:54
  34.3 2.3 %collective-permute-start.12 = (bf16[384,1536]{1,0:T(8,128)(2,1)S(1)}, bf16[384,1536]{1,0:T(8,128)(2,1)}, u32[]{:S(2)}, u32[]{:S(2)}) collective-permute-start(bf16[384,1536]{1,0:T(8,128)(2,1)S(1)} %pad_maximum_fusion.refs_0_), channel_id=1, source_target_pairs={{0,2},{1,3},{2,0},{3,1},{4,6},{5,7},{6,4},{7,5},{8,10},{9,11},{10,... | collective-permute-start | bytes 3538952 | tf_op jit(solution)/shard_map/ppermute | solution.py:38
  37.4 3.5 %project_qkv.1 = (bf16[8,144,128]{2,1,0:T(8,128)(2,1)}, bf16[8,144,128]{2,1,0:T(8,128)(2,1)}) custom-call(s32[1]{0:T(128)} %bitcast.2.chip_ref, bf16[16,128]{1,0:T(8,128)(2,1)S(1)} %marker.3.ready, bf16[128,1536]{1,0:T(8,128)(2,1)S(1)} %fusion.5.own_x, bf16[128,1536]{1,0:T(8,128)(2,1)} %collective-permute-done.5.peer_x, bf16[144,1536]{1,0:T(8,128)(2,1)S(1)} %bitcast.50, ...), custom_call_target="tpu_custom_call" | custom-call | flops 1000 | bytes 1000 | tf_op jit(solution)/shard_map/project_qkv/pallas_call | solution.py:96
  42.6 1.9 %place_heads.1 = bf16[16,192,128]{2,1,0:T(8,128)(2,1)} custom-call(s32[1]{0:T(128)} %bitcast.core_ref, bf16[8,144,128]{2,1,0:T(8,128)(2,1)} %get-tuple-element.37.mine, bf16[8,144,128]{2,1,0:T(8,128)(2,1)S(1)} %collective-permute-done.9.other), custom_call_target="tpu_custom_call" | custom-call | flops 1000 | bytes 1000 | tf_op jit(solution)/shard_map/place_heads/pallas_call | solution.py:138
  44.5 8.7 %all-to-all-start = ((bf16[16,192,128]{2,1,0:T(8,128)(2,1)}), bf16[16,192,128]{2,1,0:T(8,128)(2,1)}, u32[]{:S(2)}, u32[]{:S(2)}) async-start(bf16[16,192,128]{2,1,0:T(8,128)(2,1)} %place_heads.1), calls=%async_computation | async-start | bytes 1572864 | tf_op jit(solution)/shard_map/all_to_all | solution.py:535
  53.3 4.8 %collective-permute-done.11.refs_1_.refs_2_ = bf16[384,1536]{1,0:T(8,128)(2,1)S(1)} collective-permute-done((bf16[384,1536]{1,0:T(8,128)(2,1)S(1)}, bf16[384,1536]{1,0:T(8,128)(2,1)S(1)}, u32[]{:S(2)}, u32[]{:S(2)}) %collective-permute-start.11) | collective-permute-done | bytes 1179680 | tf_op jit(solution)/shard_map/ppermute | solution.py:54
  59.0 3.7 %collective-permute-start.14 = (bf16[192,1536]{1,0:T(8,128)(2,1)}, bf16[192,1536]{1,0:T(8,128)(2,1)S(1)}, u32[]{:S(2)}, u32[]{:S(2)}) collective-permute-start(bf16[192,1536]{1,0:T(8,128)(2,1)} %slice.54), channel_id=1, source_target_pairs={{0,12},{1,13},{2,14},{3,15},{4,0},{5,1},{6,2},{7,3},{8,4},{9,5},{1... | collective-permute-start | bytes 1769480 | tf_op jit(solution)/shard_map/ppermute | solution.py:54
  63.6 1.9 %slice.62 = bf16[192,1536]{1,0:T(8,128)(2,1)} slice(bf16[384,1536]{1,0:T(8,128)(2,1)} %collective-permute-done.10.refs_0_.refs_1_), slice={[0:192], [0:1536]} | slice | bytes 1179648 | tf_op jit(solution)/shard_map/slice | solution.py:64
  65.6 3.2 %collective-permute-start.17 = (bf16[384,1536]{1,0:T(8,128)(2,1)}, bf16[384,1536]{1,0:T(8,128)(2,1)}, u32[]{:S(2)}, u32[]{:S(2)}) collective-permute-start(bf16[384,1536]{1,0:T(8,128)(2,1)} %collective-permute-done.12.refs_2_.refs_3_), channel_id=1, source_target_pairs={{0,12},{1,13},{2,14},{3,15},{4,0},{5,1},{6,2},{7,3},{8,4},{9,5},{1... | collective-permute-start | bytes 3538952 | tf_op jit(solution)/shard_map/ppermute | solution.py:54
  70.4 3.1 %all-to-all-done.parts = bf16[16,192,128]{2,1,0:T(8,128)(2,1)} async-done(((bf16[16,192,128]{2,1,0:T(8,128)(2,1)}), bf16[16,192,128]{2,1,0:T(8,128)(2,1)}, u32[]{:S(2)}, u32[]{:S(2)}) %all-to-all-start) | async-done | bytes 786464 | tf_op jit(solution)/shard_map/all_to_all | solution.py:535
  73.5 12.5 %attend.1 = bf16[16,64,128]{2,1,0:T(8,128)(2,1)} custom-call(s32[1]{0:T(128)S(6)} %copy.32.count_ref, bf16[16,192,128]{2,1,0:T(8,128)(2,1)} %all-to-all-done.parts, bf16[128,256]{1,0:T(8,128)(2,1)S(1)} %text_keys.1.text, bf16[16,128]{1,0:T(8,128)(2,1)S(1)} %marker.4.mark), custom_call_target="tpu_custom_call" | custom-call | flops 1000 | bytes 1000 | tf_op jit(solution)/shard_map/attend/pallas_call | solution.py:254
  88.0 9.3 %all-to-all-start.1 = ((bf16[16,64,128]{2,1,0:T(8,128)(2,1)}), bf16[16,64,128]{2,1,0:T(8,128)(2,1)}, u32[]{:S(2)}, u32[]{:S(2)}) async-start(bf16[16,64,128]{2,1,0:T(8,128)(2,1)} %attend.1), calls=%async_computation.1 | async-start | bytes 524288 | tf_op jit(solution)/shard_map/all_to_all | solution.py:550
  98.9 5.4 %collective-permute-done.16.refs_1_.refs_5_ = bf16[384,1536]{1,0:T(8,128)(2,1)} collective-permute-done((bf16[384,1536]{1,0:T(8,128)(2,1)}, bf16[384,1536]{1,0:T(8,128)(2,1)}, u32[]{:S(2)}, u32[]{:S(2)}) %collective-permute-start.16) | collective-permute-done | bytes 1179680 | tf_op jit(solution)/shard_map/ppermute | solution.py:54
  107.8 3.2 %collective-permute-start.19 = (bf16[96,1536]{1,0:T(8,128)(2,1)}, bf16[96,1536]{1,0:T(8,128)(2,1)}, u32[]{:S(2)}, u32[]{:S(2)}) collective-permute-start(bf16[96,1536]{1,0:T(8,128)(2,1)} %slice.67), channel_id=1, source_target_pairs={{0,12},{1,13},{2,14},{3,15},{4,0},{5,1},{6,2},{7,3},{8,4},{9,5},{1... | collective-permute-start | bytes 884744 | tf_op jit(solution)/shard_map/ppermute | solution.py:54
  112.1 2.2 %collective-permute-done.18.refs_3_.refs_7_ = bf16[96,1536]{1,0:T(8,128)(2,1)} collective-permute-done((bf16[96,1536]{1,0:T(8,128)(2,1)}, bf16[96,1536]{1,0:T(8,128)(2,1)}, u32[]{:S(2)}, u32[]{:S(2)}) %collective-permute-start.18) | collective-permute-done | bytes 294944 | tf_op jit(solution)/shard_map/ppermute | solution.py:54
  118.7 1.7 %collective-permute-done.20.peer_x = bf16[128,1536]{1,0:T(8,128)(2,1)S(1)} collective-permute-done((bf16[128,1536]{1,0:T(8,128)(2,1)S(1)}, bf16[128,1536]{1,0:T(8,128)(2,1)S(1)}, u32[]{:S(2)}, u32[]{:S(2)}) %collective-permute-start.20) | collective-permute-done | bytes 393248 | tf_op jit(solution)/shard_map/ppermute | solution.py:38
  120.4 3.6 %mlp_first.1.own_act = bf16[8,192,256]{2,1,0:T(8,128)(2,1)S(1)} custom-call(s32[1]{0:T(128)} %bitcast.2.chip_ref, bf16[128,1536]{1,0:T(8,128)(2,1)S(1)} %get-tuple-element.49.own_x, bf16[128,1536]{1,0:T(8,128)(2,1)S(1)} %collective-permute-done.20.peer_x, bf16[384,1536]{1,0:T(8,128)(2,1)S(1)} %pad_maximum_fusion.refs_0_, ...), custom_call_target="tpu_custom_call" | custom-call | flops 1000 | bytes 1000 | tf_op jit(solution)/shard_map/mlp_first/pallas_call | solution.py:326
  124.2 2.1 %collective-permute-done.21.peer_act = bf16[8,192,256]{2,1,0:T(8,128)(2,1)S(1)} collective-permute-done((bf16[8,192,256]{2,1,0:T(8,128)(2,1)S(1)}, bf16[8,192,256]{2,1,0:T(8,128)(2,1)S(1)}, u32[]{:S(2)}, u32[]{:S(2)}) %collective-permute-start.21) | collective-permute-done | bytes 786464 | tf_op jit(solution)/shard_map/ppermute | solution.py:38
  126.4 4.2 %mlp_second.1 = (f32[8,96,128]{2,1,0:T(8,128)}, f32[8,96,128]{2,1,0:T(8,128)}) custom-call(s32[1]{0:T(128)} %bitcast.2.chip_ref, s32[1]{0:T(128)} %bitcast.core_ref, bf16[8,192,256]{2,1,0:T(8,128)(2,1)S(1)} %mlp_first.1.own_act, bf16[8,192,256]{2,1,0:T(8,128)(2,1)S(1)} %collective-permute-done.21.peer_act, bf16[384,1536]{1,0:T(8,128)(2,1)S(1)} %pad_maximum_fusion.refs_0_, ...), custom_call_target="tpu_custom_call" | custom-call | flops 1000 | bytes 1000 | tf_op jit(solution)/shard_map/mlp_second/pallas_call | solution.py:366
  132.5 2.1 %last.1 = (f32[128,64]{1,0:T(8,128)S(1)}, f32[128,64]{1,0:T(8,128)S(1)}, bf16[128,64]{1,0:T(8,128)(2,1)S(1)}, bf16[64,32]{1,0:T(8,128)(2,1)S(1)}, bf16[64,32]{1,0:T(8,128)(2,1)S(1)}) custom-call(s32[1]{0:T(128)} %bitcast.core_ref, s32[1]{0:T(128)S(6)} %convert_element_type.12.live_ref, f32[1]{0:T(128)S(6)} %sub.27.gap_ref, ...), custom_call_target="tpu_custom_call" | custom-call | flops 1000 | bytes 1000 | tf_op jit(solution)/shard_map/last/pallas_call | solution.py:417
  134.7 5.8 %collective-permute-start.23 = (bf16[64,32]{1,0:T(8,128)(2,1)S(1)}, bf16[64,32]{1,0:T(8,128)(2,1)S(1)}, u32[]{:S(2)}, u32[]{:S(2)}) collective-permute-start(bf16[64,32]{1,0:T(8,128)(2,1)S(1)} %get-tuple-element.58), channel_id=1, source_target_pairs={{0,16},{16,32},{32,48},{48,64},{64,80},{80,96},{96,112},{112,128},... | collective-permute-start | bytes 12296 | tf_op jit(solution)/shard_map/ppermute | solution.py:574
  140.5 1.9 %collective-permute-start.24 = (bf16[64,32]{1,0:T(8,128)(2,1)S(1)}, bf16[64,32]{1,0:T(8,128)(2,1)S(1)}, u32[]{:S(2)}, u32[]{:S(2)}) collective-permute-start(bf16[64,32]{1,0:T(8,128)(2,1)S(1)} %get-tuple-element.59), channel_id=1, source_target_pairs={{16,0},{32,16},{48,32},{64,48},{80,64},{96,80},{112,96},{128,112},... | collective-permute-start | bytes 12296 | tf_op jit(solution)/shard_map/ppermute | solution.py:575
  144.5 3.7 %collective-permute-done.24.after = bf16[64,32]{1,0:T(8,128)(2,1)S(1)} collective-permute-done((bf16[64,32]{1,0:T(8,128)(2,1)S(1)}, bf16[64,32]{1,0:T(8,128)(2,1)S(1)}, u32[]{:S(2)}, u32[]{:S(2)}) %collective-permute-start.24) | collective-permute-done | bytes 4128 | tf_op jit(solution)/shard_map/ppermute | solution.py:575
  148.2 1.7 %convolve.1 = bf16[4,128,512]{2,1,0:T(8,128)(2,1)} custom-call(s32[1]{0:T(128)S(6)} %convert_element_type.12.live_ref, bf16[128,64]{1,0:T(8,128)(2,1)S(1)} %get-tuple-element.57.scaled, bf16[64,32]{1,0:T(8,128)(2,1)S(1)} %collective-permute-done.23.before, bf16[64,32]{1,0:T(8,128)(2,1)S(1)} %collective-permute-done.24.after, ...), custom_call_target="tpu_custom_call" | custom-call | flops 1000 | bytes 1000 | tf_op jit(solution)/shard_map/convolve/pallas_call | solution.py:467
  (108 shorter events, 29.0 us)
Async XLA Ops:
  0.7 13.4 %collective-permute-start = (bf16[144,1536]{1,0:T(8,128)(2,1)}, bf16[144,1536]{1,0:T(8,128)(2,1)S(1)}, u32[]{:S(2)}, u32[]{:S(2)}) collective-permute-start(bf16[144,1536]{1,0:T(8,128)(2,1)} %bitcast.47), channel_id=1, source_target_pairs={{0,4},{1,5},{2,6},{3,7},{4,8},{5,9},{6,10},{7,11},{8,12},{9,13},{1... | collective-permute-start | bytes 1327112 | tf_op jit(solution)/shard_map/ppermute | solution.py:54
  2.2 12.2 %collective-permute-start.2 = (bf16[144,1536]{1,0:T(8,128)(2,1)}, bf16[144,1536]{1,0:T(8,128)(2,1)S(1)}, u32[]{:S(2)}, u32[]{:S(2)}) collective-permute-start(bf16[144,1536]{1,0:T(8,128)(2,1)} %bitcast.48), channel_id=1, source_target_pairs={{0,12},{1,13},{2,14},{3,15},{4,0},{5,1},{6,2},{7,3},{8,4},{9,5},{1... | collective-permute-start | bytes 1327112 | tf_op jit(solution)/shard_map/ppermute | solution.py:54
  4.7 13.1 %collective-permute-start.6 = (bf16[144,1536]{1,0:T(8,128)(2,1)}, bf16[144,1536]{1,0:T(8,128)(2,1)S(1)}, u32[]{:S(2)}, u32[]{:S(2)}) collective-permute-start(bf16[144,1536]{1,0:T(8,128)(2,1)} %bitcast.49), channel_id=1, source_target_pairs={{0,2},{1,3},{2,0},{3,1},{4,6},{5,7},{6,4},{7,5},{8,10},{9,11},{10,... | collective-permute-start | bytes 1327112 | tf_op jit(solution)/shard_map/ppermute | solution.py:38
  14.1 9.2 %collective-permute-start.1 = (bf16[72,1536]{1,0:T(8,128)(2,1)S(1)}, bf16[72,1536]{1,0:T(8,128)(2,1)S(1)}, u32[]{:S(2)}, u32[]{:S(2)}) collective-permute-start(bf16[72,1536]{1,0:T(8,128)(2,1)S(1)} %slice.60), channel_id=1, source_target_pairs={{0,4},{1,5},{2,6},{3,7},{4,8},{5,9},{6,10},{7,11},{8,12},{9,13},{1... | collective-permute-start | bytes 663560 | tf_op jit(solution)/shard_map/ppermute | solution.py:54
  14.4 16.8 %copy-start.3 = (bf16[144,1536]{1,0:T(8,128)(2,1)}, bf16[144,1536]{1,0:T(8,128)(2,1)S(1)}, u32[]{:S(2)}) copy-start(bf16[144,1536]{1,0:T(8,128)(2,1)S(1)} %collective-permute-done.2.refs_2_) | copy-start | bytes 1327108
  14.5 9.5 %collective-permute-start.3 = (bf16[72,1536]{1,0:T(8,128)(2,1)S(1)}, bf16[72,1536]{1,0:T(8,128)(2,1)S(1)}, u32[]{:S(2)}, u32[]{:S(2)}) collective-permute-start(bf16[72,1536]{1,0:T(8,128)(2,1)S(1)} %slice.61), channel_id=1, source_target_pairs={{0,12},{1,13},{2,14},{3,15},{4,0},{5,1},{6,2},{7,3},{8,4},{9,5},{1... | collective-permute-start | bytes 663560 | tf_op jit(solution)/shard_map/ppermute | solution.py:54
  17.9 13.4 %collective-permute-start.7 = (bf16[144,1536]{1,0:T(8,128)(2,1)S(1)}, bf16[144,1536]{1,0:T(8,128)(2,1)}, u32[]{:S(2)}, u32[]{:S(2)}) collective-permute-start(bf16[144,1536]{1,0:T(8,128)(2,1)S(1)} %collective-permute-done.6.refs_3_), channel_id=1, source_target_pairs={{0,4},{1,5},{2,6},{3,7},{4,8},{5,9},{6,10},{7,11},{8,12},{9,13},{1... | collective-permute-start | bytes 1327112 | tf_op jit(solution)/shard_map/ppermute | solution.py:54
  18.1 13.1 %collective-permute-start.8 = (bf16[144,1536]{1,0:T(8,128)(2,1)S(1)}, bf16[144,1536]{1,0:T(8,128)(2,1)}, u32[]{:S(2)}, u32[]{:S(2)}) collective-permute-start(bf16[144,1536]{1,0:T(8,128)(2,1)S(1)} %collective-permute-done.6.refs_3_), channel_id=1, source_target_pairs={{0,12},{1,13},{2,14},{3,15},{4,0},{5,1},{6,2},{7,3},{8,4},{9,5},{1... | collective-permute-start | bytes 1327112 | tf_op jit(solution)/shard_map/ppermute | solution.py:54
  24.7 11.9 %collective-permute-start.4 = (bf16[144,1536]{1,0:T(8,128)(2,1)}, bf16[144,1536]{1,0:T(8,128)(2,1)}, u32[]{:S(2)}, u32[]{:S(2)}) collective-permute-start(bf16[144,1536]{1,0:T(8,128)(2,1)} %constant_dynamic-update-slice_fusion.refs_4_), channel_id=1, source_target_pairs={{0,2},{1,3},{2,0},{3,1},{4,6},{5,7},{6,4},{7,5},{8,10},{9,11},{10,... | collective-permute-start | bytes 1327112 | tf_op jit(solution)/shard_map/ppermute | solution.py:38
  27.3 10.0 %collective-permute-start.5 = (bf16[128,1536]{1,0:T(8,128)(2,1)S(1)}, bf16[128,1536]{1,0:T(8,128)(2,1)}, u32[]{:S(2)}, u32[]{:S(2)}) collective-permute-start(bf16[128,1536]{1,0:T(8,128)(2,1)S(1)} %fusion.5.own_x), channel_id=1, source_target_pairs={{0,1},{1,0},{2,3},{3,2},{4,5},{5,4},{6,7},{7,6},{8,9},{9,8},{10,11... | collective-permute-start | bytes 1179656 | tf_op jit(solution)/shard_map/ppermute | solution.py:38
  31.3 26.7 %collective-permute-start.11 = (bf16[384,1536]{1,0:T(8,128)(2,1)S(1)}, bf16[384,1536]{1,0:T(8,128)(2,1)S(1)}, u32[]{:S(2)}, u32[]{:S(2)}) collective-permute-start(bf16[384,1536]{1,0:T(8,128)(2,1)S(1)} %pad_maximum_fusion.refs_0_), channel_id=1, source_target_pairs={{0,12},{1,13},{2,14},{3,15},{4,0},{5,1},{6,2},{7,3},{8,4},{9,5},{1... | collective-permute-start | bytes 3538952 | tf_op jit(solution)/shard_map/ppermute | solution.py:54
  34.3 31.2 %collective-permute-start.12 = (bf16[384,1536]{1,0:T(8,128)(2,1)S(1)}, bf16[384,1536]{1,0:T(8,128)(2,1)}, u32[]{:S(2)}, u32[]{:S(2)}) collective-permute-start(bf16[384,1536]{1,0:T(8,128)(2,1)S(1)} %pad_maximum_fusion.refs_0_), channel_id=1, source_target_pairs={{0,2},{1,3},{2,0},{3,1},{4,6},{5,7},{6,4},{7,5},{8,10},{9,11},{10,... | collective-permute-start | bytes 3538952 | tf_op jit(solution)/shard_map/ppermute | solution.py:38
  36.6 26.9 %collective-permute-start.10 = (bf16[384,1536]{1,0:T(8,128)(2,1)S(1)}, bf16[384,1536]{1,0:T(8,128)(2,1)}, u32[]{:S(2)}, u32[]{:S(2)}) collective-permute-start(bf16[384,1536]{1,0:T(8,128)(2,1)S(1)} %pad_maximum_fusion.refs_0_), channel_id=1, source_target_pairs={{0,4},{1,5},{2,6},{3,7},{4,8},{5,9},{6,10},{7,11},{8,12},{9,13},{1... | collective-permute-start | bytes 3538952 | tf_op jit(solution)/shard_map/ppermute | solution.py:54
  40.8 1.8 %collective-permute-start.9 = (bf16[8,144,128]{2,1,0:T(8,128)(2,1)}, bf16[8,144,128]{2,1,0:T(8,128)(2,1)S(1)}, u32[]{:S(2)}, u32[]{:S(2)}) collective-permute-start(bf16[8,144,128]{2,1,0:T(8,128)(2,1)} %get-tuple-element.38), channel_id=1, source_target_pairs={{0,1},{1,0},{2,3},{3,2},{4,5},{5,4},{6,7},{7,6},{8,9},{9,8},{10,11... | collective-permute-start | bytes 884744 | tf_op jit(solution)/shard_map/ppermute | solution.py:38
  44.5 25.0 %slice-start = ((s8[4718592]{0:T(1024)(128)(4,1)}), s8[524288]{0:T(1024)(128)(4,1)S(1)}, s32[]{:S(2)}) async-start(s8[4718592]{0:T(1024)(128)(4,1)} %bitcast.42), calls=%async_computation.2 | async-start | bytes 1048576
  44.5 29.0 %all-to-all-start = ((bf16[16,192,128]{2,1,0:T(8,128)(2,1)}), bf16[16,192,128]{2,1,0:T(8,128)(2,1)}, u32[]{:S(2)}, u32[]{:S(2)}) async-start(bf16[16,192,128]{2,1,0:T(8,128)(2,1)} %place_heads.1), calls=%async_computation | async-start | bytes 1572864 | tf_op jit(solution)/shard_map/all_to_all | solution.py:535
  59.0 27.0 %collective-permute-start.14 = (bf16[192,1536]{1,0:T(8,128)(2,1)}, bf16[192,1536]{1,0:T(8,128)(2,1)S(1)}, u32[]{:S(2)}, u32[]{:S(2)}) collective-permute-start(bf16[192,1536]{1,0:T(8,128)(2,1)} %slice.54), channel_id=1, source_target_pairs={{0,12},{1,13},{2,14},{3,15},{4,0},{5,1},{6,2},{7,3},{8,4},{9,5},{1... | collective-permute-start | bytes 1769480 | tf_op jit(solution)/shard_map/ppermute | solution.py:54
  65.5 20.5 %collective-permute-start.13 = (bf16[192,1536]{1,0:T(8,128)(2,1)}, bf16[192,1536]{1,0:T(8,128)(2,1)}, u32[]{:S(2)}, u32[]{:S(2)}) collective-permute-start(bf16[192,1536]{1,0:T(8,128)(2,1)} %slice.62), channel_id=1, source_target_pairs={{0,4},{1,5},{2,6},{3,7},{4,8},{5,9},{6,10},{7,11},{8,12},{9,13},{1... | collective-permute-start | bytes 1769480 | tf_op jit(solution)/shard_map/ppermute | solution.py:54
  65.5 38.8 %collective-permute-start.16 = (bf16[384,1536]{1,0:T(8,128)(2,1)}, bf16[384,1536]{1,0:T(8,128)(2,1)}, u32[]{:S(2)}, u32[]{:S(2)}) collective-permute-start(bf16[384,1536]{1,0:T(8,128)(2,1)} %collective-permute-done.12.refs_2_.refs_3_), channel_id=1, source_target_pairs={{0,4},{1,5},{2,6},{3,7},{4,8},{5,9},{6,10},{7,11},{8,12},{9,13},{1... | collective-permute-start | bytes 3538952 | tf_op jit(solution)/shard_map/ppermute | solution.py:54
  65.6 40.5 %collective-permute-start.17 = (bf16[384,1536]{1,0:T(8,128)(2,1)}, bf16[384,1536]{1,0:T(8,128)(2,1)}, u32[]{:S(2)}, u32[]{:S(2)}) collective-permute-start(bf16[384,1536]{1,0:T(8,128)(2,1)} %collective-permute-done.12.refs_2_.refs_3_), channel_id=1, source_target_pairs={{0,12},{1,13},{2,14},{3,15},{4,0},{5,1},{6,2},{7,3},{8,4},{9,5},{1... | collective-permute-start | bytes 3538952 | tf_op jit(solution)/shard_map/ppermute | solution.py:54
  70.4 26.9 %copy-start.12 = (bf16[144,512]{1,0:T(8,128)(2,1)S(1)}, bf16[144,512]{1,0:T(8,128)(2,1)}, u32[]{:S(2)}) copy-start(bf16[144,512]{1,0:T(8,128)(2,1)} %param.30) | copy-start | bytes 442372
  70.4 28.2 %copy-start.16 = (f32[1,4,2048]{2,1,0:T(4,128)S(1)}, f32[1,4,2048]{2,1,0:T(4,128)}, u32[]{:S(2)}) copy-start(f32[1,4,2048]{2,1,0:T(4,128)} %param.18) | copy-start | bytes 98308
  86.0 26.1 %collective-permute-start.15 = (bf16[192,1536]{1,0:T(8,128)(2,1)}, bf16[192,1536]{1,0:T(8,128)(2,1)}, u32[]{:S(2)}, u32[]{:S(2)}) collective-permute-start(bf16[192,1536]{1,0:T(8,128)(2,1)} %collective-permute-done.13.refs_4_), channel_id=1, source_target_pairs={{0,2},{1,3},{2,0},{3,1},{4,6},{5,7},{6,4},{7,5},{8,10},{9,11},{10,... | collective-permute-start | bytes 1769480 | tf_op jit(solution)/shard_map/ppermute | solution.py:38
  88.0 23.1 %all-to-all-start.1 = ((bf16[16,64,128]{2,1,0:T(8,128)(2,1)}), bf16[16,64,128]{2,1,0:T(8,128)(2,1)}, u32[]{:S(2)}, u32[]{:S(2)}) async-start(bf16[16,64,128]{2,1,0:T(8,128)(2,1)} %attend.1), calls=%async_computation.1 | async-start | bytes 524288 | tf_op jit(solution)/shard_map/all_to_all | solution.py:550
  106.1 8.2 %collective-permute-start.18 = (bf16[96,1536]{1,0:T(8,128)(2,1)}, bf16[96,1536]{1,0:T(8,128)(2,1)}, u32[]{:S(2)}, u32[]{:S(2)}) collective-permute-start(bf16[96,1536]{1,0:T(8,128)(2,1)} %slice.66), channel_id=1, source_target_pairs={{0,4},{1,5},{2,6},{3,7},{4,8},{5,9},{6,10},{7,11},{8,12},{9,13},{1... | collective-permute-start | bytes 884744 | tf_op jit(solution)/shard_map/ppermute | solution.py:54
  107.8 7.8 %collective-permute-start.19 = (bf16[96,1536]{1,0:T(8,128)(2,1)}, bf16[96,1536]{1,0:T(8,128)(2,1)}, u32[]{:S(2)}, u32[]{:S(2)}) collective-permute-start(bf16[96,1536]{1,0:T(8,128)(2,1)} %slice.67), channel_id=1, source_target_pairs={{0,12},{1,13},{2,14},{3,15},{4,0},{5,1},{6,2},{7,3},{8,4},{9,5},{1... | collective-permute-start | bytes 884744 | tf_op jit(solution)/shard_map/ppermute | solution.py:54
  118.7 1.7 %collective-permute-start.20 = (bf16[128,1536]{1,0:T(8,128)(2,1)S(1)}, bf16[128,1536]{1,0:T(8,128)(2,1)S(1)}, u32[]{:S(2)}, u32[]{:S(2)}) collective-permute-start(bf16[128,1536]{1,0:T(8,128)(2,1)S(1)} %get-tuple-element.49.own_x), channel_id=1, source_target_pairs={{0,1},{1,0},{2,3},{3,2},{4,5},{5,4},{6,7},{7,6},{8,9},{9,8},{10,11... | collective-permute-start | bytes 1179656 | tf_op jit(solution)/shard_map/ppermute | solution.py:38
  124.0 2.4 %collective-permute-start.21 = (bf16[8,192,256]{2,1,0:T(8,128)(2,1)S(1)}, bf16[8,192,256]{2,1,0:T(8,128)(2,1)S(1)}, u32[]{:S(2)}, u32[]{:S(2)}) collective-permute-start(bf16[8,192,256]{2,1,0:T(8,128)(2,1)S(1)} %mlp_first.1.own_act), channel_id=1, source_target_pairs={{0,1},{1,0},{2,3},{3,2},{4,5},{5,4},{6,7},{7,6},{8,9},{9,8},{10,11... | collective-permute-start | bytes 2359304 | tf_op jit(solution)/shard_map/ppermute | solution.py:38
  130.6 1.9 %collective-permute-start.22 = (f32[8,96,128]{2,1,0:T(8,128)}, f32[8,96,128]{2,1,0:T(8,128)S(1)}, u32[]{:S(2)}, u32[]{:S(2)}) collective-permute-start(f32[8,96,128]{2,1,0:T(8,128)} %get-tuple-element.52), channel_id=1, source_target_pairs={{0,1},{1,0},{2,3},{3,2},{4,5},{5,4},{6,7},{7,6},{8,9},{9,8},{10,11... | collective-permute-start | bytes 1179656 | tf_op jit(solution)/shard_map/ppermute | solution.py:38
  132.5 15.7 %copy-start.11 = (f32[512]{0:T(512)S(1)}, f32[512]{0:T(512)}, u32[]{:S(2)}) copy-start(f32[512]{0:T(512)} %param.31) | copy-start | bytes 6148
  134.7 9.8 %collective-permute-start.23 = (bf16[64,32]{1,0:T(8,128)(2,1)S(1)}, bf16[64,32]{1,0:T(8,128)(2,1)S(1)}, u32[]{:S(2)}, u32[]{:S(2)}) collective-permute-start(bf16[64,32]{1,0:T(8,128)(2,1)S(1)} %get-tuple-element.58), channel_id=1, source_target_pairs={{0,16},{16,32},{32,48},{48,64},{64,80},{80,96},{96,112},{112,128},... | collective-permute-start | bytes 12296 | tf_op jit(solution)/shard_map/ppermute | solution.py:574
  140.5 7.7 %collective-permute-start.24 = (bf16[64,32]{1,0:T(8,128)(2,1)S(1)}, bf16[64,32]{1,0:T(8,128)(2,1)S(1)}, u32[]{:S(2)}, u32[]{:S(2)}) collective-permute-start(bf16[64,32]{1,0:T(8,128)(2,1)S(1)} %get-tuple-element.59), channel_id=1, source_target_pairs={{16,0},{32,16},{48,32},{64,48},{80,64},{96,80},{112,96},{128,112},... | collective-permute-start | bytes 12296 | tf_op jit(solution)/shard_map/ppermute | solution.py:575
  (14 other events, 104.1 us)

commit v12 on v11

--- a/solution.py
+++ b/solution.py
@@ -244,7 +244,7 @@
         out[2 * t + 1] = turned[:, rows:]
         return carry
 
-    lax.fori_loop(0, blocks // 2, step, 0)
+    lax.fori_loop(0, blocks // 2, step, 0, unroll=2)
 
 
 def attend(count, parts, text, mark):

time: 152 us -> 152 us (level)
  waiting for transfers between devices: 38.1 us -> 40 us
  Pallas kernels: 34 us -> 32.2 us
    ppermute x14, waiting for transfers between devices: 25 us -> 26.8 us  [ring(): return lax.ppermute(x, axis, [(i, (i + step) % size) for i in range(size)])]
    pallas_call x1, Pallas kernels: 12.5 us -> 10.6 us  [attend(): pl.pallas_call(attend_body, out_shape=jax.ShapeDtypeStruct((blocks, HEAD,...]
  transfers between devices with their start and end apart: 27 -> 27, of which waited for: 15 -> 15; matrix products, arithmetic and copies ran while one was open for 11% -> 11% of each run, Pallas kernels for 13% -> 12%
where the time goes in v12:
time: 152 us; the launch traced here: 150 us
  starting transfers between devices  57.7 us (38%)
  waiting for transfers between devices  40 us (26%)
  Pallas kernels  32.2 us (21%)
  local copies, waits for them, and re-layouts  15.2 us (10%)
  other arithmetic  2.58 us (2%)
  between operations  2.41 us (2%)
    ppermute x14, waiting for transfers between devices, ring(): return lax.ppermute(x, axis, [(i, (i + step) % size) for i in range(size)])  26.8 us
    ppermute x14, starting transfers between devices, ring(): return lax.ppermute(x, axis, [(i, (i + step) % size) for i in range(size)])  23.2 us
    pallas_call x1, Pallas kernels, attend(): pl.pallas_call(attend_body, out_shape=jax.ShapeDtypeStruct((blocks, HEAD,...  10.6 us
    all_to_all x1, starting transfers between devices, per_device(): lax.all_to_all(mixed, 'blk', 0, 0, tiled=True)[:HEADS]  9.28 us
    all_to_all x1, starting transfers between devices, per_device(): parts = lax.all_to_all(heads, 'blk', 0, 0, tiled=True)  8.72 us
    ppermute x9, starting transfers between devices, swap(): lax.ppermute(x, axis, [(i, i ^ bits) for i in range(lax.axis_size(axis))])  8.69 us
    ppermute x9, waiting for transfers between devices, swap(): lax.ppermute(x, axis, [(i, i ^ bits) for i in range(lax.axis_size(axis))])  6.3 us
    ppermute x1, starting transfers between devices, per_device(): before = lax.ppermute(bottom, 'blk', [(i, i + 1) for i in range(size - 1)])  5.83 us
  transfers between devices with their start and end apart: 27, of which 15 were waited for; matrix products, arithmetic and copies ran while one was open for 11% of the time, Pallas kernels for 12%

profile of v12, /device:TPU:104, one launch (start us, length us, event | category | flops | bytes accessed | tf_op | source)
XLA Modules:
  0.0 149.9 jit_solution(8688080657189364786)
XLA Ops:
  2.2 1.7 %collective-permute-start.2 = (bf16[144,1536]{1,0:T(8,128)(2,1)}, bf16[144,1536]{1,0:T(8,128)(2,1)S(1)}, u32[]{:S(2)}, u32[]{:S(2)}) collective-permute-start(bf16[144,1536]{1,0:T(8,128)(2,1)} %bitcast.48), channel_id=1, source_target_pairs={{0,12},{1,13},{2,14},{3,15},{4,0},{5,1},{6,2},{7,3},{8,4},{9,5},{1... | collective-permute-start | bytes 1327112 | tf_op jit(solution)/shard_map/ppermute | solution.py:54
  4.7 2.4 %collective-permute-start.6 = (bf16[144,1536]{1,0:T(8,128)(2,1)}, bf16[144,1536]{1,0:T(8,128)(2,1)S(1)}, u32[]{:S(2)}, u32[]{:S(2)}) collective-permute-start(bf16[144,1536]{1,0:T(8,128)(2,1)} %bitcast.49), channel_id=1, source_target_pairs={{0,2},{1,3},{2,0},{3,1},{4,6},{5,7},{6,4},{7,5},{8,10},{9,11},{10,... | collective-permute-start | bytes 1327112 | tf_op jit(solution)/shard_map/ppermute | solution.py:38
  9.7 4.4 %collective-permute-done.refs_1_ = bf16[144,1536]{1,0:T(8,128)(2,1)S(1)} collective-permute-done((bf16[144,1536]{1,0:T(8,128)(2,1)}, bf16[144,1536]{1,0:T(8,128)(2,1)S(1)}, u32[]{:S(2)}, u32[]{:S(2)}) %collective-permute-start) | collective-permute-done | bytes 442400 | tf_op jit(solution)/shard_map/ppermute | solution.py:54
  14.5 3.0 %collective-permute-start.3 = (bf16[72,1536]{1,0:T(8,128)(2,1)S(1)}, bf16[72,1536]{1,0:T(8,128)(2,1)S(1)}, u32[]{:S(2)}, u32[]{:S(2)}) collective-permute-start(bf16[72,1536]{1,0:T(8,128)(2,1)S(1)} %slice.61), channel_id=1, source_target_pairs={{0,12},{1,13},{2,14},{3,15},{4,0},{5,1},{6,2},{7,3},{8,4},{9,5},{1... | collective-permute-start | bytes 663560 | tf_op jit(solution)/shard_map/ppermute | solution.py:54
  18.1 3.0 %collective-permute-start.8 = (bf16[144,1536]{1,0:T(8,128)(2,1)S(1)}, bf16[144,1536]{1,0:T(8,128)(2,1)}, u32[]{:S(2)}, u32[]{:S(2)}) collective-permute-start(bf16[144,1536]{1,0:T(8,128)(2,1)S(1)} %collective-permute-done.6.refs_3_), channel_id=1, source_target_pairs={{0,12},{1,13},{2,14},{3,15},{4,0},{5,1},{6,2},{7,3},{8,4},{9,5},{1... | collective-permute-start | bytes 1327112 | tf_op jit(solution)/shard_map/ppermute | solution.py:54
  21.1 2.2 %collective-permute-done.1 = bf16[72,1536]{1,0:T(8,128)(2,1)S(1)} collective-permute-done((bf16[72,1536]{1,0:T(8,128)(2,1)S(1)}, bf16[72,1536]{1,0:T(8,128)(2,1)S(1)}, u32[]{:S(2)}, u32[]{:S(2)}) %collective-permute-start.1) | collective-permute-done | bytes 221216 | tf_op jit(solution)/shard_map/ppermute | solution.py:54
  24.7 2.3 %collective-permute-start.4 = (bf16[144,1536]{1,0:T(8,128)(2,1)}, bf16[144,1536]{1,0:T(8,128)(2,1)}, u32[]{:S(2)}, u32[]{:S(2)}) collective-permute-start(bf16[144,1536]{1,0:T(8,128)(2,1)} %constant_dynamic-update-slice_fusion.refs_4_), channel_id=1, source_target_pairs={{0,2},{1,3},{2,0},{3,1},{4,6},{5,7},{6,4},{7,5},{8,10},{9,11},{10,... | collective-permute-start | bytes 1327112 | tf_op jit(solution)/shard_map/ppermute | solution.py:38
  27.4 3.8 %collective-permute-done.7.refs_5_ = bf16[144,1536]{1,0:T(8,128)(2,1)} collective-permute-done((bf16[144,1536]{1,0:T(8,128)(2,1)S(1)}, bf16[144,1536]{1,0:T(8,128)(2,1)}, u32[]{:S(2)}, u32[]{:S(2)}) %collective-permute-start.7) | collective-permute-done | bytes 442400 | tf_op jit(solution)/shard_map/ppermute | solution.py:54
  31.3 3.0 %collective-permute-start.11 = (bf16[384,1536]{1,0:T(8,128)(2,1)S(1)}, bf16[384,1536]{1,0:T(8,128)(2,1)S(1)}, u32[]{:S(2)}, u32[]{:S(2)}) collective-permute-start(bf16[384,1536]{1,0:T(8,128)(2,1)S(1)} %pad_maximum_fusion.refs_0_), channel_id=1, source_target_pairs={{0,12},{1,13},{2,14},{3,15},{4,0},{5,1},{6,2},{7,3},{8,4},{9,5},{1... | collective-permute-start | bytes 3538952 | tf_op jit(solution)/shard_map/ppermute | solution.py:54
  34.3 2.3 %collective-permute-start.12 = (bf16[384,1536]{1,0:T(8,128)(2,1)S(1)}, bf16[384,1536]{1,0:T(8,128)(2,1)}, u32[]{:S(2)}, u32[]{:S(2)}) collective-permute-start(bf16[384,1536]{1,0:T(8,128)(2,1)S(1)} %pad_maximum_fusion.refs_0_), channel_id=1, source_target_pairs={{0,2},{1,3},{2,0},{3,1},{4,6},{5,7},{6,4},{7,5},{8,10},{9,11},{10,... | collective-permute-start | bytes 3538952 | tf_op jit(solution)/shard_map/ppermute | solution.py:38
  37.4 3.5 %project_qkv.1 = (bf16[8,144,128]{2,1,0:T(8,128)(2,1)}, bf16[8,144,128]{2,1,0:T(8,128)(2,1)}) custom-call(s32[1]{0:T(128)} %bitcast.2.chip_ref, bf16[16,128]{1,0:T(8,128)(2,1)S(1)} %marker.3.ready, bf16[128,1536]{1,0:T(8,128)(2,1)S(1)} %fusion.5.own_x, bf16[128,1536]{1,0:T(8,128)(2,1)} %collective-permute-done.5.peer_x, bf16[144,1536]{1,0:T(8,128)(2,1)S(1)} %bitcast.50, ...), custom_call_target="tpu_custom_call" | custom-call | flops 1000 | bytes 1000 | tf_op jit(solution)/shard_map/project_qkv/pallas_call | solution.py:96
  42.6 1.9 %place_heads.1 = bf16[16,192,128]{2,1,0:T(8,128)(2,1)} custom-call(s32[1]{0:T(128)} %bitcast.core_ref, bf16[8,144,128]{2,1,0:T(8,128)(2,1)} %get-tuple-element.37.mine, bf16[8,144,128]{2,1,0:T(8,128)(2,1)S(1)} %collective-permute-done.9.other), custom_call_target="tpu_custom_call" | custom-call | flops 1000 | bytes 1000 | tf_op jit(solution)/shard_map/place_heads/pallas_call | solution.py:138
  44.5 8.7 %all-to-all-start = ((bf16[16,192,128]{2,1,0:T(8,128)(2,1)}), bf16[16,192,128]{2,1,0:T(8,128)(2,1)}, u32[]{:S(2)}, u32[]{:S(2)}) async-start(bf16[16,192,128]{2,1,0:T(8,128)(2,1)} %place_heads.1), calls=%async_computation | async-start | bytes 1572864 | tf_op jit(solution)/shard_map/all_to_all | solution.py:535
  53.3 4.8 %collective-permute-done.11.refs_1_.refs_2_ = bf16[384,1536]{1,0:T(8,128)(2,1)S(1)} collective-permute-done((bf16[384,1536]{1,0:T(8,128)(2,1)S(1)}, bf16[384,1536]{1,0:T(8,128)(2,1)S(1)}, u32[]{:S(2)}, u32[]{:S(2)}) %collective-permute-start.11) | collective-permute-done | bytes 1179680 | tf_op jit(solution)/shard_map/ppermute | solution.py:54
  59.0 3.7 %collective-permute-start.14 = (bf16[192,1536]{1,0:T(8,128)(2,1)}, bf16[192,1536]{1,0:T(8,128)(2,1)S(1)}, u32[]{:S(2)}, u32[]{:S(2)}) collective-permute-start(bf16[192,1536]{1,0:T(8,128)(2,1)} %slice.54), channel_id=1, source_target_pairs={{0,12},{1,13},{2,14},{3,15},{4,0},{5,1},{6,2},{7,3},{8,4},{9,5},{1... | collective-permute-start | bytes 1769480 | tf_op jit(solution)/shard_map/ppermute | solution.py:54
  63.6 1.9 %slice.62 = bf16[192,1536]{1,0:T(8,128)(2,1)} slice(bf16[384,1536]{1,0:T(8,128)(2,1)} %collective-permute-done.10.refs_0_.refs_1_), slice={[0:192], [0:1536]} | slice | bytes 1179648 | tf_op jit(solution)/shard_map/slice | solution.py:64
  65.6 3.2 %collective-permute-start.17 = (bf16[384,1536]{1,0:T(8,128)(2,1)}, bf16[384,1536]{1,0:T(8,128)(2,1)}, u32[]{:S(2)}, u32[]{:S(2)}) collective-permute-start(bf16[384,1536]{1,0:T(8,128)(2,1)} %collective-permute-done.12.refs_2_.refs_3_), channel_id=1, source_target_pairs={{0,12},{1,13},{2,14},{3,15},{4,0},{5,1},{6,2},{7,3},{8,4},{9,5},{1... | collective-permute-start | bytes 3538952 | tf_op jit(solution)/shard_map/ppermute | solution.py:54
  70.4 3.1 %all-to-all-done.parts = bf16[16,192,128]{2,1,0:T(8,128)(2,1)} async-done(((bf16[16,192,128]{2,1,0:T(8,128)(2,1)}), bf16[16,192,128]{2,1,0:T(8,128)(2,1)}, u32[]{:S(2)}, u32[]{:S(2)}) %all-to-all-start) | async-done | bytes 786464 | tf_op jit(solution)/shard_map/all_to_all | solution.py:535
  73.5 10.6 %attend.1 = bf16[16,64,128]{2,1,0:T(8,128)(2,1)} custom-call(s32[1]{0:T(128)S(6)} %copy.32.count_ref, bf16[16,192,128]{2,1,0:T(8,128)(2,1)} %all-to-all-done.parts, bf16[128,256]{1,0:T(8,128)(2,1)S(1)} %text_keys.1.text, bf16[16,128]{1,0:T(8,128)(2,1)S(1)} %marker.4.mark), custom_call_target="tpu_custom_call" | custom-call | flops 1000 | bytes 1000 | tf_op jit(solution)/shard_map/attend/pallas_call | solution.py:254
  86.1 9.3 %all-to-all-start.1 = ((bf16[16,64,128]{2,1,0:T(8,128)(2,1)}), bf16[16,64,128]{2,1,0:T(8,128)(2,1)}, u32[]{:S(2)}, u32[]{:S(2)}) async-start(bf16[16,64,128]{2,1,0:T(8,128)(2,1)} %attend.1), calls=%async_computation.1 | async-start | bytes 524288 | tf_op jit(solution)/shard_map/all_to_all | solution.py:550
  97.1 7.3 %collective-permute-done.16.refs_1_.refs_5_ = bf16[384,1536]{1,0:T(8,128)(2,1)} collective-permute-done((bf16[384,1536]{1,0:T(8,128)(2,1)}, bf16[384,1536]{1,0:T(8,128)(2,1)}, u32[]{:S(2)}, u32[]{:S(2)}) %collective-permute-start.16) | collective-permute-done | bytes 1179680 | tf_op jit(solution)/shard_map/ppermute | solution.py:54
  107.8 3.2 %collective-permute-start.19 = (bf16[96,1536]{1,0:T(8,128)(2,1)}, bf16[96,1536]{1,0:T(8,128)(2,1)}, u32[]{:S(2)}, u32[]{:S(2)}) collective-permute-start(bf16[96,1536]{1,0:T(8,128)(2,1)} %slice.67), channel_id=1, source_target_pairs={{0,12},{1,13},{2,14},{3,15},{4,0},{5,1},{6,2},{7,3},{8,4},{9,5},{1... | collective-permute-start | bytes 884744 | tf_op jit(solution)/shard_map/ppermute | solution.py:54
  112.1 2.2 %collective-permute-done.18.refs_3_.refs_7_ = bf16[96,1536]{1,0:T(8,128)(2,1)} collective-permute-done((bf16[96,1536]{1,0:T(8,128)(2,1)}, bf16[96,1536]{1,0:T(8,128)(2,1)}, u32[]{:S(2)}, u32[]{:S(2)}) %collective-permute-start.18) | collective-permute-done | bytes 294944 | tf_op jit(solution)/shard_map/ppermute | solution.py:54
  118.7 1.7 %collective-permute-done.20.peer_x = bf16[128,1536]{1,0:T(8,128)(2,1)S(1)} collective-permute-done((bf16[128,1536]{1,0:T(8,128)(2,1)S(1)}, bf16[128,1536]{1,0:T(8,128)(2,1)S(1)}, u32[]{:S(2)}, u32[]{:S(2)}) %collective-permute-start.20) | collective-permute-done | bytes 393248 | tf_op jit(solution)/shard_map/ppermute | solution.py:38
  120.4 3.6 %mlp_first.1.own_act = bf16[8,192,256]{2,1,0:T(8,128)(2,1)S(1)} custom-call(s32[1]{0:T(128)} %bitcast.2.chip_ref, bf16[128,1536]{1,0:T(8,128)(2,1)S(1)} %get-tuple-element.49.own_x, bf16[128,1536]{1,0:T(8,128)(2,1)S(1)} %collective-permute-done.20.peer_x, bf16[384,1536]{1,0:T(8,128)(2,1)S(1)} %pad_maximum_fusion.refs_0_, ...), custom_call_target="tpu_custom_call" | custom-call | flops 1000 | bytes 1000 | tf_op jit(solution)/shard_map/mlp_first/pallas_call | solution.py:326
  124.2 2.1 %collective-permute-done.21.peer_act = bf16[8,192,256]{2,1,0:T(8,128)(2,1)S(1)} collective-permute-done((bf16[8,192,256]{2,1,0:T(8,128)(2,1)S(1)}, bf16[8,192,256]{2,1,0:T(8,128)(2,1)S(1)}, u32[]{:S(2)}, u32[]{:S(2)}) %collective-permute-start.21) | collective-permute-done | bytes 786464 | tf_op jit(solution)/shard_map/ppermute | solution.py:38
  126.4 4.2 %mlp_second.1 = (f32[8,96,128]{2,1,0:T(8,128)}, f32[8,96,128]{2,1,0:T(8,128)}) custom-call(s32[1]{0:T(128)} %bitcast.2.chip_ref, s32[1]{0:T(128)} %bitcast.core_ref, bf16[8,192,256]{2,1,0:T(8,128)(2,1)S(1)} %mlp_first.1.own_act, bf16[8,192,256]{2,1,0:T(8,128)(2,1)S(1)} %collective-permute-done.21.peer_act, bf16[384,1536]{1,0:T(8,128)(2,1)S(1)} %pad_maximum_fusion.refs_0_, ...), custom_call_target="tpu_custom_call" | custom-call | flops 1000 | bytes 1000 | tf_op jit(solution)/shard_map/mlp_second/pallas_call | solution.py:366
  132.5 2.1 %last.1 = (f32[128,64]{1,0:T(8,128)S(1)}, f32[128,64]{1,0:T(8,128)S(1)}, bf16[128,64]{1,0:T(8,128)(2,1)S(1)}, bf16[64,32]{1,0:T(8,128)(2,1)S(1)}, bf16[64,32]{1,0:T(8,128)(2,1)S(1)}) custom-call(s32[1]{0:T(128)} %bitcast.core_ref, s32[1]{0:T(128)S(6)} %convert_element_type.12.live_ref, f32[1]{0:T(128)S(6)} %sub.27.gap_ref, ...), custom_call_target="tpu_custom_call" | custom-call | flops 1000 | bytes 1000 | tf_op jit(solution)/shard_map/last/pallas_call | solution.py:417
  134.7 5.8 %collective-permute-start.23 = (bf16[64,32]{1,0:T(8,128)(2,1)S(1)}, bf16[64,32]{1,0:T(8,128)(2,1)S(1)}, u32[]{:S(2)}, u32[]{:S(2)}) collective-permute-start(bf16[64,32]{1,0:T(8,128)(2,1)S(1)} %get-tuple-element.58), channel_id=1, source_target_pairs={{0,16},{16,32},{32,48},{48,64},{64,80},{80,96},{96,112},{112,128},... | collective-permute-start | bytes 12296 | tf_op jit(solution)/shard_map/ppermute | solution.py:574
  140.5 1.9 %collective-permute-start.24 = (bf16[64,32]{1,0:T(8,128)(2,1)S(1)}, bf16[64,32]{1,0:T(8,128)(2,1)S(1)}, u32[]{:S(2)}, u32[]{:S(2)}) collective-permute-start(bf16[64,32]{1,0:T(8,128)(2,1)S(1)} %get-tuple-element.59), channel_id=1, source_target_pairs={{16,0},{32,16},{48,32},{64,48},{80,64},{96,80},{112,96},{128,112},... | collective-permute-start | bytes 12296 | tf_op jit(solution)/shard_map/ppermute | solution.py:575
  144.5 3.7 %collective-permute-done.24.after = bf16[64,32]{1,0:T(8,128)(2,1)S(1)} collective-permute-done((bf16[64,32]{1,0:T(8,128)(2,1)S(1)}, bf16[64,32]{1,0:T(8,128)(2,1)S(1)}, u32[]{:S(2)}, u32[]{:S(2)}) %collective-permute-start.24) | collective-permute-done | bytes 4128 | tf_op jit(solution)/shard_map/ppermute | solution.py:575
  148.2 1.7 %convolve.1 = bf16[4,128,512]{2,1,0:T(8,128)(2,1)} custom-call(s32[1]{0:T(128)S(6)} %convert_element_type.12.live_ref, bf16[128,64]{1,0:T(8,128)(2,1)S(1)} %get-tuple-element.57.scaled, bf16[64,32]{1,0:T(8,128)(2,1)S(1)} %collective-permute-done.23.before, bf16[64,32]{1,0:T(8,128)(2,1)S(1)} %collective-permute-done.24.after, ...), custom_call_target="tpu_custom_call" | custom-call | flops 1000 | bytes 1000 | tf_op jit(solution)/shard_map/convolve/pallas_call | solution.py:467
  (108 shorter events, 29.0 us)
Async XLA Ops:
  0.7 13.4 %collective-permute-start = (bf16[144,1536]{1,0:T(8,128)(2,1)}, bf16[144,1536]{1,0:T(8,128)(2,1)S(1)}, u32[]{:S(2)}, u32[]{:S(2)}) collective-permute-start(bf16[144,1536]{1,0:T(8,128)(2,1)} %bitcast.47), channel_id=1, source_target_pairs={{0,4},{1,5},{2,6},{3,7},{4,8},{5,9},{6,10},{7,11},{8,12},{9,13},{1... | collective-permute-start | bytes 1327112 | tf_op jit(solution)/shard_map/ppermute | solution.py:54
  2.2 12.2 %collective-permute-start.2 = (bf16[144,1536]{1,0:T(8,128)(2,1)}, bf16[144,1536]{1,0:T(8,128)(2,1)S(1)}, u32[]{:S(2)}, u32[]{:S(2)}) collective-permute-start(bf16[144,1536]{1,0:T(8,128)(2,1)} %bitcast.48), channel_id=1, source_target_pairs={{0,12},{1,13},{2,14},{3,15},{4,0},{5,1},{6,2},{7,3},{8,4},{9,5},{1... | collective-permute-start | bytes 1327112 | tf_op jit(solution)/shard_map/ppermute | solution.py:54
  4.7 13.1 %collective-permute-start.6 = (bf16[144,1536]{1,0:T(8,128)(2,1)}, bf16[144,1536]{1,0:T(8,128)(2,1)S(1)}, u32[]{:S(2)}, u32[]{:S(2)}) collective-permute-start(bf16[144,1536]{1,0:T(8,128)(2,1)} %bitcast.49), channel_id=1, source_target_pairs={{0,2},{1,3},{2,0},{3,1},{4,6},{5,7},{6,4},{7,5},{8,10},{9,11},{10,... | collective-permute-start | bytes 1327112 | tf_op jit(solution)/shard_map/ppermute | solution.py:38
  14.1 9.2 %collective-permute-start.1 = (bf16[72,1536]{1,0:T(8,128)(2,1)S(1)}, bf16[72,1536]{1,0:T(8,128)(2,1)S(1)}, u32[]{:S(2)}, u32[]{:S(2)}) collective-permute-start(bf16[72,1536]{1,0:T(8,128)(2,1)S(1)} %slice.60), channel_id=1, source_target_pairs={{0,4},{1,5},{2,6},{3,7},{4,8},{5,9},{6,10},{7,11},{8,12},{9,13},{1... | collective-permute-start | bytes 663560 | tf_op jit(solution)/shard_map/ppermute | solution.py:54
  14.4 16.8 %copy-start.3 = (bf16[144,1536]{1,0:T(8,128)(2,1)}, bf16[144,1536]{1,0:T(8,128)(2,1)S(1)}, u32[]{:S(2)}) copy-start(bf16[144,1536]{1,0:T(8,128)(2,1)S(1)} %collective-permute-done.2.refs_2_) | copy-start | bytes 1327108
  14.5 9.5 %collective-permute-start.3 = (bf16[72,1536]{1,0:T(8,128)(2,1)S(1)}, bf16[72,1536]{1,0:T(8,128)(2,1)S(1)}, u32[]{:S(2)}, u32[]{:S(2)}) collective-permute-start(bf16[72,1536]{1,0:T(8,128)(2,1)S(1)} %slice.61), channel_id=1, source_target_pairs={{0,12},{1,13},{2,14},{3,15},{4,0},{5,1},{6,2},{7,3},{8,4},{9,5},{1... | collective-permute-start | bytes 663560 | tf_op jit(solution)/shard_map/ppermute | solution.py:54
  17.9 13.4 %collective-permute-start.7 = (bf16[144,1536]{1,0:T(8,128)(2,1)S(1)}, bf16[144,1536]{1,0:T(8,128)(2,1)}, u32[]{:S(2)}, u32[]{:S(2)}) collective-permute-start(bf16[144,1536]{1,0:T(8,128)(2,1)S(1)} %collective-permute-done.6.refs_3_), channel_id=1, source_target_pairs={{0,4},{1,5},{2,6},{3,7},{4,8},{5,9},{6,10},{7,11},{8,12},{9,13},{1... | collective-permute-start | bytes 1327112 | tf_op jit(solution)/shard_map/ppermute | solution.py:54
  18.1 13.1 %collective-permute-start.8 = (bf16[144,1536]{1,0:T(8,128)(2,1)S(1)}, bf16[144,1536]{1,0:T(8,128)(2,1)}, u32[]{:S(2)}, u32[]{:S(2)}) collective-permute-start(bf16[144,1536]{1,0:T(8,128)(2,1)S(1)} %collective-permute-done.6.refs_3_), channel_id=1, source_target_pairs={{0,12},{1,13},{2,14},{3,15},{4,0},{5,1},{6,2},{7,3},{8,4},{9,5},{1... | collective-permute-start | bytes 1327112 | tf_op jit(solution)/shard_map/ppermute | solution.py:54
  24.7 11.9 %collective-permute-start.4 = (bf16[144,1536]{1,0:T(8,128)(2,1)}, bf16[144,1536]{1,0:T(8,128)(2,1)}, u32[]{:S(2)}, u32[]{:S(2)}) collective-permute-start(bf16[144,1536]{1,0:T(8,128)(2,1)} %constant_dynamic-update-slice_fusion.refs_4_), channel_id=1, source_target_pairs={{0,2},{1,3},{2,0},{3,1},{4,6},{5,7},{6,4},{7,5},{8,10},{9,11},{10,... | collective-permute-start | bytes 1327112 | tf_op jit(solution)/shard_map/ppermute | solution.py:38
  27.3 10.0 %collective-permute-start.5 = (bf16[128,1536]{1,0:T(8,128)(2,1)S(1)}, bf16[128,1536]{1,0:T(8,128)(2,1)}, u32[]{:S(2)}, u32[]{:S(2)}) collective-permute-start(bf16[128,1536]{1,0:T(8,128)(2,1)S(1)} %fusion.5.own_x), channel_id=1, source_target_pairs={{0,1},{1,0},{2,3},{3,2},{4,5},{5,4},{6,7},{7,6},{8,9},{9,8},{10,11... | collective-permute-start | bytes 1179656 | tf_op jit(solution)/shard_map/ppermute | solution.py:38
  31.3 26.7 %collective-permute-start.11 = (bf16[384,1536]{1,0:T(8,128)(2,1)S(1)}, bf16[384,1536]{1,0:T(8,128)(2,1)S(1)}, u32[]{:S(2)}, u32[]{:S(2)}) collective-permute-start(bf16[384,1536]{1,0:T(8,128)(2,1)S(1)} %pad_maximum_fusion.refs_0_), channel_id=1, source_target_pairs={{0,12},{1,13},{2,14},{3,15},{4,0},{5,1},{6,2},{7,3},{8,4},{9,5},{1... | collective-permute-start | bytes 3538952 | tf_op jit(solution)/shard_map/ppermute | solution.py:54
  34.3 31.2 %collective-permute-start.12 = (bf16[384,1536]{1,0:T(8,128)(2,1)S(1)}, bf16[384,1536]{1,0:T(8,128)(2,1)}, u32[]{:S(2)}, u32[]{:S(2)}) collective-permute-start(bf16[384,1536]{1,0:T(8,128)(2,1)S(1)} %pad_maximum_fusion.refs_0_), channel_id=1, source_target_pairs={{0,2},{1,3},{2,0},{3,1},{4,6},{5,7},{6,4},{7,5},{8,10},{9,11},{10,... | collective-permute-start | bytes 3538952 | tf_op jit(solution)/shard_map/ppermute | solution.py:38
  36.6 26.9 %collective-permute-start.10 = (bf16[384,1536]{1,0:T(8,128)(2,1)S(1)}, bf16[384,1536]{1,0:T(8,128)(2,1)}, u32[]{:S(2)}, u32[]{:S(2)}) collective-permute-start(bf16[384,1536]{1,0:T(8,128)(2,1)S(1)} %pad_maximum_fusion.refs_0_), channel_id=1, source_target_pairs={{0,4},{1,5},{2,6},{3,7},{4,8},{5,9},{6,10},{7,11},{8,12},{9,13},{1... | collective-permute-start | bytes 3538952 | tf_op jit(solution)/shard_map/ppermute | solution.py:54
  40.8 1.8 %collective-permute-start.9 = (bf16[8,144,128]{2,1,0:T(8,128)(2,1)}, bf16[8,144,128]{2,1,0:T(8,128)(2,1)S(1)}, u32[]{:S(2)}, u32[]{:S(2)}) collective-permute-start(bf16[8,144,128]{2,1,0:T(8,128)(2,1)} %get-tuple-element.38), channel_id=1, source_target_pairs={{0,1},{1,0},{2,3},{3,2},{4,5},{5,4},{6,7},{7,6},{8,9},{9,8},{10,11... | collective-permute-start | bytes 884744 | tf_op jit(solution)/shard_map/ppermute | solution.py:38
  44.5 25.0 %slice-start = ((s8[4718592]{0:T(1024)(128)(4,1)}), s8[524288]{0:T(1024)(128)(4,1)S(1)}, s32[]{:S(2)}) async-start(s8[4718592]{0:T(1024)(128)(4,1)} %bitcast.42), calls=%async_computation.2 | async-start | bytes 1048576
  44.5 29.0 %all-to-all-start = ((bf16[16,192,128]{2,1,0:T(8,128)(2,1)}), bf16[16,192,128]{2,1,0:T(8,128)(2,1)}, u32[]{:S(2)}, u32[]{:S(2)}) async-start(bf16[16,192,128]{2,1,0:T(8,128)(2,1)} %place_heads.1), calls=%async_computation | async-start | bytes 1572864 | tf_op jit(solution)/shard_map/all_to_all | solution.py:535
  59.0 25.2 %collective-permute-start.14 = (bf16[192,1536]{1,0:T(8,128)(2,1)}, bf16[192,1536]{1,0:T(8,128)(2,1)S(1)}, u32[]{:S(2)}, u32[]{:S(2)}) collective-permute-start(bf16[192,1536]{1,0:T(8,128)(2,1)} %slice.54), channel_id=1, source_target_pairs={{0,12},{1,13},{2,14},{3,15},{4,0},{5,1},{6,2},{7,3},{8,4},{9,5},{1... | collective-permute-start | bytes 1769480 | tf_op jit(solution)/shard_map/ppermute | solution.py:54
  65.5 18.6 %collective-permute-start.13 = (bf16[192,1536]{1,0:T(8,128)(2,1)}, bf16[192,1536]{1,0:T(8,128)(2,1)}, u32[]{:S(2)}, u32[]{:S(2)}) collective-permute-start(bf16[192,1536]{1,0:T(8,128)(2,1)} %slice.62), channel_id=1, source_target_pairs={{0,4},{1,5},{2,6},{3,7},{4,8},{5,9},{6,10},{7,11},{8,12},{9,13},{1... | collective-permute-start | bytes 1769480 | tf_op jit(solution)/shard_map/ppermute | solution.py:54
  65.5 38.8 %collective-permute-start.16 = (bf16[384,1536]{1,0:T(8,128)(2,1)}, bf16[384,1536]{1,0:T(8,128)(2,1)}, u32[]{:S(2)}, u32[]{:S(2)}) collective-permute-start(bf16[384,1536]{1,0:T(8,128)(2,1)} %collective-permute-done.12.refs_2_.refs_3_), channel_id=1, source_target_pairs={{0,4},{1,5},{2,6},{3,7},{4,8},{5,9},{6,10},{7,11},{8,12},{9,13},{1... | collective-permute-start | bytes 3538952 | tf_op jit(solution)/shard_map/ppermute | solution.py:54
  65.6 40.5 %collective-permute-start.17 = (bf16[384,1536]{1,0:T(8,128)(2,1)}, bf16[384,1536]{1,0:T(8,128)(2,1)}, u32[]{:S(2)}, u32[]{:S(2)}) collective-permute-start(bf16[384,1536]{1,0:T(8,128)(2,1)} %collective-permute-done.12.refs_2_.refs_3_), channel_id=1, source_target_pairs={{0,12},{1,13},{2,14},{3,15},{4,0},{5,1},{6,2},{7,3},{8,4},{9,5},{1... | collective-permute-start | bytes 3538952 | tf_op jit(solution)/shard_map/ppermute | solution.py:54
  70.4 25.0 %copy-start.12 = (bf16[144,512]{1,0:T(8,128)(2,1)S(1)}, bf16[144,512]{1,0:T(8,128)(2,1)}, u32[]{:S(2)}) copy-start(bf16[144,512]{1,0:T(8,128)(2,1)} %param.30) | copy-start | bytes 442372
  70.4 26.3 %copy-start.16 = (f32[1,4,2048]{2,1,0:T(4,128)S(1)}, f32[1,4,2048]{2,1,0:T(4,128)}, u32[]{:S(2)}) copy-start(f32[1,4,2048]{2,1,0:T(4,128)} %param.18) | copy-start | bytes 98308
  84.1 27.9 %collective-permute-start.15 = (bf16[192,1536]{1,0:T(8,128)(2,1)}, bf16[192,1536]{1,0:T(8,128)(2,1)}, u32[]{:S(2)}, u32[]{:S(2)}) collective-permute-start(bf16[192,1536]{1,0:T(8,128)(2,1)} %collective-permute-done.13.refs_4_), channel_id=1, source_target_pairs={{0,2},{1,3},{2,0},{3,1},{4,6},{5,7},{6,4},{7,5},{8,10},{9,11},{10,... | collective-permute-start | bytes 1769480 | tf_op jit(solution)/shard_map/ppermute | solution.py:38
  86.1 24.9 %all-to-all-start.1 = ((bf16[16,64,128]{2,1,0:T(8,128)(2,1)}), bf16[16,64,128]{2,1,0:T(8,128)(2,1)}, u32[]{:S(2)}, u32[]{:S(2)}) async-start(bf16[16,64,128]{2,1,0:T(8,128)(2,1)} %attend.1), calls=%async_computation.1 | async-start | bytes 524288 | tf_op jit(solution)/shard_map/all_to_all | solution.py:550
  106.1 8.2 %collective-permute-start.18 = (bf16[96,1536]{1,0:T(8,128)(2,1)}, bf16[96,1536]{1,0:T(8,128)(2,1)}, u32[]{:S(2)}, u32[]{:S(2)}) collective-permute-start(bf16[96,1536]{1,0:T(8,128)(2,1)} %slice.66), channel_id=1, source_target_pairs={{0,4},{1,5},{2,6},{3,7},{4,8},{5,9},{6,10},{7,11},{8,12},{9,13},{1... | collective-permute-start | bytes 884744 | tf_op jit(solution)/shard_map/ppermute | solution.py:54
  107.8 7.8 %collective-permute-start.19 = (bf16[96,1536]{1,0:T(8,128)(2,1)}, bf16[96,1536]{1,0:T(8,128)(2,1)}, u32[]{:S(2)}, u32[]{:S(2)}) collective-permute-start(bf16[96,1536]{1,0:T(8,128)(2,1)} %slice.67), channel_id=1, source_target_pairs={{0,12},{1,13},{2,14},{3,15},{4,0},{5,1},{6,2},{7,3},{8,4},{9,5},{1... | collective-permute-start | bytes 884744 | tf_op jit(solution)/shard_map/ppermute | solution.py:54
  118.7 1.7 %collective-permute-start.20 = (bf16[128,1536]{1,0:T(8,128)(2,1)S(1)}, bf16[128,1536]{1,0:T(8,128)(2,1)S(1)}, u32[]{:S(2)}, u32[]{:S(2)}) collective-permute-start(bf16[128,1536]{1,0:T(8,128)(2,1)S(1)} %get-tuple-element.49.own_x), channel_id=1, source_target_pairs={{0,1},{1,0},{2,3},{3,2},{4,5},{5,4},{6,7},{7,6},{8,9},{9,8},{10,11... | collective-permute-start | bytes 1179656 | tf_op jit(solution)/shard_map/ppermute | solution.py:38
  124.0 2.4 %collective-permute-start.21 = (bf16[8,192,256]{2,1,0:T(8,128)(2,1)S(1)}, bf16[8,192,256]{2,1,0:T(8,128)(2,1)S(1)}, u32[]{:S(2)}, u32[]{:S(2)}) collective-permute-start(bf16[8,192,256]{2,1,0:T(8,128)(2,1)S(1)} %mlp_first.1.own_act), channel_id=1, source_target_pairs={{0,1},{1,0},{2,3},{3,2},{4,5},{5,4},{6,7},{7,6},{8,9},{9,8},{10,11... | collective-permute-start | bytes 2359304 | tf_op jit(solution)/shard_map/ppermute | solution.py:38
  130.6 1.9 %collective-permute-start.22 = (f32[8,96,128]{2,1,0:T(8,128)}, f32[8,96,128]{2,1,0:T(8,128)S(1)}, u32[]{:S(2)}, u32[]{:S(2)}) collective-permute-start(f32[8,96,128]{2,1,0:T(8,128)} %get-tuple-element.52), channel_id=1, source_target_pairs={{0,1},{1,0},{2,3},{3,2},{4,5},{5,4},{6,7},{7,6},{8,9},{9,8},{10,11... | collective-permute-start | bytes 1179656 | tf_op jit(solution)/shard_map/ppermute | solution.py:38
  132.5 15.7 %copy-start.11 = (f32[512]{0:T(512)S(1)}, f32[512]{0:T(512)}, u32[]{:S(2)}) copy-start(f32[512]{0:T(512)} %param.31) | copy-start | bytes 6148
  134.7 9.8 %collective-permute-start.23 = (bf16[64,32]{1,0:T(8,128)(2,1)S(1)}, bf16[64,32]{1,0:T(8,128)(2,1)S(1)}, u32[]{:S(2)}, u32[]{:S(2)}) collective-permute-start(bf16[64,32]{1,0:T(8,128)(2,1)S(1)} %get-tuple-element.58), channel_id=1, source_target_pairs={{0,16},{16,32},{32,48},{48,64},{64,80},{80,96},{96,112},{112,128},... | collective-permute-start | bytes 12296 | tf_op jit(solution)/shard_map/ppermute | solution.py:574
  140.5 7.7 %collective-permute-start.24 = (bf16[64,32]{1,0:T(8,128)(2,1)S(1)}, bf16[64,32]{1,0:T(8,128)(2,1)S(1)}, u32[]{:S(2)}, u32[]{:S(2)}) collective-permute-start(bf16[64,32]{1,0:T(8,128)(2,1)S(1)} %get-tuple-element.59), channel_id=1, source_target_pairs={{16,0},{32,16},{48,32},{64,48},{80,64},{96,80},{112,96},{128,112},... | collective-permute-start | bytes 12296 | tf_op jit(solution)/shard_map/ppermute | solution.py:575
  (14 other events, 107.8 us)
